TPU v7x, 512 devices: a whole 4x8x8 slice. The times are simulated.
512 devices in a mesh: seq: 16 (over y, z_hi), tp: 32 (over z_lo, x, core).
Axes of the slice: x: 4, y: 8, z: 8 (z_hi: 2, z_lo: 4; z = z_hi * 4 + z_lo), core: 2. Of those that a mesh axis runs over, the one named last changes fastest.
Arguments:
- hidden_in: bfloat16 [4096, 5120], P('seq', 'tp'), may hold values from -16 to 16
- seg_ids: int32 [4096], P('seq'), may hold values from 0 to 3, never falling along the last dimension, each value on 1 to 2176 neighbouring positions
- positions: int32 [3, 4096], P(None, 'seq'), may hold values from 0 to 63
- mod_table: float32 [4, 3, 5120], P(None, None, 'tp'), may hold values from -4 to 4
- w_qkv: bfloat16 [5120, 3, 4096], P('seq', None, 'tp')
- q_gain: float32 [4096], P('tp'), may hold values from 0.5 to 3.5
- k_gain: float32 [4096], P('tp'), may hold values from 0.5 to 3.5
- w_out: bfloat16 [4096, 5120], P('tp', 'seq'), may hold values from -0.1875 to 0.1875
Outputs:
- hidden_out: bfloat16 [4096, 5120], P('seq', 'tp')
- k_cache: bfloat16 [4096, 4096], P('seq', 'tp')
- v_cache: bfloat16 [4096, 4096], P('seq', 'tp')
Inputs may be any that keep to these rules, and one draw needn't show every extreme that they name: `seg_ids`: segment ids never fall along the stream; each segment holds 1 to 2176 tokens, and one holds exactly 2176.
All inputs are finite; a program needn't handle non-finite values.
Results may differ from a plain program's by a relative error of at most 0.018.
Values may be sent and summed in bfloat16 or wider, within the bound.
No kernel may reach another device: no remote copies, remote signals or barrier semaphores. Data moves between devices by JAX's collectives and lax.ppermute only.
A program may use at most 64 MiB of HBM per device.

v0:
```python
import math

import jax
import jax.numpy as jnp
from jax import lax
from jax.sharding import PartitionSpec as P

HEAD_DIM = 128


EPSILON = 1e-06
NEG_FILL = -1e30


def rope_tables(positions):
    part_width = HEAD_DIM // 6
    widths = (HEAD_DIM - 4 * part_width, 2 * part_width, 2 * part_width)
    angle_list = []
    for axis_number in range(3):
        exponent = jnp.arange(0, widths[axis_number], 2, dtype=jnp.float32) / widths[axis_number]
        frequency = 1.0 / 10000.0**exponent
        angle_list.append(positions[axis_number].astype(jnp.float32)[:, None] * frequency[None, :])
    angle_all = jnp.concatenate(angle_list, axis=1)
    return (jnp.cos(angle_all), jnp.sin(angle_all))


def rotate_pairs(field, cosine, sine):
    even_part = field[..., 0::2]
    odd_part = field[..., 1::2]
    cos_wide = cosine[:, None, :]
    sin_wide = sine[:, None, :]
    new_even = even_part * cos_wide - odd_part * sin_wide
    new_odd = even_part * sin_wide + odd_part * cos_wide
    return jnp.stack([new_even, new_odd], axis=-1).reshape(field.shape)


def empty_state(query_rows, heads_here):
    maxima = jnp.full((heads_here, query_rows), NEG_FILL, jnp.float32)
    totals = jnp.zeros((heads_here, query_rows), jnp.float32)
    weighted = jnp.zeros((heads_here, query_rows, HEAD_DIM), jnp.float32)
    return (maxima, totals, weighted)


def merge_states(first, second):
    largest = jnp.maximum(first[0], second[0])
    first_factor = jnp.exp(first[0] - largest)
    second_factor = jnp.exp(second[0] - largest)
    totals = first[1] * first_factor + second[1] * second_factor
    weighted = first[2] * first_factor[..., None] + second[2] * second_factor[..., None]
    return (largest, totals, weighted)


def block_state(q_heads, seg_q, key_heads, value_heads, seg_k):
    score_scale = 1.0 / math.sqrt(HEAD_DIM)
    scores = (
        jnp.einsum("qhd,khd->hqk", q_heads, key_heads, preferred_element_type=jnp.float32)
        * score_scale
    )
    same_seg = seg_q[:, None] == seg_k[None, :]
    masked = jnp.where(same_seg[None], scores, NEG_FILL)
    maxima = jnp.max(masked, axis=2)
    weights = jnp.where(same_seg[None], jnp.exp(masked - maxima[..., None]), 0.0)
    totals = jnp.sum(weights, axis=2)
    weighted = jnp.einsum(
        "hqk,khd->hqd",
        weights.astype(jnp.bfloat16),
        value_heads,
        preferred_element_type=jnp.float32,
    )
    return (maxima, totals, weighted)


def absorb_keys(carry_state, q_heads, seg_q, key_rows, value_rows, seg_k):
    row_count = key_rows.shape[0]
    heads_here = q_heads.shape[1]
    block_rows = 512
    block_count = row_count // block_rows
    key_blocks = key_rows.reshape(block_count, block_rows, heads_here, HEAD_DIM)
    value_blocks = value_rows.reshape(block_count, block_rows, heads_here, HEAD_DIM)
    seg_blocks = seg_k.reshape(block_count, block_rows)

    def step_block(state_now, operands):
        key_block, value_block, seg_block = operands
        return (
            merge_states(state_now, block_state(q_heads, seg_q, key_block, value_block, seg_block)),
            None,
        )

    return lax.scan(step_block, carry_state, (key_blocks, value_blocks, seg_blocks))[0]


def body(hidden_in, seg_ids, positions, mod_table, w_qkv, q_gain, k_gain, w_out):
    tok_rows, feat_local = hidden_in.shape
    model_width = feat_local * lax.axis_size("tp")
    heads_width = w_qkv.shape[2]
    heads_here = heads_width // HEAD_DIM
    all_heads_width = heads_width * lax.axis_size("tp")
    x_float = hidden_in.astype(jnp.float32)
    row_sums, row_squares = lax.psum(
        (jnp.sum(x_float, axis=1), jnp.sum(x_float * x_float, axis=1)), "tp"
    )
    mean_value = row_sums / model_width
    variance = row_squares / model_width - mean_value * mean_value
    normed = (x_float - mean_value[:, None]) * lax.rsqrt(variance[:, None] + EPSILON)
    segment_count = mod_table.shape[0]
    table = mod_table.reshape(segment_count, 3 * feat_local)
    onehot = (seg_ids[:, None] == jnp.arange(segment_count, dtype=jnp.int32)[None, :]).astype(
        jnp.float32
    )
    modulation = jnp.dot(onehot, table, precision=lax.Precision.HIGHEST).reshape(
        tok_rows, 3, feat_local
    )
    modded = (normed * (1.0 + modulation[:, 1]) + modulation[:, 0]).astype(jnp.bfloat16)
    full_rows = lax.all_gather(modded, "tp", axis=1, tiled=True)
    portion = lax.all_gather(w_qkv, "seq", axis=0, tiled=True)
    flat = portion.reshape(portion.shape[0], 3 * heads_width)
    projected = jnp.dot(full_rows, flat, preferred_element_type=jnp.float32)
    query_f = projected[:, :heads_width]
    key_f = projected[:, heads_width : 2 * heads_width]
    value_f = projected[:, 2 * heads_width :]
    query_sq, key_sq = lax.psum(
        (jnp.sum(query_f * query_f, axis=1), jnp.sum(key_f * key_f, axis=1)), "tp"
    )
    query_n = query_f * lax.rsqrt(query_sq / all_heads_width + EPSILON)[:, None] * q_gain[None, :]
    key_n = key_f * lax.rsqrt(key_sq / all_heads_width + EPSILON)[:, None] * k_gain[None, :]
    cosine, sine = rope_tables(positions)
    q_heads = rotate_pairs(query_n.reshape(tok_rows, heads_here, HEAD_DIM), cosine, sine).astype(
        jnp.bfloat16
    )
    k_heads = rotate_pairs(key_n.reshape(tok_rows, heads_here, HEAD_DIM), cosine, sine).astype(
        jnp.bfloat16
    )
    k_cache = k_heads.reshape(tok_rows, heads_width)
    v_cache = value_f.astype(jnp.bfloat16)
    key_rows = lax.all_gather(k_cache, "seq", axis=0, tiled=True)
    value_rows = lax.all_gather(v_cache, "seq", axis=0, tiled=True)
    seg_k = lax.all_gather(seg_ids, "seq", axis=0, tiled=True)
    state_end = absorb_keys(
        empty_state(tok_rows, heads_here), q_heads, seg_ids, key_rows, value_rows, seg_k
    )
    attention = (state_end[2] / state_end[1][..., None]).transpose(1, 0, 2)
    attn_out = attention.reshape(tok_rows, heads_width).astype(jnp.bfloat16)
    terms = jnp.dot(
        attn_out,
        lax.all_gather(w_out, "seq", axis=1, tiled=True),
        preferred_element_type=jnp.float32,
    )
    mixed = lax.psum_scatter(
        terms.astype(jnp.bfloat16), "tp", scatter_dimension=1, tiled=True
    ).astype(jnp.float32)
    hidden_out = (x_float + modulation[:, 2] * mixed).astype(jnp.bfloat16)
    return (hidden_out, k_cache, v_cache)


def solution(mesh):
    in_specs = (
        P("seq", "tp"),
        P("seq"),
        P(None, "seq"),
        P(None, None, "tp"),
        P("seq", None, "tp"),
        P("tp"),
        P("tp"),
        P("tp", "seq"),
    )
    out_specs = (P("seq", "tp"), P("seq", "tp"), P("seq", "tp"))
    return jax.shard_map(body, mesh=mesh, in_specs=in_specs, out_specs=out_specs, check_vma=False)
```

profile of v0, /device:TPU:1, one launch (start us, length us, event | category | flops | bytes accessed | tf_op | source)
XLA Modules:
  0.0 719.6 jit_solution(4609387725667530620)
XLA Ops:
  9.8 73.9 %all-reduce.1 = (f32[256]{0:T(256)S(1)}, f32[256]{0:T(256)S(1)}) all-reduce(f32[256]{0:T(256)S(1)} %get-tuple-element.119, f32[256]{0:T(256)S(1)} %get-tuple-element.118), channel_id=1, replica_groups=mesh['seq'=16,'tp'=32] {'tp'}, use_global_device_ids=true, to_apply=%region_3.0 | all-reduce | flops 512 | bytes 4096 | tf_op jit(solution)/shard_map/psum | solution.py:99
  84.8 1.6 fusion.25
  87.5 55.8 %all-gather.9.cloned.1.call-done = bf16[5120,3,128]{2,0,1:T(8,128)(2,1)} async-done(((bf16[320,3,128]{2,0,1:T(8,128)(2,1)}), bf16[5120,3,128]{2,0,1:T(8,128)(2,1)}) %all-gather.9.cloned.1.call-update) | async-done | bytes 3932176 | tf_op jit(solution)/shard_map/all_gather | solution.py:115
  143.3 6.3 copy.24
  149.6 58.5 %all-gather.7.cloned.1.call-done = bf16[256,5120]{0,1:T(8,128)(2,1)} async-done(((bf16[256,160]{0,1:T(8,128)(2,1)}), bf16[256,5120]{0,1:T(8,128)(2,1)}) %all-gather.7.cloned.1.call-update) | async-done | bytes 2621456 | tf_op jit(solution)/shard_map/all_gather | solution.py:114
  208.1 4.5 fusion.46
  212.7 67.0 %all-reduce = (f32[256]{0:T(256)S(1)}, f32[256]{0:T(256)S(1)}) all-reduce(f32[256]{0:T(256)S(1)} %get-tuple-element.117, f32[256]{0:T(256)S(1)} %get-tuple-element.116), channel_id=1, replica_groups=mesh['seq'=16,'tp'=32] {'tp'}, use_global_device_ids=true, to_apply=%region_5.0 | all-reduce | flops 512 | bytes 4096 | tf_op jit(solution)/shard_map/psum | solution.py:121
  279.9 2.4 slice.51
  282.3 2.3 slice.50
  284.6 2.4 slice.48
  287.0 2.3 slice.44
  292.2 44.6 %all-gather = s32[16,1,256]{2,1,0:T(1,128)S(1)} all-gather(s32[1,1,256]{2,1,0:T(1,128)S(1)} %bitcast.110), channel_id=1, replica_groups=mesh['seq'=16,'tp'=32] {'seq'}, dimensions={0}, use_global_device_ids=true | all-gather | bytes 17408 | tf_op jit(solution)/shard_map/all_gather | solution.py:137
  337.2 42.7 %all-gather.11.cloned.1.call-done = bf16[4096,128]{0,1:T(8,128)(2,1)} async-done(((bf16[256,128]{0,1:T(8,128)(2,1)}), bf16[4096,128]{0,1:T(8,128)(2,1)}) %all-gather.11.cloned.1.call-update) | async-done | bytes 1048592 | tf_op jit(solution)/shard_map/all_gather | solution.py:135
  379.9 1.6 copy.31
  381.6 88.6 %all-gather.13.cloned.1.call-done = bf16[4096,128]{1,0:T(8,128)(2,1)} async-done(((bf16[256,128]{1,0:T(8,128)(2,1)}), bf16[4096,128]{1,0:T(8,128)(2,1)}) %all-gather.13.cloned.1.call-update) | async-done | bytes 1048592 | tf_op jit(solution)/shard_map/all_gather | solution.py:136
  470.1 14.4 %while.15 = (s32[]{:T(128)}, f32[1,256]{1,0:T(1,128)S(1)}, f32[1,256]{1,0:T(1,128)S(1)}, f32[1,256,128]{2,1,0:T(8,128)S(1)}, s32[256]{0:T(256)S(1)}, /*index=5*/...) while((s32[]{:T(128)}, f32[1,256]{1,0:T(1,128)S(1)}, ...), condition=%wide.region_11.12_spmd.clone, body=%wide.region_8.11_spmd.clone.sunk | while | flops 68814336 | bytes 2190476 | solution.py:89
  470.6 1.3 fusion.61
  472.4 1.3 fusion.61
  476.0 1.3 fusion.61
  483.2 1.3 fusion.61
  484.5 79.3 %all-gather.15.cloned.1.call-done = bf16[128,5120]{0,1:T(8,128)(2,1)} async-done(((bf16[128,320]{0,1:T(8,128)(2,1)}), bf16[128,5120]{0,1:T(8,128)(2,1)}) %all-gather.15.cloned.1.call-update) | async-done | bytes 1310736 | tf_op jit(solution)/shard_map/all_gather | solution.py:145
  563.8 3.8 convolution_convert_fusion
  568.3 142.8 %reduce-scatter.2.cloned.1.call-done = bf16[256,160]{0,1:T(8,128)(2,1)} async-done(((bf16[256,5120]{0,1:T(8,128)(2,1)}), bf16[256,160]{0,1:T(8,128)(2,1)}) %reduce-scatter.2.cloned.1.call-update) | async-done | bytes 81936 | tf_op jit(solution)/shard_map/reduce_scatter | solution.py:148
  711.2 1.6 fusion.27
  (88 shorter events, 17.9 us)
Async XLA Ops:
  7.2 136.1 %all-gather.9.cloned.1.call-start = ((), (), s32[]{:S(2)}) async-start(), calls=%async_computation.2 | async-start | bytes 4177920 | tf_op jit(solution)/shard_map/all_gather | solution.py:115
  7.9 200.2 %all-gather.7.cloned.1.call-start = ((), (), s32[]{:S(2)}) async-start(), calls=%async_computation.1 | async-start | bytes 2703360 | tf_op jit(solution)/shard_map/all_gather | solution.py:114
  86.4 293.5 %all-gather.11.cloned.1.call-start = ((), (), s32[]{:S(2)}) async-start(), calls=%async_computation.3 | async-start | bytes 1114112 | tf_op jit(solution)/shard_map/all_gather | solution.py:135
  208.1 71.7 %copy-start.3 = (f32[128]{0:T(128)S(1)}, f32[128]{0:T(128)}, u32[]{:S(2)}) copy-start(f32[128]{0:T(128)} %param.15) | copy-start | bytes 1540
  208.1 71.7 %copy-start.4 = (f32[128]{0:T(128)S(1)}, f32[128]{0:T(128)}, u32[]{:S(2)}) copy-start(f32[128]{0:T(128)} %param.16) | copy-start | bytes 1540
  212.6 79.6 %copy-start.2 = (s32[256]{0:T(256)S(1)}, s32[256]{0:T(256)}, u32[]{:S(2)}) copy-start(s32[256]{0:T(256)} %param.11) | copy-start | bytes 3076
  290.8 179.3 %all-gather.13.cloned.1.call-start = ((), (), s32[]{:S(2)}) async-start(), calls=%async_computation.4 | async-start | bytes 1114112 | tf_op jit(solution)/shard_map/all_gather | solution.py:136
  291.5 272.2 %all-gather.15.cloned.1.call-start = ((), (), s32[]{:S(2)}) async-start(), calls=%async_computation.5 | async-start | bytes 1392640 | tf_op jit(solution)/shard_map/all_gather | solution.py:145
  292.1 419.0 %reduce-scatter.2.cloned.1.call-start = ((), (), s32[]{:S(2)}) async-start(), calls=%async_computation.6 | async-start | bytes 2703360 | tf_op jit(solution)/shard_map/reduce_scatter | solution.py:148
  563.8 3.8 copy-start.1
  563.8 147.4 %copy-start = (bf16[256,160]{0,1:T(8,128)(2,1)S(1)}, bf16[256,160]{0,1:T(8,128)(2,1)}, u32[]{:S(2)}) copy-start(bf16[256,160]{0,1:T(8,128)(2,1)} %param.10) | copy-start | bytes 245764
Sparse Core Ops, SparseCore 0:
  11.2 132.0 all-gather.8
  146.0 62.0 all-gather.6
  291.0 88.9 all-gather.10
  383.5 86.5 all-gather.12
  473.2 90.5 all-gather.14
  567.7 143.3 reduce-scatter.1
where the time goes:
time: 724 us; the launch traced here: 720 us
  waiting for transfers between devices  469 us (65%)
  blocking collectives  185 us (26%)
  matrix products  22 us (3%)
  local copies, waits for them, and re-layouts  20.7 us (3%)
  between operations  14.3 us (2%)
  other arithmetic  7.58 us (1%)
    reduce_scatter x1, waiting for transfers between devices, body(): lax.psum_scatter(terms.astype(jnp.bfloat16), 'tp', scatter_dimension=1, t...  143 us
    all_gather x1, waiting for transfers between devices, body(): value_rows = lax.all_gather(v_cache, 'seq', axis=0, tiled=True)  88.6 us
    all_gather x1, waiting for transfers between devices, body(): lax.all_gather(w_out, 'seq', axis=1, tiled=True)  79.3 us
    psum x1, blocking collectives, body(): lax.psum((jnp.sum(x_float, axis=1), jnp.sum(x_float * x_float, axis=1)),...  73.9 us
    psum x1, blocking collectives, body(): lax.psum((jnp.sum(query_f * query_f, axis=1), jnp.sum(key_f * key_f, axis...  67 us
    all_gather x1, waiting for transfers between devices, body(): full_rows = lax.all_gather(modded, 'tp', axis=1, tiled=True)  58.5 us
    all_gather x1, waiting for transfers between devices, body(): portion = lax.all_gather(w_qkv, 'seq', axis=0, tiled=True)  55.8 us
    all_gather x1, blocking collectives, body(): seg_k = lax.all_gather(seg_ids, 'seq', axis=0, tiled=True)  44.6 us
  transfers between devices with their start and end apart: 6, of which 6 were waited for; matrix products, arithmetic and copies ran while one was open for 4% of the time, Pallas kernels for 0%

commit v1 on v0

v1 whole, which is shorter than its diff:
```python
import functools
import itertools
import math

import jax
import jax.numpy as jnp
import numpy as np
from jax import lax
from jax.experimental import pallas as pl
from jax.experimental.pallas import tpu as pltpu
from jax.sharding import Mesh
from jax.sharding import PartitionSpec as P

HEAD_DIM = 128
EPSILON = 1e-06
NEG_FILL = -1e30
LOG2E = 1.4426950408889634

SEQ = ("ya", "yb", "yc", "zh")
TP = ("zl", "xh", "xl", "c")
SIZES = {"ya": 2, "yb": 2, "yc": 2, "zh": 2, "zl": 4, "xh": 2, "xl": 2, "c": 2}

F32 = jnp.float32
BF16 = jnp.bfloat16
VMEM_LIMIT = 48 << 20


def permute(value, axes, move):
    sizes = [SIZES[a] for a in axes]
    pairs = []
    for at in itertools.product(*[range(n) for n in sizes]):
        to = move(*at)
        pairs.append((int(np.ravel_multi_index(at, sizes)), int(np.ravel_multi_index(to, sizes))))
    return lax.ppermute(value, axes, pairs)


def contract_first(lhs, rhs):
    return lax.dot_general(lhs, rhs, (((0,), (0,)), ((), ())), preferred_element_type=F32)


def call(kernel, out_shape, operands, scalars=None, scratch=(), name=None, cost=None):
    vmem = pl.BlockSpec(memory_space=pltpu.VMEM)
    smem = pl.BlockSpec(memory_space=pltpu.SMEM)
    specs = ([] if scalars is None else [smem]) + [vmem] * len(operands)
    args = ([] if scalars is None else [scalars]) + list(operands)
    return pl.pallas_call(
        kernel,
        out_shape=out_shape,
        in_specs=specs,
        out_specs=jax.tree.map(lambda _: vmem, out_shape),
        scratch_shapes=list(scratch),
        compiler_params=pltpu.CompilerParams(vmem_limit_bytes=VMEM_LIMIT),
        cost_estimate=cost,
        name=name,
    )(*args)


def shaped(shape, dtype):
    return jax.ShapeDtypeStruct(shape, dtype)


def project_kernel(at, *refs):
    xs, w, mine_q, mine_kv, message, meta, acc = refs[:8], refs[8], *refs[9:]
    zl, x, c, zh = at[0], at[1], at[2], at[3]
    acc[...] = jnp.zeros_like(acc)
    first = lax.rem(x, 2)
    for i in range(2):
        core = lax.rem(c + i, 2)
        for j in range(2):
            high = lax.rem(x // 2 + j, 2)
            left, right = xs[4 * i + 2 * j], xs[4 * i + 2 * j + 1]
            total = None
            for k in range(4):
                z_from = lax.rem(zl - k + 4, 4)
                both = jnp.concatenate([left[k, :160, :], right[k, :160, :]], axis=1)
                block = z_from * 2 + high
                weights = jnp.concatenate([w[block, p, core] for p in range(3)], axis=1)
                term = contract_first(weights, both)
                total = term if total is None else total + term
            acc[first] += total[:, :256]
            acc[1 - first] += total[:, 256:]
            if i == 0 and j == 0:
                meta[first] = left[0, 160:168, :].astype(F32)
                meta[1 - first] = right[0, 160:168, :].astype(F32)
    for block in range(2):
        part = acc[block]
        mine_q[block] = part[:128]
        message[block] = part[:128].astype(BF16)
    own = acc[zh]
    mine_kv[0] = own[128:256]
    mine_kv[1] = own[256:]
    other = acc[1 - zh]
    message[2] = other[128:256].astype(BF16)
    message[3] = other[256:].astype(BF16)


def square_kernel(mine_q, mine_kv, got, full_q, full_kv, stats):
    for block in range(2):
        full_q[block] = mine_q[block] + got[block].astype(F32)
        full_kv[block] = mine_kv[block] + got[2 + block].astype(F32)
    rows = []
    for value in (full_q[0], full_q[1], full_kv[0]):
        row = jnp.sum(value * value, axis=0, keepdims=True)
        rows += [row[:, :128], row[:, 128:]]
    rows += [jnp.zeros((2, 128), F32)]
    packed = jnp.concatenate(rows, axis=0)
    for t in range(stats.shape[0]):
        stats[t] = packed


def rotate_kernel(width, got, full_q, full_kv, cosine, sine, qg, kg, meta, at, q_out, k_cache, v_cache, message):
    totals = jnp.sum(got[...], axis=0)
    zh = at[0]
    even = lax.rem(lax.broadcasted_iota(jnp.int32, (HEAD_DIM, 256), 0), 2) == 0

    def rotated(value, gain, row, cos, sin):
        factor = jnp.concatenate([totals[row : row + 1], totals[row + 1 : row + 2]], axis=1)
        factor = lax.rsqrt(factor / width + EPSILON)
        normed = value * factor * gain
        after = pltpu.roll(normed, HEAD_DIM - 1, 0)
        before = pltpu.roll(normed, 1, 0)
        partner = jnp.where(even, -after, before)
        return normed * cos + partner * sin

    for block in range(2):
        q_out[:, 256 * block : 256 * block + 256] = rotated(
            full_q[block], qg[...], 2 * block, cosine[block], sine[block]
        ).astype(BF16)
    k_rot = rotated(full_kv[0], kg[...], 4, cosine[zh], sine[zh])
    value = full_kv[1]
    k_cache[...] = k_rot.T.astype(BF16)
    v_cache[...] = value.T.astype(BF16)
    k_low = k_rot.astype(BF16)
    v_low = value.astype(BF16)
    extra = jnp.concatenate([meta[zh], jnp.zeros((8, 256), F32)], axis=0).astype(BF16)
    for t in range(message.shape[0]):
        message[t, :128] = k_low
        message[t, 128:256] = v_low
        message[t, 256:272] = extra


def attend_kernel(at, q, meta, keys, mine, mine_lse, message, held):
    zh = at[0]
    count = keys.shape[0]
    scale = LOG2E / math.sqrt(HEAD_DIM)
    q_low = q[...]
    seg_q = jnp.concatenate([meta[0, 3:4], meta[1, 3:4]], axis=1)
    top = None
    for b in range(count):
        seg_k = keys[b, 256:272].astype(F32).T[:, 3:4]
        scores = contract_first(keys[b, :128], q_low) * scale
        scores = jnp.where(seg_k == seg_q, scores, NEG_FILL)
        held[b] = scores
        here = jnp.max(scores, axis=0, keepdims=True)
        top = here if top is None else jnp.maximum(top, here)
    top = jnp.maximum(top, -1e20)
    total = jnp.zeros((1, 512), F32)
    weighted = jnp.zeros((HEAD_DIM, 512), F32)
    for b in range(count):
        weights = jnp.exp2(held[b] - top)
        total = total + jnp.sum(weights, axis=0, keepdims=True)
        weighted = weighted + jnp.dot(
            keys[b, 128:256], weights.astype(BF16), preferred_element_type=F32
        )
    some = total > 0.0
    safe = jnp.where(some, total, 1.0)
    out = weighted / safe
    lse = jnp.where(some, top + jnp.log2(safe), NEG_FILL)
    first = zh == 0
    own = jnp.where(first, out[:, :256], out[:, 256:])
    other = jnp.where(first, out[:, 256:], out[:, :256])
    own_lse = jnp.where(first, lse[:, :256], lse[:, 256:])
    other_lse = jnp.where(first, lse[:, 256:], lse[:, :256])
    mine[...] = own
    mine_lse[...] = jnp.broadcast_to(own_lse, (8, 256))
    high = other_lse.astype(BF16)
    rest = other_lse - high.astype(F32)
    middle = rest.astype(BF16)
    low = (rest - middle.astype(F32)).astype(BF16)
    message[:128] = other.astype(BF16)
    message[128:144] = jnp.concatenate(
        [high.astype(F32), middle.astype(F32), low.astype(F32), jnp.zeros((13, 256), F32)], axis=0
    ).astype(BF16)


def merge_kernel(mine, mine_lse, got, out):
    rows = got[128:144].astype(F32)
    other_lse = rows[0:1] + rows[1:2] + rows[2:3]
    own_lse = mine_lse[0:1]
    top = jnp.maximum(own_lse, other_lse)
    own_weight = jnp.exp2(own_lse - top)
    other_weight = jnp.exp2(other_lse - top)
    both = own_weight + other_weight
    out[...] = (
        mine[...] * (own_weight / both) + got[:128].astype(F32) * (other_weight / both)
    ).astype(BF16)


def output_kernel(at, *refs):
    heads, w, mine, message, held = refs[:4], refs[4], *refs[5:]
    zl, x, c, zh = at[0], at[1], at[2], at[3]
    total = None
    for j in range(4):
        x_from = lax.rem(x // 2 + j // 2, 2) * 2 + lax.rem(x + j, 2)
        for k in range(4):
            chip = lax.rem(zl - k + 4, 4) * 4 + x_from
            flip = lax.rem(lax.rem(chip, 2) + zh, 2)
            term = jnp.dot(w[chip // 2, flip], heads[j][k], preferred_element_type=F32)
            total = term if total is None else total + term
    held[0] = total[:160]
    held[1] = total[160:]
    mine[...] = held[c]
    message[...] = held[1 - c]


def body(hidden_in, seg_ids, positions, mod_table, w_qkv, q_gain, k_gain, w_out):
    tok_rows, feat_local = hidden_in.shape
    model_width = feat_local * 32
    heads_width = 4096
    zl, c = lax.axis_index("zl"), lax.axis_index("c")
    zh = lax.axis_index("zh")
    x = lax.axis_index("xh") * 2 + lax.axis_index("xl")
    at = jnp.stack([zl, x, c, zh]).astype(jnp.int32)
    at_zh = jnp.stack([zh]).astype(jnp.int32)

    w_local = jnp.transpose(w_qkv, (1, 0, 2))
    w_all = lax.all_gather(w_local, ("ya", "yb", "yc"), axis=0, tiled=False)
    w_all = w_all.reshape(8, 3, 2, 160, 128)

    axes = SEQ + TP

    def turned(flip):
        def move(ya, yb, yc, zh, zl, xh, xl, c):
            s = (ya * 4 + yb * 2 + yc) * 2 + zh
            chip = (zl * 2 + xh) * 2 + xl
            to_s = chip ^ flip
            return (to_s >> 3, (to_s >> 2) & 1, (to_s >> 1) & 1, to_s & 1, s >> 2, (s >> 1) & 1, s & 1, c)

        return permute(w_out.T, axes, move)

    wo_pair = jnp.stack([turned(0), turned(1)])
    wo_all = lax.all_gather(wo_pair, ("ya", "yb", "yc"), axis=0, tiled=False)

    x_t = hidden_in.T.astype(F32)
    sums = jnp.stack([jnp.sum(x_t, axis=0), jnp.sum(x_t * x_t, axis=0)]).reshape(4, 128)
    sums = jnp.concatenate([sums, jnp.zeros((4, 128), F32)], axis=0)
    sums = lax.all_to_all(jnp.broadcast_to(sums, (32, 8, 128)), TP, 0, 0, tiled=True)
    sums = jnp.sum(sums, axis=0)[:4].reshape(2, tok_rows)
    mean_value = sums[0:1] / model_width
    variance = sums[1:2] / model_width - mean_value * mean_value
    normed = (x_t - mean_value) * lax.rsqrt(variance + EPSILON)
    segment_count = mod_table.shape[0]
    onehot = (seg_ids[None, :] == jnp.arange(segment_count, dtype=jnp.int32)[:, None]).astype(F32)
    modulation = lax.dot_general(
        mod_table.reshape(segment_count, 3 * feat_local),
        onehot,
        (((0,), (0,)), ((), ())),
        precision=lax.Precision.HIGHEST,
    ).reshape(3, feat_local, tok_rows)
    modded = (normed * (1.0 + modulation[1]) + modulation[0]).astype(BF16)
    marks = jnp.concatenate([positions, seg_ids[None, :], jnp.zeros((4, tok_rows), jnp.int32)], axis=0)
    packet = jnp.concatenate([modded, marks.astype(BF16)], axis=0)

    slots = [
        permute(
            packet,
            ("zh", "zl", "xh", "xl"),
            lambda zh, zl, xh, xl, k=k: (xl, (zl + k) % 4, xh, zh),
        )
        for k in range(4)
    ]
    held = jnp.stack(slots)
    along_x = [held] + [
        permute(held, ("xh", "xl"), lambda xh, xl, j=j: (xh ^ (j >> 1), xl ^ (j & 1)))
        for j in range(1, 4)
    ]
    swapped = [permute(part, ("c",), lambda c: (1 - c,)) for part in along_x]

    mine_q, mine_kv, message, meta = call(
        project_kernel,
        (
            shaped((2, 128, 256), F32),
            shaped((2, 128, 256), F32),
            shaped((4, 128, 256), BF16),
            shaped((2, 8, 256), F32),
        ),
        along_x + swapped + [w_all],
        scalars=at,
        scratch=[pltpu.VMEM((2, 384, 256), F32)],
        name="project",
        cost=pl.CostEstimate(flops=2 * 512 * 2560 * 384, bytes_accessed=5 << 20, transcendentals=0),
    )
    got = permute(message, ("zh",), lambda zh: (1 - zh,))

    part_width = HEAD_DIM // 6
    widths = (HEAD_DIM - 4 * part_width, 2 * part_width, 2 * part_width)
    angles = []
    for axis_number in range(3):
        width = widths[axis_number]
        exponent = jnp.arange(0, width, 2, dtype=F32) / width
        frequency = jnp.repeat(1.0 / 10000.0**exponent, 2)
        angles.append(meta[:, axis_number][:, None, :] * frequency[None, :, None])
    angle = jnp.concatenate(angles, axis=1)
    cosine, sine = jnp.cos(angle), jnp.sin(angle)

    full_q, full_kv, stats = call(
        square_kernel,
        (shaped((2, 128, 256), F32), shaped((2, 128, 256), F32), shaped((32, 8, 128), F32)),
        [mine_q, mine_kv, got],
        name="square",
    )
    stats = lax.all_to_all(stats, TP, 0, 0, tiled=True)
    q_rot, k_cache, v_cache, kv_message = call(
        lambda at, *refs: rotate_kernel(heads_width, *refs[:8], at, *refs[8:]),
        (
            shaped((128, 512), BF16),
            shaped((256, 128), BF16),
            shaped((256, 128), BF16),
            shaped((8, 272, 256), BF16),
        ),
        [stats, full_q, full_kv, cosine, sine, q_gain.reshape(128, 1), k_gain.reshape(128, 1), meta],
        scalars=at_zh,
        name="rotate",
    )
    keys = lax.all_to_all(kv_message, ("ya", "yb", "yc"), 0, 0, tiled=True)
    mine, mine_lse, o_message = call(
        attend_kernel,
        (shaped((128, 256), F32), shaped((8, 256), F32), shaped((144, 256), BF16)),
        [q_rot, meta, keys],
        scalars=at_zh,
        scratch=[pltpu.VMEM((8, 256, 512), F32)],
        name="attend",
    )
    o_got = permute(o_message, ("zh",), lambda zh: (1 - zh,))
    attention = call(merge_kernel, shaped((128, 256), BF16), [mine, mine_lse, o_got], name="merge")

    by_z = [attention] + [
        permute(attention, ("zl",), lambda zl, k=k: ((zl + k) % 4,)) for k in range(1, 4)
    ]
    by_z = jnp.stack(by_z)
    by_x = [by_z] + [
        permute(by_z, ("xh", "xl"), lambda xh, xl, j=j: (xh ^ (j >> 1), xl ^ (j & 1)))
        for j in range(1, 4)
    ]
    out_mine, out_message = call(
        output_kernel,
        (shaped((160, 256), F32), shaped((160, 256), F32)),
        by_x + [wo_all],
        scalars=at,
        scratch=[pltpu.VMEM((2, 160, 256), F32)],
        name="output",
    )
    out_got = permute(out_message, ("c",), lambda c: (1 - c,))
    mixed = out_mine + out_got
    hidden_out = (x_t + modulation[2] * mixed).T.astype(BF16)
    return (hidden_out, k_cache, v_cache)


def solution(mesh):
    split = Mesh(mesh.devices.reshape(tuple(SIZES.values())), tuple(SIZES))
    in_specs = (
        P(SEQ, TP),
        P(SEQ),
        P(None, SEQ),
        P(None, None, TP),
        P(SEQ, None, TP),
        P(TP),
        P(TP),
        P(TP, SEQ),
    )
    out_specs = (P(SEQ, TP), P(SEQ, TP), P(SEQ, TP))
    return jax.shard_map(body, mesh=split, in_specs=in_specs, out_specs=out_specs, check_vma=False)
```

time: 724 us -> 239 us (0.33)
  waiting for transfers between devices: 469 us -> 95.4 us
  blocking collectives: 185 us -> 0 us
  starting transfers between devices: 0.24 us -> 106 us
  matrix products: 22 us -> 1.12 us
  local copies, waits for them, and re-layouts: 20.7 us -> 5.03 us
  Pallas kernels: 0 us -> 8.92 us
    all_gather x5 -> x2, waiting for transfers between devices: 325 us -> 0.04 us  [the longest x1 0.02 us: body(): w_all = lax.all_gather(w_local, ('ya', 'yb', 'yc'), axis=0, tiled=False)]
    reduce_scatter x1 -> x0, waiting for transfers between devices: 143 us -> none  [body(): lax.psum_scatter(terms.astype(jnp.bfloat16), 'tp', scatter_dimension=1, t...]
    psum x2 -> x0, blocking collectives: 141 us -> none  [the longest x1 73.9 us: body(): lax.psum((jnp.sum(x_float, axis=1), jnp.sum(x_float * x_float, axis=1)),...]
    ppermute x0 -> x22, starting transfers between devices: none -> 81 us  [permute(): return lax.ppermute(value, axes, pairs)]
    all_to_all x0 -> x3, waiting for transfers between devices: none -> 47.3 us  [the longest x1 34.7 us: body(): keys = lax.all_to_all(kv_message, ('ya', 'yb', 'yc'), 0, 0, tiled=True)]
    ppermute x0 -> x22, waiting for transfers between devices: none -> 47.3 us  [permute(): return lax.ppermute(value, axes, pairs)]
    all_gather x1 -> x0, blocking collectives: 44.6 us -> none  [body(): seg_k = lax.all_gather(seg_ids, 'seq', axis=0, tiled=True)]
    all_to_all x0 -> x3, starting transfers between devices: none -> 25.1 us  [the longest x1 11.4 us: body(): lax.all_to_all(jnp.broadcast_to(sums, (32, 8, 128)), TP, 0, 0, tiled=True)]
  transfers between devices with their start and end apart: 6 -> 27, of which waited for: 6 -> 10; matrix products, arithmetic and copies ran while one was open for 4% -> 4% of each run, Pallas kernels for 0% -> 3%
where the time goes in v1:
time: 239 us; the launch traced here: 238 us
  starting transfers between devices  106 us (44%)
  waiting for transfers between devices  95.4 us (40%)
  between operations  14.5 us (6%)
  Pallas kernels  8.92 us (4%)
  other arithmetic  7.04 us (3%)
  local copies, waits for them, and re-layouts  5.03 us (2%)
    ppermute x22, starting transfers between devices, permute(): return lax.ppermute(value, axes, pairs)  81 us
    ppermute x22, waiting for transfers between devices, permute(): return lax.ppermute(value, axes, pairs)  47.3 us
    all_to_all x1, waiting for transfers between devices, body(): keys = lax.all_to_all(kv_message, ('ya', 'yb', 'yc'), 0, 0, tiled=True)  34.7 us
    all_to_all x1, starting transfers between devices, body(): lax.all_to_all(jnp.broadcast_to(sums, (32, 8, 128)), TP, 0, 0, tiled=True)  11.4 us
    all_to_all x1, starting transfers between devices, body(): keys = lax.all_to_all(kv_message, ('ya', 'yb', 'yc'), 0, 0, tiled=True)  9.49 us
    pallas_call x6, Pallas kernels, call(): pl.pallas_call(kernel, out_shape=out_shape, in_specs=specs, out_specs=jax...  8.92 us
    all_to_all x1, waiting for transfers between devices, body(): stats = lax.all_to_all(stats, TP, 0, 0, tiled=True)  7.48 us
    all_to_all x1, waiting for transfers between devices, body(): lax.all_to_all(jnp.broadcast_to(sums, (32, 8, 128)), TP, 0, 0, tiled=True)  5.15 us
  transfers between devices with their start and end apart: 27, of which 10 were waited for; matrix products, arithmetic and copies ran while one was open for 4% of the time, Pallas kernels for 3%

profile of v1, /device:TPU:1, one launch (start us, length us, event | category | flops | bytes accessed | tf_op | source)
XLA Modules:
  0.0 238.2 jit_solution(10087955899025579368)
XLA Ops:
  10.5 11.4 %all-to-all-start = ((f32[32,8,128]{2,1,0:T(8,128)}), f32[32,8,128]{2,1,0:T(8,128)S(1)}, u32[]{:S(2)}, u32[]{:S(2)}) async-start(f32[32,8,128]{2,1,0:T(8,128)} %broadcast_in_dim.22), calls=%async_computation | async-start | bytes 262144 | tf_op jit(solution)/shard_map/all_to_all | solution.py:247
  25.3 5.1 %all-to-all-done = f32[32,8,128]{2,1,0:T(8,128)S(1)} async-done(((f32[32,8,128]{2,1,0:T(8,128)}), f32[32,8,128]{2,1,0:T(8,128)S(1)}, u32[]{:S(2)}, u32[]{:S(2)}) %all-to-all-start) | async-done | bytes 131104 | tf_op jit(solution)/shard_map/all_to_all | solution.py:247
  33.6 2.9 %collective-permute-start.2 = (bf16[168,256]{1,0:T(8,128)(2,1)S(1)}, bf16[168,256]{1,0:T(8,128)(2,1)S(1)}, u32[]{:S(2)}, u32[]{:S(2)}) collective-permute-start(bf16[168,256]{1,0:T(8,128)(2,1)S(1)} %maximum_maximum_fusion), channel_id=1, source_target_pairs={{0,16},{2,48},{4,20},{6,52},{8,24},{10,56},{12,28},{14,60},{16,0},... | collective-permute-start | bytes 258056 | tf_op jit(solution)/shard_map/ppermute | solution.py:34
  36.5 3.8 %collective-permute-start.3 = (bf16[168,256]{1,0:T(8,128)(2,1)S(1)}, bf16[168,256]{1,0:T(8,128)(2,1)S(1)}, u32[]{:S(2)}, u32[]{:S(2)}) collective-permute-start(bf16[168,256]{1,0:T(8,128)(2,1)S(1)} %maximum_maximum_fusion), channel_id=1, source_target_pairs={{0,24},{2,56},{4,28},{6,60},{8,0},{10,32},{12,4},{14,36},{16,8},{1... | collective-permute-start | bytes 258056 | tf_op jit(solution)/shard_map/ppermute | solution.py:34
  40.4 4.8 %collective-permute-done.2 = bf16[168,256]{1,0:T(8,128)(2,1)S(1)} collective-permute-done((bf16[168,256]{1,0:T(8,128)(2,1)S(1)}, bf16[168,256]{1,0:T(8,128)(2,1)S(1)}, u32[]{:S(2)}, u32[]{:S(2)}) %collective-permute-start.2) | collective-permute-done | bytes 86048 | tf_op jit(solution)/shard_map/ppermute | solution.py:34
  45.2 13.5 %collective-permute-start.6 = (bf16[4,168,256]{2,1,0:T(8,128)(2,1)S(1)}, bf16[4,168,256]{2,1,0:T(8,128)(2,1)S(1)}, u32[]{:S(2)}, u32[]{:S(2)}) collective-permute-start(bf16[4,168,256]{2,1,0:T(8,128)(2,1)S(1)} %pad_maximum_fusion.refs_0_), channel_id=1, source_target_pairs={{0,6},{2,4},{4,2},{6,0},{1,7},{3,5},{5,3},{7,1},{8,14},{10,12},{12... | collective-permute-start | bytes 1032200 | tf_op jit(solution)/shard_map/ppermute | solution.py:34
  61.2 3.7 %collective-permute-start.5 = (bf16[4,168,256]{2,1,0:T(8,128)(2,1)S(1)}, bf16[4,168,256]{2,1,0:T(8,128)(2,1)S(1)}, u32[]{:S(2)}, u32[]{:S(2)}) collective-permute-start(bf16[4,168,256]{2,1,0:T(8,128)(2,1)S(1)} %pad_maximum_fusion.refs_0_), channel_id=1, source_target_pairs={{0,4},{2,6},{4,0},{6,2},{1,5},{3,7},{5,1},{7,3},{8,12},{10,14},{12... | collective-permute-start | bytes 1032200 | tf_op jit(solution)/shard_map/ppermute | solution.py:34
  64.9 4.7 %collective-permute-start.7 = (bf16[4,168,256]{2,1,0:T(8,128)(2,1)S(1)}, bf16[4,168,256]{2,1,0:T(8,128)(2,1)S(1)}, u32[]{:S(2)}, u32[]{:S(2)}) collective-permute-start(bf16[4,168,256]{2,1,0:T(8,128)(2,1)S(1)} %pad_maximum_fusion.refs_0_), channel_id=1, source_target_pairs={{0,1},{1,0},{2,3},{3,2},{4,5},{5,4},{6,7},{7,6},{8,9},{9,8},{10,11... | collective-permute-start | bytes 1032200 | tf_op jit(solution)/shard_map/ppermute | solution.py:34
  71.5 4.8 %collective-permute-start.8 = (bf16[4,168,256]{2,1,0:T(8,128)(2,1)S(1)}, bf16[4,168,256]{2,1,0:T(8,128)(2,1)S(1)}, u32[]{:S(2)}, u32[]{:S(2)}) collective-permute-start(bf16[4,168,256]{2,1,0:T(8,128)(2,1)S(1)} %collective-permute-done.4.refs_1_), channel_id=1, source_target_pairs={{0,1},{1,0},{2,3},{3,2},{4,5},{5,4},{6,7},{7,6},{8,9},{9,8},{10,11... | collective-permute-start | bytes 1032200 | tf_op jit(solution)/shard_map/ppermute | solution.py:34
  76.3 4.9 %collective-permute-start.9 = (bf16[4,168,256]{2,1,0:T(8,128)(2,1)S(1)}, bf16[4,168,256]{2,1,0:T(8,128)(2,1)S(1)}, u32[]{:S(2)}, u32[]{:S(2)}) collective-permute-start(bf16[4,168,256]{2,1,0:T(8,128)(2,1)S(1)} %collective-permute-done.5.refs_2_), channel_id=1, source_target_pairs={{0,1},{1,0},{2,3},{3,2},{4,5},{5,4},{6,7},{7,6},{8,9},{9,8},{10,11... | collective-permute-start | bytes 1032200 | tf_op jit(solution)/shard_map/ppermute | solution.py:34
  84.1 7.6 %collective-permute-start.20 = (bf16[320,128]{1,0:T(8,128)(2,1)}, bf16[320,128]{1,0:T(8,128)(2,1)}, u32[]{:S(2)}, u32[]{:S(2)}) collective-permute-start(bf16[320,128]{1,0:T(8,128)(2,1)} %bitcast.83), channel_id=1, source_target_pairs={{0,32},{1,33},{2,0},{3,1},{4,96},{5,97},{6,64},{7,65},{8,160},{9,1... | collective-permute-start | bytes 245768 | tf_op jit(solution)/shard_map/ppermute | solution.py:34
  93.4 3.1 %project.1 = (f32[2,128,256]{2,1,0:T(8,128)S(1)}, f32[2,128,256]{2,1,0:T(8,128)S(1)}, bf16[4,128,256]{2,1,0:T(8,128)(2,1)S(1)}, f32[2,8,256]{2,1,0:T(8,128)S(1)}) custom-call(s32[4]{0:T(128)S(1)} %pad_add_fusion.at, bf16[4,168,256]{2,1,0:T(8,128)(2,1)S(1)} %pad_maximum_fusion.refs_0_, bf16[4,168,256]{2,1,0:T(8,128)(2,1)S(1)} %collective-permute-done.4.refs_1_, ...), custom_call_target="tpu_custom_call" | custom-call | flops 1006632960 | bytes 5242880 | tf_op jit(solution)/shard_map/project/pallas_call | solution.py:46
  98.5 21.5 %collective-permute-done.11.got = bf16[4,128,256]{2,1,0:T(8,128)(2,1)S(1)} collective-permute-done((bf16[4,128,256]{2,1,0:T(8,128)(2,1)S(1)}, bf16[4,128,256]{2,1,0:T(8,128)(2,1)S(1)}, u32[]{:S(2)}, u32[]{:S(2)}) %collective-permute-start.11) | collective-permute-done | bytes 262176 | tf_op jit(solution)/shard_map/ppermute | solution.py:34
  120.8 4.3 %all-to-all-start.1 = ((f32[32,8,128]{2,1,0:T(8,128)}), f32[32,8,128]{2,1,0:T(8,128)S(1)}, u32[]{:S(2)}, u32[]{:S(2)}) async-start(f32[32,8,128]{2,1,0:T(8,128)} %get-tuple-element.22), calls=%async_computation.1 | async-start | bytes 262144 | tf_op jit(solution)/shard_map/all_to_all | solution.py:312
  126.1 7.5 %all-to-all-done.1.refs_0_ = f32[32,8,128]{2,1,0:T(8,128)S(1)} async-done(((f32[32,8,128]{2,1,0:T(8,128)}), f32[32,8,128]{2,1,0:T(8,128)S(1)}, u32[]{:S(2)}, u32[]{:S(2)}) %all-to-all-start.1) | async-done | bytes 131104 | tf_op jit(solution)/shard_map/all_to_all | solution.py:312
  135.0 9.5 %all-to-all-start.2 = ((bf16[8,272,256]{2,1,0:T(8,128)(2,1)}), bf16[8,272,256]{2,1,0:T(8,128)(2,1)S(1)}, u32[]{:S(2)}, u32[]{:S(2)}) async-start(bf16[8,272,256]{2,1,0:T(8,128)(2,1)} %get-tuple-element.27), calls=%async_computation.2 | async-start | bytes 2228224 | tf_op jit(solution)/shard_map/all_to_all | solution.py:325
  146.2 34.7 %all-to-all-done.2.keys = bf16[8,272,256]{2,1,0:T(8,128)(2,1)S(1)} async-done(((bf16[8,272,256]{2,1,0:T(8,128)(2,1)}), bf16[8,272,256]{2,1,0:T(8,128)(2,1)S(1)}, u32[]{:S(2)}, u32[]{:S(2)}) %all-to-all-start.2) | async-done | bytes 1114144 | tf_op jit(solution)/shard_map/all_to_all | solution.py:325
  185.0 7.1 %collective-permute-done.12.got = bf16[144,256]{1,0:T(8,128)(2,1)S(1)} collective-permute-done((bf16[144,256]{1,0:T(8,128)(2,1)S(1)}, bf16[144,256]{1,0:T(8,128)(2,1)S(1)}, u32[]{:S(2)}, u32[]{:S(2)}) %collective-permute-start.12) | collective-permute-done | bytes 73760 | tf_op jit(solution)/shard_map/ppermute | solution.py:34
  196.1 5.0 %collective-permute-start.15 = (bf16[128,256]{1,0:T(8,128)(2,1)S(1)}, bf16[128,256]{1,0:T(8,128)(2,1)S(1)}, u32[]{:S(2)}, u32[]{:S(2)}) collective-permute-start(bf16[128,256]{1,0:T(8,128)(2,1)S(1)} %merge.1), channel_id=1, source_target_pairs={{0,24},{8,0},{16,8},{24,16},{1,25},{9,1},{17,9},{25,17},{2,26},{10... | collective-permute-start | bytes 196616 | tf_op jit(solution)/shard_map/ppermute | solution.py:34
  206.0 2.8 %collective-permute-start.17 = (bf16[4,128,256]{2,1,0:T(8,128)(2,1)S(1)}, bf16[4,128,256]{2,1,0:T(8,128)(2,1)S(1)}, u32[]{:S(2)}, u32[]{:S(2)}) collective-permute-start(bf16[4,128,256]{2,1,0:T(8,128)(2,1)S(1)} %pad_maximum_fusion.2.refs_0_), channel_id=1, source_target_pairs={{0,4},{2,6},{4,0},{6,2},{1,5},{3,7},{5,1},{7,3},{8,12},{10,14},{12... | collective-permute-start | bytes 786440 | tf_op jit(solution)/shard_map/ppermute | solution.py:34
  208.8 4.9 %collective-permute-start.18 = (bf16[4,128,256]{2,1,0:T(8,128)(2,1)S(1)}, bf16[4,128,256]{2,1,0:T(8,128)(2,1)S(1)}, u32[]{:S(2)}, u32[]{:S(2)}) collective-permute-start(bf16[4,128,256]{2,1,0:T(8,128)(2,1)S(1)} %pad_maximum_fusion.2.refs_0_), channel_id=1, source_target_pairs={{0,6},{2,4},{4,2},{6,0},{1,7},{3,5},{5,3},{7,1},{8,14},{10,12},{12... | collective-permute-start | bytes 786440 | tf_op jit(solution)/shard_map/ppermute | solution.py:34
  213.7 4.0 %collective-permute-done.17.refs_2_ = bf16[4,128,256]{2,1,0:T(8,128)(2,1)S(1)} collective-permute-done((bf16[4,128,256]{2,1,0:T(8,128)(2,1)S(1)}, bf16[4,128,256]{2,1,0:T(8,128)(2,1)S(1)}, u32[]{:S(2)}, u32[]{:S(2)}) %collective-permute-start.17) | collective-permute-done | bytes 262176 | tf_op jit(solution)/shard_map/ppermute | solution.py:34
  217.7 6.1 %collective-permute-done.18.refs_3_ = bf16[4,128,256]{2,1,0:T(8,128)(2,1)S(1)} collective-permute-done((bf16[4,128,256]{2,1,0:T(8,128)(2,1)S(1)}, bf16[4,128,256]{2,1,0:T(8,128)(2,1)S(1)}, u32[]{:S(2)}, u32[]{:S(2)}) %collective-permute-start.18) | collective-permute-done | bytes 262176 | tf_op jit(solution)/shard_map/ppermute | solution.py:34
  226.5 3.2 %collective-permute-start.21 = (f32[160,256]{1,0:T(8,128)S(1)}, f32[160,256]{1,0:T(8,128)S(1)}, u32[]{:S(2)}, u32[]{:S(2)}) collective-permute-start(f32[160,256]{1,0:T(8,128)S(1)} %get-tuple-element.32), channel_id=1, source_target_pairs={{0,1},{1,0},{2,3},{3,2},{4,5},{5,4},{6,7},{7,6},{8,9},{9,8},{10,11... | collective-permute-start | bytes 491528 | tf_op jit(solution)/shard_map/ppermute | solution.py:34
  (86 shorter events, 42.8 us)
Async XLA Ops:
  7.2 84.6 %all-gather.5.cloned.1.call-start = ((), (), s32[]{:S(2)}) async-start(), calls=%async_computation.3 | async-start | bytes 2211840 | tf_op jit(solution)/shard_map/all_gather | solution.py:227
  10.5 19.9 %all-to-all-start = ((f32[32,8,128]{2,1,0:T(8,128)}), f32[32,8,128]{2,1,0:T(8,128)S(1)}, u32[]{:S(2)}, u32[]{:S(2)}) async-start(f32[32,8,128]{2,1,0:T(8,128)} %broadcast_in_dim.22), calls=%async_computation | async-start | bytes 262144 | tf_op jit(solution)/shard_map/all_to_all | solution.py:247
  30.6 9.7 %collective-permute-start = (bf16[168,256]{1,0:T(8,128)(2,1)S(1)}, bf16[168,256]{1,0:T(8,128)(2,1)S(1)}, u32[]{:S(2)}, u32[]{:S(2)}) collective-permute-start(bf16[168,256]{1,0:T(8,128)(2,1)S(1)} %maximum_maximum_fusion), channel_id=1, source_target_pairs={{0,0},{2,32},{4,4},{6,36},{8,8},{10,40},{12,12},{14,44},{16,16},{1... | collective-permute-start | bytes 258056 | tf_op jit(solution)/shard_map/ppermute | solution.py:34
  31.3 9.0 %collective-permute-start.1 = (bf16[168,256]{1,0:T(8,128)(2,1)S(1)}, bf16[168,256]{1,0:T(8,128)(2,1)S(1)}, u32[]{:S(2)}, u32[]{:S(2)}) collective-permute-start(bf16[168,256]{1,0:T(8,128)(2,1)S(1)} %maximum_maximum_fusion), channel_id=1, source_target_pairs={{0,8},{2,40},{4,12},{6,44},{8,16},{10,48},{12,20},{14,52},{16,24},... | collective-permute-start | bytes 258056 | tf_op jit(solution)/shard_map/ppermute | solution.py:34
  33.6 11.5 %collective-permute-start.2 = (bf16[168,256]{1,0:T(8,128)(2,1)S(1)}, bf16[168,256]{1,0:T(8,128)(2,1)S(1)}, u32[]{:S(2)}, u32[]{:S(2)}) collective-permute-start(bf16[168,256]{1,0:T(8,128)(2,1)S(1)} %maximum_maximum_fusion), channel_id=1, source_target_pairs={{0,16},{2,48},{4,20},{6,52},{8,24},{10,56},{12,28},{14,60},{16,0},... | collective-permute-start | bytes 258056 | tf_op jit(solution)/shard_map/ppermute | solution.py:34
  36.5 8.6 %collective-permute-start.3 = (bf16[168,256]{1,0:T(8,128)(2,1)S(1)}, bf16[168,256]{1,0:T(8,128)(2,1)S(1)}, u32[]{:S(2)}, u32[]{:S(2)}) collective-permute-start(bf16[168,256]{1,0:T(8,128)(2,1)S(1)} %maximum_maximum_fusion), channel_id=1, source_target_pairs={{0,24},{2,56},{4,28},{6,60},{8,0},{10,32},{12,4},{14,36},{16,8},{1... | collective-permute-start | bytes 258056 | tf_op jit(solution)/shard_map/ppermute | solution.py:34
  45.2 24.4 %collective-permute-start.6 = (bf16[4,168,256]{2,1,0:T(8,128)(2,1)S(1)}, bf16[4,168,256]{2,1,0:T(8,128)(2,1)S(1)}, u32[]{:S(2)}, u32[]{:S(2)}) collective-permute-start(bf16[4,168,256]{2,1,0:T(8,128)(2,1)S(1)} %pad_maximum_fusion.refs_0_), channel_id=1, source_target_pairs={{0,6},{2,4},{4,2},{6,0},{1,7},{3,5},{5,3},{7,1},{8,14},{10,12},{12... | collective-permute-start | bytes 1032200 | tf_op jit(solution)/shard_map/ppermute | solution.py:34
  58.8 12.8 %collective-permute-start.4 = (bf16[4,168,256]{2,1,0:T(8,128)(2,1)S(1)}, bf16[4,168,256]{2,1,0:T(8,128)(2,1)S(1)}, u32[]{:S(2)}, u32[]{:S(2)}) collective-permute-start(bf16[4,168,256]{2,1,0:T(8,128)(2,1)S(1)} %pad_maximum_fusion.refs_0_), channel_id=1, source_target_pairs={{0,2},{2,0},{4,6},{6,4},{1,3},{3,1},{5,7},{7,5},{8,10},{10,8},{12,... | collective-permute-start | bytes 1032200 | tf_op jit(solution)/shard_map/ppermute | solution.py:34
  61.2 15.1 %collective-permute-start.5 = (bf16[4,168,256]{2,1,0:T(8,128)(2,1)S(1)}, bf16[4,168,256]{2,1,0:T(8,128)(2,1)S(1)}, u32[]{:S(2)}, u32[]{:S(2)}) collective-permute-start(bf16[4,168,256]{2,1,0:T(8,128)(2,1)S(1)} %pad_maximum_fusion.refs_0_), channel_id=1, source_target_pairs={{0,4},{2,6},{4,0},{6,2},{1,5},{3,7},{5,1},{7,3},{8,12},{10,14},{12... | collective-permute-start | bytes 1032200 | tf_op jit(solution)/shard_map/ppermute | solution.py:34
  64.9 19.2 %collective-permute-start.7 = (bf16[4,168,256]{2,1,0:T(8,128)(2,1)S(1)}, bf16[4,168,256]{2,1,0:T(8,128)(2,1)S(1)}, u32[]{:S(2)}, u32[]{:S(2)}) collective-permute-start(bf16[4,168,256]{2,1,0:T(8,128)(2,1)S(1)} %pad_maximum_fusion.refs_0_), channel_id=1, source_target_pairs={{0,1},{1,0},{2,3},{3,2},{4,5},{5,4},{6,7},{7,6},{8,9},{9,8},{10,11... | collective-permute-start | bytes 1032200 | tf_op jit(solution)/shard_map/ppermute | solution.py:34
  69.6 22.1 %collective-permute-start.10 = (bf16[4,168,256]{2,1,0:T(8,128)(2,1)S(1)}, bf16[4,168,256]{2,1,0:T(8,128)(2,1)S(1)}, u32[]{:S(2)}, u32[]{:S(2)}) collective-permute-start(bf16[4,168,256]{2,1,0:T(8,128)(2,1)S(1)} %collective-permute-done.6.refs_3_), channel_id=1, source_target_pairs={{0,1},{1,0},{2,3},{3,2},{4,5},{5,4},{6,7},{7,6},{8,9},{9,8},{10,11... | collective-permute-start | bytes 1032200 | tf_op jit(solution)/shard_map/ppermute | solution.py:34
  71.5 20.2 %collective-permute-start.8 = (bf16[4,168,256]{2,1,0:T(8,128)(2,1)S(1)}, bf16[4,168,256]{2,1,0:T(8,128)(2,1)S(1)}, u32[]{:S(2)}, u32[]{:S(2)}) collective-permute-start(bf16[4,168,256]{2,1,0:T(8,128)(2,1)S(1)} %collective-permute-done.4.refs_1_), channel_id=1, source_target_pairs={{0,1},{1,0},{2,3},{3,2},{4,5},{5,4},{6,7},{7,6},{8,9},{9,8},{10,11... | collective-permute-start | bytes 1032200 | tf_op jit(solution)/shard_map/ppermute | solution.py:34
  76.3 15.5 %collective-permute-start.9 = (bf16[4,168,256]{2,1,0:T(8,128)(2,1)S(1)}, bf16[4,168,256]{2,1,0:T(8,128)(2,1)S(1)}, u32[]{:S(2)}, u32[]{:S(2)}) collective-permute-start(bf16[4,168,256]{2,1,0:T(8,128)(2,1)S(1)} %collective-permute-done.5.refs_2_), channel_id=1, source_target_pairs={{0,1},{1,0},{2,3},{3,2},{4,5},{5,4},{6,7},{7,6},{8,9},{9,8},{10,11... | collective-permute-start | bytes 1032200 | tf_op jit(solution)/shard_map/ppermute | solution.py:34
  81.3 63.2 %collective-permute-start.19 = (bf16[320,128]{1,0:T(8,128)(2,1)}, bf16[320,128]{1,0:T(8,128)(2,1)}, u32[]{:S(2)}, u32[]{:S(2)}) collective-permute-start(bf16[320,128]{1,0:T(8,128)(2,1)} %bitcast.82), channel_id=1, source_target_pairs={{0,0},{1,1},{2,32},{3,33},{4,64},{5,65},{6,96},{7,97},{8,128},{9,1... | collective-permute-start | bytes 245768 | tf_op jit(solution)/shard_map/ppermute | solution.py:34
  84.1 60.4 %collective-permute-start.20 = (bf16[320,128]{1,0:T(8,128)(2,1)}, bf16[320,128]{1,0:T(8,128)(2,1)}, u32[]{:S(2)}, u32[]{:S(2)}) collective-permute-start(bf16[320,128]{1,0:T(8,128)(2,1)} %bitcast.83), channel_id=1, source_target_pairs={{0,32},{1,33},{2,0},{3,1},{4,96},{5,97},{6,64},{7,65},{8,160},{9,1... | collective-permute-start | bytes 245768 | tf_op jit(solution)/shard_map/ppermute | solution.py:34
  96.5 23.5 %collective-permute-start.11 = (bf16[4,128,256]{2,1,0:T(8,128)(2,1)S(1)}, bf16[4,128,256]{2,1,0:T(8,128)(2,1)S(1)}, u32[]{:S(2)}, u32[]{:S(2)}) collective-permute-start(bf16[4,128,256]{2,1,0:T(8,128)(2,1)S(1)} %get-tuple-element.21), channel_id=1, source_target_pairs={{0,32},{32,0},{1,33},{33,1},{2,34},{34,2},{3,35},{35,3},{4,36},{36... | collective-permute-start | bytes 786440 | tf_op jit(solution)/shard_map/ppermute | solution.py:34
  120.8 12.8 %all-to-all-start.1 = ((f32[32,8,128]{2,1,0:T(8,128)}), f32[32,8,128]{2,1,0:T(8,128)S(1)}, u32[]{:S(2)}, u32[]{:S(2)}) async-start(f32[32,8,128]{2,1,0:T(8,128)} %get-tuple-element.22), calls=%async_computation.1 | async-start | bytes 262144 | tf_op jit(solution)/shard_map/all_to_all | solution.py:312
  135.0 45.9 %all-to-all-start.2 = ((bf16[8,272,256]{2,1,0:T(8,128)(2,1)}), bf16[8,272,256]{2,1,0:T(8,128)(2,1)S(1)}, u32[]{:S(2)}, u32[]{:S(2)}) async-start(bf16[8,272,256]{2,1,0:T(8,128)(2,1)} %get-tuple-element.27), calls=%async_computation.2 | async-start | bytes 2228224 | tf_op jit(solution)/shard_map/all_to_all | solution.py:325
  144.5 69.2 %all-gather.7.cloned.1.call-start = ((), (), s32[]{:S(2)}) async-start(), calls=%async_computation.4 | async-start | bytes 1474560 | tf_op jit(solution)/shard_map/all_gather | solution.py:242
  183.1 9.0 %collective-permute-start.12 = (bf16[144,256]{1,0:T(8,128)(2,1)S(1)}, bf16[144,256]{1,0:T(8,128)(2,1)S(1)}, u32[]{:S(2)}, u32[]{:S(2)}) collective-permute-start(bf16[144,256]{1,0:T(8,128)(2,1)S(1)} %get-tuple-element.30), channel_id=1, source_target_pairs={{0,32},{32,0},{1,33},{33,1},{2,34},{34,2},{3,35},{35,3},{4,36},{36... | collective-permute-start | bytes 221192 | tf_op jit(solution)/shard_map/ppermute | solution.py:34
  192.2 9.0 %collective-permute-start.13 = (bf16[128,256]{1,0:T(8,128)(2,1)S(1)}, bf16[128,256]{1,0:T(8,128)(2,1)S(1)}, u32[]{:S(2)}, u32[]{:S(2)}) collective-permute-start(bf16[128,256]{1,0:T(8,128)(2,1)S(1)} %merge.1), channel_id=1, source_target_pairs={{0,8},{8,16},{16,24},{24,0},{1,9},{9,17},{17,25},{25,1},{2,10},{10... | collective-permute-start | bytes 196616 | tf_op jit(solution)/shard_map/ppermute | solution.py:34
  204.0 9.6 %collective-permute-start.16 = (bf16[4,128,256]{2,1,0:T(8,128)(2,1)S(1)}, bf16[4,128,256]{2,1,0:T(8,128)(2,1)S(1)}, u32[]{:S(2)}, u32[]{:S(2)}) collective-permute-start(bf16[4,128,256]{2,1,0:T(8,128)(2,1)S(1)} %pad_maximum_fusion.2.refs_0_), channel_id=1, source_target_pairs={{0,2},{2,0},{4,6},{6,4},{1,3},{3,1},{5,7},{7,5},{8,10},{10,8},{12,... | collective-permute-start | bytes 786440 | tf_op jit(solution)/shard_map/ppermute | solution.py:34
  206.0 11.7 %collective-permute-start.17 = (bf16[4,128,256]{2,1,0:T(8,128)(2,1)S(1)}, bf16[4,128,256]{2,1,0:T(8,128)(2,1)S(1)}, u32[]{:S(2)}, u32[]{:S(2)}) collective-permute-start(bf16[4,128,256]{2,1,0:T(8,128)(2,1)S(1)} %pad_maximum_fusion.2.refs_0_), channel_id=1, source_target_pairs={{0,4},{2,6},{4,0},{6,2},{1,5},{3,7},{5,1},{7,3},{8,12},{10,14},{12... | collective-permute-start | bytes 786440 | tf_op jit(solution)/shard_map/ppermute | solution.py:34
  208.8 15.0 %collective-permute-start.18 = (bf16[4,128,256]{2,1,0:T(8,128)(2,1)S(1)}, bf16[4,128,256]{2,1,0:T(8,128)(2,1)S(1)}, u32[]{:S(2)}, u32[]{:S(2)}) collective-permute-start(bf16[4,128,256]{2,1,0:T(8,128)(2,1)S(1)} %pad_maximum_fusion.2.refs_0_), channel_id=1, source_target_pairs={{0,6},{2,4},{4,2},{6,0},{1,7},{3,5},{5,3},{7,1},{8,14},{10,12},{12... | collective-permute-start | bytes 786440 | tf_op jit(solution)/shard_map/ppermute | solution.py:34
  (8 other events, 194.3 us)
Sparse Core Ops, SparseCore 0:
  10.1 45.0 all-gather.4
  147.4 42.3 all-gather.6

commit v2 on v1

--- a/solution.py
+++ b/solution.py
@@ -61,19 +61,20 @@
 
 def project_kernel(at, *refs):
     xs, w, mine_q, mine_kv, message, meta, acc = refs[:8], refs[8], *refs[9:]
-    zl, x, c, zh = at[0], at[1], at[2], at[3]
+    zl, x, c, yc = at[0], at[1], at[2], at[3]
     acc[...] = jnp.zeros_like(acc)
-    first = lax.rem(x, 2)
     for i in range(2):
         core = lax.rem(c + i, 2)
         for j in range(2):
-            high = lax.rem(x // 2 + j, 2)
-            left, right = xs[4 * i + 2 * j], xs[4 * i + 2 * j + 1]
+            x_first = lax.rem(x - j + 4, 4)
+            first = x_first // 2
+            low = lax.rem(x_first, 2)
+            left, right = xs[4 * i + j], xs[4 * i + j + 2]
             total = None
             for k in range(4):
                 z_from = lax.rem(zl - k + 4, 4)
                 both = jnp.concatenate([left[k, :160, :], right[k, :160, :]], axis=1)
-                block = z_from * 2 + high
+                block = z_from * 2 + low
                 weights = jnp.concatenate([w[block, p, core] for p in range(3)], axis=1)
                 term = contract_first(weights, both)
                 total = term if total is None else total + term
@@ -86,10 +87,10 @@
         part = acc[block]
         mine_q[block] = part[:128]
         message[block] = part[:128].astype(BF16)
-    own = acc[zh]
+    own = acc[yc]
     mine_kv[0] = own[128:256]
     mine_kv[1] = own[256:]
-    other = acc[1 - zh]
+    other = acc[1 - yc]
     message[2] = other[128:256].astype(BF16)
     message[3] = other[256:].astype(BF16)
 
@@ -110,7 +111,7 @@
 
 def rotate_kernel(width, got, full_q, full_kv, cosine, sine, qg, kg, meta, at, q_out, k_cache, v_cache, message):
     totals = jnp.sum(got[...], axis=0)
-    zh = at[0]
+    yc = at[0]
     even = lax.rem(lax.broadcasted_iota(jnp.int32, (HEAD_DIM, 256), 0), 2) == 0
 
     def rotated(value, gain, row, cos, sin):
@@ -123,28 +124,31 @@
         return normed * cos + partner * sin
 
     for block in range(2):
-        q_out[:, 256 * block : 256 * block + 256] = rotated(
+        here = pl.ds(256 * block, 256)
+        q_out[128:144, here] = jnp.concatenate([meta[block], jnp.zeros((8, 256), F32)], axis=0).astype(BF16)
+        q_out[:128, here] = rotated(
             full_q[block], qg[...], 2 * block, cosine[block], sine[block]
         ).astype(BF16)
-    k_rot = rotated(full_kv[0], kg[...], 4, cosine[zh], sine[zh])
+    k_rot = rotated(full_kv[0], kg[...], 4, cosine[yc], sine[yc])
     value = full_kv[1]
     k_cache[...] = k_rot.T.astype(BF16)
     v_cache[...] = value.T.astype(BF16)
     k_low = k_rot.astype(BF16)
     v_low = value.astype(BF16)
-    extra = jnp.concatenate([meta[zh], jnp.zeros((8, 256), F32)], axis=0).astype(BF16)
+    extra = jnp.concatenate([meta[yc], jnp.zeros((8, 256), F32)], axis=0).astype(BF16)
     for t in range(message.shape[0]):
         message[t, :128] = k_low
         message[t, 128:256] = v_low
         message[t, 256:272] = extra
 
 
-def attend_kernel(at, q, meta, keys, mine, mine_lse, message, held):
-    zh = at[0]
+def attend_kernel(at, q, q_got, keys, mine, mine_lse, m1, m2, m3, held):
+    messages = (m1, m2, m3)
+    yc = at[0]
     count = keys.shape[0]
     scale = LOG2E / math.sqrt(HEAD_DIM)
-    q_low = q[...]
-    seg_q = jnp.concatenate([meta[0, 3:4], meta[1, 3:4]], axis=1)
+    q_low = jnp.concatenate([q[:128], q_got[:128]], axis=1)
+    seg_q = jnp.concatenate([q[128:144], q_got[128:144]], axis=1).astype(F32)[3:4]
     top = None
     for b in range(count):
         seg_k = keys[b, 256:272].astype(F32).T[:, 3:4]
@@ -154,8 +158,8 @@
         here = jnp.max(scores, axis=0, keepdims=True)
         top = here if top is None else jnp.maximum(top, here)
     top = jnp.maximum(top, -1e20)
-    total = jnp.zeros((1, 512), F32)
-    weighted = jnp.zeros((HEAD_DIM, 512), F32)
+    total = jnp.zeros((1, 1024), F32)
+    weighted = jnp.zeros((HEAD_DIM, 1024), F32)
     for b in range(count):
         weights = jnp.exp2(held[b] - top)
         total = total + jnp.sum(weights, axis=0, keepdims=True)
@@ -166,42 +170,51 @@
     safe = jnp.where(some, total, 1.0)
     out = weighted / safe
     lse = jnp.where(some, top + jnp.log2(safe), NEG_FILL)
-    first = zh == 0
-    own = jnp.where(first, out[:, :256], out[:, 256:])
-    other = jnp.where(first, out[:, 256:], out[:, :256])
-    own_lse = jnp.where(first, lse[:, :256], lse[:, 256:])
-    other_lse = jnp.where(first, lse[:, 256:], lse[:, :256])
-    mine[...] = own
-    mine_lse[...] = jnp.broadcast_to(own_lse, (8, 256))
-    high = other_lse.astype(BF16)
-    rest = other_lse - high.astype(F32)
-    middle = rest.astype(BF16)
-    low = (rest - middle.astype(F32)).astype(BF16)
-    message[:128] = other.astype(BF16)
-    message[128:144] = jnp.concatenate(
-        [high.astype(F32), middle.astype(F32), low.astype(F32), jnp.zeros((13, 256), F32)], axis=0
-    ).astype(BF16)
-
-
-def merge_kernel(mine, mine_lse, got, out):
-    rows = got[128:144].astype(F32)
-    other_lse = rows[0:1] + rows[1:2] + rows[2:3]
-    own_lse = mine_lse[0:1]
-    top = jnp.maximum(own_lse, other_lse)
-    own_weight = jnp.exp2(own_lse - top)
-    other_weight = jnp.exp2(other_lse - top)
-    both = own_weight + other_weight
-    out[...] = (
-        mine[...] * (own_weight / both) + got[:128].astype(F32) * (other_weight / both)
-    ).astype(BF16)
+    first = yc == 0
+    for pair in range(2):
+        a, b = slice(512 * pair, 512 * pair + 256), slice(512 * pair + 256, 512 * pair + 512)
+        for swap in range(2):
+            keep, give = (a, b) if swap == 0 else (b, a)
+            part = jnp.where(first, out[:, keep], out[:, give])
+            part_lse = jnp.where(first, lse[:, keep], lse[:, give])
+            if pair == 0 and swap == 0:
+                mine[...] = part
+                mine_lse[...] = jnp.broadcast_to(part_lse, (8, 256))
+                continue
+            message = messages[2 * pair + swap - 1]
+            high = part_lse.astype(BF16)
+            rest = part_lse - high.astype(F32)
+            middle = rest.astype(BF16)
+            low = (rest - middle.astype(F32)).astype(BF16)
+            message[:128] = part.astype(BF16)
+            message[128:144] = jnp.concatenate(
+                [high.astype(F32), middle.astype(F32), low.astype(F32), jnp.zeros((13, 256), F32)],
+                axis=0,
+            ).astype(BF16)
+
+
+def merge_kernel(mine, mine_lse, *refs):
+    gots, out = refs[:-1], refs[-1]
+    parts = [(mine_lse[0:1], mine[...])]
+    for got in gots:
+        rows = got[128:144].astype(F32)
+        parts.append((rows[0:1] + rows[1:2] + rows[2:3], got[:128].astype(F32)))
+    top = functools.reduce(jnp.maximum, [lse for lse, _ in parts])
+    weights = [jnp.exp2(lse - top) for lse, _ in parts]
+    total = sum(weights[1:], weights[0])
+    value = None
+    for weight, (_, part) in zip(weights, parts, strict=True):
+        term = part * (weight / total)
+        value = term if value is None else value + term
+    out[...] = value.astype(BF16)
 
 
 def output_kernel(at, *refs):
     heads, w, mine, message, held = refs[:4], refs[4], *refs[5:]
-    zl, x, c, zh = at[0], at[1], at[2], at[3]
+    zl, x, c, zh = at[0], at[1], at[2], at[4]
     total = None
     for j in range(4):
-        x_from = lax.rem(x // 2 + j // 2, 2) * 2 + lax.rem(x + j, 2)
+        x_from = lax.rem(x - j + 4, 4)
         for k in range(4):
             chip = lax.rem(zl - k + 4, 4) * 4 + x_from
             flip = lax.rem(lax.rem(chip, 2) + zh, 2)
@@ -218,13 +231,15 @@
     model_width = feat_local * 32
     heads_width = 4096
     zl, c = lax.axis_index("zl"), lax.axis_index("c")
-    zh = lax.axis_index("zh")
+    yc, zh = lax.axis_index("yc"), lax.axis_index("zh")
     x = lax.axis_index("xh") * 2 + lax.axis_index("xl")
-    at = jnp.stack([zl, x, c, zh]).astype(jnp.int32)
-    at_zh = jnp.stack([zh]).astype(jnp.int32)
+    at = jnp.stack([zl, x, c, yc, zh]).astype(jnp.int32)
+    at_yc = jnp.stack([yc]).astype(jnp.int32)
 
     w_local = jnp.transpose(w_qkv, (1, 0, 2))
-    w_all = lax.all_gather(w_local, ("ya", "yb", "yc"), axis=0, tiled=False)
+    w_all = lax.all_to_all(
+        jnp.broadcast_to(w_local, (8,) + w_local.shape), ("ya", "yb", "zh"), 0, 0, tiled=True
+    )
     w_all = w_all.reshape(8, 3, 2, 160, 128)
 
     axes = SEQ + TP
@@ -238,13 +253,14 @@
 
         return permute(w_out.T, axes, move)
 
-    wo_pair = jnp.stack([turned(0), turned(1)])
-    wo_all = lax.all_gather(wo_pair, ("ya", "yb", "yc"), axis=0, tiled=False)
+    wo_turned = (turned(0), turned(1))
 
     x_t = hidden_in.T.astype(F32)
     sums = jnp.stack([jnp.sum(x_t, axis=0), jnp.sum(x_t * x_t, axis=0)]).reshape(4, 128)
     sums = jnp.concatenate([sums, jnp.zeros((4, 128), F32)], axis=0)
     sums = lax.all_to_all(jnp.broadcast_to(sums, (32, 8, 128)), TP, 0, 0, tiled=True)
+    sums, wo_turned = lax.optimization_barrier((sums, wo_turned))
+    wo_all = lax.all_gather(jnp.stack(wo_turned), ("ya", "yb", "yc"), axis=0, tiled=False)
     sums = jnp.sum(sums, axis=0)[:4].reshape(2, tok_rows)
     mean_value = sums[0:1] / model_width
     variance = sums[1:2] / model_width - mean_value * mean_value
@@ -264,14 +280,14 @@
     slots = [
         permute(
             packet,
-            ("zh", "zl", "xh", "xl"),
-            lambda zh, zl, xh, xl, k=k: (xl, (zl + k) % 4, xh, zh),
+            ("yc", "zl", "xh", "xl"),
+            lambda yc, zl, xh, xl, k=k: (xh, (zl + k) % 4, yc, xl),
         )
         for k in range(4)
     ]
     held = jnp.stack(slots)
     along_x = [held] + [
-        permute(held, ("xh", "xl"), lambda xh, xl, j=j: (xh ^ (j >> 1), xl ^ (j & 1)))
+        permute(held, ("xh", "xl"), lambda xh, xl, j=j: divmod((xh * 2 + xl + j) % 4, 2))
         for j in range(1, 4)
     ]
     swapped = [permute(part, ("c",), lambda c: (1 - c,)) for part in along_x]
@@ -290,7 +306,7 @@
         name="project",
         cost=pl.CostEstimate(flops=2 * 512 * 2560 * 384, bytes_accessed=5 << 20, transcendentals=0),
     )
-    got = permute(message, ("zh",), lambda zh: (1 - zh,))
+    got = permute(message, ("yc",), lambda yc: (1 - yc,))
 
     part_width = HEAD_DIM // 6
     widths = (HEAD_DIM - 4 * part_width, 2 * part_width, 2 * part_width)
@@ -313,33 +329,37 @@
     q_rot, k_cache, v_cache, kv_message = call(
         lambda at, *refs: rotate_kernel(heads_width, *refs[:8], at, *refs[8:]),
         (
-            shaped((128, 512), BF16),
+            shaped((144, 512), BF16),
             shaped((256, 128), BF16),
             shaped((256, 128), BF16),
-            shaped((8, 272, 256), BF16),
+            shaped((4, 272, 256), BF16),
         ),
         [stats, full_q, full_kv, cosine, sine, q_gain.reshape(128, 1), k_gain.reshape(128, 1), meta],
-        scalars=at_zh,
+        scalars=at_yc,
         name="rotate",
     )
-    keys = lax.all_to_all(kv_message, ("ya", "yb", "yc"), 0, 0, tiled=True)
-    mine, mine_lse, o_message = call(
+    q_got = permute(q_rot, ("yb",), lambda yb: (1 - yb,))
+    keys = lax.all_to_all(kv_message, ("ya", "zh"), 0, 0, tiled=True)
+    mine, mine_lse, *o_messages = call(
         attend_kernel,
-        (shaped((128, 256), F32), shaped((8, 256), F32), shaped((144, 256), BF16)),
-        [q_rot, meta, keys],
-        scalars=at_zh,
-        scratch=[pltpu.VMEM((8, 256, 512), F32)],
+        (shaped((128, 256), F32), shaped((8, 256), F32)) + (shaped((144, 256), BF16),) * 3,
+        [q_rot, q_got, keys],
+        scalars=at_yc,
+        scratch=[pltpu.VMEM((4, 256, 1024), F32)],
         name="attend",
     )
-    o_got = permute(o_message, ("zh",), lambda zh: (1 - zh,))
-    attention = call(merge_kernel, shaped((128, 256), BF16), [mine, mine_lse, o_got], name="merge")
+    o_got = [
+        permute(o, ("yb", "yc"), lambda yb, yc, d=d: (yb ^ (d >> 1), yc ^ (d & 1)))
+        for d, o in enumerate(o_messages, 1)
+    ]
+    attention = call(merge_kernel, shaped((128, 256), BF16), [mine, mine_lse] + o_got, name="merge")
 
     by_z = [attention] + [
         permute(attention, ("zl",), lambda zl, k=k: ((zl + k) % 4,)) for k in range(1, 4)
     ]
     by_z = jnp.stack(by_z)
     by_x = [by_z] + [
-        permute(by_z, ("xh", "xl"), lambda xh, xl, j=j: (xh ^ (j >> 1), xl ^ (j & 1)))
+        permute(by_z, ("xh", "xl"), lambda xh, xl, j=j: divmod((xh * 2 + xl + j) % 4, 2))
         for j in range(1, 4)
     ]
     out_mine, out_message = call(

time: 239 us -> 288 us (1.21)
  starting transfers between devices: 106 us -> 149 us
  blocking collectives: 0 us -> 19.7 us
  waiting for transfers between devices: 95.4 us -> 81.8 us
    all_to_all x2, waiting for transfers between devices: 39.9 us -> 0.01 us  [the longest x1 0.01 us: body(): keys = lax.all_to_all(kv_message, ('ya', 'zh'), 0, 0, tiled=True)]
    ppermute x22 -> x25, starting transfers between devices: 81 us -> 119 us  [permute(): return lax.ppermute(value, axes, pairs)]
    ppermute x22 -> x25, waiting for transfers between devices: 47.3 us -> 74.3 us  [permute(): return lax.ppermute(value, axes, pairs)]
    all_to_all x0 -> x1, blocking collectives: none -> 19.7 us  [body(): lax.all_to_all(jnp.broadcast_to(sums, (32, 8, 128)), TP, 0, 0, tiled=True)]
    all_to_all x1, starting transfers between devices: 4.26 us -> 7.79 us  [body(): stats = lax.all_to_all(stats, TP, 0, 0, tiled=True)]
  transfers between devices with their start and end apart: 27 -> 29, of which waited for: 10 -> 12; matrix products, arithmetic and copies ran while one was open for 4% -> 2% of each run, Pallas kernels for 3% -> 3%
where the time goes in v2:
time: 288 us; the launch traced here: 286 us
  starting transfers between devices  149 us (52%)
  waiting for transfers between devices  81.8 us (28%)
  blocking collectives  19.7 us (7%)
  between operations  14.6 us (5%)
  Pallas kernels  8.73 us (3%)
  other arithmetic  6.5 us (2%)
  local copies, waits for them, and re-layouts  4.96 us (2%)
    ppermute x25, starting transfers between devices, permute(): return lax.ppermute(value, axes, pairs)  119 us
    ppermute x25, waiting for transfers between devices, permute(): return lax.ppermute(value, axes, pairs)  74.3 us
    all_to_all x1, blocking collectives, body(): lax.all_to_all(jnp.broadcast_to(sums, (32, 8, 128)), TP, 0, 0, tiled=True)  19.7 us
    all_to_all x1, starting transfers between devices, body(): lax.all_to_all(jnp.broadcast_to(w_local, (8,) + w_local.shape), ('ya', 'y...  12.7 us
    all_to_all x1, starting transfers between devices, body(): keys = lax.all_to_all(kv_message, ('ya', 'zh'), 0, 0, tiled=True)  9.78 us
    pallas_call x6, Pallas kernels, call(): pl.pallas_call(kernel, out_shape=out_shape, in_specs=specs, out_specs=jax...  8.73 us
    all_to_all x1, starting transfers between devices, body(): stats = lax.all_to_all(stats, TP, 0, 0, tiled=True)  7.79 us
    all_to_all x1, waiting for transfers between devices, body(): stats = lax.all_to_all(stats, TP, 0, 0, tiled=True)  7.48 us
  transfers between devices with their start and end apart: 29, of which 12 were waited for; matrix products, arithmetic and copies ran while one was open for 2% of the time, Pallas kernels for 3%

profile of v2, /device:TPU:1, one launch (start us, length us, event | category | flops | bytes accessed | tf_op | source)
XLA Modules:
  0.0 286.2 jit_solution(3238969033399981557)
XLA Ops:
  9.1 19.7 %all_to_all.20 = f32[32,8,128]{2,1,0:T(8,128)S(1)} all-to-all(f32[32,8,128]{2,1,0:T(8,128)S(1)} %broadcast_in_dim.25), channel_id=1, replica_groups=mesh['ya'=2,'yb'=2,'yc'=2,'zh'=2,'zl'=4,'xh'=2,'xl'=2,'c'=2] {'zl','xh',..., dimensions={0} | all-to-all | bytes 262144 | tf_op jit(solution)/shard_map/all_to_all | solution.py:261
  31.5 12.7 %all-to-all-start.1 = ((bf16[8,3,320,128]{3,2,1,0:T(8,128)(2,1)}), bf16[8,3,320,128]{3,2,1,0:T(8,128)(2,1)S(1)}, u32[]{:S(2)}, u32[]{:S(2)}) async-start(bf16[8,3,320,128]{3,2,1,0:T(8,128)(2,1)} %broadcast_in_dim.28), calls=%async_computation.1 | async-start | bytes 3932160 | tf_op jit(solution)/shard_map/all_to_all | solution.py:240
  45.0 8.5 %collective-permute-start.1 = (bf16[320,128]{1,0:T(8,128)(2,1)S(1)}, bf16[320,128]{1,0:T(8,128)(2,1)S(1)}, u32[]{:S(2)}, u32[]{:S(2)}) collective-permute-start(bf16[320,128]{1,0:T(8,128)(2,1)S(1)} %bitcast.86), channel_id=1, source_target_pairs={{0,32},{1,33},{2,0},{3,1},{4,96},{5,97},{6,64},{7,65},{8,160},{9,1... | collective-permute-start | bytes 245768 | tf_op jit(solution)/shard_map/ppermute | solution.py:34
  54.3 31.0 %collective-permute-done.1 = bf16[320,128]{1,0:T(8,128)(2,1)S(1)} collective-permute-done((bf16[320,128]{1,0:T(8,128)(2,1)S(1)}, bf16[320,128]{1,0:T(8,128)(2,1)S(1)}, u32[]{:S(2)}, u32[]{:S(2)}) %collective-permute-start.1) | collective-permute-done | bytes 81952 | tf_op jit(solution)/shard_map/ppermute | solution.py:34
  86.2 26.2 %collective-permute-start.3 = (bf16[168,256]{1,0:T(8,128)(2,1)S(1)}, bf16[168,256]{1,0:T(8,128)(2,1)S(1)}, u32[]{:S(2)}, u32[]{:S(2)}) collective-permute-start(bf16[168,256]{1,0:T(8,128)(2,1)S(1)} %maximum_maximum_fusion), channel_id=1, source_target_pairs={{0,8},{2,10},{4,72},{6,74},{8,16},{10,18},{12,80},{14,82},{16,24},... | collective-permute-start | bytes 258056 | tf_op jit(solution)/shard_map/ppermute | solution.py:34
  114.3 4.0 %collective-permute-start.5 = (bf16[168,256]{1,0:T(8,128)(2,1)S(1)}, bf16[168,256]{1,0:T(8,128)(2,1)S(1)}, u32[]{:S(2)}, u32[]{:S(2)}) collective-permute-start(bf16[168,256]{1,0:T(8,128)(2,1)S(1)} %maximum_maximum_fusion), channel_id=1, source_target_pairs={{0,24},{2,26},{4,88},{6,90},{8,0},{10,2},{12,64},{14,66},{16,8},{1... | collective-permute-start | bytes 258056 | tf_op jit(solution)/shard_map/ppermute | solution.py:34
  118.3 3.7 %collective-permute-done.4 = bf16[168,256]{1,0:T(8,128)(2,1)S(1)} collective-permute-done((bf16[168,256]{1,0:T(8,128)(2,1)S(1)}, bf16[168,256]{1,0:T(8,128)(2,1)S(1)}, u32[]{:S(2)}, u32[]{:S(2)}) %collective-permute-start.4) | collective-permute-done | bytes 86048 | tf_op jit(solution)/shard_map/ppermute | solution.py:34
  122.1 5.0 %collective-permute-start.6 = (bf16[4,168,256]{2,1,0:T(8,128)(2,1)S(1)}, bf16[4,168,256]{2,1,0:T(8,128)(2,1)S(1)}, u32[]{:S(2)}, u32[]{:S(2)}) collective-permute-start(bf16[4,168,256]{2,1,0:T(8,128)(2,1)S(1)} %pad_maximum_fusion.refs_0_), channel_id=1, source_target_pairs={{0,2},{2,4},{4,6},{6,0},{1,3},{3,5},{5,7},{7,1},{8,10},{10,12},{12... | collective-permute-start | bytes 1032200 | tf_op jit(solution)/shard_map/ppermute | solution.py:34
  127.1 13.8 %collective-permute-start.7 = (bf16[4,168,256]{2,1,0:T(8,128)(2,1)S(1)}, bf16[4,168,256]{2,1,0:T(8,128)(2,1)S(1)}, u32[]{:S(2)}, u32[]{:S(2)}) collective-permute-start(bf16[4,168,256]{2,1,0:T(8,128)(2,1)S(1)} %pad_maximum_fusion.refs_0_), channel_id=1, source_target_pairs={{0,4},{2,6},{4,0},{6,2},{1,5},{3,7},{5,1},{7,3},{8,12},{10,14},{12... | collective-permute-start | bytes 1032200 | tf_op jit(solution)/shard_map/ppermute | solution.py:34
  142.8 5.9 %collective-permute-start.9 = (bf16[4,168,256]{2,1,0:T(8,128)(2,1)S(1)}, bf16[4,168,256]{2,1,0:T(8,128)(2,1)}, u32[]{:S(2)}, u32[]{:S(2)}) collective-permute-start(bf16[4,168,256]{2,1,0:T(8,128)(2,1)S(1)} %pad_maximum_fusion.refs_0_), channel_id=1, source_target_pairs={{0,1},{1,0},{2,3},{3,2},{4,5},{5,4},{6,7},{7,6},{8,9},{9,8},{10,11... | collective-permute-start | bytes 1032200 | tf_op jit(solution)/shard_map/ppermute | solution.py:34
  151.5 5.7 %collective-permute-start.11 = (bf16[4,168,256]{2,1,0:T(8,128)(2,1)S(1)}, bf16[4,168,256]{2,1,0:T(8,128)(2,1)}, u32[]{:S(2)}, u32[]{:S(2)}) collective-permute-start(bf16[4,168,256]{2,1,0:T(8,128)(2,1)S(1)} %collective-permute-done.7.refs_2_), channel_id=1, source_target_pairs={{0,1},{1,0},{2,3},{3,2},{4,5},{5,4},{6,7},{7,6},{8,9},{9,8},{10,11... | collective-permute-start | bytes 1032200 | tf_op jit(solution)/shard_map/ppermute | solution.py:34
  161.6 3.3 %project.1 = (f32[2,128,256]{2,1,0:T(8,128)S(1)}, f32[2,128,256]{2,1,0:T(8,128)S(1)}, bf16[4,128,256]{2,1,0:T(8,128)(2,1)S(1)}, f32[2,8,256]{2,1,0:T(8,128)S(1)}) custom-call(s32[5]{0:T(128)S(1)} %stack.72.at, bf16[4,168,256]{2,1,0:T(8,128)(2,1)S(1)} %pad_maximum_fusion.refs_0_, bf16[4,168,256]{2,1,0:T(8,128)(2,1)S(1)} %collective-permute-done.6.refs_1_, ...), custom_call_target="tpu_custom_call" | custom-call | flops 1006632960 | bytes 5242880 | tf_op jit(solution)/shard_map/project/pallas_call | solution.py:46
  165.0 4.7 %collective-permute-start.13 = (bf16[4,128,256]{2,1,0:T(8,128)(2,1)S(1)}, bf16[4,128,256]{2,1,0:T(8,128)(2,1)S(1)}, u32[]{:S(2)}, u32[]{:S(2)}) collective-permute-start(bf16[4,128,256]{2,1,0:T(8,128)(2,1)S(1)} %get-tuple-element.27), channel_id=1, source_target_pairs={{0,64},{64,0},{1,65},{65,1},{2,66},{66,2},{3,67},{67,3},{4,68},{68... | collective-permute-start | bytes 786440 | tf_op jit(solution)/shard_map/ppermute | solution.py:34
  169.8 6.5 %collective-permute-done.13.got = bf16[4,128,256]{2,1,0:T(8,128)(2,1)S(1)} collective-permute-done((bf16[4,128,256]{2,1,0:T(8,128)(2,1)S(1)}, bf16[4,128,256]{2,1,0:T(8,128)(2,1)S(1)}, u32[]{:S(2)}, u32[]{:S(2)}) %collective-permute-start.13) | collective-permute-done | bytes 262176 | tf_op jit(solution)/shard_map/ppermute | solution.py:34
  177.0 7.8 %all-to-all-start.2 = ((f32[32,8,128]{2,1,0:T(8,128)}), f32[32,8,128]{2,1,0:T(8,128)S(1)}, u32[]{:S(2)}, u32[]{:S(2)}) async-start(f32[32,8,128]{2,1,0:T(8,128)} %get-tuple-element.28), calls=%async_computation.2 | async-start | bytes 262144 | tf_op jit(solution)/shard_map/all_to_all | solution.py:328
  185.9 7.5 %all-to-all-done.2.refs_0_ = f32[32,8,128]{2,1,0:T(8,128)S(1)} async-done(((f32[32,8,128]{2,1,0:T(8,128)}), f32[32,8,128]{2,1,0:T(8,128)S(1)}, u32[]{:S(2)}, u32[]{:S(2)}) %all-to-all-start.2) | async-done | bytes 131104 | tf_op jit(solution)/shard_map/all_to_all | solution.py:328
  194.5 9.8 %all-to-all-start.3 = ((bf16[4,272,256]{2,1,0:T(8,128)(2,1)}), bf16[4,272,256]{2,1,0:T(8,128)(2,1)S(1)}, u32[]{:S(2)}, u32[]{:S(2)}) async-start(bf16[4,272,256]{2,1,0:T(8,128)(2,1)} %get-tuple-element.33), calls=%async_computation.3 | async-start | bytes 1114112 | tf_op jit(solution)/shard_map/all_to_all | solution.py:342
  204.3 3.3 %collective-permute-start.14 = (bf16[144,512]{1,0:T(8,128)(2,1)S(1)}, bf16[144,512]{1,0:T(8,128)(2,1)S(1)}, u32[]{:S(2)}, u32[]{:S(2)}) collective-permute-start(bf16[144,512]{1,0:T(8,128)(2,1)S(1)} %get-tuple-element.32.q), channel_id=1, source_target_pairs={{0,128},{128,0},{1,129},{129,1},{2,130},{130,2},{3,131},{131,3},{4... | collective-permute-start | bytes 442376 | tf_op jit(solution)/shard_map/ppermute | solution.py:34
  207.6 19.2 %collective-permute-done.14.q_got = bf16[144,512]{1,0:T(8,128)(2,1)S(1)} collective-permute-done((bf16[144,512]{1,0:T(8,128)(2,1)S(1)}, bf16[144,512]{1,0:T(8,128)(2,1)S(1)}, u32[]{:S(2)}, u32[]{:S(2)}) %collective-permute-start.14) | collective-permute-done | bytes 147488 | tf_op jit(solution)/shard_map/ppermute | solution.py:34
  233.4 4.8 %collective-permute-start.17 = (bf16[144,256]{1,0:T(8,128)(2,1)S(1)}, bf16[144,256]{1,0:T(8,128)(2,1)S(1)}, u32[]{:S(2)}, u32[]{:S(2)}) collective-permute-start(bf16[144,256]{1,0:T(8,128)(2,1)S(1)} %get-tuple-element.38), channel_id=1, source_target_pairs={{0,192},{64,128},{128,64},{192,0},{1,193},{65,129},{129,65},{193,1... | collective-permute-start | bytes 221192 | tf_op jit(solution)/shard_map/ppermute | solution.py:34
  245.5 3.9 %collective-permute-start.20 = (bf16[128,256]{1,0:T(8,128)(2,1)S(1)}, bf16[128,256]{1,0:T(8,128)(2,1)S(1)}, u32[]{:S(2)}, u32[]{:S(2)}) collective-permute-start(bf16[128,256]{1,0:T(8,128)(2,1)S(1)} %merge.1), channel_id=1, source_target_pairs={{0,24},{8,0},{16,8},{24,16},{1,25},{9,1},{17,9},{25,17},{2,26},{10... | collective-permute-start | bytes 196616 | tf_op jit(solution)/shard_map/ppermute | solution.py:34
  254.3 3.9 %collective-permute-start.22 = (bf16[4,128,256]{2,1,0:T(8,128)(2,1)S(1)}, bf16[4,128,256]{2,1,0:T(8,128)(2,1)S(1)}, u32[]{:S(2)}, u32[]{:S(2)}) collective-permute-start(bf16[4,128,256]{2,1,0:T(8,128)(2,1)S(1)} %pad_maximum_fusion.2.refs_0_), channel_id=1, source_target_pairs={{0,4},{2,6},{4,0},{6,2},{1,5},{3,7},{5,1},{7,3},{8,12},{10,14},{12... | collective-permute-start | bytes 786440 | tf_op jit(solution)/shard_map/ppermute | solution.py:34
  261.6 3.8 %collective-permute-done.22.refs_2_ = bf16[4,128,256]{2,1,0:T(8,128)(2,1)S(1)} collective-permute-done((bf16[4,128,256]{2,1,0:T(8,128)(2,1)S(1)}, bf16[4,128,256]{2,1,0:T(8,128)(2,1)S(1)}, u32[]{:S(2)}, u32[]{:S(2)}) %collective-permute-start.22) | collective-permute-done | bytes 262176 | tf_op jit(solution)/shard_map/ppermute | solution.py:34
  271.4 5.4 %collective-permute-start.24 = (f32[160,256]{1,0:T(8,128)S(1)}, f32[160,256]{1,0:T(8,128)S(1)}, u32[]{:S(2)}, u32[]{:S(2)}) collective-permute-start(f32[160,256]{1,0:T(8,128)S(1)} %get-tuple-element.42), channel_id=1, source_target_pairs={{0,1},{1,0},{2,3},{3,2},{4,5},{5,4},{6,7},{7,6},{8,9},{9,8},{10,11... | collective-permute-start | bytes 491528 | tf_op jit(solution)/shard_map/ppermute | solution.py:34
  (105 shorter events, 51.4 us)
Async XLA Ops:
  31.5 130.1 %all-to-all-start.1 = ((bf16[8,3,320,128]{3,2,1,0:T(8,128)(2,1)}), bf16[8,3,320,128]{3,2,1,0:T(8,128)(2,1)S(1)}, u32[]{:S(2)}, u32[]{:S(2)}) async-start(bf16[8,3,320,128]{3,2,1,0:T(8,128)(2,1)} %broadcast_in_dim.28), calls=%async_computation.1 | async-start | bytes 3932160 | tf_op jit(solution)/shard_map/all_to_all | solution.py:240
  44.3 216.4 %all-gather.3.cloned.1.call-start = ((), (), s32[]{:S(2)}) async-start(), calls=%async_computation.4 | async-start | bytes 1474560 | tf_op jit(solution)/shard_map/all_gather | solution.py:263
  44.3 9.9 %collective-permute-start = (bf16[320,128]{1,0:T(8,128)(2,1)S(1)}, bf16[320,128]{1,0:T(8,128)(2,1)S(1)}, u32[]{:S(2)}, u32[]{:S(2)}) collective-permute-start(bf16[320,128]{1,0:T(8,128)(2,1)S(1)} %bitcast.85), channel_id=1, source_target_pairs={{0,0},{1,1},{2,32},{3,33},{4,64},{5,65},{6,96},{7,97},{8,128},{9,1... | collective-permute-start | bytes 245768 | tf_op jit(solution)/shard_map/ppermute | solution.py:34
  45.0 40.3 %collective-permute-start.1 = (bf16[320,128]{1,0:T(8,128)(2,1)S(1)}, bf16[320,128]{1,0:T(8,128)(2,1)S(1)}, u32[]{:S(2)}, u32[]{:S(2)}) collective-permute-start(bf16[320,128]{1,0:T(8,128)(2,1)S(1)} %bitcast.86), channel_id=1, source_target_pairs={{0,32},{1,33},{2,0},{3,1},{4,96},{5,97},{6,64},{7,65},{8,160},{9,1... | collective-permute-start | bytes 245768 | tf_op jit(solution)/shard_map/ppermute | solution.py:34
  85.5 32.8 %collective-permute-start.2 = (bf16[168,256]{1,0:T(8,128)(2,1)S(1)}, bf16[168,256]{1,0:T(8,128)(2,1)S(1)}, u32[]{:S(2)}, u32[]{:S(2)}) collective-permute-start(bf16[168,256]{1,0:T(8,128)(2,1)S(1)} %maximum_maximum_fusion), channel_id=1, source_target_pairs={{0,0},{2,2},{4,64},{6,66},{8,8},{10,10},{12,72},{14,74},{16,16},{1... | collective-permute-start | bytes 258056 | tf_op jit(solution)/shard_map/ppermute | solution.py:34
  86.2 32.1 %collective-permute-start.3 = (bf16[168,256]{1,0:T(8,128)(2,1)S(1)}, bf16[168,256]{1,0:T(8,128)(2,1)S(1)}, u32[]{:S(2)}, u32[]{:S(2)}) collective-permute-start(bf16[168,256]{1,0:T(8,128)(2,1)S(1)} %maximum_maximum_fusion), channel_id=1, source_target_pairs={{0,8},{2,10},{4,72},{6,74},{8,16},{10,18},{12,80},{14,82},{16,24},... | collective-permute-start | bytes 258056 | tf_op jit(solution)/shard_map/ppermute | solution.py:34
  112.4 9.6 %collective-permute-start.4 = (bf16[168,256]{1,0:T(8,128)(2,1)S(1)}, bf16[168,256]{1,0:T(8,128)(2,1)S(1)}, u32[]{:S(2)}, u32[]{:S(2)}) collective-permute-start(bf16[168,256]{1,0:T(8,128)(2,1)S(1)} %maximum_maximum_fusion), channel_id=1, source_target_pairs={{0,16},{2,18},{4,80},{6,82},{8,24},{10,26},{12,88},{14,90},{16,0},... | collective-permute-start | bytes 258056 | tf_op jit(solution)/shard_map/ppermute | solution.py:34
  114.3 7.7 %collective-permute-start.5 = (bf16[168,256]{1,0:T(8,128)(2,1)S(1)}, bf16[168,256]{1,0:T(8,128)(2,1)S(1)}, u32[]{:S(2)}, u32[]{:S(2)}) collective-permute-start(bf16[168,256]{1,0:T(8,128)(2,1)S(1)} %maximum_maximum_fusion), channel_id=1, source_target_pairs={{0,24},{2,26},{4,88},{6,90},{8,0},{10,2},{12,64},{14,66},{16,8},{1... | collective-permute-start | bytes 258056 | tf_op jit(solution)/shard_map/ppermute | solution.py:34
  122.1 26.7 %collective-permute-start.6 = (bf16[4,168,256]{2,1,0:T(8,128)(2,1)S(1)}, bf16[4,168,256]{2,1,0:T(8,128)(2,1)S(1)}, u32[]{:S(2)}, u32[]{:S(2)}) collective-permute-start(bf16[4,168,256]{2,1,0:T(8,128)(2,1)S(1)} %pad_maximum_fusion.refs_0_), channel_id=1, source_target_pairs={{0,2},{2,4},{4,6},{6,0},{1,3},{3,5},{5,7},{7,1},{8,10},{10,12},{12... | collective-permute-start | bytes 1032200 | tf_op jit(solution)/shard_map/ppermute | solution.py:34
  127.1 24.4 %collective-permute-start.7 = (bf16[4,168,256]{2,1,0:T(8,128)(2,1)S(1)}, bf16[4,168,256]{2,1,0:T(8,128)(2,1)S(1)}, u32[]{:S(2)}, u32[]{:S(2)}) collective-permute-start(bf16[4,168,256]{2,1,0:T(8,128)(2,1)S(1)} %pad_maximum_fusion.refs_0_), channel_id=1, source_target_pairs={{0,4},{2,6},{4,0},{6,2},{1,5},{3,7},{5,1},{7,3},{8,12},{10,14},{12... | collective-permute-start | bytes 1032200 | tf_op jit(solution)/shard_map/ppermute | solution.py:34
  140.9 16.4 %collective-permute-start.8 = (bf16[4,168,256]{2,1,0:T(8,128)(2,1)S(1)}, bf16[4,168,256]{2,1,0:T(8,128)(2,1)S(1)}, u32[]{:S(2)}, u32[]{:S(2)}) collective-permute-start(bf16[4,168,256]{2,1,0:T(8,128)(2,1)S(1)} %pad_maximum_fusion.refs_0_), channel_id=1, source_target_pairs={{0,6},{2,0},{4,2},{6,4},{1,7},{3,1},{5,3},{7,5},{8,14},{10,8},{12,... | collective-permute-start | bytes 1032200 | tf_op jit(solution)/shard_map/ppermute | solution.py:34
  142.8 18.7 %collective-permute-start.9 = (bf16[4,168,256]{2,1,0:T(8,128)(2,1)S(1)}, bf16[4,168,256]{2,1,0:T(8,128)(2,1)}, u32[]{:S(2)}, u32[]{:S(2)}) collective-permute-start(bf16[4,168,256]{2,1,0:T(8,128)(2,1)S(1)} %pad_maximum_fusion.refs_0_), channel_id=1, source_target_pairs={{0,1},{1,0},{2,3},{3,2},{4,5},{5,4},{6,7},{7,6},{8,9},{9,8},{10,11... | collective-permute-start | bytes 1032200 | tf_op jit(solution)/shard_map/ppermute | solution.py:34
  148.8 12.8 %collective-permute-start.10 = (bf16[4,168,256]{2,1,0:T(8,128)(2,1)S(1)}, bf16[4,168,256]{2,1,0:T(8,128)(2,1)}, u32[]{:S(2)}, u32[]{:S(2)}) collective-permute-start(bf16[4,168,256]{2,1,0:T(8,128)(2,1)S(1)} %collective-permute-done.6.refs_1_), channel_id=1, source_target_pairs={{0,1},{1,0},{2,3},{3,2},{4,5},{5,4},{6,7},{7,6},{8,9},{9,8},{10,11... | collective-permute-start | bytes 1032200 | tf_op jit(solution)/shard_map/ppermute | solution.py:34
  151.5 10.0 %collective-permute-start.11 = (bf16[4,168,256]{2,1,0:T(8,128)(2,1)S(1)}, bf16[4,168,256]{2,1,0:T(8,128)(2,1)}, u32[]{:S(2)}, u32[]{:S(2)}) collective-permute-start(bf16[4,168,256]{2,1,0:T(8,128)(2,1)S(1)} %collective-permute-done.7.refs_2_), channel_id=1, source_target_pairs={{0,1},{1,0},{2,3},{3,2},{4,5},{5,4},{6,7},{7,6},{8,9},{9,8},{10,11... | collective-permute-start | bytes 1032200 | tf_op jit(solution)/shard_map/ppermute | solution.py:34
  165.0 11.3 %collective-permute-start.13 = (bf16[4,128,256]{2,1,0:T(8,128)(2,1)S(1)}, bf16[4,128,256]{2,1,0:T(8,128)(2,1)S(1)}, u32[]{:S(2)}, u32[]{:S(2)}) collective-permute-start(bf16[4,128,256]{2,1,0:T(8,128)(2,1)S(1)} %get-tuple-element.27), channel_id=1, source_target_pairs={{0,64},{64,0},{1,65},{65,1},{2,66},{66,2},{3,67},{67,3},{4,68},{68... | collective-permute-start | bytes 786440 | tf_op jit(solution)/shard_map/ppermute | solution.py:34
  177.0 16.3 %all-to-all-start.2 = ((f32[32,8,128]{2,1,0:T(8,128)}), f32[32,8,128]{2,1,0:T(8,128)S(1)}, u32[]{:S(2)}, u32[]{:S(2)}) async-start(f32[32,8,128]{2,1,0:T(8,128)} %get-tuple-element.28), calls=%async_computation.2 | async-start | bytes 262144 | tf_op jit(solution)/shard_map/all_to_all | solution.py:328
  194.5 32.3 %all-to-all-start.3 = ((bf16[4,272,256]{2,1,0:T(8,128)(2,1)}), bf16[4,272,256]{2,1,0:T(8,128)(2,1)S(1)}, u32[]{:S(2)}, u32[]{:S(2)}) async-start(bf16[4,272,256]{2,1,0:T(8,128)(2,1)} %get-tuple-element.33), calls=%async_computation.3 | async-start | bytes 1114112 | tf_op jit(solution)/shard_map/all_to_all | solution.py:342
  204.3 22.6 %collective-permute-start.14 = (bf16[144,512]{1,0:T(8,128)(2,1)S(1)}, bf16[144,512]{1,0:T(8,128)(2,1)S(1)}, u32[]{:S(2)}, u32[]{:S(2)}) collective-permute-start(bf16[144,512]{1,0:T(8,128)(2,1)S(1)} %get-tuple-element.32.q), channel_id=1, source_target_pairs={{0,128},{128,0},{1,129},{129,1},{2,130},{130,2},{3,131},{131,3},{4... | collective-permute-start | bytes 442376 | tf_op jit(solution)/shard_map/ppermute | solution.py:34
  228.9 9.3 %collective-permute-start.15 = (bf16[144,256]{1,0:T(8,128)(2,1)S(1)}, bf16[144,256]{1,0:T(8,128)(2,1)S(1)}, u32[]{:S(2)}, u32[]{:S(2)}) collective-permute-start(bf16[144,256]{1,0:T(8,128)(2,1)S(1)} %get-tuple-element.36), channel_id=1, source_target_pairs={{0,64},{64,0},{128,192},{192,128},{1,65},{65,1},{129,193},{193,129... | collective-permute-start | bytes 221192 | tf_op jit(solution)/shard_map/ppermute | solution.py:34
  240.3 9.0 %collective-permute-start.18 = (bf16[128,256]{1,0:T(8,128)(2,1)S(1)}, bf16[128,256]{1,0:T(8,128)(2,1)S(1)}, u32[]{:S(2)}, u32[]{:S(2)}) collective-permute-start(bf16[128,256]{1,0:T(8,128)(2,1)S(1)} %merge.1), channel_id=1, source_target_pairs={{0,8},{8,16},{16,24},{24,0},{1,9},{9,17},{17,25},{25,1},{2,10},{10... | collective-permute-start | bytes 196616 | tf_op jit(solution)/shard_map/ppermute | solution.py:34
  242.6 7.6 %collective-permute-start.19 = (bf16[128,256]{1,0:T(8,128)(2,1)S(1)}, bf16[128,256]{1,0:T(8,128)(2,1)S(1)}, u32[]{:S(2)}, u32[]{:S(2)}) collective-permute-start(bf16[128,256]{1,0:T(8,128)(2,1)S(1)} %merge.1), channel_id=1, source_target_pairs={{0,16},{8,24},{16,0},{24,8},{1,17},{9,25},{17,1},{25,9},{2,18},{10... | collective-permute-start | bytes 196616 | tf_op jit(solution)/shard_map/ppermute | solution.py:34
  252.2 9.4 %collective-permute-start.21 = (bf16[4,128,256]{2,1,0:T(8,128)(2,1)S(1)}, bf16[4,128,256]{2,1,0:T(8,128)(2,1)S(1)}, u32[]{:S(2)}, u32[]{:S(2)}) collective-permute-start(bf16[4,128,256]{2,1,0:T(8,128)(2,1)S(1)} %pad_maximum_fusion.2.refs_0_), channel_id=1, source_target_pairs={{0,2},{2,4},{4,6},{6,0},{1,3},{3,5},{5,7},{7,1},{8,10},{10,12},{12... | collective-permute-start | bytes 786440 | tf_op jit(solution)/shard_map/ppermute | solution.py:34
  254.3 11.1 %collective-permute-start.22 = (bf16[4,128,256]{2,1,0:T(8,128)(2,1)S(1)}, bf16[4,128,256]{2,1,0:T(8,128)(2,1)S(1)}, u32[]{:S(2)}, u32[]{:S(2)}) collective-permute-start(bf16[4,128,256]{2,1,0:T(8,128)(2,1)S(1)} %pad_maximum_fusion.2.refs_0_), channel_id=1, source_target_pairs={{0,4},{2,6},{4,0},{6,2},{1,5},{3,7},{5,1},{7,3},{8,12},{10,14},{12... | collective-permute-start | bytes 786440 | tf_op jit(solution)/shard_map/ppermute | solution.py:34
  258.2 10.4 %collective-permute-start.23 = (bf16[4,128,256]{2,1,0:T(8,128)(2,1)S(1)}, bf16[4,128,256]{2,1,0:T(8,128)(2,1)S(1)}, u32[]{:S(2)}, u32[]{:S(2)}) collective-permute-start(bf16[4,128,256]{2,1,0:T(8,128)(2,1)S(1)} %pad_maximum_fusion.2.refs_0_), channel_id=1, source_target_pairs={{0,6},{2,0},{4,2},{6,4},{1,7},{3,1},{5,3},{7,5},{8,14},{10,8},{12,... | collective-permute-start | bytes 786440 | tf_op jit(solution)/shard_map/ppermute | solution.py:34
  (17 other events, 643.3 us)
Sparse Core Ops, SparseCore 0:
  161.7 39.2 all-gather.2

commit v3 on v1

v3 whole, which is shorter than its diff:
```python
import functools
import itertools
import math

import jax
import jax.numpy as jnp
import numpy as np
from jax import lax
from jax.experimental import pallas as pl
from jax.experimental.pallas import tpu as pltpu
from jax.sharding import Mesh
from jax.sharding import PartitionSpec as P

HEAD_DIM = 128
EPSILON = 1e-06
NEG_FILL = -1e30
LOG2E = 1.4426950408889634

SEQ = ("ya", "yb", "yc", "zh")
TP = ("zl", "xh", "xl", "c")
SIZES = {"ya": 2, "yb": 2, "yc": 2, "zh": 2, "zl": 4, "xh": 2, "xl": 2, "c": 2}

F32 = jnp.float32
BF16 = jnp.bfloat16
VMEM_LIMIT = 48 << 20


def permute(value, axes, move):
    sizes = [SIZES[a] for a in axes]
    pairs = []
    for at in itertools.product(*[range(n) for n in sizes]):
        to = move(*at)
        pairs.append((int(np.ravel_multi_index(at, sizes)), int(np.ravel_multi_index(to, sizes))))
    return lax.ppermute(value, axes, pairs)


def contract_first(lhs, rhs):
    return lax.dot_general(lhs, rhs, (((0,), (0,)), ((), ())), preferred_element_type=F32)


def call(kernel, out_shape, operands, scalars=None, scratch=(), name=None, cost=None):
    vmem = pl.BlockSpec(memory_space=pltpu.VMEM)
    smem = pl.BlockSpec(memory_space=pltpu.SMEM)
    specs = ([] if scalars is None else [smem]) + [vmem] * len(operands)
    args = ([] if scalars is None else [scalars]) + list(operands)
    return pl.pallas_call(
        kernel,
        out_shape=out_shape,
        in_specs=specs,
        out_specs=jax.tree.map(lambda _: vmem, out_shape),
        scratch_shapes=list(scratch),
        compiler_params=pltpu.CompilerParams(vmem_limit_bytes=VMEM_LIMIT),
        cost_estimate=cost,
        name=name,
    )(*args)


def shaped(shape, dtype):
    return jax.ShapeDtypeStruct(shape, dtype)


def project_kernel(at, *refs):
    xs, w, out_q, out_kv, stats = refs[:8], refs[8], *refs[9:]
    zl, x, c = at[0], at[1], at[2]
    total = None
    for i in range(2):
        core = lax.rem(c + i, 2)
        for j in range(4):
            x_from = lax.rem(x - j + 4, 4)
            for k in range(4):
                chip = lax.rem(zl - k + 4, 4) * 4 + x_from
                weights = jnp.concatenate([w[chip, p, core] for p in range(3)], axis=1)
                term = contract_first(weights, xs[4 * i + j][k])
                total = term if total is None else total + term
    query, key, value = total[:128], total[128:256], total[256:]
    out_q[...] = query
    out_kv[0] = key
    out_kv[1] = value
    rows = []
    for part in (query, key):
        row = jnp.sum(part * part, axis=0, keepdims=True)
        rows += [row[:, :128], row[:, 128:]]
    packed = jnp.concatenate(rows + [jnp.zeros((4, 128), F32)], axis=0)
    for t in range(stats.shape[0]):
        stats[t] = packed


def rotate_kernel(width, got, q, kv, cosine, sine, qg, kg, marks, q_out, k_cache, v_cache, message):
    totals = jnp.sum(got[...], axis=0)
    even = lax.rem(lax.broadcasted_iota(jnp.int32, (HEAD_DIM, 256), 0), 2) == 0
    cos, sin = cosine[...], sine[...]

    def rotated(value, gain, row):
        factor = jnp.concatenate([totals[row : row + 1], totals[row + 1 : row + 2]], axis=1)
        factor = lax.rsqrt(factor / width + EPSILON)
        normed = value * factor * gain
        after = pltpu.roll(normed, HEAD_DIM - 1, 0)
        before = pltpu.roll(normed, 1, 0)
        partner = jnp.where(even, -after, before)
        return normed * cos + partner * sin

    extra = marks[...].astype(BF16)
    q_out[:128] = rotated(q[...], qg[...], 0).astype(BF16)
    q_out[128:144] = extra
    k_rot = rotated(kv[0], kg[...], 2)
    value = kv[1]
    k_low = k_rot.astype(BF16)
    v_low = value.astype(BF16)
    for t in range(message.shape[0]):
        message[t, :128] = k_low
        message[t, 128:256] = v_low
        message[t, 256:272] = extra
    k_cache[...] = k_rot.T.astype(BF16)
    v_cache[...] = value.T.astype(BF16)


def attend_kernel(q, q_got, keys, mine, mine_lse, message, held):
    count = keys.shape[0]
    scale = LOG2E / math.sqrt(HEAD_DIM)
    q_low = jnp.concatenate([q[:128], q_got[:128]], axis=1)
    seg_q = jnp.concatenate([q[128:144], q_got[128:144]], axis=1).astype(F32)[:1]
    top = None
    for b in range(count):
        seg_k = keys[b, 256:272].astype(F32).T[:, :1]
        scores = contract_first(keys[b, :128], q_low) * scale
        scores = jnp.where(seg_k == seg_q, scores, NEG_FILL)
        held[b] = scores
        here = jnp.max(scores, axis=0, keepdims=True)
        top = here if top is None else jnp.maximum(top, here)
    top = jnp.maximum(top, -1e20)
    total = jnp.zeros((1, 512), F32)
    weighted = jnp.zeros((HEAD_DIM, 512), F32)
    for b in range(count):
        weights = jnp.exp2(held[b] - top)
        total = total + jnp.sum(weights, axis=0, keepdims=True)
        weighted = weighted + jnp.dot(
            keys[b, 128:256], weights.astype(BF16), preferred_element_type=F32
        )
    some = total > 0.0
    safe = jnp.where(some, total, 1.0)
    out = weighted / safe
    lse = jnp.where(some, top + jnp.log2(safe), NEG_FILL)
    mine[...] = out[:, :256]
    mine_lse[...] = jnp.broadcast_to(lse[:, :256], (8, 256))
    other_lse = lse[:, 256:]
    high = other_lse.astype(BF16)
    rest = other_lse - high.astype(F32)
    middle = rest.astype(BF16)
    low = (rest - middle.astype(F32)).astype(BF16)
    message[:128] = out[:, 256:].astype(BF16)
    message[128:144] = jnp.concatenate(
        [high.astype(F32), middle.astype(F32), low.astype(F32), jnp.zeros((13, 256), F32)], axis=0
    ).astype(BF16)


def merge_kernel(mine, mine_lse, *refs):
    gots, out = refs[:-1], refs[-1]
    parts = [(mine_lse[0:1], mine[...])]
    for got in gots:
        rows = got[128:144].astype(F32)
        parts.append((rows[0:1] + rows[1:2] + rows[2:3], got[:128].astype(F32)))
    top = functools.reduce(jnp.maximum, [lse for lse, _ in parts])
    weights = [jnp.exp2(lse - top) for lse, _ in parts]
    total = sum(weights[1:], weights[0])
    value = None
    for weight, (_, part) in zip(weights, parts, strict=True):
        term = part * (weight / total)
        value = term if value is None else value + term
    out[...] = value.astype(BF16)


def output_kernel(at, *refs):
    heads, w, mine, message, held = refs[:4], refs[4], *refs[5:]
    zl, x, c, zh = at[0], at[1], at[2], at[3]
    total = None
    for j in range(4):
        x_from = lax.rem(x - j + 4, 4)
        for k in range(4):
            chip = lax.rem(zl - k + 4, 4) * 4 + x_from
            flip = lax.rem(lax.rem(chip, 2) + zh, 2)
            term = jnp.dot(w[chip // 2, flip], heads[j][k], preferred_element_type=F32)
            total = term if total is None else total + term
    held[0] = total[:160]
    held[1] = total[160:]
    mine[...] = held[c]
    message[...] = held[1 - c]


def body(hidden_in, seg_ids, positions, mod_table, w_qkv, q_gain, k_gain, w_out):
    tok_rows, feat_local = hidden_in.shape
    model_width = feat_local * 32
    heads_width = 4096
    zl, c, zh = lax.axis_index("zl"), lax.axis_index("c"), lax.axis_index("zh")
    x = lax.axis_index("xh") * 2 + lax.axis_index("xl")
    at = jnp.stack([zl, x, c, zh]).astype(jnp.int32)

    w_pair = lax.all_gather(jnp.transpose(w_qkv, (1, 0, 2)), "zh", axis=0, tiled=False)
    w_all = lax.all_gather(w_pair, ("ya", "yb", "yc"), axis=0, tiled=False)
    w_all = w_all.reshape(16, 3, 2, 160, 128)

    x_t = hidden_in.T.astype(F32)
    sums = jnp.stack([jnp.sum(x_t, axis=0), jnp.sum(x_t * x_t, axis=0)]).reshape(4, 128)
    sums = jnp.concatenate([sums, jnp.zeros((4, 128), F32)], axis=0)
    sums, w_pair = lax.optimization_barrier((sums, w_pair))
    sums = lax.all_to_all(jnp.broadcast_to(sums, (32, 8, 128)), TP, 0, 0, tiled=True)
    sums = jnp.sum(sums, axis=0)[:4].reshape(2, tok_rows)
    mean_value = sums[0:1] / model_width
    variance = sums[1:2] / model_width - mean_value * mean_value
    normed = (x_t - mean_value) * lax.rsqrt(variance + EPSILON)
    segment_count = mod_table.shape[0]
    onehot = (seg_ids[None, :] == jnp.arange(segment_count, dtype=jnp.int32)[:, None]).astype(F32)
    modulation = lax.dot_general(
        mod_table.reshape(segment_count, 3 * feat_local),
        onehot,
        (((0,), (0,)), ((), ())),
        precision=lax.Precision.HIGHEST,
    ).reshape(3, feat_local, tok_rows)
    packet = (normed * (1.0 + modulation[1]) + modulation[0]).astype(BF16)

    held = jnp.stack(
        [packet]
        + [permute(packet, ("zl",), lambda zl, k=k: ((zl + k) % 4,)) for k in range(1, 4)]
    )
    along_x = [held] + [
        permute(held, ("xh", "xl"), lambda xh, xl, j=j: divmod((xh * 2 + xl + j) % 4, 2))
        for j in range(1, 4)
    ]
    swapped = [permute(part, ("c",), lambda c: (1 - c,)) for part in along_x]

    part_width = HEAD_DIM // 6
    widths = (HEAD_DIM - 4 * part_width, 2 * part_width, 2 * part_width)
    angles = []
    for axis_number in range(3):
        width = widths[axis_number]
        exponent = jnp.arange(0, width, 2, dtype=F32) / width
        frequency = jnp.repeat(1.0 / 10000.0**exponent, 2)
        angles.append(positions[axis_number].astype(F32)[None, :] * frequency[:, None])
    angle = jnp.concatenate(angles, axis=0)
    cosine, sine = jnp.cos(angle), jnp.sin(angle)
    marks = jnp.broadcast_to(seg_ids[None, :].astype(F32), (16, tok_rows))

    query, key_value, stats = call(
        project_kernel,
        (shaped((128, 256), F32), shaped((2, 128, 256), F32), shaped((32, 8, 128), F32)),
        along_x + swapped + [w_all],
        scalars=at,
        name="project",
        cost=pl.CostEstimate(flops=2 * 256 * 5120 * 384, bytes_accessed=6 << 20, transcendentals=0),
    )
    stats = lax.all_to_all(stats, TP, 0, 0, tiled=True)
    q_rot, k_cache, v_cache, kv_message = call(
        functools.partial(rotate_kernel, heads_width),
        (
            shaped((144, 256), BF16),
            shaped((256, 128), BF16),
            shaped((256, 128), BF16),
            shaped((8, 272, 256), BF16),
        ),
        [stats, query, key_value, cosine, sine, q_gain.reshape(128, 1), k_gain.reshape(128, 1), marks],
        name="rotate",
    )
    keys = lax.all_to_all(kv_message, ("ya", "yb", "yc"), 0, 0, tiled=True)
    q_got = permute(q_rot, ("zh",), lambda zh: (1 - zh,))

    def turned(value, flip):
        def move(ya, yb, yc, zh, zl, xh, xl, c):
            s = (ya * 4 + yb * 2 + yc) * 2 + zh
            chip = (zl * 2 + xh) * 2 + xl
            to_s = chip ^ flip
            return (to_s >> 3, (to_s >> 2) & 1, (to_s >> 1) & 1, to_s & 1, s >> 2, (s >> 1) & 1, s & 1, c)

        return permute(value, SEQ + TP, move)

    wo_local, q_got = lax.optimization_barrier((w_out.T, q_got))
    wo_pair = jnp.stack([turned(wo_local, 0), turned(wo_local, 1)])
    wo_pair, keys = lax.optimization_barrier((wo_pair, keys))
    wo_all = lax.all_gather(wo_pair, ("ya", "yb", "yc"), axis=0, tiled=False)

    mine, mine_lse, o_message = call(
        attend_kernel,
        (shaped((128, 256), F32), shaped((8, 256), F32), shaped((144, 256), BF16)),
        [q_rot, q_got, keys],
        scratch=[pltpu.VMEM((8, 256, 512), F32)],
        name="attend",
    )
    o_got = permute(o_message, ("zh",), lambda zh: (1 - zh,))
    attention = call(merge_kernel, shaped((128, 256), BF16), [mine, mine_lse, o_got], name="merge")

    by_z = [attention] + [
        permute(attention, ("zl",), lambda zl, k=k: ((zl + k) % 4,)) for k in range(1, 4)
    ]
    by_z = jnp.stack(by_z)
    by_x = [by_z] + [
        permute(by_z, ("xh", "xl"), lambda xh, xl, j=j: divmod((xh * 2 + xl + j) % 4, 2))
        for j in range(1, 4)
    ]
    out_mine, out_message = call(
        output_kernel,
        (shaped((160, 256), F32), shaped((160, 256), F32)),
        by_x + [wo_all],
        scalars=at,
        scratch=[pltpu.VMEM((2, 160, 256), F32)],
        name="output",
    )
    out_got = permute(out_message, ("c",), lambda c: (1 - c,))
    mixed = out_mine + out_got
    hidden_out = (x_t + modulation[2] * mixed).T.astype(BF16)
    return (hidden_out, k_cache, v_cache)


def solution(mesh):
    split = Mesh(mesh.devices.reshape(tuple(SIZES.values())), tuple(SIZES))
    in_specs = (
        P(SEQ, TP),
        P(SEQ),
        P(None, SEQ),
        P(None, None, TP),
        P(SEQ, None, TP),
        P(TP),
        P(TP),
        P(TP, SEQ),
    )
    out_specs = (P(SEQ, TP), P(SEQ, TP), P(SEQ, TP))
    return jax.shard_map(body, mesh=split, in_specs=in_specs, out_specs=out_specs, check_vma=False)
```

time: 239 us -> 219 us (0.916)
  waiting for transfers between devices: 95.4 us -> 56.3 us
  blocking collectives: 0 us -> 19.2 us
  starting transfers between devices: 106 us -> 111 us
  other arithmetic: 7.04 us -> 4.15 us
    all_to_all x1, waiting for transfers between devices: 34.7 us -> 8.16 us  [body(): keys = lax.all_to_all(kv_message, ('ya', 'yb', 'yc'), 0, 0, tiled=True)]
    all_gather x0 -> x1, blocking collectives: none -> 19.2 us  [body(): lax.all_gather(jnp.transpose(w_qkv, (1, 0, 2)), 'zh', axis=0, tiled=False)]
    ppermute x22 -> x21, waiting for transfers between devices: 47.3 us -> 32.1 us  [permute(): return lax.ppermute(value, axes, pairs)]
    ppermute x22 -> x21, starting transfers between devices: 81 us -> 86.2 us  [permute(): return lax.ppermute(value, axes, pairs)]
    all_to_all x1, waiting for transfers between devices: 5.15 us -> 7.96 us  [body(): lax.all_to_all(jnp.broadcast_to(sums, (32, 8, 128)), TP, 0, 0, tiled=True)]
    all_to_all x1, starting transfers between devices: 9.49 us -> 6.95 us  [body(): keys = lax.all_to_all(kv_message, ('ya', 'yb', 'yc'), 0, 0, tiled=True)]
    pallas_call x6 -> x5, Pallas kernels: 8.92 us -> 9.58 us  [call(): pl.pallas_call(kernel, out_shape=out_shape, in_specs=specs, out_specs=jax...]
  transfers between devices with their start and end apart: 27 -> 26, of which waited for: 10 -> 15; matrix products, arithmetic and copies ran while one was open for 4% -> 2% of each run, Pallas kernels for 3% -> 1%
where the time goes in v3:
time: 219 us; the launch traced here: 218 us
  starting transfers between devices  111 us (51%)
  waiting for transfers between devices  56.3 us (26%)
  blocking collectives  19.2 us (9%)
  between operations  14.5 us (7%)
  Pallas kernels  9.58 us (4%)
  other arithmetic  4.15 us (2%)
  local copies, waits for them, and re-layouts  2.7 us (1%)
    ppermute x21, starting transfers between devices, permute(): return lax.ppermute(value, axes, pairs)  86.2 us
    ppermute x21, waiting for transfers between devices, permute(): return lax.ppermute(value, axes, pairs)  32.1 us
    all_gather x1, blocking collectives, body(): lax.all_gather(jnp.transpose(w_qkv, (1, 0, 2)), 'zh', axis=0, tiled=False)  19.2 us
    all_to_all x1, starting transfers between devices, body(): lax.all_to_all(jnp.broadcast_to(sums, (32, 8, 128)), TP, 0, 0, tiled=True)  13.6 us
    pallas_call x5, Pallas kernels, call(): pl.pallas_call(kernel, out_shape=out_shape, in_specs=specs, out_specs=jax...  9.58 us
    all_to_all x1, waiting for transfers between devices, body(): keys = lax.all_to_all(kv_message, ('ya', 'yb', 'yc'), 0, 0, tiled=True)  8.16 us
    all_to_all x1, waiting for transfers between devices, body(): stats = lax.all_to_all(stats, TP, 0, 0, tiled=True)  8.11 us
    all_to_all x1, waiting for transfers between devices, body(): lax.all_to_all(jnp.broadcast_to(sums, (32, 8, 128)), TP, 0, 0, tiled=True)  7.96 us
  transfers between devices with their start and end apart: 26, of which 15 were waited for; matrix products, arithmetic and copies ran while one was open for 2% of the time, Pallas kernels for 1%

profile of v3, /device:TPU:1, one launch (start us, length us, event | category | flops | bytes accessed | tf_op | source)
XLA Modules:
  0.0 217.6 jit_solution(17886264411901608443)
XLA Ops:
  7.2 19.2 %all-gather = bf16[6,320,128]{2,1,0:T(8,128)(2,1)} all-gather(bf16[3,320,128]{2,1,0:T(8,128)(2,1)} %bitcast.68), channel_id=2, replica_groups=mesh['ya'=2,'yb'=2,'yc'=2,'zh'=2,'zl'=4,'xh'=2,'xl'=2,'c'=2] {'zh'}, dimensions={0}, use_global_device_ids=true | all-gather | bytes 737280 | tf_op jit(solution)/shard_map/all_gather | solution.py:197
  28.2 13.6 %all-to-all-start = ((f32[32,8,128]{2,1,0:T(8,128)}), f32[32,8,128]{2,1,0:T(8,128)S(1)}, u32[]{:S(2)}, u32[]{:S(2)}) async-start(f32[32,8,128]{2,1,0:T(8,128)} %broadcast_in_dim.10), calls=%async_computation | async-start | bytes 262144 | tf_op jit(solution)/shard_map/all_to_all | solution.py:205
  42.3 8.0 %all-to-all-done = f32[32,8,128]{2,1,0:T(8,128)S(1)} async-done(((f32[32,8,128]{2,1,0:T(8,128)}), f32[32,8,128]{2,1,0:T(8,128)S(1)}, u32[]{:S(2)}, u32[]{:S(2)}) %all-to-all-start) | async-done | bytes 131104 | tf_op jit(solution)/shard_map/all_to_all | solution.py:205
  52.7 2.9 %collective-permute-start.1 = (bf16[160,256]{1,0:T(8,128)(2,1)S(1)}, bf16[160,256]{1,0:T(8,128)(2,1)S(1)}, u32[]{:S(2)}, u32[]{:S(2)}) collective-permute-start(bf16[160,256]{1,0:T(8,128)(2,1)S(1)} %fusion.7), channel_id=1, source_target_pairs={{0,16},{8,24},{16,0},{24,8},{1,17},{9,25},{17,1},{25,9},{2,18},{10... | collective-permute-start | bytes 245768 | tf_op jit(solution)/shard_map/ppermute | solution.py:34
  55.6 3.8 %collective-permute-start.2 = (bf16[160,256]{1,0:T(8,128)(2,1)S(1)}, bf16[160,256]{1,0:T(8,128)(2,1)S(1)}, u32[]{:S(2)}, u32[]{:S(2)}) collective-permute-start(bf16[160,256]{1,0:T(8,128)(2,1)S(1)} %fusion.7), channel_id=1, source_target_pairs={{0,24},{8,0},{16,8},{24,16},{1,25},{9,1},{17,9},{25,17},{2,26},{10... | collective-permute-start | bytes 245768 | tf_op jit(solution)/shard_map/ppermute | solution.py:34
  66.1 3.8 %collective-permute-start.4 = (bf16[4,160,256]{2,1,0:T(8,128)(2,1)S(1)}, bf16[4,160,256]{2,1,0:T(8,128)(2,1)S(1)}, u32[]{:S(2)}, u32[]{:S(2)}) collective-permute-start(bf16[4,160,256]{2,1,0:T(8,128)(2,1)S(1)} %pad_maximum_fusion.refs_0_), channel_id=1, source_target_pairs={{0,4},{2,6},{4,0},{6,2},{1,5},{3,7},{5,1},{7,3},{8,12},{10,14},{12... | collective-permute-start | bytes 983048 | tf_op jit(solution)/shard_map/ppermute | solution.py:34
  72.9 3.1 %collective-permute-start.6 = (bf16[4,160,256]{2,1,0:T(8,128)(2,1)S(1)}, bf16[4,160,256]{2,1,0:T(8,128)(2,1)S(1)}, u32[]{:S(2)}, u32[]{:S(2)}) collective-permute-start(bf16[4,160,256]{2,1,0:T(8,128)(2,1)S(1)} %pad_maximum_fusion.refs_0_), channel_id=1, source_target_pairs={{0,1},{1,0},{2,3},{3,2},{4,5},{5,4},{6,7},{7,6},{8,9},{9,8},{10,11... | collective-permute-start | bytes 983048 | tf_op jit(solution)/shard_map/ppermute | solution.py:34
  76.5 9.5 %collective-permute-start.7 = (bf16[4,160,256]{2,1,0:T(8,128)(2,1)S(1)}, bf16[4,160,256]{2,1,0:T(8,128)(2,1)S(1)}, u32[]{:S(2)}, u32[]{:S(2)}) collective-permute-start(bf16[4,160,256]{2,1,0:T(8,128)(2,1)S(1)} %collective-permute-done.3.refs_1_), channel_id=1, source_target_pairs={{0,1},{1,0},{2,3},{3,2},{4,5},{5,4},{6,7},{7,6},{8,9},{9,8},{10,11... | collective-permute-start | bytes 983048 | tf_op jit(solution)/shard_map/ppermute | solution.py:34
  91.7 4.7 %project.1 = (f32[128,256]{1,0:T(8,128)S(1)}, f32[2,128,256]{2,1,0:T(8,128)S(1)}, f32[32,8,128]{2,1,0:T(8,128)}) custom-call(s32[4]{0:T(128)S(1)} %pad_add_fusion.at, bf16[4,160,256]{2,1,0:T(8,128)(2,1)S(1)} %pad_maximum_fusion.refs_0_, bf16[4,160,256]{2,1,0:T(8,128)(2,1)S(1)} %collective-permute-done.3.refs_1_, ...), custom_call_target="tpu_custom_call" | custom-call | flops 1006632960 | bytes 6291456 | tf_op jit(solution)/shard_map/project/pallas_call | solution.py:46
  96.3 3.9 %all-to-all-start.1 = ((f32[32,8,128]{2,1,0:T(8,128)}), f32[32,8,128]{2,1,0:T(8,128)S(1)}, u32[]{:S(2)}, u32[]{:S(2)}) async-start(f32[32,8,128]{2,1,0:T(8,128)} %get-tuple-element.21), calls=%async_computation.1 | async-start | bytes 262144 | tf_op jit(solution)/shard_map/all_to_all | solution.py:250
  100.8 8.1 %all-to-all-done.1.got = f32[32,8,128]{2,1,0:T(8,128)S(1)} async-done(((f32[32,8,128]{2,1,0:T(8,128)}), f32[32,8,128]{2,1,0:T(8,128)S(1)}, u32[]{:S(2)}, u32[]{:S(2)}) %all-to-all-start.1) | async-done | bytes 131104 | tf_op jit(solution)/shard_map/all_to_all | solution.py:250
  110.2 7.0 %all-to-all-start.2 = ((bf16[8,272,256]{2,1,0:T(8,128)(2,1)}), bf16[8,272,256]{2,1,0:T(8,128)(2,1)S(1)}, u32[]{:S(2)}, u32[]{:S(2)}) async-start(bf16[8,272,256]{2,1,0:T(8,128)(2,1)} %get-tuple-element.27), calls=%async_computation.2 | async-start | bytes 2228224 | tf_op jit(solution)/shard_map/all_to_all | solution.py:262
  117.2 4.4 %collective-permute-start.10 = (bf16[144,256]{1,0:T(8,128)(2,1)S(1)}, bf16[144,256]{1,0:T(8,128)(2,1)S(1)}, u32[]{:S(2)}, u32[]{:S(2)}) collective-permute-start(bf16[144,256]{1,0:T(8,128)(2,1)S(1)} %get-tuple-element.24.q), channel_id=1, source_target_pairs={{0,32},{32,0},{1,33},{33,1},{2,34},{34,2},{3,35},{35,3},{4,36},{36... | collective-permute-start | bytes 221192 | tf_op jit(solution)/shard_map/ppermute | solution.py:34
  121.6 5.7 %collective-permute-done.10.q_got = bf16[144,256]{1,0:T(8,128)(2,1)S(1)} collective-permute-done((bf16[144,256]{1,0:T(8,128)(2,1)S(1)}, bf16[144,256]{1,0:T(8,128)(2,1)S(1)}, u32[]{:S(2)}, u32[]{:S(2)}) %collective-permute-start.10) | collective-permute-done | bytes 73760 | tf_op jit(solution)/shard_map/ppermute | solution.py:34
  127.9 9.3 %collective-permute-start.12 = (bf16[320,128]{1,0:T(8,128)(2,1)S(1)}, bf16[320,128]{1,0:T(8,128)(2,1)S(1)}, u32[]{:S(2)}, u32[]{:S(2)}) collective-permute-start(bf16[320,128]{1,0:T(8,128)(2,1)S(1)} %bitcast.85), channel_id=1, source_target_pairs={{0,32},{1,33},{2,0},{3,1},{4,96},{5,97},{6,64},{7,65},{8,160},{9,1... | collective-permute-start | bytes 245768 | tf_op jit(solution)/shard_map/ppermute | solution.py:34
  139.6 8.2 %all-to-all-done.2.keys = bf16[8,272,256]{2,1,0:T(8,128)(2,1)S(1)} async-done(((bf16[8,272,256]{2,1,0:T(8,128)(2,1)}), bf16[8,272,256]{2,1,0:T(8,128)(2,1)S(1)}, u32[]{:S(2)}, u32[]{:S(2)}) %all-to-all-start.2) | async-done | bytes 1114144 | tf_op jit(solution)/shard_map/all_to_all | solution.py:262
  150.0 4.4 %collective-permute-start.13 = (bf16[144,256]{1,0:T(8,128)(2,1)S(1)}, bf16[144,256]{1,0:T(8,128)(2,1)S(1)}, u32[]{:S(2)}, u32[]{:S(2)}) collective-permute-start(bf16[144,256]{1,0:T(8,128)(2,1)S(1)} %get-tuple-element.31), channel_id=1, source_target_pairs={{0,32},{32,0},{1,33},{33,1},{2,34},{34,2},{3,35},{35,3},{4,36},{36... | collective-permute-start | bytes 221192 | tf_op jit(solution)/shard_map/ppermute | solution.py:34
  154.4 7.1 %collective-permute-done.13.refs_0_ = bf16[144,256]{1,0:T(8,128)(2,1)S(1)} collective-permute-done((bf16[144,256]{1,0:T(8,128)(2,1)S(1)}, bf16[144,256]{1,0:T(8,128)(2,1)S(1)}, u32[]{:S(2)}, u32[]{:S(2)}) %collective-permute-start.13) | collective-permute-done | bytes 73760 | tf_op jit(solution)/shard_map/ppermute | solution.py:34
  161.6 4.4 %collective-permute-start.14 = (bf16[128,256]{1,0:T(8,128)(2,1)S(1)}, bf16[128,256]{1,0:T(8,128)(2,1)S(1)}, u32[]{:S(2)}, u32[]{:S(2)}) collective-permute-start(bf16[128,256]{1,0:T(8,128)(2,1)S(1)} %merge.1), channel_id=1, source_target_pairs={{0,8},{8,16},{16,24},{24,0},{1,9},{9,17},{17,25},{25,1},{2,10},{10... | collective-permute-start | bytes 196616 | tf_op jit(solution)/shard_map/ppermute | solution.py:34
  166.0 9.8 %collective-permute-start.15 = (bf16[128,256]{1,0:T(8,128)(2,1)S(1)}, bf16[128,256]{1,0:T(8,128)(2,1)S(1)}, u32[]{:S(2)}, u32[]{:S(2)}) collective-permute-start(bf16[128,256]{1,0:T(8,128)(2,1)S(1)} %merge.1), channel_id=1, source_target_pairs={{0,16},{8,24},{16,0},{24,8},{1,17},{9,25},{17,1},{25,9},{2,18},{10... | collective-permute-start | bytes 196616 | tf_op jit(solution)/shard_map/ppermute | solution.py:34
  183.6 6.5 %collective-permute-start.18 = (bf16[4,128,256]{2,1,0:T(8,128)(2,1)S(1)}, bf16[4,128,256]{2,1,0:T(8,128)(2,1)S(1)}, u32[]{:S(2)}, u32[]{:S(2)}) collective-permute-start(bf16[4,128,256]{2,1,0:T(8,128)(2,1)S(1)} %pad_maximum_fusion.1.refs_0_), channel_id=1, source_target_pairs={{0,4},{2,6},{4,0},{6,2},{1,5},{3,7},{5,1},{7,3},{8,12},{10,14},{12... | collective-permute-start | bytes 786440 | tf_op jit(solution)/shard_map/ppermute | solution.py:34
  190.1 3.0 %collective-permute-start.19 = (bf16[4,128,256]{2,1,0:T(8,128)(2,1)S(1)}, bf16[4,128,256]{2,1,0:T(8,128)(2,1)S(1)}, u32[]{:S(2)}, u32[]{:S(2)}) collective-permute-start(bf16[4,128,256]{2,1,0:T(8,128)(2,1)S(1)} %pad_maximum_fusion.1.refs_0_), channel_id=1, source_target_pairs={{0,6},{2,0},{4,2},{6,4},{1,7},{3,1},{5,3},{7,5},{8,14},{10,8},{12,... | collective-permute-start | bytes 786440 | tf_op jit(solution)/shard_map/ppermute | solution.py:34
  196.0 4.0 %collective-permute-done.19.refs_3_ = bf16[4,128,256]{2,1,0:T(8,128)(2,1)S(1)} collective-permute-done((bf16[4,128,256]{2,1,0:T(8,128)(2,1)S(1)}, bf16[4,128,256]{2,1,0:T(8,128)(2,1)S(1)}, u32[]{:S(2)}, u32[]{:S(2)}) %collective-permute-start.19) | collective-permute-done | bytes 262176 | tf_op jit(solution)/shard_map/ppermute | solution.py:34
  202.7 5.4 %collective-permute-start.20 = (f32[160,256]{1,0:T(8,128)S(1)}, f32[160,256]{1,0:T(8,128)S(1)}, u32[]{:S(2)}, u32[]{:S(2)}) collective-permute-start(f32[160,256]{1,0:T(8,128)S(1)} %get-tuple-element.34), channel_id=1, source_target_pairs={{0,1},{1,0},{2,3},{3,2},{4,5},{5,4},{6,7},{7,6},{8,9},{9,8},{10,11... | collective-permute-start | bytes 491528 | tf_op jit(solution)/shard_map/ppermute | solution.py:34
  (86 shorter events, 43.4 us)
Async XLA Ops:
  7.2 84.5 %all-gather.6.cloned.1.call-start = ((), (), s32[]{:S(2)}) async-start(), calls=%async_computation.3 | async-start | bytes 4423680 | tf_op jit(solution)/shard_map/all_gather | solution.py:198
  28.2 22.1 %all-to-all-start = ((f32[32,8,128]{2,1,0:T(8,128)}), f32[32,8,128]{2,1,0:T(8,128)S(1)}, u32[]{:S(2)}, u32[]{:S(2)}) async-start(f32[32,8,128]{2,1,0:T(8,128)} %broadcast_in_dim.10), calls=%async_computation | async-start | bytes 262144 | tf_op jit(solution)/shard_map/all_to_all | solution.py:205
  50.4 9.2 %collective-permute-start = (bf16[160,256]{1,0:T(8,128)(2,1)S(1)}, bf16[160,256]{1,0:T(8,128)(2,1)S(1)}, u32[]{:S(2)}, u32[]{:S(2)}) collective-permute-start(bf16[160,256]{1,0:T(8,128)(2,1)S(1)} %fusion.7), channel_id=1, source_target_pairs={{0,8},{8,16},{16,24},{24,0},{1,9},{9,17},{17,25},{25,1},{2,10},{10... | collective-permute-start | bytes 245768 | tf_op jit(solution)/shard_map/ppermute | solution.py:34
  52.7 9.3 %collective-permute-start.1 = (bf16[160,256]{1,0:T(8,128)(2,1)S(1)}, bf16[160,256]{1,0:T(8,128)(2,1)S(1)}, u32[]{:S(2)}, u32[]{:S(2)}) collective-permute-start(bf16[160,256]{1,0:T(8,128)(2,1)S(1)} %fusion.7), channel_id=1, source_target_pairs={{0,16},{8,24},{16,0},{24,8},{1,17},{9,25},{17,1},{25,9},{2,18},{10... | collective-permute-start | bytes 245768 | tf_op jit(solution)/shard_map/ppermute | solution.py:34
  55.6 8.2 %collective-permute-start.2 = (bf16[160,256]{1,0:T(8,128)(2,1)S(1)}, bf16[160,256]{1,0:T(8,128)(2,1)S(1)}, u32[]{:S(2)}, u32[]{:S(2)}) collective-permute-start(bf16[160,256]{1,0:T(8,128)(2,1)S(1)} %fusion.7), channel_id=1, source_target_pairs={{0,24},{8,0},{16,8},{24,16},{1,25},{9,1},{17,9},{25,17},{2,26},{10... | collective-permute-start | bytes 245768 | tf_op jit(solution)/shard_map/ppermute | solution.py:34
  63.9 12.6 %collective-permute-start.3 = (bf16[4,160,256]{2,1,0:T(8,128)(2,1)S(1)}, bf16[4,160,256]{2,1,0:T(8,128)(2,1)S(1)}, u32[]{:S(2)}, u32[]{:S(2)}) collective-permute-start(bf16[4,160,256]{2,1,0:T(8,128)(2,1)S(1)} %pad_maximum_fusion.refs_0_), channel_id=1, source_target_pairs={{0,2},{2,4},{4,6},{6,0},{1,3},{3,5},{5,7},{7,1},{8,10},{10,12},{12... | collective-permute-start | bytes 983048 | tf_op jit(solution)/shard_map/ppermute | solution.py:34
  66.1 19.9 %collective-permute-start.4 = (bf16[4,160,256]{2,1,0:T(8,128)(2,1)S(1)}, bf16[4,160,256]{2,1,0:T(8,128)(2,1)S(1)}, u32[]{:S(2)}, u32[]{:S(2)}) collective-permute-start(bf16[4,160,256]{2,1,0:T(8,128)(2,1)S(1)} %pad_maximum_fusion.refs_0_), channel_id=1, source_target_pairs={{0,4},{2,6},{4,0},{6,2},{1,5},{3,7},{5,1},{7,3},{8,12},{10,14},{12... | collective-permute-start | bytes 983048 | tf_op jit(solution)/shard_map/ppermute | solution.py:34
  69.9 18.1 %collective-permute-start.5 = (bf16[4,160,256]{2,1,0:T(8,128)(2,1)S(1)}, bf16[4,160,256]{2,1,0:T(8,128)(2,1)S(1)}, u32[]{:S(2)}, u32[]{:S(2)}) collective-permute-start(bf16[4,160,256]{2,1,0:T(8,128)(2,1)S(1)} %pad_maximum_fusion.refs_0_), channel_id=1, source_target_pairs={{0,6},{2,0},{4,2},{6,4},{1,7},{3,1},{5,3},{7,5},{8,14},{10,8},{12,... | collective-permute-start | bytes 983048 | tf_op jit(solution)/shard_map/ppermute | solution.py:34
  72.9 17.7 %collective-permute-start.6 = (bf16[4,160,256]{2,1,0:T(8,128)(2,1)S(1)}, bf16[4,160,256]{2,1,0:T(8,128)(2,1)S(1)}, u32[]{:S(2)}, u32[]{:S(2)}) collective-permute-start(bf16[4,160,256]{2,1,0:T(8,128)(2,1)S(1)} %pad_maximum_fusion.refs_0_), channel_id=1, source_target_pairs={{0,1},{1,0},{2,3},{3,2},{4,5},{5,4},{6,7},{7,6},{8,9},{9,8},{10,11... | collective-permute-start | bytes 983048 | tf_op jit(solution)/shard_map/ppermute | solution.py:34
  76.5 14.1 %collective-permute-start.7 = (bf16[4,160,256]{2,1,0:T(8,128)(2,1)S(1)}, bf16[4,160,256]{2,1,0:T(8,128)(2,1)S(1)}, u32[]{:S(2)}, u32[]{:S(2)}) collective-permute-start(bf16[4,160,256]{2,1,0:T(8,128)(2,1)S(1)} %collective-permute-done.3.refs_1_), channel_id=1, source_target_pairs={{0,1},{1,0},{2,3},{3,2},{4,5},{5,4},{6,7},{7,6},{8,9},{9,8},{10,11... | collective-permute-start | bytes 983048 | tf_op jit(solution)/shard_map/ppermute | solution.py:34
  96.3 12.5 %all-to-all-start.1 = ((f32[32,8,128]{2,1,0:T(8,128)}), f32[32,8,128]{2,1,0:T(8,128)S(1)}, u32[]{:S(2)}, u32[]{:S(2)}) async-start(f32[32,8,128]{2,1,0:T(8,128)} %get-tuple-element.21), calls=%async_computation.1 | async-start | bytes 262144 | tf_op jit(solution)/shard_map/all_to_all | solution.py:250
  110.2 37.6 %all-to-all-start.2 = ((bf16[8,272,256]{2,1,0:T(8,128)(2,1)}), bf16[8,272,256]{2,1,0:T(8,128)(2,1)S(1)}, u32[]{:S(2)}, u32[]{:S(2)}) async-start(bf16[8,272,256]{2,1,0:T(8,128)(2,1)} %get-tuple-element.27), calls=%async_computation.2 | async-start | bytes 2228224 | tf_op jit(solution)/shard_map/all_to_all | solution.py:262
  117.1 82.9 %all-gather.8.cloned.1.call-start = ((), (), s32[]{:S(2)}) async-start(), calls=%async_computation.4 | async-start | bytes 1474560 | tf_op jit(solution)/shard_map/all_gather | solution.py:277
  117.2 10.1 %collective-permute-start.10 = (bf16[144,256]{1,0:T(8,128)(2,1)S(1)}, bf16[144,256]{1,0:T(8,128)(2,1)S(1)}, u32[]{:S(2)}, u32[]{:S(2)}) collective-permute-start(bf16[144,256]{1,0:T(8,128)(2,1)S(1)} %get-tuple-element.24.q), channel_id=1, source_target_pairs={{0,32},{32,0},{1,33},{33,1},{2,34},{34,2},{3,35},{35,3},{4,36},{36... | collective-permute-start | bytes 221192 | tf_op jit(solution)/shard_map/ppermute | solution.py:34
  127.3 10.0 %collective-permute-start.11 = (bf16[320,128]{1,0:T(8,128)(2,1)S(1)}, bf16[320,128]{1,0:T(8,128)(2,1)S(1)}, u32[]{:S(2)}, u32[]{:S(2)}) collective-permute-start(bf16[320,128]{1,0:T(8,128)(2,1)S(1)} %bitcast.84), channel_id=1, source_target_pairs={{0,0},{1,1},{2,32},{3,33},{4,64},{5,65},{6,96},{7,97},{8,128},{9,1... | collective-permute-start | bytes 245768 | tf_op jit(solution)/shard_map/ppermute | solution.py:34
  127.9 11.0 %collective-permute-start.12 = (bf16[320,128]{1,0:T(8,128)(2,1)S(1)}, bf16[320,128]{1,0:T(8,128)(2,1)S(1)}, u32[]{:S(2)}, u32[]{:S(2)}) collective-permute-start(bf16[320,128]{1,0:T(8,128)(2,1)S(1)} %bitcast.85), channel_id=1, source_target_pairs={{0,32},{1,33},{2,0},{3,1},{4,96},{5,97},{6,64},{7,65},{8,160},{9,1... | collective-permute-start | bytes 245768 | tf_op jit(solution)/shard_map/ppermute | solution.py:34
  150.0 11.5 %collective-permute-start.13 = (bf16[144,256]{1,0:T(8,128)(2,1)S(1)}, bf16[144,256]{1,0:T(8,128)(2,1)S(1)}, u32[]{:S(2)}, u32[]{:S(2)}) collective-permute-start(bf16[144,256]{1,0:T(8,128)(2,1)S(1)} %get-tuple-element.31), channel_id=1, source_target_pairs={{0,32},{32,0},{1,33},{33,1},{2,34},{34,2},{3,35},{35,3},{4,36},{36... | collective-permute-start | bytes 221192 | tf_op jit(solution)/shard_map/ppermute | solution.py:34
  161.6 16.1 %collective-permute-start.14 = (bf16[128,256]{1,0:T(8,128)(2,1)S(1)}, bf16[128,256]{1,0:T(8,128)(2,1)S(1)}, u32[]{:S(2)}, u32[]{:S(2)}) collective-permute-start(bf16[128,256]{1,0:T(8,128)(2,1)S(1)} %merge.1), channel_id=1, source_target_pairs={{0,8},{8,16},{16,24},{24,0},{1,9},{9,17},{17,25},{25,1},{2,10},{10... | collective-permute-start | bytes 196616 | tf_op jit(solution)/shard_map/ppermute | solution.py:34
  166.0 13.0 %collective-permute-start.15 = (bf16[128,256]{1,0:T(8,128)(2,1)S(1)}, bf16[128,256]{1,0:T(8,128)(2,1)S(1)}, u32[]{:S(2)}, u32[]{:S(2)}) collective-permute-start(bf16[128,256]{1,0:T(8,128)(2,1)S(1)} %merge.1), channel_id=1, source_target_pairs={{0,16},{8,24},{16,0},{24,8},{1,17},{9,25},{17,1},{25,9},{2,18},{10... | collective-permute-start | bytes 196616 | tf_op jit(solution)/shard_map/ppermute | solution.py:34
  175.8 5.9 %collective-permute-start.16 = (bf16[128,256]{1,0:T(8,128)(2,1)S(1)}, bf16[128,256]{1,0:T(8,128)(2,1)S(1)}, u32[]{:S(2)}, u32[]{:S(2)}) collective-permute-start(bf16[128,256]{1,0:T(8,128)(2,1)S(1)} %merge.1), channel_id=1, source_target_pairs={{0,24},{8,0},{16,8},{24,16},{1,25},{9,1},{17,9},{25,17},{2,26},{10... | collective-permute-start | bytes 196616 | tf_op jit(solution)/shard_map/ppermute | solution.py:34
  181.7 11.4 %collective-permute-start.17 = (bf16[4,128,256]{2,1,0:T(8,128)(2,1)S(1)}, bf16[4,128,256]{2,1,0:T(8,128)(2,1)S(1)}, u32[]{:S(2)}, u32[]{:S(2)}) collective-permute-start(bf16[4,128,256]{2,1,0:T(8,128)(2,1)S(1)} %pad_maximum_fusion.1.refs_0_), channel_id=1, source_target_pairs={{0,2},{2,4},{4,6},{6,0},{1,3},{3,5},{5,7},{7,1},{8,10},{10,12},{12... | collective-permute-start | bytes 786440 | tf_op jit(solution)/shard_map/ppermute | solution.py:34
  183.6 12.4 %collective-permute-start.18 = (bf16[4,128,256]{2,1,0:T(8,128)(2,1)S(1)}, bf16[4,128,256]{2,1,0:T(8,128)(2,1)S(1)}, u32[]{:S(2)}, u32[]{:S(2)}) collective-permute-start(bf16[4,128,256]{2,1,0:T(8,128)(2,1)S(1)} %pad_maximum_fusion.1.refs_0_), channel_id=1, source_target_pairs={{0,4},{2,6},{4,0},{6,2},{1,5},{3,7},{5,1},{7,3},{8,12},{10,14},{12... | collective-permute-start | bytes 786440 | tf_op jit(solution)/shard_map/ppermute | solution.py:34
  190.1 9.9 %collective-permute-start.19 = (bf16[4,128,256]{2,1,0:T(8,128)(2,1)S(1)}, bf16[4,128,256]{2,1,0:T(8,128)(2,1)S(1)}, u32[]{:S(2)}, u32[]{:S(2)}) collective-permute-start(bf16[4,128,256]{2,1,0:T(8,128)(2,1)S(1)} %pad_maximum_fusion.1.refs_0_), channel_id=1, source_target_pairs={{0,6},{2,0},{4,2},{6,4},{1,7},{3,1},{5,3},{7,5},{8,14},{10,8},{12,... | collective-permute-start | bytes 786440 | tf_op jit(solution)/shard_map/ppermute | solution.py:34
  202.7 6.4 %collective-permute-start.20 = (f32[160,256]{1,0:T(8,128)S(1)}, f32[160,256]{1,0:T(8,128)S(1)}, u32[]{:S(2)}, u32[]{:S(2)}) collective-permute-start(f32[160,256]{1,0:T(8,128)S(1)} %get-tuple-element.34), channel_id=1, source_target_pairs={{0,1},{1,0},{2,3},{3,2},{4,5},{5,4},{6,7},{7,6},{8,9},{9,8},{10,11... | collective-permute-start | bytes 491528 | tf_op jit(solution)/shard_map/ppermute | solution.py:34
  (11 other events, 276.5 us)
Sparse Core Ops, SparseCore 0:
  26.6 59.2 all-gather.5
  147.9 46.2 all-gather.7

commit v4 on v3

--- a/solution.py
+++ b/solution.py
@@ -198,6 +198,17 @@
     w_all = lax.all_gather(w_pair, ("ya", "yb", "yc"), axis=0, tiled=False)
     w_all = w_all.reshape(16, 3, 2, 160, 128)
 
+    def turned(flip):
+        def move(ya, yb, yc, zh, zl, xh, xl, c):
+            s = (ya * 4 + yb * 2 + yc) * 2 + zh
+            chip = (zl * 2 + xh) * 2 + xl
+            to_s = chip ^ flip
+            return (to_s >> 3, (to_s >> 2) & 1, (to_s >> 1) & 1, to_s & 1, s >> 2, (s >> 1) & 1, s & 1, c)
+
+        return permute(w_out.T, SEQ + TP, move)
+
+    wo_turned = (turned(0), turned(1))
+
     x_t = hidden_in.T.astype(F32)
     sums = jnp.stack([jnp.sum(x_t, axis=0), jnp.sum(x_t * x_t, axis=0)]).reshape(4, 128)
     sums = jnp.concatenate([sums, jnp.zeros((4, 128), F32)], axis=0)
@@ -216,6 +227,7 @@
         precision=lax.Precision.HIGHEST,
     ).reshape(3, feat_local, tok_rows)
     packet = (normed * (1.0 + modulation[1]) + modulation[0]).astype(BF16)
+    packet, wo_turned = lax.optimization_barrier((packet, wo_turned))
 
     held = jnp.stack(
         [packet]
@@ -262,18 +274,7 @@
     keys = lax.all_to_all(kv_message, ("ya", "yb", "yc"), 0, 0, tiled=True)
     q_got = permute(q_rot, ("zh",), lambda zh: (1 - zh,))
 
-    def turned(value, flip):
-        def move(ya, yb, yc, zh, zl, xh, xl, c):
-            s = (ya * 4 + yb * 2 + yc) * 2 + zh
-            chip = (zl * 2 + xh) * 2 + xl
-            to_s = chip ^ flip
-            return (to_s >> 3, (to_s >> 2) & 1, (to_s >> 1) & 1, to_s & 1, s >> 2, (s >> 1) & 1, s & 1, c)
-
-        return permute(value, SEQ + TP, move)
-
-    wo_local, q_got = lax.optimization_barrier((w_out.T, q_got))
-    wo_pair = jnp.stack([turned(wo_local, 0), turned(wo_local, 1)])
-    wo_pair, keys = lax.optimization_barrier((wo_pair, keys))
+    wo_pair, keys, q_got = lax.optimization_barrier((jnp.stack(wo_turned), keys, q_got))
     wo_all = lax.all_gather(wo_pair, ("ya", "yb", "yc"), axis=0, tiled=False)
 
     mine, mine_lse, o_message = call(

time: 219 us -> 227 us (1.037)
  waiting for transfers between devices: 56.3 us -> 70.1 us
  starting transfers between devices: 111 us -> 105 us
    all_to_all x1, waiting for transfers between devices: 8.16 us -> 19.7 us  [body(): keys = lax.all_to_all(kv_message, ('ya', 'yb', 'yc'), 0, 0, tiled=True)]
    ppermute x21, waiting for transfers between devices: 32.1 us -> 42.4 us  [permute(): return lax.ppermute(value, axes, pairs)]
    all_to_all x1, waiting for transfers between devices: 7.96 us -> 0.01 us  [body(): lax.all_to_all(jnp.broadcast_to(sums, (32, 8, 128)), TP, 0, 0, tiled=True)]
    ppermute x21, starting transfers between devices: 86.2 us -> 79.4 us  [permute(): return lax.ppermute(value, axes, pairs)]
where the time goes in v4:
time: 227 us; the launch traced here: 226 us
  starting transfers between devices  105 us (46%)
  waiting for transfers between devices  70.1 us (31%)
  blocking collectives  19.3 us (9%)
  between operations  14.5 us (6%)
  Pallas kernels  9.58 us (4%)
  other arithmetic  4.15 us (2%)
  local copies, waits for them, and re-layouts  2.7 us (1%)
    ppermute x21, starting transfers between devices, permute(): return lax.ppermute(value, axes, pairs)  79.4 us
    ppermute x21, waiting for transfers between devices, permute(): return lax.ppermute(value, axes, pairs)  42.4 us
    all_to_all x1, waiting for transfers between devices, body(): keys = lax.all_to_all(kv_message, ('ya', 'yb', 'yc'), 0, 0, tiled=True)  19.7 us
    all_gather x1, blocking collectives, body(): lax.all_gather(jnp.transpose(w_qkv, (1, 0, 2)), 'zh', axis=0, tiled=False)  19.3 us
    all_to_all x1, starting transfers between devices, body(): lax.all_to_all(jnp.broadcast_to(sums, (32, 8, 128)), TP, 0, 0, tiled=True)  13.6 us
    pallas_call x5, Pallas kernels, call(): pl.pallas_call(kernel, out_shape=out_shape, in_specs=specs, out_specs=jax...  9.58 us
    all_to_all x1, waiting for transfers between devices, body(): stats = lax.all_to_all(stats, TP, 0, 0, tiled=True)  7.99 us
    all_to_all x1, starting transfers between devices, body(): keys = lax.all_to_all(kv_message, ('ya', 'yb', 'yc'), 0, 0, tiled=True)  6.08 us
  transfers between devices with their start and end apart: 26, of which 15 were waited for; matrix products, arithmetic and copies ran while one was open for 2% of the time, Pallas kernels for 1%

profile of v4, /device:TPU:1, one launch (start us, length us, event | category | flops | bytes accessed | tf_op | source)
XLA Modules:
  0.0 225.5 jit_solution(10963453760650089815)
XLA Ops:
  7.3 19.3 %all-gather = bf16[6,320,128]{2,1,0:T(8,128)(2,1)} all-gather(bf16[3,320,128]{2,1,0:T(8,128)(2,1)} %bitcast.68), channel_id=2, replica_groups=mesh['ya'=2,'yb'=2,'yc'=2,'zh'=2,'zl'=4,'xh'=2,'xl'=2,'c'=2] {'zh'}, dimensions={0}, use_global_device_ids=true | all-gather | bytes 737280 | tf_op jit(solution)/shard_map/all_gather | solution.py:197
  28.3 13.6 %all-to-all-start = ((f32[32,8,128]{2,1,0:T(8,128)}), f32[32,8,128]{2,1,0:T(8,128)S(1)}, u32[]{:S(2)}, u32[]{:S(2)}) async-start(f32[32,8,128]{2,1,0:T(8,128)} %broadcast_in_dim.10), calls=%async_computation | async-start | bytes 262144 | tf_op jit(solution)/shard_map/all_to_all | solution.py:216
  42.6 9.6 %collective-permute-start.1 = (bf16[320,128]{1,0:T(8,128)(2,1)S(1)}, bf16[320,128]{1,0:T(8,128)(2,1)S(1)}, u32[]{:S(2)}, u32[]{:S(2)}) collective-permute-start(bf16[320,128]{1,0:T(8,128)(2,1)S(1)} %bitcast.85), channel_id=1, source_target_pairs={{0,32},{1,33},{2,0},{3,1},{4,96},{5,97},{6,64},{7,65},{8,160},{9,1... | collective-permute-start | bytes 245768 | tf_op jit(solution)/shard_map/ppermute | solution.py:34
  52.9 8.7 %collective-permute-done.1 = bf16[320,128]{1,0:T(8,128)(2,1)S(1)} collective-permute-done((bf16[320,128]{1,0:T(8,128)(2,1)S(1)}, bf16[320,128]{1,0:T(8,128)(2,1)S(1)}, u32[]{:S(2)}, u32[]{:S(2)}) %collective-permute-start.1) | collective-permute-done | bytes 81952 | tf_op jit(solution)/shard_map/ppermute | solution.py:34
  64.0 9.5 %collective-permute-start.3 = (bf16[160,256]{1,0:T(8,128)(2,1)S(1)}, bf16[160,256]{1,0:T(8,128)(2,1)S(1)}, u32[]{:S(2)}, u32[]{:S(2)}) collective-permute-start(bf16[160,256]{1,0:T(8,128)(2,1)S(1)} %fusion.7), channel_id=1, source_target_pairs={{0,16},{8,24},{16,0},{24,8},{1,17},{9,25},{17,1},{25,9},{2,18},{10... | collective-permute-start | bytes 245768 | tf_op jit(solution)/shard_map/ppermute | solution.py:34
  75.7 2.8 %collective-permute-done.3 = bf16[160,256]{1,0:T(8,128)(2,1)S(1)} collective-permute-done((bf16[160,256]{1,0:T(8,128)(2,1)S(1)}, bf16[160,256]{1,0:T(8,128)(2,1)S(1)}, u32[]{:S(2)}, u32[]{:S(2)}) %collective-permute-start.3) | collective-permute-done | bytes 81952 | tf_op jit(solution)/shard_map/ppermute | solution.py:34
  79.6 8.1 %collective-permute-start.6 = (bf16[4,160,256]{2,1,0:T(8,128)(2,1)S(1)}, bf16[4,160,256]{2,1,0:T(8,128)(2,1)S(1)}, u32[]{:S(2)}, u32[]{:S(2)}) collective-permute-start(bf16[4,160,256]{2,1,0:T(8,128)(2,1)S(1)} %pad_maximum_fusion.refs_0_), channel_id=1, source_target_pairs={{0,4},{2,6},{4,0},{6,2},{1,5},{3,7},{5,1},{7,3},{8,12},{10,14},{12... | collective-permute-start | bytes 983048 | tf_op jit(solution)/shard_map/ppermute | solution.py:34
  89.7 3.3 %collective-permute-start.5 = (bf16[4,160,256]{2,1,0:T(8,128)(2,1)S(1)}, bf16[4,160,256]{2,1,0:T(8,128)(2,1)S(1)}, u32[]{:S(2)}, u32[]{:S(2)}) collective-permute-start(bf16[4,160,256]{2,1,0:T(8,128)(2,1)S(1)} %pad_maximum_fusion.refs_0_), channel_id=1, source_target_pairs={{0,2},{2,4},{4,6},{6,0},{1,3},{3,5},{5,7},{7,1},{8,10},{10,12},{12... | collective-permute-start | bytes 983048 | tf_op jit(solution)/shard_map/ppermute | solution.py:34
  93.4 4.9 %collective-permute-start.8 = (bf16[4,160,256]{2,1,0:T(8,128)(2,1)S(1)}, bf16[4,160,256]{2,1,0:T(8,128)(2,1)S(1)}, u32[]{:S(2)}, u32[]{:S(2)}) collective-permute-start(bf16[4,160,256]{2,1,0:T(8,128)(2,1)S(1)} %pad_maximum_fusion.refs_0_), channel_id=1, source_target_pairs={{0,1},{1,0},{2,3},{3,2},{4,5},{5,4},{6,7},{7,6},{8,9},{9,8},{10,11... | collective-permute-start | bytes 983048 | tf_op jit(solution)/shard_map/ppermute | solution.py:34
  102.5 3.5 %collective-permute-start.11 = (bf16[4,160,256]{2,1,0:T(8,128)(2,1)S(1)}, bf16[4,160,256]{2,1,0:T(8,128)(2,1)S(1)}, u32[]{:S(2)}, u32[]{:S(2)}) collective-permute-start(bf16[4,160,256]{2,1,0:T(8,128)(2,1)S(1)} %collective-permute-done.7.refs_3_), channel_id=1, source_target_pairs={{0,1},{1,0},{2,3},{3,2},{4,5},{5,4},{6,7},{7,6},{8,9},{9,8},{10,11... | collective-permute-start | bytes 983048 | tf_op jit(solution)/shard_map/ppermute | solution.py:34
  109.5 4.7 %project.1 = (f32[128,256]{1,0:T(8,128)S(1)}, f32[2,128,256]{2,1,0:T(8,128)S(1)}, f32[32,8,128]{2,1,0:T(8,128)}) custom-call(s32[4]{0:T(128)S(1)} %pad_add_fusion.at, bf16[4,160,256]{2,1,0:T(8,128)(2,1)S(1)} %pad_maximum_fusion.refs_0_, bf16[4,160,256]{2,1,0:T(8,128)(2,1)S(1)} %collective-permute-done.5.refs_1_, ...), custom_call_target="tpu_custom_call" | custom-call | flops 1006632960 | bytes 6291456 | tf_op jit(solution)/shard_map/project/pallas_call | solution.py:46
  114.2 5.6 %all-to-all-start.1 = ((f32[32,8,128]{2,1,0:T(8,128)}), f32[32,8,128]{2,1,0:T(8,128)S(1)}, u32[]{:S(2)}, u32[]{:S(2)}) async-start(f32[32,8,128]{2,1,0:T(8,128)} %get-tuple-element.24), calls=%async_computation.1 | async-start | bytes 262144 | tf_op jit(solution)/shard_map/all_to_all | solution.py:262
  120.4 8.0 %all-to-all-done.1.got = f32[32,8,128]{2,1,0:T(8,128)S(1)} async-done(((f32[32,8,128]{2,1,0:T(8,128)}), f32[32,8,128]{2,1,0:T(8,128)S(1)}, u32[]{:S(2)}, u32[]{:S(2)}) %all-to-all-start.1) | async-done | bytes 131104 | tf_op jit(solution)/shard_map/all_to_all | solution.py:262
  129.7 6.1 %all-to-all-start.2 = ((bf16[8,272,256]{2,1,0:T(8,128)(2,1)}), bf16[8,272,256]{2,1,0:T(8,128)(2,1)S(1)}, u32[]{:S(2)}, u32[]{:S(2)}) async-start(bf16[8,272,256]{2,1,0:T(8,128)(2,1)} %get-tuple-element.30), calls=%async_computation.2 | async-start | bytes 2228224 | tf_op jit(solution)/shard_map/all_to_all | solution.py:274
  135.8 4.2 %collective-permute-start.12 = (bf16[144,256]{1,0:T(8,128)(2,1)S(1)}, bf16[144,256]{1,0:T(8,128)(2,1)S(1)}, u32[]{:S(2)}, u32[]{:S(2)}) collective-permute-start(bf16[144,256]{1,0:T(8,128)(2,1)S(1)} %get-tuple-element.27.q), channel_id=1, source_target_pairs={{0,32},{32,0},{1,33},{33,1},{2,34},{34,2},{3,35},{35,3},{4,36},{36... | collective-permute-start | bytes 221192 | tf_op jit(solution)/shard_map/ppermute | solution.py:34
  140.7 6.1 %collective-permute-done.12.q_got = bf16[144,256]{1,0:T(8,128)(2,1)S(1)} collective-permute-done((bf16[144,256]{1,0:T(8,128)(2,1)S(1)}, bf16[144,256]{1,0:T(8,128)(2,1)S(1)}, u32[]{:S(2)}, u32[]{:S(2)}) %collective-permute-start.12) | collective-permute-done | bytes 73760 | tf_op jit(solution)/shard_map/ppermute | solution.py:34
  146.7 19.7 %all-to-all-done.2.keys = bf16[8,272,256]{2,1,0:T(8,128)(2,1)S(1)} async-done(((bf16[8,272,256]{2,1,0:T(8,128)(2,1)}), bf16[8,272,256]{2,1,0:T(8,128)(2,1)S(1)}, u32[]{:S(2)}, u32[]{:S(2)}) %all-to-all-start.2) | async-done | bytes 1114144 | tf_op jit(solution)/shard_map/all_to_all | solution.py:274
  168.6 4.2 %collective-permute-start.13 = (bf16[144,256]{1,0:T(8,128)(2,1)S(1)}, bf16[144,256]{1,0:T(8,128)(2,1)S(1)}, u32[]{:S(2)}, u32[]{:S(2)}) collective-permute-start(bf16[144,256]{1,0:T(8,128)(2,1)S(1)} %get-tuple-element.35), channel_id=1, source_target_pairs={{0,32},{32,0},{1,33},{33,1},{2,34},{34,2},{3,35},{35,3},{4,36},{36... | collective-permute-start | bytes 221192 | tf_op jit(solution)/shard_map/ppermute | solution.py:34
  172.8 6.9 %collective-permute-done.13.refs_0_ = bf16[144,256]{1,0:T(8,128)(2,1)S(1)} collective-permute-done((bf16[144,256]{1,0:T(8,128)(2,1)S(1)}, bf16[144,256]{1,0:T(8,128)(2,1)S(1)}, u32[]{:S(2)}, u32[]{:S(2)}) %collective-permute-start.13) | collective-permute-done | bytes 73760 | tf_op jit(solution)/shard_map/ppermute | solution.py:34
  183.6 5.2 %collective-permute-start.16 = (bf16[128,256]{1,0:T(8,128)(2,1)S(1)}, bf16[128,256]{1,0:T(8,128)(2,1)S(1)}, u32[]{:S(2)}, u32[]{:S(2)}) collective-permute-start(bf16[128,256]{1,0:T(8,128)(2,1)S(1)} %merge.1), channel_id=1, source_target_pairs={{0,24},{8,0},{16,8},{24,16},{1,25},{9,1},{17,9},{25,17},{2,26},{10... | collective-permute-start | bytes 196616 | tf_op jit(solution)/shard_map/ppermute | solution.py:34
  193.7 4.1 %collective-permute-start.18 = (bf16[4,128,256]{2,1,0:T(8,128)(2,1)S(1)}, bf16[4,128,256]{2,1,0:T(8,128)(2,1)S(1)}, u32[]{:S(2)}, u32[]{:S(2)}) collective-permute-start(bf16[4,128,256]{2,1,0:T(8,128)(2,1)S(1)} %pad_maximum_fusion.1.refs_0_), channel_id=1, source_target_pairs={{0,4},{2,6},{4,0},{6,2},{1,5},{3,7},{5,1},{7,3},{8,12},{10,14},{12... | collective-permute-start | bytes 786440 | tf_op jit(solution)/shard_map/ppermute | solution.py:34
  200.8 5.7 %collective-permute-done.18.refs_2_ = bf16[4,128,256]{2,1,0:T(8,128)(2,1)S(1)} collective-permute-done((bf16[4,128,256]{2,1,0:T(8,128)(2,1)S(1)}, bf16[4,128,256]{2,1,0:T(8,128)(2,1)S(1)}, u32[]{:S(2)}, u32[]{:S(2)}) %collective-permute-start.18) | collective-permute-done | bytes 262176 | tf_op jit(solution)/shard_map/ppermute | solution.py:34
  206.5 3.0 %collective-permute-done.19.refs_3_ = bf16[4,128,256]{2,1,0:T(8,128)(2,1)S(1)} collective-permute-done((bf16[4,128,256]{2,1,0:T(8,128)(2,1)S(1)}, bf16[4,128,256]{2,1,0:T(8,128)(2,1)S(1)}, u32[]{:S(2)}, u32[]{:S(2)}) %collective-permute-start.19) | collective-permute-done | bytes 262176 | tf_op jit(solution)/shard_map/ppermute | solution.py:34
  212.2 3.9 %collective-permute-start.20 = (f32[160,256]{1,0:T(8,128)S(1)}, f32[160,256]{1,0:T(8,128)S(1)}, u32[]{:S(2)}, u32[]{:S(2)}) collective-permute-start(f32[160,256]{1,0:T(8,128)S(1)} %get-tuple-element.38), channel_id=1, source_target_pairs={{0,1},{1,0},{2,3},{3,2},{4,5},{5,4},{6,7},{7,6},{8,9},{9,8},{10,11... | collective-permute-start | bytes 491528 | tf_op jit(solution)/shard_map/ppermute | solution.py:34
  (86 shorter events, 40.5 us)
Async XLA Ops:
  7.2 102.3 %all-gather.6.cloned.1.call-start = ((), (), s32[]{:S(2)}) async-start(), calls=%async_computation.3 | async-start | bytes 4423680 | tf_op jit(solution)/shard_map/all_gather | solution.py:198
  28.3 24.5 %all-to-all-start = ((f32[32,8,128]{2,1,0:T(8,128)}), f32[32,8,128]{2,1,0:T(8,128)S(1)}, u32[]{:S(2)}, u32[]{:S(2)}) async-start(f32[32,8,128]{2,1,0:T(8,128)} %broadcast_in_dim.10), calls=%async_computation | async-start | bytes 262144 | tf_op jit(solution)/shard_map/all_to_all | solution.py:216
  41.9 11.0 %collective-permute-start = (bf16[320,128]{1,0:T(8,128)(2,1)S(1)}, bf16[320,128]{1,0:T(8,128)(2,1)S(1)}, u32[]{:S(2)}, u32[]{:S(2)}) collective-permute-start(bf16[320,128]{1,0:T(8,128)(2,1)S(1)} %bitcast.84), channel_id=1, source_target_pairs={{0,0},{1,1},{2,32},{3,33},{4,64},{5,65},{6,96},{7,97},{8,128},{9,1... | collective-permute-start | bytes 245768 | tf_op jit(solution)/shard_map/ppermute | solution.py:34
  42.6 19.1 %collective-permute-start.1 = (bf16[320,128]{1,0:T(8,128)(2,1)S(1)}, bf16[320,128]{1,0:T(8,128)(2,1)S(1)}, u32[]{:S(2)}, u32[]{:S(2)}) collective-permute-start(bf16[320,128]{1,0:T(8,128)(2,1)S(1)} %bitcast.85), channel_id=1, source_target_pairs={{0,32},{1,33},{2,0},{3,1},{4,96},{5,97},{6,64},{7,65},{8,160},{9,1... | collective-permute-start | bytes 245768 | tf_op jit(solution)/shard_map/ppermute | solution.py:34
  61.7 14.0 %collective-permute-start.2 = (bf16[160,256]{1,0:T(8,128)(2,1)S(1)}, bf16[160,256]{1,0:T(8,128)(2,1)S(1)}, u32[]{:S(2)}, u32[]{:S(2)}) collective-permute-start(bf16[160,256]{1,0:T(8,128)(2,1)S(1)} %fusion.7), channel_id=1, source_target_pairs={{0,8},{8,16},{16,24},{24,0},{1,9},{9,17},{17,25},{25,1},{2,10},{10... | collective-permute-start | bytes 245768 | tf_op jit(solution)/shard_map/ppermute | solution.py:34
  64.0 14.5 %collective-permute-start.3 = (bf16[160,256]{1,0:T(8,128)(2,1)S(1)}, bf16[160,256]{1,0:T(8,128)(2,1)S(1)}, u32[]{:S(2)}, u32[]{:S(2)}) collective-permute-start(bf16[160,256]{1,0:T(8,128)(2,1)S(1)} %fusion.7), channel_id=1, source_target_pairs={{0,16},{8,24},{16,0},{24,8},{1,17},{9,25},{17,1},{25,9},{2,18},{10... | collective-permute-start | bytes 245768 | tf_op jit(solution)/shard_map/ppermute | solution.py:34
  73.5 6.0 %collective-permute-start.4 = (bf16[160,256]{1,0:T(8,128)(2,1)S(1)}, bf16[160,256]{1,0:T(8,128)(2,1)S(1)}, u32[]{:S(2)}, u32[]{:S(2)}) collective-permute-start(bf16[160,256]{1,0:T(8,128)(2,1)S(1)} %fusion.7), channel_id=1, source_target_pairs={{0,24},{8,0},{16,8},{24,16},{1,25},{9,1},{17,9},{25,17},{2,26},{10... | collective-permute-start | bytes 245768 | tf_op jit(solution)/shard_map/ppermute | solution.py:34
  79.6 18.8 %collective-permute-start.6 = (bf16[4,160,256]{2,1,0:T(8,128)(2,1)S(1)}, bf16[4,160,256]{2,1,0:T(8,128)(2,1)S(1)}, u32[]{:S(2)}, u32[]{:S(2)}) collective-permute-start(bf16[4,160,256]{2,1,0:T(8,128)(2,1)S(1)} %pad_maximum_fusion.refs_0_), channel_id=1, source_target_pairs={{0,4},{2,6},{4,0},{6,2},{1,5},{3,7},{5,1},{7,3},{8,12},{10,14},{12... | collective-permute-start | bytes 983048 | tf_op jit(solution)/shard_map/ppermute | solution.py:34
  87.7 14.8 %collective-permute-start.7 = (bf16[4,160,256]{2,1,0:T(8,128)(2,1)S(1)}, bf16[4,160,256]{2,1,0:T(8,128)(2,1)S(1)}, u32[]{:S(2)}, u32[]{:S(2)}) collective-permute-start(bf16[4,160,256]{2,1,0:T(8,128)(2,1)S(1)} %pad_maximum_fusion.refs_0_), channel_id=1, source_target_pairs={{0,6},{2,0},{4,2},{6,4},{1,7},{3,1},{5,3},{7,5},{8,14},{10,8},{12,... | collective-permute-start | bytes 983048 | tf_op jit(solution)/shard_map/ppermute | solution.py:34
  89.7 16.3 %collective-permute-start.5 = (bf16[4,160,256]{2,1,0:T(8,128)(2,1)S(1)}, bf16[4,160,256]{2,1,0:T(8,128)(2,1)S(1)}, u32[]{:S(2)}, u32[]{:S(2)}) collective-permute-start(bf16[4,160,256]{2,1,0:T(8,128)(2,1)S(1)} %pad_maximum_fusion.refs_0_), channel_id=1, source_target_pairs={{0,2},{2,4},{4,6},{6,0},{1,3},{3,5},{5,7},{7,1},{8,10},{10,12},{12... | collective-permute-start | bytes 983048 | tf_op jit(solution)/shard_map/ppermute | solution.py:34
  93.4 14.6 %collective-permute-start.8 = (bf16[4,160,256]{2,1,0:T(8,128)(2,1)S(1)}, bf16[4,160,256]{2,1,0:T(8,128)(2,1)S(1)}, u32[]{:S(2)}, u32[]{:S(2)}) collective-permute-start(bf16[4,160,256]{2,1,0:T(8,128)(2,1)S(1)} %pad_maximum_fusion.refs_0_), channel_id=1, source_target_pairs={{0,1},{1,0},{2,3},{3,2},{4,5},{5,4},{6,7},{7,6},{8,9},{9,8},{10,11... | collective-permute-start | bytes 983048 | tf_op jit(solution)/shard_map/ppermute | solution.py:34
  98.3 9.7 %collective-permute-start.10 = (bf16[4,160,256]{2,1,0:T(8,128)(2,1)S(1)}, bf16[4,160,256]{2,1,0:T(8,128)(2,1)S(1)}, u32[]{:S(2)}, u32[]{:S(2)}) collective-permute-start(bf16[4,160,256]{2,1,0:T(8,128)(2,1)S(1)} %collective-permute-done.6.refs_2_), channel_id=1, source_target_pairs={{0,1},{1,0},{2,3},{3,2},{4,5},{5,4},{6,7},{7,6},{8,9},{9,8},{10,11... | collective-permute-start | bytes 983048 | tf_op jit(solution)/shard_map/ppermute | solution.py:34
  102.5 5.6 %collective-permute-start.11 = (bf16[4,160,256]{2,1,0:T(8,128)(2,1)S(1)}, bf16[4,160,256]{2,1,0:T(8,128)(2,1)S(1)}, u32[]{:S(2)}, u32[]{:S(2)}) collective-permute-start(bf16[4,160,256]{2,1,0:T(8,128)(2,1)S(1)} %collective-permute-done.7.refs_3_), channel_id=1, source_target_pairs={{0,1},{1,0},{2,3},{3,2},{4,5},{5,4},{6,7},{7,6},{8,9},{9,8},{10,11... | collective-permute-start | bytes 983048 | tf_op jit(solution)/shard_map/ppermute | solution.py:34
  114.2 14.2 %all-to-all-start.1 = ((f32[32,8,128]{2,1,0:T(8,128)}), f32[32,8,128]{2,1,0:T(8,128)S(1)}, u32[]{:S(2)}, u32[]{:S(2)}) async-start(f32[32,8,128]{2,1,0:T(8,128)} %get-tuple-element.24), calls=%async_computation.1 | async-start | bytes 262144 | tf_op jit(solution)/shard_map/all_to_all | solution.py:262
  129.7 36.7 %all-to-all-start.2 = ((bf16[8,272,256]{2,1,0:T(8,128)(2,1)}), bf16[8,272,256]{2,1,0:T(8,128)(2,1)S(1)}, u32[]{:S(2)}, u32[]{:S(2)}) async-start(bf16[8,272,256]{2,1,0:T(8,128)(2,1)} %get-tuple-element.30), calls=%async_computation.2 | async-start | bytes 2228224 | tf_op jit(solution)/shard_map/all_to_all | solution.py:274
  135.7 73.7 %all-gather.8.cloned.1.call-start = ((), (), s32[]{:S(2)}) async-start(), calls=%async_computation.4 | async-start | bytes 1474560 | tf_op jit(solution)/shard_map/all_gather | solution.py:278
  135.8 10.9 %collective-permute-start.12 = (bf16[144,256]{1,0:T(8,128)(2,1)S(1)}, bf16[144,256]{1,0:T(8,128)(2,1)S(1)}, u32[]{:S(2)}, u32[]{:S(2)}) collective-permute-start(bf16[144,256]{1,0:T(8,128)(2,1)S(1)} %get-tuple-element.27.q), channel_id=1, source_target_pairs={{0,32},{32,0},{1,33},{33,1},{2,34},{34,2},{3,35},{35,3},{4,36},{36... | collective-permute-start | bytes 221192 | tf_op jit(solution)/shard_map/ppermute | solution.py:34
  168.6 11.1 %collective-permute-start.13 = (bf16[144,256]{1,0:T(8,128)(2,1)S(1)}, bf16[144,256]{1,0:T(8,128)(2,1)S(1)}, u32[]{:S(2)}, u32[]{:S(2)}) collective-permute-start(bf16[144,256]{1,0:T(8,128)(2,1)S(1)} %get-tuple-element.35), channel_id=1, source_target_pairs={{0,32},{32,0},{1,33},{33,1},{2,34},{34,2},{3,35},{35,3},{4,36},{36... | collective-permute-start | bytes 221192 | tf_op jit(solution)/shard_map/ppermute | solution.py:34
  179.7 9.0 %collective-permute-start.14 = (bf16[128,256]{1,0:T(8,128)(2,1)S(1)}, bf16[128,256]{1,0:T(8,128)(2,1)S(1)}, u32[]{:S(2)}, u32[]{:S(2)}) collective-permute-start(bf16[128,256]{1,0:T(8,128)(2,1)S(1)} %merge.1), channel_id=1, source_target_pairs={{0,8},{8,16},{16,24},{24,0},{1,9},{9,17},{17,25},{25,1},{2,10},{10... | collective-permute-start | bytes 196616 | tf_op jit(solution)/shard_map/ppermute | solution.py:34
  181.6 7.8 %collective-permute-start.15 = (bf16[128,256]{1,0:T(8,128)(2,1)S(1)}, bf16[128,256]{1,0:T(8,128)(2,1)S(1)}, u32[]{:S(2)}, u32[]{:S(2)}) collective-permute-start(bf16[128,256]{1,0:T(8,128)(2,1)S(1)} %merge.1), channel_id=1, source_target_pairs={{0,16},{8,24},{16,0},{24,8},{1,17},{9,25},{17,1},{25,9},{2,18},{10... | collective-permute-start | bytes 196616 | tf_op jit(solution)/shard_map/ppermute | solution.py:34
  183.6 7.9 %collective-permute-start.16 = (bf16[128,256]{1,0:T(8,128)(2,1)S(1)}, bf16[128,256]{1,0:T(8,128)(2,1)S(1)}, u32[]{:S(2)}, u32[]{:S(2)}) collective-permute-start(bf16[128,256]{1,0:T(8,128)(2,1)S(1)} %merge.1), channel_id=1, source_target_pairs={{0,24},{8,0},{16,8},{24,16},{1,25},{9,1},{17,9},{25,17},{2,26},{10... | collective-permute-start | bytes 196616 | tf_op jit(solution)/shard_map/ppermute | solution.py:34
  191.5 9.3 %collective-permute-start.17 = (bf16[4,128,256]{2,1,0:T(8,128)(2,1)S(1)}, bf16[4,128,256]{2,1,0:T(8,128)(2,1)S(1)}, u32[]{:S(2)}, u32[]{:S(2)}) collective-permute-start(bf16[4,128,256]{2,1,0:T(8,128)(2,1)S(1)} %pad_maximum_fusion.1.refs_0_), channel_id=1, source_target_pairs={{0,2},{2,4},{4,6},{6,0},{1,3},{3,5},{5,7},{7,1},{8,10},{10,12},{12... | collective-permute-start | bytes 786440 | tf_op jit(solution)/shard_map/ppermute | solution.py:34
  193.7 12.8 %collective-permute-start.18 = (bf16[4,128,256]{2,1,0:T(8,128)(2,1)S(1)}, bf16[4,128,256]{2,1,0:T(8,128)(2,1)S(1)}, u32[]{:S(2)}, u32[]{:S(2)}) collective-permute-start(bf16[4,128,256]{2,1,0:T(8,128)(2,1)S(1)} %pad_maximum_fusion.1.refs_0_), channel_id=1, source_target_pairs={{0,4},{2,6},{4,0},{6,2},{1,5},{3,7},{5,1},{7,3},{8,12},{10,14},{12... | collective-permute-start | bytes 786440 | tf_op jit(solution)/shard_map/ppermute | solution.py:34
  197.8 11.7 %collective-permute-start.19 = (bf16[4,128,256]{2,1,0:T(8,128)(2,1)S(1)}, bf16[4,128,256]{2,1,0:T(8,128)(2,1)S(1)}, u32[]{:S(2)}, u32[]{:S(2)}) collective-permute-start(bf16[4,128,256]{2,1,0:T(8,128)(2,1)S(1)} %pad_maximum_fusion.1.refs_0_), channel_id=1, source_target_pairs={{0,6},{2,0},{4,2},{6,4},{1,7},{3,1},{5,3},{7,5},{8,14},{10,8},{12,... | collective-permute-start | bytes 786440 | tf_op jit(solution)/shard_map/ppermute | solution.py:34
  (11 other events, 381.8 us)
Sparse Core Ops, SparseCore 0:
  26.7 74.3 all-gather.5
  166.5 28.5 all-gather.7

commit v5 on v4

--- a/solution.py
+++ b/solution.py
@@ -114,11 +114,12 @@
     v_cache[...] = value.T.astype(BF16)
 
 
-def attend_kernel(q, q_got, keys, mine, mine_lse, message, held):
+def attend_kernel(q, q1, q2, q3, keys, mine, mine_lse, m1, m2, m3, held):
     count = keys.shape[0]
     scale = LOG2E / math.sqrt(HEAD_DIM)
-    q_low = jnp.concatenate([q[:128], q_got[:128]], axis=1)
-    seg_q = jnp.concatenate([q[128:144], q_got[128:144]], axis=1).astype(F32)[:1]
+    parts = (q, q1, q2, q3)
+    q_low = jnp.concatenate([part[:128] for part in parts], axis=1)
+    seg_q = jnp.concatenate([part[128:144] for part in parts], axis=1).astype(F32)[:1]
     top = None
     for b in range(count):
         seg_k = keys[b, 256:272].astype(F32).T[:, :1]
@@ -128,8 +129,8 @@
         here = jnp.max(scores, axis=0, keepdims=True)
         top = here if top is None else jnp.maximum(top, here)
     top = jnp.maximum(top, -1e20)
-    total = jnp.zeros((1, 512), F32)
-    weighted = jnp.zeros((HEAD_DIM, 512), F32)
+    total = jnp.zeros((1, 1024), F32)
+    weighted = jnp.zeros((HEAD_DIM, 1024), F32)
     for b in range(count):
         weights = jnp.exp2(held[b] - top)
         total = total + jnp.sum(weights, axis=0, keepdims=True)
@@ -142,15 +143,16 @@
     lse = jnp.where(some, top + jnp.log2(safe), NEG_FILL)
     mine[...] = out[:, :256]
     mine_lse[...] = jnp.broadcast_to(lse[:, :256], (8, 256))
-    other_lse = lse[:, 256:]
-    high = other_lse.astype(BF16)
-    rest = other_lse - high.astype(F32)
-    middle = rest.astype(BF16)
-    low = (rest - middle.astype(F32)).astype(BF16)
-    message[:128] = out[:, 256:].astype(BF16)
-    message[128:144] = jnp.concatenate(
-        [high.astype(F32), middle.astype(F32), low.astype(F32), jnp.zeros((13, 256), F32)], axis=0
-    ).astype(BF16)
+    for d, message in enumerate((m1, m2, m3), 1):
+        here = slice(256 * d, 256 * d + 256)
+        high = lse[:, here].astype(BF16)
+        rest = lse[:, here] - high.astype(F32)
+        middle = rest.astype(BF16)
+        low = (rest - middle.astype(F32)).astype(BF16)
+        message[:128] = out[:, here].astype(BF16)
+        message[128:144] = jnp.concatenate(
+            [high.astype(F32), middle.astype(F32), low.astype(F32), jnp.zeros((13, 256), F32)], axis=0
+        ).astype(BF16)
 
 
 def merge_kernel(mine, mine_lse, *refs):
@@ -169,21 +171,33 @@
     out[...] = value.astype(BF16)
 
 
-def output_kernel(at, *refs):
-    heads, w, mine, message, held = refs[:4], refs[4], *refs[5:]
-    zl, x, c, zh = at[0], at[1], at[2], at[3]
-    total = None
+def partial_kernel(at, own, other, w, mine, *messages):
+    x = at[1]
+    heads = jnp.concatenate([own[...], other[...]], axis=0)
     for j in range(4):
-        x_from = lax.rem(x - j + 4, 4)
-        for k in range(4):
-            chip = lax.rem(zl - k + 4, 4) * 4 + x_from
-            flip = lax.rem(lax.rem(chip, 2) + zh, 2)
-            term = jnp.dot(w[chip // 2, flip], heads[j][k], preferred_element_type=F32)
-            total = term if total is None else total + term
-    held[0] = total[:160]
-    held[1] = total[160:]
-    mine[...] = held[c]
-    message[...] = held[1 - c]
+        x_to = lax.rem(x + j, 4)
+        high, low = x_to // 2, lax.rem(x_to, 2)
+        for z in range(4):
+            block = 2 * z + high
+            weights = jnp.concatenate([w[block, 0, low], w[block, 1, low]], axis=1)
+            term = jnp.dot(weights, heads, preferred_element_type=F32)
+            if j == 0:
+                mine[z] = term
+            else:
+                messages[j - 1][z] = term.astype(BF16)
+
+
+def along_z_kernel(at, own, g1, g2, g3, mine, m1, m2, m3):
+    zl = at[0]
+    for k in range(4):
+        z = lax.rem(zl + k, 4)
+        total = own[z]
+        for got in (g1, g2, g3):
+            total = total + got[z].astype(F32)
+        if k == 0:
+            mine[...] = total
+        else:
+            (m1, m2, m3)[k - 1][...] = total.astype(BF16)
 
 
 def body(hidden_in, seg_ids, positions, mod_table, w_qkv, q_gain, k_gain, w_out):
@@ -194,20 +208,11 @@
     x = lax.axis_index("xh") * 2 + lax.axis_index("xl")
     at = jnp.stack([zl, x, c, zh]).astype(jnp.int32)
 
-    w_pair = lax.all_gather(jnp.transpose(w_qkv, (1, 0, 2)), "zh", axis=0, tiled=False)
+    local = jnp.concatenate([jnp.transpose(w_qkv, (1, 0, 2)), w_out.T[None]], axis=0)
+    pair = lax.all_gather(local, "zh", axis=0, tiled=False)
+    w_pair, wo_pair = pair[:, :3], pair[:, 3].reshape(2, 2, 160, 128)
     w_all = lax.all_gather(w_pair, ("ya", "yb", "yc"), axis=0, tiled=False)
     w_all = w_all.reshape(16, 3, 2, 160, 128)
-
-    def turned(flip):
-        def move(ya, yb, yc, zh, zl, xh, xl, c):
-            s = (ya * 4 + yb * 2 + yc) * 2 + zh
-            chip = (zl * 2 + xh) * 2 + xl
-            to_s = chip ^ flip
-            return (to_s >> 3, (to_s >> 2) & 1, (to_s >> 1) & 1, to_s & 1, s >> 2, (s >> 1) & 1, s & 1, c)
-
-        return permute(w_out.T, SEQ + TP, move)
-
-    wo_turned = (turned(0), turned(1))
 
     x_t = hidden_in.T.astype(F32)
     sums = jnp.stack([jnp.sum(x_t, axis=0), jnp.sum(x_t * x_t, axis=0)]).reshape(4, 128)
@@ -227,7 +232,6 @@
         precision=lax.Precision.HIGHEST,
     ).reshape(3, feat_local, tok_rows)
     packet = (normed * (1.0 + modulation[1]) + modulation[0]).astype(BF16)
-    packet, wo_turned = lax.optimization_barrier((packet, wo_turned))
 
     held = jnp.stack(
         [packet]
@@ -266,45 +270,57 @@
             shaped((144, 256), BF16),
             shaped((256, 128), BF16),
             shaped((256, 128), BF16),
-            shaped((8, 272, 256), BF16),
+            shaped((4, 272, 256), BF16),
         ),
         [stats, query, key_value, cosine, sine, q_gain.reshape(128, 1), k_gain.reshape(128, 1), marks],
         name="rotate",
     )
-    keys = lax.all_to_all(kv_message, ("ya", "yb", "yc"), 0, 0, tiled=True)
-    q_got = permute(q_rot, ("zh",), lambda zh: (1 - zh,))
-
-    wo_pair, keys, q_got = lax.optimization_barrier((jnp.stack(wo_turned), keys, q_got))
-    wo_all = lax.all_gather(wo_pair, ("ya", "yb", "yc"), axis=0, tiled=False)
-
-    mine, mine_lse, o_message = call(
+    keys = lax.all_to_all(kv_message, ("ya", "yb"), 0, 0, tiled=True)
+    q_gots = [
+        permute(q_rot, ("yc", "zh"), lambda yc, zh, d=d: (yc ^ (d & 1), zh ^ (d >> 1)))
+        for d in (2, 3, 1)
+    ]
+
+    give = lax.dynamic_index_in_dim(wo_pair, 1 - c, axis=1, keepdims=False)
+    keep = lax.dynamic_index_in_dim(wo_pair, c, axis=1, keepdims=False)
+    take = permute(give, ("c",), lambda c: (1 - c,))
+    wo_all = lax.all_gather(jnp.stack([keep, take]), ("ya", "yb", "yc"), axis=0, tiled=False)
+
+    mine, mine_lse, *o_messages = call(
         attend_kernel,
-        (shaped((128, 256), F32), shaped((8, 256), F32), shaped((144, 256), BF16)),
-        [q_rot, q_got, keys],
-        scratch=[pltpu.VMEM((8, 256, 512), F32)],
+        (shaped((128, 256), F32), shaped((8, 256), F32)) + (shaped((144, 256), BF16),) * 3,
+        [q_rot] + q_gots + [keys],
+        scratch=[pltpu.VMEM((4, 256, 1024), F32)],
         name="attend",
     )
-    o_got = permute(o_message, ("zh",), lambda zh: (1 - zh,))
-    attention = call(merge_kernel, shaped((128, 256), BF16), [mine, mine_lse, o_got], name="merge")
-
-    by_z = [attention] + [
-        permute(attention, ("zl",), lambda zl, k=k: ((zl + k) % 4,)) for k in range(1, 4)
+    o_gots = [
+        permute(o, ("yc", "zh"), lambda yc, zh, d=d: (yc ^ (d & 1), zh ^ (d >> 1)))
+        for d, o in zip((2, 3, 1), o_messages, strict=True)
     ]
-    by_z = jnp.stack(by_z)
-    by_x = [by_z] + [
-        permute(by_z, ("xh", "xl"), lambda xh, xl, j=j: divmod((xh * 2 + xl + j) % 4, 2))
-        for j in range(1, 4)
+    attention = call(merge_kernel, shaped((128, 256), BF16), [mine, mine_lse] + o_gots, name="merge")
+    other = permute(attention, ("c",), lambda c: (1 - c,))
+
+    own, *messages = call(
+        partial_kernel,
+        (shaped((4, 160, 256), F32),) + (shaped((4, 160, 256), BF16),) * 3,
+        [attention, other, wo_all],
+        scalars=at,
+        name="partial",
+    )
+    gots = [
+        permute(part, ("xh", "xl"), lambda xh, xl, j=j: divmod((xh * 2 + xl + j) % 4, 2))
+        for j, part in enumerate(messages, 1)
     ]
-    out_mine, out_message = call(
-        output_kernel,
-        (shaped((160, 256), F32), shaped((160, 256), F32)),
-        by_x + [wo_all],
+    own, *messages = call(
+        along_z_kernel,
+        (shaped((160, 256), F32),) + (shaped((160, 256), BF16),) * 3,
+        [own] + gots,
         scalars=at,
-        scratch=[pltpu.VMEM((2, 160, 256), F32)],
-        name="output",
-    )
-    out_got = permute(out_message, ("c",), lambda c: (1 - c,))
-    mixed = out_mine + out_got
+        name="along_z",
+    )
+    mixed = own
+    for k, part in enumerate(messages, 1):
+        mixed = mixed + permute(part, ("zl",), lambda zl, k=k: ((zl + k) % 4,)).astype(F32)
     hidden_out = (x_t + modulation[2] * mixed).T.astype(BF16)
     return (hidden_out, k_cache, v_cache)
 

time: 227 us -> 215 us (0.947)
  waiting for transfers between devices: 70.1 us -> 50.4 us
  starting transfers between devices: 105 us -> 111 us
  blocking collectives: 19.3 us -> 16.7 us
    all_to_all x1, waiting for transfers between devices: 19.7 us -> 0.01 us  [body(): keys = lax.all_to_all(kv_message, ('ya', 'yb'), 0, 0, tiled=True)]
    ppermute x21 -> x24, starting transfers between devices: 79.4 us -> 84.3 us  [permute(): return lax.ppermute(value, axes, pairs)]
    ppermute x21 -> x24, waiting for transfers between devices: 42.4 us -> 37.8 us  [permute(): return lax.ppermute(value, axes, pairs)]
    all_to_all x1, waiting for transfers between devices: 0.01 us -> 4.57 us  [body(): lax.all_to_all(jnp.broadcast_to(sums, (32, 8, 128)), TP, 0, 0, tiled=True)]
    all_gather x1, blocking collectives: 19.3 us -> 16.7 us  [body(): pair = lax.all_gather(local, 'zh', axis=0, tiled=False)]
    pallas_call x5 -> x6, Pallas kernels: 9.58 us -> 9.57 us  [call(): pl.pallas_call(kernel, out_shape=out_shape, in_specs=specs, out_specs=jax...]
  transfers between devices with their start and end apart: 26 -> 29, of which waited for: 15 -> 16; matrix products, arithmetic and copies ran while one was open for 2% -> 2% of each run, Pallas kernels for 1% -> 4%
where the time goes in v5:
time: 215 us; the launch traced here: 212 us
  starting transfers between devices  111 us (52%)
  waiting for transfers between devices  50.4 us (23%)
  blocking collectives  16.7 us (8%)
  between operations  14.6 us (7%)
  Pallas kernels  9.57 us (4%)
  other arithmetic  6.07 us (3%)
  local copies, waits for them, and re-layouts  3.55 us (2%)
    ppermute x24, starting transfers between devices, permute(): return lax.ppermute(value, axes, pairs)  84.3 us
    ppermute x24, waiting for transfers between devices, permute(): return lax.ppermute(value, axes, pairs)  37.8 us
    all_gather x1, blocking collectives, body(): pair = lax.all_gather(local, 'zh', axis=0, tiled=False)  16.7 us
    all_to_all x1, starting transfers between devices, body(): lax.all_to_all(jnp.broadcast_to(sums, (32, 8, 128)), TP, 0, 0, tiled=True)  15.6 us
    pallas_call x6, Pallas kernels, call(): pl.pallas_call(kernel, out_shape=out_shape, in_specs=specs, out_specs=jax...  9.57 us
    all_to_all x1, waiting for transfers between devices, body(): stats = lax.all_to_all(stats, TP, 0, 0, tiled=True)  7.99 us
    all_to_all x1, starting transfers between devices, body(): keys = lax.all_to_all(kv_message, ('ya', 'yb'), 0, 0, tiled=True)  5.85 us
    all_to_all x1, starting transfers between devices, body(): stats = lax.all_to_all(stats, TP, 0, 0, tiled=True)  4.95 us
  transfers between devices with their start and end apart: 29, of which 16 were waited for; matrix products, arithmetic and copies ran while one was open for 2% of the time, Pallas kernels for 4%

profile of v5, /device:TPU:1, one launch (start us, length us, event | category | flops | bytes accessed | tf_op | source)
XLA Modules:
  0.0 212.1 jit_solution(16188434498364679645)
XLA Ops:
  8.3 16.7 %all-gather = bf16[8,320,128]{2,1,0:T(8,128)(2,1)S(1)} all-gather(bf16[4,320,128]{2,1,0:T(8,128)(2,1)S(1)} %pad_maximum_fusion), channel_id=2, replica_groups=mesh['ya'=2,'yb'=2,'yc'=2,'zh'=2,'zl'=4,'xh'=2,'xl'=2,'c'=2] {'zh'}, dimensions={0}, use_global_device_ids=true | all-gather | bytes 983040 | tf_op jit(solution)/shard_map/all_gather | solution.py:212
  28.4 15.6 %all-to-all-start = ((f32[32,8,128]{2,1,0:T(8,128)}), f32[32,8,128]{2,1,0:T(8,128)S(1)}, u32[]{:S(2)}, u32[]{:S(2)}) async-start(f32[32,8,128]{2,1,0:T(8,128)} %broadcast_in_dim.13), calls=%async_computation | async-start | bytes 262144 | tf_op jit(solution)/shard_map/all_to_all | solution.py:221
  48.0 4.6 %all-to-all-done = f32[32,8,128]{2,1,0:T(8,128)S(1)} async-done(((f32[32,8,128]{2,1,0:T(8,128)}), f32[32,8,128]{2,1,0:T(8,128)S(1)}, u32[]{:S(2)}, u32[]{:S(2)}) %all-to-all-start) | async-done | bytes 131104 | tf_op jit(solution)/shard_map/all_to_all | solution.py:221
  57.9 3.8 %collective-permute-start.2 = (bf16[160,256]{1,0:T(8,128)(2,1)S(1)}, bf16[160,256]{1,0:T(8,128)(2,1)S(1)}, u32[]{:S(2)}, u32[]{:S(2)}) collective-permute-start(bf16[160,256]{1,0:T(8,128)(2,1)S(1)} %fusion.7), channel_id=1, source_target_pairs={{0,24},{8,0},{16,8},{24,16},{1,25},{9,1},{17,9},{25,17},{2,26},{10... | collective-permute-start | bytes 245768 | tf_op jit(solution)/shard_map/ppermute | solution.py:34
  68.4 3.8 %collective-permute-start.4 = (bf16[4,160,256]{2,1,0:T(8,128)(2,1)S(1)}, bf16[4,160,256]{2,1,0:T(8,128)(2,1)S(1)}, u32[]{:S(2)}, u32[]{:S(2)}) collective-permute-start(bf16[4,160,256]{2,1,0:T(8,128)(2,1)S(1)} %pad_maximum_fusion.1.refs_0_), channel_id=1, source_target_pairs={{0,4},{2,6},{4,0},{6,2},{1,5},{3,7},{5,1},{7,3},{8,12},{10,14},{12... | collective-permute-start | bytes 983048 | tf_op jit(solution)/shard_map/ppermute | solution.py:34
  75.2 3.1 %collective-permute-start.6 = (bf16[4,160,256]{2,1,0:T(8,128)(2,1)S(1)}, bf16[4,160,256]{2,1,0:T(8,128)(2,1)S(1)}, u32[]{:S(2)}, u32[]{:S(2)}) collective-permute-start(bf16[4,160,256]{2,1,0:T(8,128)(2,1)S(1)} %pad_maximum_fusion.1.refs_0_), channel_id=1, source_target_pairs={{0,1},{1,0},{2,3},{3,2},{4,5},{5,4},{6,7},{7,6},{8,9},{9,8},{10,11... | collective-permute-start | bytes 983048 | tf_op jit(solution)/shard_map/ppermute | solution.py:34
  78.8 9.5 %collective-permute-start.7 = (bf16[4,160,256]{2,1,0:T(8,128)(2,1)S(1)}, bf16[4,160,256]{2,1,0:T(8,128)(2,1)S(1)}, u32[]{:S(2)}, u32[]{:S(2)}) collective-permute-start(bf16[4,160,256]{2,1,0:T(8,128)(2,1)S(1)} %collective-permute-done.3.refs_1_), channel_id=1, source_target_pairs={{0,1},{1,0},{2,3},{3,2},{4,5},{5,4},{6,7},{7,6},{8,9},{9,8},{10,11... | collective-permute-start | bytes 983048 | tf_op jit(solution)/shard_map/ppermute | solution.py:34
  93.9 4.7 %project.1 = (f32[128,256]{1,0:T(8,128)S(1)}, f32[2,128,256]{2,1,0:T(8,128)S(1)}, f32[32,8,128]{2,1,0:T(8,128)}) custom-call(s32[4]{0:T(128)S(1)} %pad_add_fusion.at, bf16[4,160,256]{2,1,0:T(8,128)(2,1)S(1)} %pad_maximum_fusion.1.refs_0_, bf16[4,160,256]{2,1,0:T(8,128)(2,1)S(1)} %collective-permute-done.3.refs_1_, ...), custom_call_target="tpu_custom_call" | custom-call | flops 1006632960 | bytes 6291456 | tf_op jit(solution)/shard_map/project/pallas_call | solution.py:46
  98.6 4.9 %all-to-all-start.1 = ((f32[32,8,128]{2,1,0:T(8,128)}), f32[32,8,128]{2,1,0:T(8,128)S(1)}, u32[]{:S(2)}, u32[]{:S(2)}) async-start(f32[32,8,128]{2,1,0:T(8,128)} %get-tuple-element.25), calls=%async_computation.1 | async-start | bytes 262144 | tf_op jit(solution)/shard_map/all_to_all | solution.py:266
  104.1 8.0 %all-to-all-done.1.got = f32[32,8,128]{2,1,0:T(8,128)S(1)} async-done(((f32[32,8,128]{2,1,0:T(8,128)}), f32[32,8,128]{2,1,0:T(8,128)S(1)}, u32[]{:S(2)}, u32[]{:S(2)}) %all-to-all-start.1) | async-done | bytes 131104 | tf_op jit(solution)/shard_map/all_to_all | solution.py:266
  113.2 5.8 %all-to-all-start.2 = ((bf16[4,272,256]{2,1,0:T(8,128)(2,1)}), bf16[4,272,256]{2,1,0:T(8,128)(2,1)S(1)}, u32[]{:S(2)}, u32[]{:S(2)}) async-start(bf16[4,272,256]{2,1,0:T(8,128)(2,1)} %get-tuple-element.29), calls=%async_computation.2 | async-start | bytes 1114112 | tf_op jit(solution)/shard_map/all_to_all | solution.py:278
  119.0 7.0 %collective-permute-start.10 = (bf16[144,256]{1,0:T(8,128)(2,1)S(1)}, bf16[144,256]{1,0:T(8,128)(2,1)S(1)}, u32[]{:S(2)}, u32[]{:S(2)}) collective-permute-start(bf16[144,256]{1,0:T(8,128)(2,1)S(1)} %get-tuple-element.28.q), channel_id=1, source_target_pairs={{0,32},{32,0},{64,96},{96,64},{1,33},{33,1},{65,97},{97,65},{2,34}... | collective-permute-start | bytes 221192 | tf_op jit(solution)/shard_map/ppermute | solution.py:34
  128.3 3.0 %collective-permute-start.12 = (bf16[144,256]{1,0:T(8,128)(2,1)S(1)}, bf16[144,256]{1,0:T(8,128)(2,1)S(1)}, u32[]{:S(2)}, u32[]{:S(2)}) collective-permute-start(bf16[144,256]{1,0:T(8,128)(2,1)S(1)} %get-tuple-element.28.q), channel_id=1, source_target_pairs={{0,64},{32,96},{64,0},{96,32},{1,65},{33,97},{65,1},{97,33},{2,66}... | collective-permute-start | bytes 221192 | tf_op jit(solution)/shard_map/ppermute | solution.py:34
  131.3 13.8 %collective-permute-done.11.q2 = bf16[144,256]{1,0:T(8,128)(2,1)S(1)} collective-permute-done((bf16[144,256]{1,0:T(8,128)(2,1)S(1)}, bf16[144,256]{1,0:T(8,128)(2,1)S(1)}, u32[]{:S(2)}, u32[]{:S(2)}) %collective-permute-start.11) | collective-permute-done | bytes 73760 | tf_op jit(solution)/shard_map/ppermute | solution.py:34
  147.1 3.8 %collective-permute-start.13 = (bf16[144,256]{1,0:T(8,128)(2,1)S(1)}, bf16[144,256]{1,0:T(8,128)(2,1)S(1)}, u32[]{:S(2)}, u32[]{:S(2)}) collective-permute-start(bf16[144,256]{1,0:T(8,128)(2,1)S(1)} %get-tuple-element.32), channel_id=1, source_target_pairs={{0,32},{32,0},{64,96},{96,64},{1,33},{33,1},{65,97},{97,65},{2,34}... | collective-permute-start | bytes 221192 | tf_op jit(solution)/shard_map/ppermute | solution.py:34
  150.9 5.4 %collective-permute-start.14 = (bf16[144,256]{1,0:T(8,128)(2,1)S(1)}, bf16[144,256]{1,0:T(8,128)(2,1)S(1)}, u32[]{:S(2)}, u32[]{:S(2)}) collective-permute-start(bf16[144,256]{1,0:T(8,128)(2,1)S(1)} %get-tuple-element.33), channel_id=1, source_target_pairs={{0,96},{32,64},{64,32},{96,0},{1,97},{33,65},{65,33},{97,1},{2,98}... | collective-permute-start | bytes 221192 | tf_op jit(solution)/shard_map/ppermute | solution.py:34
  156.3 3.1 %collective-permute-start.15 = (bf16[144,256]{1,0:T(8,128)(2,1)S(1)}, bf16[144,256]{1,0:T(8,128)(2,1)S(1)}, u32[]{:S(2)}, u32[]{:S(2)}) collective-permute-start(bf16[144,256]{1,0:T(8,128)(2,1)S(1)} %get-tuple-element.34), channel_id=1, source_target_pairs={{0,64},{32,96},{64,0},{96,32},{1,65},{33,97},{65,1},{97,33},{2,66}... | collective-permute-start | bytes 221192 | tf_op jit(solution)/shard_map/ppermute | solution.py:34
  162.1 4.0 %collective-permute-start.16 = (bf16[128,256]{1,0:T(8,128)(2,1)S(1)}, bf16[128,256]{1,0:T(8,128)(2,1)S(1)}, u32[]{:S(2)}, u32[]{:S(2)}) collective-permute-start(bf16[128,256]{1,0:T(8,128)(2,1)S(1)} %merge.1.own), channel_id=1, source_target_pairs={{0,1},{1,0},{2,3},{3,2},{4,5},{5,4},{6,7},{7,6},{8,9},{9,8},{10,11... | collective-permute-start | bytes 196616 | tf_op jit(solution)/shard_map/ppermute | solution.py:34
  169.3 3.1 %collective-permute-start.18 = (bf16[4,160,256]{2,1,0:T(8,128)(2,1)S(1)}, bf16[4,160,256]{2,1,0:T(8,128)(2,1)S(1)}, u32[]{:S(2)}, u32[]{:S(2)}) collective-permute-start(bf16[4,160,256]{2,1,0:T(8,128)(2,1)S(1)} %get-tuple-element.36), channel_id=1, source_target_pairs={{0,2},{2,4},{4,6},{6,0},{1,3},{3,5},{5,7},{7,1},{8,10},{10,12},{12... | collective-permute-start | bytes 983048 | tf_op jit(solution)/shard_map/ppermute | solution.py:34
  172.5 3.7 %collective-permute-start.19 = (bf16[4,160,256]{2,1,0:T(8,128)(2,1)S(1)}, bf16[4,160,256]{2,1,0:T(8,128)(2,1)S(1)}, u32[]{:S(2)}, u32[]{:S(2)}) collective-permute-start(bf16[4,160,256]{2,1,0:T(8,128)(2,1)S(1)} %get-tuple-element.37), channel_id=1, source_target_pairs={{0,4},{2,6},{4,0},{6,2},{1,5},{3,7},{5,1},{7,3},{8,12},{10,14},{12... | collective-permute-start | bytes 983048 | tf_op jit(solution)/shard_map/ppermute | solution.py:34
  176.2 3.3 %collective-permute-start.20 = (bf16[4,160,256]{2,1,0:T(8,128)(2,1)S(1)}, bf16[4,160,256]{2,1,0:T(8,128)(2,1)S(1)}, u32[]{:S(2)}, u32[]{:S(2)}) collective-permute-start(bf16[4,160,256]{2,1,0:T(8,128)(2,1)S(1)} %get-tuple-element.38), channel_id=1, source_target_pairs={{0,6},{2,0},{4,2},{6,4},{1,7},{3,1},{5,3},{7,5},{8,14},{10,8},{12,... | collective-permute-start | bytes 983048 | tf_op jit(solution)/shard_map/ppermute | solution.py:34
  181.4 7.3 %collective-permute-done.19.g2 = bf16[4,160,256]{2,1,0:T(8,128)(2,1)S(1)} collective-permute-done((bf16[4,160,256]{2,1,0:T(8,128)(2,1)S(1)}, bf16[4,160,256]{2,1,0:T(8,128)(2,1)S(1)}, u32[]{:S(2)}, u32[]{:S(2)}) %collective-permute-start.19) | collective-permute-done | bytes 327712 | tf_op jit(solution)/shard_map/ppermute | solution.py:34
  196.4 3.9 %collective-permute-start.23 = (bf16[160,256]{1,0:T(8,128)(2,1)S(1)}, bf16[160,256]{1,0:T(8,128)(2,1)S(1)}, u32[]{:S(2)}, u32[]{:S(2)}) collective-permute-start(bf16[160,256]{1,0:T(8,128)(2,1)S(1)} %get-tuple-element.42), channel_id=1, source_target_pairs={{0,24},{8,0},{16,8},{24,16},{1,25},{9,1},{17,9},{25,17},{2,26},{10... | collective-permute-start | bytes 245768 | tf_op jit(solution)/shard_map/ppermute | solution.py:34
  200.3 2.9 %collective-permute-done.22 = bf16[160,256]{1,0:T(8,128)(2,1)S(1)} collective-permute-done((bf16[160,256]{1,0:T(8,128)(2,1)S(1)}, bf16[160,256]{1,0:T(8,128)(2,1)S(1)}, u32[]{:S(2)}, u32[]{:S(2)}) %collective-permute-start.22) | collective-permute-done | bytes 81952 | tf_op jit(solution)/shard_map/ppermute | solution.py:34
  (94 shorter events, 52.6 us)
Async XLA Ops:
  7.2 86.7 %all-gather.6.cloned.1.call-start = ((), (), s32[]{:S(2)}) async-start(), calls=%async_computation.3 | async-start | bytes 4423680 | tf_op jit(solution)/shard_map/all_gather | solution.py:214
  28.4 24.2 %all-to-all-start = ((f32[32,8,128]{2,1,0:T(8,128)}), f32[32,8,128]{2,1,0:T(8,128)S(1)}, u32[]{:S(2)}, u32[]{:S(2)}) async-start(f32[32,8,128]{2,1,0:T(8,128)} %broadcast_in_dim.13), calls=%async_computation | async-start | bytes 262144 | tf_op jit(solution)/shard_map/all_to_all | solution.py:221
  44.0 122.1 %all-gather.8.cloned.1.call-start = ((), (), s32[]{:S(2)}) async-start(), calls=%async_computation.4 | async-start | bytes 1474560 | tf_op jit(solution)/shard_map/all_gather | solution.py:287
  52.7 9.2 %collective-permute-start = (bf16[160,256]{1,0:T(8,128)(2,1)S(1)}, bf16[160,256]{1,0:T(8,128)(2,1)S(1)}, u32[]{:S(2)}, u32[]{:S(2)}) collective-permute-start(bf16[160,256]{1,0:T(8,128)(2,1)S(1)} %fusion.7), channel_id=1, source_target_pairs={{0,8},{8,16},{16,24},{24,0},{1,9},{9,17},{17,25},{25,1},{2,10},{10... | collective-permute-start | bytes 245768 | tf_op jit(solution)/shard_map/ppermute | solution.py:34
  55.0 9.3 %collective-permute-start.1 = (bf16[160,256]{1,0:T(8,128)(2,1)S(1)}, bf16[160,256]{1,0:T(8,128)(2,1)S(1)}, u32[]{:S(2)}, u32[]{:S(2)}) collective-permute-start(bf16[160,256]{1,0:T(8,128)(2,1)S(1)} %fusion.7), channel_id=1, source_target_pairs={{0,16},{8,24},{16,0},{24,8},{1,17},{9,25},{17,1},{25,9},{2,18},{10... | collective-permute-start | bytes 245768 | tf_op jit(solution)/shard_map/ppermute | solution.py:34
  57.9 8.2 %collective-permute-start.2 = (bf16[160,256]{1,0:T(8,128)(2,1)S(1)}, bf16[160,256]{1,0:T(8,128)(2,1)S(1)}, u32[]{:S(2)}, u32[]{:S(2)}) collective-permute-start(bf16[160,256]{1,0:T(8,128)(2,1)S(1)} %fusion.7), channel_id=1, source_target_pairs={{0,24},{8,0},{16,8},{24,16},{1,25},{9,1},{17,9},{25,17},{2,26},{10... | collective-permute-start | bytes 245768 | tf_op jit(solution)/shard_map/ppermute | solution.py:34
  66.2 12.6 %collective-permute-start.3 = (bf16[4,160,256]{2,1,0:T(8,128)(2,1)S(1)}, bf16[4,160,256]{2,1,0:T(8,128)(2,1)S(1)}, u32[]{:S(2)}, u32[]{:S(2)}) collective-permute-start(bf16[4,160,256]{2,1,0:T(8,128)(2,1)S(1)} %pad_maximum_fusion.1.refs_0_), channel_id=1, source_target_pairs={{0,2},{2,4},{4,6},{6,0},{1,3},{3,5},{5,7},{7,1},{8,10},{10,12},{12... | collective-permute-start | bytes 983048 | tf_op jit(solution)/shard_map/ppermute | solution.py:34
  68.4 19.9 %collective-permute-start.4 = (bf16[4,160,256]{2,1,0:T(8,128)(2,1)S(1)}, bf16[4,160,256]{2,1,0:T(8,128)(2,1)S(1)}, u32[]{:S(2)}, u32[]{:S(2)}) collective-permute-start(bf16[4,160,256]{2,1,0:T(8,128)(2,1)S(1)} %pad_maximum_fusion.1.refs_0_), channel_id=1, source_target_pairs={{0,4},{2,6},{4,0},{6,2},{1,5},{3,7},{5,1},{7,3},{8,12},{10,14},{12... | collective-permute-start | bytes 983048 | tf_op jit(solution)/shard_map/ppermute | solution.py:34
  72.1 18.1 %collective-permute-start.5 = (bf16[4,160,256]{2,1,0:T(8,128)(2,1)S(1)}, bf16[4,160,256]{2,1,0:T(8,128)(2,1)S(1)}, u32[]{:S(2)}, u32[]{:S(2)}) collective-permute-start(bf16[4,160,256]{2,1,0:T(8,128)(2,1)S(1)} %pad_maximum_fusion.1.refs_0_), channel_id=1, source_target_pairs={{0,6},{2,0},{4,2},{6,4},{1,7},{3,1},{5,3},{7,5},{8,14},{10,8},{12,... | collective-permute-start | bytes 983048 | tf_op jit(solution)/shard_map/ppermute | solution.py:34
  75.2 17.7 %collective-permute-start.6 = (bf16[4,160,256]{2,1,0:T(8,128)(2,1)S(1)}, bf16[4,160,256]{2,1,0:T(8,128)(2,1)S(1)}, u32[]{:S(2)}, u32[]{:S(2)}) collective-permute-start(bf16[4,160,256]{2,1,0:T(8,128)(2,1)S(1)} %pad_maximum_fusion.1.refs_0_), channel_id=1, source_target_pairs={{0,1},{1,0},{2,3},{3,2},{4,5},{5,4},{6,7},{7,6},{8,9},{9,8},{10,11... | collective-permute-start | bytes 983048 | tf_op jit(solution)/shard_map/ppermute | solution.py:34
  78.8 14.1 %collective-permute-start.7 = (bf16[4,160,256]{2,1,0:T(8,128)(2,1)S(1)}, bf16[4,160,256]{2,1,0:T(8,128)(2,1)S(1)}, u32[]{:S(2)}, u32[]{:S(2)}) collective-permute-start(bf16[4,160,256]{2,1,0:T(8,128)(2,1)S(1)} %collective-permute-done.3.refs_1_), channel_id=1, source_target_pairs={{0,1},{1,0},{2,3},{3,2},{4,5},{5,4},{6,7},{7,6},{8,9},{9,8},{10,11... | collective-permute-start | bytes 983048 | tf_op jit(solution)/shard_map/ppermute | solution.py:34
  98.6 13.5 %all-to-all-start.1 = ((f32[32,8,128]{2,1,0:T(8,128)}), f32[32,8,128]{2,1,0:T(8,128)S(1)}, u32[]{:S(2)}, u32[]{:S(2)}) async-start(f32[32,8,128]{2,1,0:T(8,128)} %get-tuple-element.25), calls=%async_computation.1 | async-start | bytes 262144 | tf_op jit(solution)/shard_map/all_to_all | solution.py:266
  113.2 31.9 %all-to-all-start.2 = ((bf16[4,272,256]{2,1,0:T(8,128)(2,1)}), bf16[4,272,256]{2,1,0:T(8,128)(2,1)S(1)}, u32[]{:S(2)}, u32[]{:S(2)}) async-start(bf16[4,272,256]{2,1,0:T(8,128)(2,1)} %get-tuple-element.29), calls=%async_computation.2 | async-start | bytes 1114112 | tf_op jit(solution)/shard_map/all_to_all | solution.py:278
  119.0 12.3 %collective-permute-start.10 = (bf16[144,256]{1,0:T(8,128)(2,1)S(1)}, bf16[144,256]{1,0:T(8,128)(2,1)S(1)}, u32[]{:S(2)}, u32[]{:S(2)}) collective-permute-start(bf16[144,256]{1,0:T(8,128)(2,1)S(1)} %get-tuple-element.28.q), channel_id=1, source_target_pairs={{0,32},{32,0},{64,96},{96,64},{1,33},{33,1},{65,97},{97,65},{2,34}... | collective-permute-start | bytes 221192 | tf_op jit(solution)/shard_map/ppermute | solution.py:34
  126.1 19.1 %collective-permute-start.11 = (bf16[144,256]{1,0:T(8,128)(2,1)S(1)}, bf16[144,256]{1,0:T(8,128)(2,1)S(1)}, u32[]{:S(2)}, u32[]{:S(2)}) collective-permute-start(bf16[144,256]{1,0:T(8,128)(2,1)S(1)} %get-tuple-element.28.q), channel_id=1, source_target_pairs={{0,96},{32,64},{64,32},{96,0},{1,97},{33,65},{65,33},{97,1},{2,98}... | collective-permute-start | bytes 221192 | tf_op jit(solution)/shard_map/ppermute | solution.py:34
  128.3 16.8 %collective-permute-start.12 = (bf16[144,256]{1,0:T(8,128)(2,1)S(1)}, bf16[144,256]{1,0:T(8,128)(2,1)S(1)}, u32[]{:S(2)}, u32[]{:S(2)}) collective-permute-start(bf16[144,256]{1,0:T(8,128)(2,1)S(1)} %get-tuple-element.28.q), channel_id=1, source_target_pairs={{0,64},{32,96},{64,0},{96,32},{1,65},{33,97},{65,1},{97,33},{2,66}... | collective-permute-start | bytes 221192 | tf_op jit(solution)/shard_map/ppermute | solution.py:34
  147.1 12.3 %collective-permute-start.13 = (bf16[144,256]{1,0:T(8,128)(2,1)S(1)}, bf16[144,256]{1,0:T(8,128)(2,1)S(1)}, u32[]{:S(2)}, u32[]{:S(2)}) collective-permute-start(bf16[144,256]{1,0:T(8,128)(2,1)S(1)} %get-tuple-element.32), channel_id=1, source_target_pairs={{0,32},{32,0},{64,96},{96,64},{1,33},{33,1},{65,97},{97,65},{2,34}... | collective-permute-start | bytes 221192 | tf_op jit(solution)/shard_map/ppermute | solution.py:34
  150.9 10.6 %collective-permute-start.14 = (bf16[144,256]{1,0:T(8,128)(2,1)S(1)}, bf16[144,256]{1,0:T(8,128)(2,1)S(1)}, u32[]{:S(2)}, u32[]{:S(2)}) collective-permute-start(bf16[144,256]{1,0:T(8,128)(2,1)S(1)} %get-tuple-element.33), channel_id=1, source_target_pairs={{0,96},{32,64},{64,32},{96,0},{1,97},{33,65},{65,33},{97,1},{2,98}... | collective-permute-start | bytes 221192 | tf_op jit(solution)/shard_map/ppermute | solution.py:34
  169.3 12.1 %collective-permute-start.18 = (bf16[4,160,256]{2,1,0:T(8,128)(2,1)S(1)}, bf16[4,160,256]{2,1,0:T(8,128)(2,1)S(1)}, u32[]{:S(2)}, u32[]{:S(2)}) collective-permute-start(bf16[4,160,256]{2,1,0:T(8,128)(2,1)S(1)} %get-tuple-element.36), channel_id=1, source_target_pairs={{0,2},{2,4},{4,6},{6,0},{1,3},{3,5},{5,7},{7,1},{8,10},{10,12},{12... | collective-permute-start | bytes 983048 | tf_op jit(solution)/shard_map/ppermute | solution.py:34
  172.5 16.3 %collective-permute-start.19 = (bf16[4,160,256]{2,1,0:T(8,128)(2,1)S(1)}, bf16[4,160,256]{2,1,0:T(8,128)(2,1)S(1)}, u32[]{:S(2)}, u32[]{:S(2)}) collective-permute-start(bf16[4,160,256]{2,1,0:T(8,128)(2,1)S(1)} %get-tuple-element.37), channel_id=1, source_target_pairs={{0,4},{2,6},{4,0},{6,2},{1,5},{3,7},{5,1},{7,3},{8,12},{10,14},{12... | collective-permute-start | bytes 983048 | tf_op jit(solution)/shard_map/ppermute | solution.py:34
  176.2 14.5 %collective-permute-start.20 = (bf16[4,160,256]{2,1,0:T(8,128)(2,1)S(1)}, bf16[4,160,256]{2,1,0:T(8,128)(2,1)S(1)}, u32[]{:S(2)}, u32[]{:S(2)}) collective-permute-start(bf16[4,160,256]{2,1,0:T(8,128)(2,1)S(1)} %get-tuple-element.38), channel_id=1, source_target_pairs={{0,6},{2,0},{4,2},{6,4},{1,7},{3,1},{5,3},{7,5},{8,14},{10,8},{12,... | collective-permute-start | bytes 983048 | tf_op jit(solution)/shard_map/ppermute | solution.py:34
  191.3 9.0 %collective-permute-start.21 = (bf16[160,256]{1,0:T(8,128)(2,1)S(1)}, bf16[160,256]{1,0:T(8,128)(2,1)S(1)}, u32[]{:S(2)}, u32[]{:S(2)}) collective-permute-start(bf16[160,256]{1,0:T(8,128)(2,1)S(1)} %get-tuple-element.40), channel_id=1, source_target_pairs={{0,8},{8,16},{16,24},{24,0},{1,9},{9,17},{17,25},{25,1},{2,10},{10... | collective-permute-start | bytes 245768 | tf_op jit(solution)/shard_map/ppermute | solution.py:34
  193.9 9.4 %collective-permute-start.22 = (bf16[160,256]{1,0:T(8,128)(2,1)S(1)}, bf16[160,256]{1,0:T(8,128)(2,1)S(1)}, u32[]{:S(2)}, u32[]{:S(2)}) collective-permute-start(bf16[160,256]{1,0:T(8,128)(2,1)S(1)} %get-tuple-element.41), channel_id=1, source_target_pairs={{0,16},{8,24},{16,0},{24,8},{1,17},{9,25},{17,1},{25,9},{2,18},{10... | collective-permute-start | bytes 245768 | tf_op jit(solution)/shard_map/ppermute | solution.py:34
  196.4 7.2 %collective-permute-start.23 = (bf16[160,256]{1,0:T(8,128)(2,1)S(1)}, bf16[160,256]{1,0:T(8,128)(2,1)S(1)}, u32[]{:S(2)}, u32[]{:S(2)}) collective-permute-start(bf16[160,256]{1,0:T(8,128)(2,1)S(1)} %get-tuple-element.42), channel_id=1, source_target_pairs={{0,24},{8,0},{16,8},{24,16},{1,25},{9,1},{17,9},{25,17},{2,26},{10... | collective-permute-start | bytes 245768 | tf_op jit(solution)/shard_map/ppermute | solution.py:34
  (13 other events, 369.6 us)
Sparse Core Ops, SparseCore 0:
  26.0 64.5 all-gather.5
  92.6 43.0 all-gather.7

commit v6 on v5

--- a/solution.py
+++ b/solution.py
@@ -61,15 +61,16 @@
 
 def project_kernel(at, *refs):
     xs, w, out_q, out_kv, stats = refs[:8], refs[8], *refs[9:]
-    zl, x, c = at[0], at[1], at[2]
+    zl, x, c, zh = at[0], at[1], at[2], at[3]
     total = None
     for i in range(2):
         core = lax.rem(c + i, 2)
         for j in range(4):
             x_from = lax.rem(x - j + 4, 4)
+            swap = lax.rem(x_from + zh, 2)
             for k in range(4):
-                chip = lax.rem(zl - k + 4, 4) * 4 + x_from
-                weights = jnp.concatenate([w[chip, p, core] for p in range(3)], axis=1)
+                block = lax.rem(zl - k + 4, 4) * 2 + x_from // 2
+                weights = jnp.concatenate([w[block, swap, p, core] for p in range(3)], axis=1)
                 term = contract_first(weights, xs[4 * i + j][k])
                 total = term if total is None else total + term
     query, key, value = total[:128], total[128:256], total[256:]
@@ -171,33 +172,31 @@
     out[...] = value.astype(BF16)
 
 
-def partial_kernel(at, own, other, w, mine, *messages):
-    x = at[1]
-    heads = jnp.concatenate([own[...], other[...]], axis=0)
+def partial_kernel(at, heads, w, mine, *messages):
+    zl, x, zh = at[0], at[1], at[3]
     for j in range(4):
         x_to = lax.rem(x + j, 4)
-        high, low = x_to // 2, lax.rem(x_to, 2)
-        for z in range(4):
-            block = 2 * z + high
-            weights = jnp.concatenate([w[block, 0, low], w[block, 1, low]], axis=1)
-            term = jnp.dot(weights, heads, preferred_element_type=F32)
-            if j == 0:
-                mine[z] = term
-            else:
-                messages[j - 1][z] = term.astype(BF16)
-
-
-def along_z_kernel(at, own, g1, g2, g3, mine, m1, m2, m3):
-    zl = at[0]
-    for k in range(4):
-        z = lax.rem(zl + k, 4)
-        total = own[z]
-        for got in (g1, g2, g3):
-            total = total + got[z].astype(F32)
-        if k == 0:
+        total = None
+        for k in range(4):
+            z_from = lax.rem(zl - k + 4, 4)
+            term = jnp.dot(w[z_from * 2 + x_to // 2, lax.rem(x_to + zh, 2)], heads[k], preferred_element_type=F32)
+            total = term if total is None else total + term
+        if j == 0:
             mine[...] = total
         else:
-            (m1, m2, m3)[k - 1][...] = total.astype(BF16)
+            messages[j - 1][...] = total.astype(BF16)
+
+
+def halves_kernel(at, own, *refs):
+    gots, mine, message, held = refs[:3], *refs[3:]
+    c = at[2]
+    total = own[...]
+    for got in gots:
+        total = total + got[...].astype(F32)
+    held[0] = total[:160]
+    held[1] = total[160:]
+    mine[...] = held[c]
+    message[...] = held[1 - c]
 
 
 def body(hidden_in, seg_ids, positions, mod_table, w_qkv, q_gain, k_gain, w_out):
@@ -208,21 +207,14 @@
     x = lax.axis_index("xh") * 2 + lax.axis_index("xl")
     at = jnp.stack([zl, x, c, zh]).astype(jnp.int32)
 
-    local = jnp.concatenate([jnp.transpose(w_qkv, (1, 0, 2)), w_out.T[None]], axis=0)
-    pair = lax.all_gather(local, "zh", axis=0, tiled=False)
-    w_pair, wo_pair = pair[:, :3], pair[:, 3].reshape(2, 2, 160, 128)
-    w_all = lax.all_gather(w_pair, ("ya", "yb", "yc"), axis=0, tiled=False)
-    w_all = w_all.reshape(16, 3, 2, 160, 128)
+    w_local = jnp.transpose(w_qkv, (1, 0, 2))
+    wo_local = w_out.T
+    got = permute(jnp.concatenate([w_local, wo_local[None]], axis=0), ("zh",), lambda zh: (1 - zh,))
 
     x_t = hidden_in.T.astype(F32)
     sums = jnp.stack([jnp.sum(x_t, axis=0), jnp.sum(x_t * x_t, axis=0)]).reshape(4, 128)
     sums = jnp.concatenate([sums, jnp.zeros((4, 128), F32)], axis=0)
-    sums, w_pair = lax.optimization_barrier((sums, w_pair))
-    sums = lax.all_to_all(jnp.broadcast_to(sums, (32, 8, 128)), TP, 0, 0, tiled=True)
-    sums = jnp.sum(sums, axis=0)[:4].reshape(2, tok_rows)
-    mean_value = sums[0:1] / model_width
-    variance = sums[1:2] / model_width - mean_value * mean_value
-    normed = (x_t - mean_value) * lax.rsqrt(variance + EPSILON)
+    sums = jnp.broadcast_to(sums, (32, 8, 128))
     segment_count = mod_table.shape[0]
     onehot = (seg_ids[None, :] == jnp.arange(segment_count, dtype=jnp.int32)[:, None]).astype(F32)
     modulation = lax.dot_general(
@@ -231,18 +223,6 @@
         (((0,), (0,)), ((), ())),
         precision=lax.Precision.HIGHEST,
     ).reshape(3, feat_local, tok_rows)
-    packet = (normed * (1.0 + modulation[1]) + modulation[0]).astype(BF16)
-
-    held = jnp.stack(
-        [packet]
-        + [permute(packet, ("zl",), lambda zl, k=k: ((zl + k) % 4,)) for k in range(1, 4)]
-    )
-    along_x = [held] + [
-        permute(held, ("xh", "xl"), lambda xh, xl, j=j: divmod((xh * 2 + xl + j) % 4, 2))
-        for j in range(1, 4)
-    ]
-    swapped = [permute(part, ("c",), lambda c: (1 - c,)) for part in along_x]
-
     part_width = HEAD_DIM // 6
     widths = (HEAD_DIM - 4 * part_width, 2 * part_width, 2 * part_width)
     angles = []
@@ -254,6 +234,32 @@
     angle = jnp.concatenate(angles, axis=0)
     cosine, sine = jnp.cos(angle), jnp.sin(angle)
     marks = jnp.broadcast_to(seg_ids[None, :].astype(F32), (16, tok_rows))
+    sums, got, modulation, cosine, sine, marks = lax.optimization_barrier(
+        (sums, got, modulation, cosine, sine, marks)
+    )
+    sums = lax.all_to_all(sums, TP, 0, 0, tiled=True)
+    w_all = lax.all_gather(jnp.stack([w_local, got[:3]]), ("ya", "yb", "yc"), axis=0, tiled=False)
+    w_all = w_all.reshape(8, 2, 3, 2, 160, 128)
+    sums = jnp.sum(sums, axis=0)[:4].reshape(2, tok_rows)
+    mean_value = sums[0:1] / model_width
+    variance = sums[1:2] / model_width - mean_value * mean_value
+    normed = (x_t - mean_value) * lax.rsqrt(variance + EPSILON)
+    packet = (normed * (1.0 + modulation[1]) + modulation[0]).astype(BF16)
+    packet, wo_pair = lax.optimization_barrier((packet, jnp.stack([wo_local, got[3]])))
+
+    held = jnp.stack(
+        [packet]
+        + [permute(packet, ("zl",), lambda zl, k=k: ((zl + k) % 4,)) for k in range(1, 4)]
+    )
+    along_x = [held] + [
+        permute(held, ("xh", "xl"), lambda xh, xl, j=j: divmod((xh * 2 + xl + j) % 4, 2))
+        for j in range(1, 4)
+    ]
+    wo_turned = permute(
+        wo_pair, ("ya", "yb", "zl"), lambda ya, yb, zl: (zl >> 1, zl & 1, ya * 2 + yb)
+    )
+    along_x[2], wo_turned = lax.optimization_barrier((along_x[2], wo_turned))
+    swapped = [permute(part, ("c",), lambda c: (1 - c,)) for part in along_x]
 
     query, key_value, stats = call(
         project_kernel,
@@ -264,6 +270,8 @@
         cost=pl.CostEstimate(flops=2 * 256 * 5120 * 384, bytes_accessed=6 << 20, transcendentals=0),
     )
     stats = lax.all_to_all(stats, TP, 0, 0, tiled=True)
+    stats, wo_turned = lax.optimization_barrier((stats, wo_turned))
+    wo_all = lax.all_gather(wo_turned, ("ya", "yb", "yc"), axis=0, tiled=False)
     q_rot, k_cache, v_cache, kv_message = call(
         functools.partial(rotate_kernel, heads_width),
         (
@@ -281,11 +289,6 @@
         for d in (2, 3, 1)
     ]
 
-    give = lax.dynamic_index_in_dim(wo_pair, 1 - c, axis=1, keepdims=False)
-    keep = lax.dynamic_index_in_dim(wo_pair, c, axis=1, keepdims=False)
-    take = permute(give, ("c",), lambda c: (1 - c,))
-    wo_all = lax.all_gather(jnp.stack([keep, take]), ("ya", "yb", "yc"), axis=0, tiled=False)
-
     mine, mine_lse, *o_messages = call(
         attend_kernel,
         (shaped((128, 256), F32), shaped((8, 256), F32)) + (shaped((144, 256), BF16),) * 3,
@@ -298,29 +301,31 @@
         for d, o in zip((2, 3, 1), o_messages, strict=True)
     ]
     attention = call(merge_kernel, shaped((128, 256), BF16), [mine, mine_lse] + o_gots, name="merge")
-    other = permute(attention, ("c",), lambda c: (1 - c,))
-
-    own, *messages = call(
+    by_z = [attention] + [
+        permute(attention, ("zl",), lambda zl, k=k: ((zl + k) % 4,)) for k in range(1, 4)
+    ]
+    by_z = jnp.stack(by_z)
+    own, *partials = call(
         partial_kernel,
-        (shaped((4, 160, 256), F32),) + (shaped((4, 160, 256), BF16),) * 3,
-        [attention, other, wo_all],
+        (shaped((320, 256), F32),) + (shaped((320, 256), BF16),) * 3,
+        [by_z, wo_all],
         scalars=at,
         name="partial",
     )
     gots = [
         permute(part, ("xh", "xl"), lambda xh, xl, j=j: divmod((xh * 2 + xl + j) % 4, 2))
-        for j, part in enumerate(messages, 1)
-    ]
-    own, *messages = call(
-        along_z_kernel,
-        (shaped((160, 256), F32),) + (shaped((160, 256), BF16),) * 3,
+        for j, part in enumerate(partials, 1)
+    ]
+    out_mine, out_message = call(
+        halves_kernel,
+        (shaped((160, 256), F32), shaped((160, 256), F32)),
         [own] + gots,
         scalars=at,
-        name="along_z",
-    )
-    mixed = own
-    for k, part in enumerate(messages, 1):
-        mixed = mixed + permute(part, ("zl",), lambda zl, k=k: ((zl + k) % 4,)).astype(F32)
+        scratch=[pltpu.VMEM((2, 160, 256), F32)],
+        name="halves",
+    )
+    out_got = permute(out_message, ("c",), lambda c: (1 - c,))
+    mixed = out_mine + out_got
     hidden_out = (x_t + modulation[2] * mixed).T.astype(BF16)
     return (hidden_out, k_cache, v_cache)
 

time: 215 us -> 217 us (level)
  other arithmetic: 6.07 us -> 8.65 us
    all_gather x1 -> x0, blocking collectives: 16.7 us -> none  [body(): pair = lax.all_gather(local, 'zh', axis=0, tiled=False)]
    all_to_all x0 -> x1, blocking collectives: none -> 15.7 us  [body(): stats = lax.all_to_all(stats, TP, 0, 0, tiled=True)]
    all_gather x2, waiting for transfers between devices: 0.02 us -> 12.8 us  [the longest x1 12.8 us: body(): lax.all_gather(jnp.stack([w_local, got[:3]]), ('ya', 'yb', 'yc'), axis=0,...]
    ppermute x24 -> x25, waiting for transfers between devices: 37.8 us -> 29.6 us  [permute(): return lax.ppermute(value, axes, pairs)]
    ppermute x24 -> x25, starting transfers between devices: 84.3 us -> 90.8 us  [permute(): return lax.ppermute(value, axes, pairs)]
    all_to_all x2 -> x1, starting transfers between devices: 20.6 us -> 15.5 us  [body(): sums = lax.all_to_all(sums, TP, 0, 0, tiled=True)]
    all_to_all x2 -> x1, waiting for transfers between devices: 12.6 us -> 8.45 us  [body(): sums = lax.all_to_all(sums, TP, 0, 0, tiled=True)]
  transfers between devices with their start and end apart: 29 -> 29, of which waited for: 16 -> 15; matrix products, arithmetic and copies ran while one was open for 2% -> 3% of each run, Pallas kernels for 4% -> 1%
where the time goes in v6:
time: 217 us; the launch traced here: 215 us
  starting transfers between devices  112 us (52%)
  waiting for transfers between devices  50.9 us (23%)
  blocking collectives  15.7 us (7%)
  between operations  14.5 us (7%)
  Pallas kernels  9.18 us (4%)
  other arithmetic  8.65 us (4%)
  local copies, waits for them, and re-layouts  3.41 us (2%)
    ppermute x25, starting transfers between devices, permute(): return lax.ppermute(value, axes, pairs)  90.8 us
    ppermute x25, waiting for transfers between devices, permute(): return lax.ppermute(value, axes, pairs)  29.6 us
    all_to_all x1, blocking collectives, body(): stats = lax.all_to_all(stats, TP, 0, 0, tiled=True)  15.7 us
    all_to_all x1, starting transfers between devices, body(): sums = lax.all_to_all(sums, TP, 0, 0, tiled=True)  15.5 us
    all_gather x1, waiting for transfers between devices, body(): lax.all_gather(jnp.stack([w_local, got[:3]]), ('ya', 'yb', 'yc'), axis=0,...  12.8 us
    pallas_call x6, Pallas kernels, call(): pl.pallas_call(kernel, out_shape=out_shape, in_specs=specs, out_specs=jax...  9.18 us
    all_to_all x1, waiting for transfers between devices, body(): sums = lax.all_to_all(sums, TP, 0, 0, tiled=True)  8.45 us
    all_to_all x1, starting transfers between devices, body(): keys = lax.all_to_all(kv_message, ('ya', 'yb'), 0, 0, tiled=True)  5.58 us
  transfers between devices with their start and end apart: 29, of which 15 were waited for; matrix products, arithmetic and copies ran while one was open for 3% of the time, Pallas kernels for 1%

profile of v6, /device:TPU:1, one launch (start us, length us, event | category | flops | bytes accessed | tf_op | source)
XLA Modules:
  0.0 215.4 jit_solution(11769271090724368056)
XLA Ops:
  8.3 11.5 %collective-permute-start = (bf16[4,320,128]{2,1,0:T(8,128)(2,1)S(1)}, bf16[4,320,128]{2,1,0:T(8,128)(2,1)S(1)}, u32[]{:S(2)}, u32[]{:S(2)}) collective-permute-start(bf16[4,320,128]{2,1,0:T(8,128)(2,1)S(1)} %pad_maximum_fusion.1), channel_id=1, source_target_pairs={{0,32},{32,0},{1,33},{33,1},{2,34},{34,2},{3,35},{35,3},{4,36},{36... | collective-permute-start | bytes 983048 | tf_op jit(solution)/shard_map/ppermute | solution.py:34
  28.8 15.5 %all-to-all-start = ((f32[32,8,128]{2,1,0:T(8,128)}), f32[32,8,128]{2,1,0:T(8,128)S(1)}, u32[]{:S(2)}, u32[]{:S(2)}) async-start(f32[32,8,128]{2,1,0:T(8,128)} %broadcast_in_dim.12), calls=%async_computation | async-start | bytes 262144 | tf_op jit(solution)/shard_map/all_to_all | solution.py:240
  44.4 8.4 %all-to-all-done = f32[32,8,128]{2,1,0:T(8,128)S(1)} async-done(((f32[32,8,128]{2,1,0:T(8,128)}), f32[32,8,128]{2,1,0:T(8,128)S(1)}, u32[]{:S(2)}, u32[]{:S(2)}) %all-to-all-start) | async-done | bytes 131104 | tf_op jit(solution)/shard_map/all_to_all | solution.py:240
  55.2 2.9 %collective-permute-start.2 = (bf16[160,256]{1,0:T(8,128)(2,1)S(1)}, bf16[160,256]{1,0:T(8,128)(2,1)S(1)}, u32[]{:S(2)}, u32[]{:S(2)}) collective-permute-start(bf16[160,256]{1,0:T(8,128)(2,1)S(1)} %fusion.7), channel_id=1, source_target_pairs={{0,16},{8,24},{16,0},{24,8},{1,17},{9,25},{17,1},{25,9},{2,18},{10... | collective-permute-start | bytes 245768 | tf_op jit(solution)/shard_map/ppermute | solution.py:34
  58.2 3.8 %collective-permute-start.3 = (bf16[160,256]{1,0:T(8,128)(2,1)S(1)}, bf16[160,256]{1,0:T(8,128)(2,1)S(1)}, u32[]{:S(2)}, u32[]{:S(2)}) collective-permute-start(bf16[160,256]{1,0:T(8,128)(2,1)S(1)} %fusion.7), channel_id=1, source_target_pairs={{0,24},{8,0},{16,8},{24,16},{1,25},{9,1},{17,9},{25,17},{2,26},{10... | collective-permute-start | bytes 245768 | tf_op jit(solution)/shard_map/ppermute | solution.py:34
  69.1 3.9 %collective-permute-start.7 = (bf16[4,160,256]{2,1,0:T(8,128)(2,1)S(1)}, bf16[4,160,256]{2,1,0:T(8,128)(2,1)S(1)}, u32[]{:S(2)}, u32[]{:S(2)}) collective-permute-start(bf16[4,160,256]{2,1,0:T(8,128)(2,1)S(1)} %pad_maximum_fusion.2.refs_0_), channel_id=1, source_target_pairs={{0,6},{2,0},{4,2},{6,4},{1,7},{3,1},{5,3},{7,5},{8,14},{10,8},{12,... | collective-permute-start | bytes 983048 | tf_op jit(solution)/shard_map/ppermute | solution.py:34
  78.7 3.9 %collective-permute-start.10 = (bf16[4,160,256]{2,1,0:T(8,128)(2,1)S(1)}, bf16[4,160,256]{2,1,0:T(8,128)(2,1)S(1)}, u32[]{:S(2)}, u32[]{:S(2)}) collective-permute-start(bf16[4,160,256]{2,1,0:T(8,128)(2,1)S(1)} %collective-permute-done.5.refs_2_), channel_id=1, source_target_pairs={{0,1},{1,0},{2,3},{3,2},{4,5},{5,4},{6,7},{7,6},{8,9},{9,8},{10,11... | collective-permute-start | bytes 983048 | tf_op jit(solution)/shard_map/ppermute | solution.py:34
  84.5 3.0 %collective-permute-start.11 = (bf16[4,160,256]{2,1,0:T(8,128)(2,1)S(1)}, bf16[4,160,256]{2,1,0:T(8,128)(2,1)S(1)}, u32[]{:S(2)}, u32[]{:S(2)}) collective-permute-start(bf16[4,160,256]{2,1,0:T(8,128)(2,1)S(1)} %collective-permute-done.7.refs_3_), channel_id=1, source_target_pairs={{0,1},{1,0},{2,3},{3,2},{4,5},{5,4},{6,7},{7,6},{8,9},{9,8},{10,11... | collective-permute-start | bytes 983048 | tf_op jit(solution)/shard_map/ppermute | solution.py:34
  91.0 12.8 %all-gather.5.cloned.1.call-done = bf16[16,3,320,128]{3,2,1,0:T(8,128)(2,1)} async-done(((bf16[2,3,320,128]{3,2,1,0:T(8,128)(2,1)}), bf16[16,3,320,128]{3,2,1,0:T(8,128)(2,1)}) %all-gather.5.cloned.1.call-update) | async-done | bytes 3932176 | tf_op jit(solution)/shard_map/all_gather | solution.py:241
  103.8 4.0 %project.1 = (f32[128,256]{1,0:T(8,128)S(1)}, f32[2,128,256]{2,1,0:T(8,128)S(1)}, f32[32,8,128]{2,1,0:T(8,128)S(1)}) custom-call(s32[4]{0:T(128)S(1)} %pad_add_fusion.at, bf16[4,160,256]{2,1,0:T(8,128)(2,1)S(1)} %pad_maximum_fusion.2.refs_0_, bf16[4,160,256]{2,1,0:T(8,128)(2,1)S(1)} %collective-permute-done.4.refs_1_, ...), custom_call_target="tpu_custom_call" | custom-call | flops 1006632960 | bytes 6291456 | tf_op jit(solution)/shard_map/project/pallas_call | solution.py:46
  107.9 15.7 %all_to_all.15.got = f32[32,8,128]{2,1,0:T(8,128)S(1)} all-to-all(f32[32,8,128]{2,1,0:T(8,128)S(1)} %get-tuple-element.39), channel_id=1, replica_groups=mesh['ya'=2,'yb'=2,'yc'=2,'zh'=2,'zl'=4,'xh'=2,'xl'=2,'c'=2] {'zl','xh',..., dimensions={0} | all-to-all | bytes 262144 | tf_op jit(solution)/shard_map/all_to_all | solution.py:272
  124.9 5.6 %all-to-all-start.2 = ((bf16[4,272,256]{2,1,0:T(8,128)(2,1)}), bf16[4,272,256]{2,1,0:T(8,128)(2,1)S(1)}, u32[]{:S(2)}, u32[]{:S(2)}) async-start(bf16[4,272,256]{2,1,0:T(8,128)(2,1)} %get-tuple-element.48), calls=%async_computation.2 | async-start | bytes 1114112 | tf_op jit(solution)/shard_map/all_to_all | solution.py:286
  130.5 6.9 %collective-permute-start.12 = (bf16[144,256]{1,0:T(8,128)(2,1)S(1)}, bf16[144,256]{1,0:T(8,128)(2,1)S(1)}, u32[]{:S(2)}, u32[]{:S(2)}) collective-permute-start(bf16[144,256]{1,0:T(8,128)(2,1)S(1)} %get-tuple-element.47.q), channel_id=1, source_target_pairs={{0,32},{32,0},{64,96},{96,64},{1,33},{33,1},{65,97},{97,65},{2,34}... | collective-permute-start | bytes 221192 | tf_op jit(solution)/shard_map/ppermute | solution.py:34
  139.9 2.9 %collective-permute-start.14 = (bf16[144,256]{1,0:T(8,128)(2,1)S(1)}, bf16[144,256]{1,0:T(8,128)(2,1)S(1)}, u32[]{:S(2)}, u32[]{:S(2)}) collective-permute-start(bf16[144,256]{1,0:T(8,128)(2,1)S(1)} %get-tuple-element.47.q), channel_id=1, source_target_pairs={{0,64},{32,96},{64,0},{96,32},{1,65},{33,97},{65,1},{97,33},{2,66}... | collective-permute-start | bytes 221192 | tf_op jit(solution)/shard_map/ppermute | solution.py:34
  142.8 9.7 %collective-permute-done.13.q2 = bf16[144,256]{1,0:T(8,128)(2,1)S(1)} collective-permute-done((bf16[144,256]{1,0:T(8,128)(2,1)S(1)}, bf16[144,256]{1,0:T(8,128)(2,1)S(1)}, u32[]{:S(2)}, u32[]{:S(2)}) %collective-permute-start.13) | collective-permute-done | bytes 73760 | tf_op jit(solution)/shard_map/ppermute | solution.py:34
  154.5 5.6 %collective-permute-start.15 = (bf16[144,256]{1,0:T(8,128)(2,1)S(1)}, bf16[144,256]{1,0:T(8,128)(2,1)S(1)}, u32[]{:S(2)}, u32[]{:S(2)}) collective-permute-start(bf16[144,256]{1,0:T(8,128)(2,1)S(1)} %get-tuple-element.51), channel_id=1, source_target_pairs={{0,32},{32,0},{64,96},{96,64},{1,33},{33,1},{65,97},{97,65},{2,34}... | collective-permute-start | bytes 221192 | tf_op jit(solution)/shard_map/ppermute | solution.py:34
  160.0 3.3 %collective-permute-start.16 = (bf16[144,256]{1,0:T(8,128)(2,1)S(1)}, bf16[144,256]{1,0:T(8,128)(2,1)S(1)}, u32[]{:S(2)}, u32[]{:S(2)}) collective-permute-start(bf16[144,256]{1,0:T(8,128)(2,1)S(1)} %get-tuple-element.52), channel_id=1, source_target_pairs={{0,96},{32,64},{64,32},{96,0},{1,97},{33,65},{65,33},{97,1},{2,98}... | collective-permute-start | bytes 221192 | tf_op jit(solution)/shard_map/ppermute | solution.py:34
  163.4 3.4 %collective-permute-start.17 = (bf16[144,256]{1,0:T(8,128)(2,1)S(1)}, bf16[144,256]{1,0:T(8,128)(2,1)S(1)}, u32[]{:S(2)}, u32[]{:S(2)}) collective-permute-start(bf16[144,256]{1,0:T(8,128)(2,1)S(1)} %get-tuple-element.53), channel_id=1, source_target_pairs={{0,64},{32,96},{64,0},{96,32},{1,65},{33,97},{65,1},{97,33},{2,66}... | collective-permute-start | bytes 221192 | tf_op jit(solution)/shard_map/ppermute | solution.py:34
  166.8 4.0 %collective-permute-done.16.refs_1_ = bf16[144,256]{1,0:T(8,128)(2,1)S(1)} collective-permute-done((bf16[144,256]{1,0:T(8,128)(2,1)S(1)}, bf16[144,256]{1,0:T(8,128)(2,1)S(1)}, u32[]{:S(2)}, u32[]{:S(2)}) %collective-permute-start.16) | collective-permute-done | bytes 73760 | tf_op jit(solution)/shard_map/ppermute | solution.py:34
  173.5 3.1 %collective-permute-start.19 = (bf16[128,256]{1,0:T(8,128)(2,1)S(1)}, bf16[128,256]{1,0:T(8,128)(2,1)S(1)}, u32[]{:S(2)}, u32[]{:S(2)}) collective-permute-start(bf16[128,256]{1,0:T(8,128)(2,1)S(1)} %merge.1), channel_id=1, source_target_pairs={{0,16},{8,24},{16,0},{24,8},{1,17},{9,25},{17,1},{25,9},{2,18},{10... | collective-permute-start | bytes 196616 | tf_op jit(solution)/shard_map/ppermute | solution.py:34
  176.6 3.2 %collective-permute-start.20 = (bf16[128,256]{1,0:T(8,128)(2,1)S(1)}, bf16[128,256]{1,0:T(8,128)(2,1)S(1)}, u32[]{:S(2)}, u32[]{:S(2)}) collective-permute-start(bf16[128,256]{1,0:T(8,128)(2,1)S(1)} %merge.1), channel_id=1, source_target_pairs={{0,24},{8,0},{16,8},{24,16},{1,25},{9,1},{17,9},{25,17},{2,26},{10... | collective-permute-start | bytes 196616 | tf_op jit(solution)/shard_map/ppermute | solution.py:34
  187.3 4.1 %collective-permute-start.22 = (bf16[320,256]{1,0:T(8,128)(2,1)S(1)}, bf16[320,256]{1,0:T(8,128)(2,1)S(1)}, u32[]{:S(2)}, u32[]{:S(2)}) collective-permute-start(bf16[320,256]{1,0:T(8,128)(2,1)S(1)} %get-tuple-element.57), channel_id=1, source_target_pairs={{0,4},{2,6},{4,0},{6,2},{1,5},{3,7},{5,1},{7,3},{8,12},{10,14},{12... | collective-permute-start | bytes 491528 | tf_op jit(solution)/shard_map/ppermute | solution.py:34
  194.9 2.9 %collective-permute-done.23.refs_2_ = bf16[320,256]{1,0:T(8,128)(2,1)S(1)} collective-permute-done((bf16[320,256]{1,0:T(8,128)(2,1)S(1)}, bf16[320,256]{1,0:T(8,128)(2,1)S(1)}, u32[]{:S(2)}, u32[]{:S(2)}) %collective-permute-start.23) | collective-permute-done | bytes 163872 | tf_op jit(solution)/shard_map/ppermute | solution.py:34
  198.4 7.5 %collective-permute-start.24 = (f32[160,256]{1,0:T(8,128)S(1)}, f32[160,256]{1,0:T(8,128)S(1)}, u32[]{:S(2)}, u32[]{:S(2)}) collective-permute-start(f32[160,256]{1,0:T(8,128)S(1)} %get-tuple-element.60), channel_id=1, source_target_pairs={{0,1},{1,0},{2,3},{3,2},{4,5},{5,4},{6,7},{7,6},{8,9},{9,8},{10,11... | collective-permute-start | bytes 491528 | tf_op jit(solution)/shard_map/ppermute | solution.py:34
  (93 shorter events, 53.4 us)
Async XLA Ops:
  7.2 96.7 %all-gather.5.cloned.1.call-start = ((), (), s32[]{:S(2)}) async-start(), calls=%async_computation.3 | async-start | bytes 4423680 | tf_op jit(solution)/shard_map/all_gather | solution.py:241
  8.3 18.0 %collective-permute-start = (bf16[4,320,128]{2,1,0:T(8,128)(2,1)S(1)}, bf16[4,320,128]{2,1,0:T(8,128)(2,1)S(1)}, u32[]{:S(2)}, u32[]{:S(2)}) collective-permute-start(bf16[4,320,128]{2,1,0:T(8,128)(2,1)S(1)} %pad_maximum_fusion.1), channel_id=1, source_target_pairs={{0,32},{32,0},{1,33},{33,1},{2,34},{34,2},{3,35},{35,3},{4,36},{36... | collective-permute-start | bytes 983048 | tf_op jit(solution)/shard_map/ppermute | solution.py:34
  28.8 24.0 %all-to-all-start = ((f32[32,8,128]{2,1,0:T(8,128)}), f32[32,8,128]{2,1,0:T(8,128)S(1)}, u32[]{:S(2)}, u32[]{:S(2)}) async-start(f32[32,8,128]{2,1,0:T(8,128)} %broadcast_in_dim.12), calls=%async_computation | async-start | bytes 262144 | tf_op jit(solution)/shard_map/all_to_all | solution.py:240
  44.3 138.4 %all-gather.7.cloned.1.call-start = ((), (), s32[]{:S(2)}) async-start(), calls=%async_computation.4 | async-start | bytes 1474560 | tf_op jit(solution)/shard_map/all_gather | solution.py:274
  53.0 9.0 %collective-permute-start.1 = (bf16[160,256]{1,0:T(8,128)(2,1)S(1)}, bf16[160,256]{1,0:T(8,128)(2,1)S(1)}, u32[]{:S(2)}, u32[]{:S(2)}) collective-permute-start(bf16[160,256]{1,0:T(8,128)(2,1)S(1)} %fusion.7), channel_id=1, source_target_pairs={{0,8},{8,16},{16,24},{24,0},{1,9},{9,17},{17,25},{25,1},{2,10},{10... | collective-permute-start | bytes 245768 | tf_op jit(solution)/shard_map/ppermute | solution.py:34
  55.2 9.3 %collective-permute-start.2 = (bf16[160,256]{1,0:T(8,128)(2,1)S(1)}, bf16[160,256]{1,0:T(8,128)(2,1)S(1)}, u32[]{:S(2)}, u32[]{:S(2)}) collective-permute-start(bf16[160,256]{1,0:T(8,128)(2,1)S(1)} %fusion.7), channel_id=1, source_target_pairs={{0,16},{8,24},{16,0},{24,8},{1,17},{9,25},{17,1},{25,9},{2,18},{10... | collective-permute-start | bytes 245768 | tf_op jit(solution)/shard_map/ppermute | solution.py:34
  58.2 8.2 %collective-permute-start.3 = (bf16[160,256]{1,0:T(8,128)(2,1)S(1)}, bf16[160,256]{1,0:T(8,128)(2,1)S(1)}, u32[]{:S(2)}, u32[]{:S(2)}) collective-permute-start(bf16[160,256]{1,0:T(8,128)(2,1)S(1)} %fusion.7), channel_id=1, source_target_pairs={{0,24},{8,0},{16,8},{24,16},{1,25},{9,1},{17,9},{25,17},{2,26},{10... | collective-permute-start | bytes 245768 | tf_op jit(solution)/shard_map/ppermute | solution.py:34
  66.4 12.3 %collective-permute-start.5 = (bf16[4,160,256]{2,1,0:T(8,128)(2,1)S(1)}, bf16[4,160,256]{2,1,0:T(8,128)(2,1)S(1)}, u32[]{:S(2)}, u32[]{:S(2)}) collective-permute-start(bf16[4,160,256]{2,1,0:T(8,128)(2,1)S(1)} %pad_maximum_fusion.2.refs_0_), channel_id=1, source_target_pairs={{0,4},{2,6},{4,0},{6,2},{1,5},{3,7},{5,1},{7,3},{8,12},{10,14},{12... | collective-permute-start | bytes 983048 | tf_op jit(solution)/shard_map/ppermute | solution.py:34
  69.1 15.4 %collective-permute-start.7 = (bf16[4,160,256]{2,1,0:T(8,128)(2,1)S(1)}, bf16[4,160,256]{2,1,0:T(8,128)(2,1)S(1)}, u32[]{:S(2)}, u32[]{:S(2)}) collective-permute-start(bf16[4,160,256]{2,1,0:T(8,128)(2,1)S(1)} %pad_maximum_fusion.2.refs_0_), channel_id=1, source_target_pairs={{0,6},{2,0},{4,2},{6,4},{1,7},{3,1},{5,3},{7,5},{8,14},{10,8},{12,... | collective-permute-start | bytes 983048 | tf_op jit(solution)/shard_map/ppermute | solution.py:34
  73.0 14.5 %collective-permute-start.4 = (bf16[4,160,256]{2,1,0:T(8,128)(2,1)S(1)}, bf16[4,160,256]{2,1,0:T(8,128)(2,1)S(1)}, u32[]{:S(2)}, u32[]{:S(2)}) collective-permute-start(bf16[4,160,256]{2,1,0:T(8,128)(2,1)S(1)} %pad_maximum_fusion.2.refs_0_), channel_id=1, source_target_pairs={{0,2},{2,4},{4,6},{6,0},{1,3},{3,5},{5,7},{7,1},{8,10},{10,12},{12... | collective-permute-start | bytes 983048 | tf_op jit(solution)/shard_map/ppermute | solution.py:34
  75.6 14.0 %collective-permute-start.8 = (bf16[4,160,256]{2,1,0:T(8,128)(2,1)S(1)}, bf16[4,160,256]{2,1,0:T(8,128)(2,1)S(1)}, u32[]{:S(2)}, u32[]{:S(2)}) collective-permute-start(bf16[4,160,256]{2,1,0:T(8,128)(2,1)S(1)} %pad_maximum_fusion.2.refs_0_), channel_id=1, source_target_pairs={{0,1},{1,0},{2,3},{3,2},{4,5},{5,4},{6,7},{7,6},{8,9},{9,8},{10,11... | collective-permute-start | bytes 983048 | tf_op jit(solution)/shard_map/ppermute | solution.py:34
  78.7 10.8 %collective-permute-start.10 = (bf16[4,160,256]{2,1,0:T(8,128)(2,1)S(1)}, bf16[4,160,256]{2,1,0:T(8,128)(2,1)S(1)}, u32[]{:S(2)}, u32[]{:S(2)}) collective-permute-start(bf16[4,160,256]{2,1,0:T(8,128)(2,1)S(1)} %collective-permute-done.5.refs_2_), channel_id=1, source_target_pairs={{0,1},{1,0},{2,3},{3,2},{4,5},{5,4},{6,7},{7,6},{8,9},{9,8},{10,11... | collective-permute-start | bytes 983048 | tf_op jit(solution)/shard_map/ppermute | solution.py:34
  124.9 27.6 %all-to-all-start.2 = ((bf16[4,272,256]{2,1,0:T(8,128)(2,1)}), bf16[4,272,256]{2,1,0:T(8,128)(2,1)S(1)}, u32[]{:S(2)}, u32[]{:S(2)}) async-start(bf16[4,272,256]{2,1,0:T(8,128)(2,1)} %get-tuple-element.48), calls=%async_computation.2 | async-start | bytes 1114112 | tf_op jit(solution)/shard_map/all_to_all | solution.py:286
  130.5 12.3 %collective-permute-start.12 = (bf16[144,256]{1,0:T(8,128)(2,1)S(1)}, bf16[144,256]{1,0:T(8,128)(2,1)S(1)}, u32[]{:S(2)}, u32[]{:S(2)}) collective-permute-start(bf16[144,256]{1,0:T(8,128)(2,1)S(1)} %get-tuple-element.47.q), channel_id=1, source_target_pairs={{0,32},{32,0},{64,96},{96,64},{1,33},{33,1},{65,97},{97,65},{2,34}... | collective-permute-start | bytes 221192 | tf_op jit(solution)/shard_map/ppermute | solution.py:34
  137.4 15.1 %collective-permute-start.13 = (bf16[144,256]{1,0:T(8,128)(2,1)S(1)}, bf16[144,256]{1,0:T(8,128)(2,1)S(1)}, u32[]{:S(2)}, u32[]{:S(2)}) collective-permute-start(bf16[144,256]{1,0:T(8,128)(2,1)S(1)} %get-tuple-element.47.q), channel_id=1, source_target_pairs={{0,96},{32,64},{64,32},{96,0},{1,97},{33,65},{65,33},{97,1},{2,98}... | collective-permute-start | bytes 221192 | tf_op jit(solution)/shard_map/ppermute | solution.py:34
  139.9 12.6 %collective-permute-start.14 = (bf16[144,256]{1,0:T(8,128)(2,1)S(1)}, bf16[144,256]{1,0:T(8,128)(2,1)S(1)}, u32[]{:S(2)}, u32[]{:S(2)}) collective-permute-start(bf16[144,256]{1,0:T(8,128)(2,1)S(1)} %get-tuple-element.47.q), channel_id=1, source_target_pairs={{0,64},{32,96},{64,0},{96,32},{1,65},{33,97},{65,1},{97,33},{2,66}... | collective-permute-start | bytes 221192 | tf_op jit(solution)/shard_map/ppermute | solution.py:34
  154.5 12.3 %collective-permute-start.15 = (bf16[144,256]{1,0:T(8,128)(2,1)S(1)}, bf16[144,256]{1,0:T(8,128)(2,1)S(1)}, u32[]{:S(2)}, u32[]{:S(2)}) collective-permute-start(bf16[144,256]{1,0:T(8,128)(2,1)S(1)} %get-tuple-element.51), channel_id=1, source_target_pairs={{0,32},{32,0},{64,96},{96,64},{1,33},{33,1},{65,97},{97,65},{2,34}... | collective-permute-start | bytes 221192 | tf_op jit(solution)/shard_map/ppermute | solution.py:34
  160.0 10.7 %collective-permute-start.16 = (bf16[144,256]{1,0:T(8,128)(2,1)S(1)}, bf16[144,256]{1,0:T(8,128)(2,1)S(1)}, u32[]{:S(2)}, u32[]{:S(2)}) collective-permute-start(bf16[144,256]{1,0:T(8,128)(2,1)S(1)} %get-tuple-element.52), channel_id=1, source_target_pairs={{0,96},{32,64},{64,32},{96,0},{1,97},{33,65},{65,33},{97,1},{2,98}... | collective-permute-start | bytes 221192 | tf_op jit(solution)/shard_map/ppermute | solution.py:34
  163.4 7.4 %collective-permute-start.17 = (bf16[144,256]{1,0:T(8,128)(2,1)S(1)}, bf16[144,256]{1,0:T(8,128)(2,1)S(1)}, u32[]{:S(2)}, u32[]{:S(2)}) collective-permute-start(bf16[144,256]{1,0:T(8,128)(2,1)S(1)} %get-tuple-element.53), channel_id=1, source_target_pairs={{0,64},{32,96},{64,0},{96,32},{1,65},{33,97},{65,1},{97,33},{2,66}... | collective-permute-start | bytes 221192 | tf_op jit(solution)/shard_map/ppermute | solution.py:34
  170.9 9.0 %collective-permute-start.18 = (bf16[128,256]{1,0:T(8,128)(2,1)S(1)}, bf16[128,256]{1,0:T(8,128)(2,1)S(1)}, u32[]{:S(2)}, u32[]{:S(2)}) collective-permute-start(bf16[128,256]{1,0:T(8,128)(2,1)S(1)} %merge.1), channel_id=1, source_target_pairs={{0,8},{8,16},{16,24},{24,0},{1,9},{9,17},{17,25},{25,1},{2,10},{10... | collective-permute-start | bytes 196616 | tf_op jit(solution)/shard_map/ppermute | solution.py:34
  173.5 6.6 %collective-permute-start.19 = (bf16[128,256]{1,0:T(8,128)(2,1)S(1)}, bf16[128,256]{1,0:T(8,128)(2,1)S(1)}, u32[]{:S(2)}, u32[]{:S(2)}) collective-permute-start(bf16[128,256]{1,0:T(8,128)(2,1)S(1)} %merge.1), channel_id=1, source_target_pairs={{0,16},{8,24},{16,0},{24,8},{1,17},{9,25},{17,1},{25,9},{2,18},{10... | collective-permute-start | bytes 196616 | tf_op jit(solution)/shard_map/ppermute | solution.py:34
  185.4 8.4 %collective-permute-start.21 = (bf16[320,256]{1,0:T(8,128)(2,1)S(1)}, bf16[320,256]{1,0:T(8,128)(2,1)S(1)}, u32[]{:S(2)}, u32[]{:S(2)}) collective-permute-start(bf16[320,256]{1,0:T(8,128)(2,1)S(1)} %get-tuple-element.56), channel_id=1, source_target_pairs={{0,2},{2,4},{4,6},{6,0},{1,3},{3,5},{5,7},{7,1},{8,10},{10,12},{12... | collective-permute-start | bytes 491528 | tf_op jit(solution)/shard_map/ppermute | solution.py:34
  187.3 7.6 %collective-permute-start.22 = (bf16[320,256]{1,0:T(8,128)(2,1)S(1)}, bf16[320,256]{1,0:T(8,128)(2,1)S(1)}, u32[]{:S(2)}, u32[]{:S(2)}) collective-permute-start(bf16[320,256]{1,0:T(8,128)(2,1)S(1)} %get-tuple-element.57), channel_id=1, source_target_pairs={{0,4},{2,6},{4,0},{6,2},{1,5},{3,7},{5,1},{7,3},{8,12},{10,14},{12... | collective-permute-start | bytes 491528 | tf_op jit(solution)/shard_map/ppermute | solution.py:34
  198.4 8.5 %collective-permute-start.24 = (f32[160,256]{1,0:T(8,128)S(1)}, f32[160,256]{1,0:T(8,128)S(1)}, u32[]{:S(2)}, u32[]{:S(2)}) collective-permute-start(f32[160,256]{1,0:T(8,128)S(1)} %get-tuple-element.60), channel_id=1, source_target_pairs={{0,1},{1,0},{2,3},{3,2},{4,5},{5,4},{6,7},{7,6},{8,9},{9,8},{10,11... | collective-permute-start | bytes 491528 | tf_op jit(solution)/shard_map/ppermute | solution.py:34
  (12 other events, 335.6 us)
Sparse Core Ops, SparseCore 0:
  28.9 74.8 all-gather.4
  123.7 42.7 all-gather.6

commit v7 on v6

v7 whole, which is shorter than its diff:
```python
import functools
import itertools
import math

import jax
import jax.numpy as jnp
import numpy as np
from jax import lax
from jax.experimental import pallas as pl
from jax.experimental.pallas import tpu as pltpu
from jax.sharding import Mesh
from jax.sharding import PartitionSpec as P

HEAD_DIM = 128
EPSILON = 1e-06
NEG_FILL = -1e30
LOG2E = 1.4426950408889634

SEQ = ("ya", "yb", "yc", "zh")
TP = ("zl", "xh", "xl", "c")
SIZES = {"ya": 2, "yb": 2, "yc": 2, "zh": 2, "zl": 4, "xh": 2, "xl": 2, "c": 2}

F32 = jnp.float32
BF16 = jnp.bfloat16
VMEM_LIMIT = 48 << 20


def permute(value, axes, move):
    sizes = [SIZES[a] for a in axes]
    pairs = []
    for at in itertools.product(*[range(n) for n in sizes]):
        to = move(*at)
        pairs.append((int(np.ravel_multi_index(at, sizes)), int(np.ravel_multi_index(to, sizes))))
    return lax.ppermute(value, axes, pairs)


def contract_first(lhs, rhs):
    return lax.dot_general(lhs, rhs, (((0,), (0,)), ((), ())), preferred_element_type=F32)


def call(kernel, out_shape, operands, scalars=None, scratch=(), name=None, cost=None):
    vmem = pl.BlockSpec(memory_space=pltpu.VMEM)
    smem = pl.BlockSpec(memory_space=pltpu.SMEM)
    specs = ([] if scalars is None else [smem]) + [vmem] * len(operands)
    args = ([] if scalars is None else [scalars]) + list(operands)
    return pl.pallas_call(
        kernel,
        out_shape=out_shape,
        in_specs=specs,
        out_specs=jax.tree.map(lambda _: vmem, out_shape),
        scratch_shapes=list(scratch),
        compiler_params=pltpu.CompilerParams(vmem_limit_bytes=VMEM_LIMIT),
        cost_estimate=cost,
        name=name,
    )(*args)


def shaped(shape, dtype):
    return jax.ShapeDtypeStruct(shape, dtype)


def project_kernel(at, mine, theirs, w, out_q, out_kv, stats):
    c = at[0]
    total = None
    for i, held in enumerate((mine, theirs)):
        core = lax.rem(c + i, 2)
        for x in range(4):
            for z in range(4):
                block, low = 2 * z + x // 2, x % 2
                weights = jnp.concatenate([w[block, low, p, core] for p in range(3)], axis=1)
                term = contract_first(weights, held[x, z])
                total = term if total is None else total + term
    query, key, value = total[:128], total[128:256], total[256:]
    out_q[...] = query
    out_kv[0] = key
    out_kv[1] = value
    rows = []
    for part in (query, key):
        row = jnp.sum(part * part, axis=0, keepdims=True)
        rows += [row[:, :128], row[:, 128:]]
    packed = jnp.concatenate(rows + [jnp.zeros((4, 128), F32)], axis=0)
    for t in range(stats.shape[0]):
        stats[t] = packed


def rotate_kernel(width, got, q, kv, cosine, sine, qg, kg, marks, q_out, k_cache, v_cache, message):
    totals = jnp.sum(got[...], axis=0)
    even = lax.rem(lax.broadcasted_iota(jnp.int32, (HEAD_DIM, 256), 0), 2) == 0
    cos, sin = cosine[...], sine[...]

    def rotated(value, gain, row):
        factor = jnp.concatenate([totals[row : row + 1], totals[row + 1 : row + 2]], axis=1)
        factor = lax.rsqrt(factor / width + EPSILON)
        normed = value * factor * gain
        after = pltpu.roll(normed, HEAD_DIM - 1, 0)
        before = pltpu.roll(normed, 1, 0)
        partner = jnp.where(even, -after, before)
        return normed * cos + partner * sin

    extra = marks[...].astype(BF16)
    q_low = rotated(q[...], qg[...], 0).astype(BF16)
    for t in range(q_out.shape[0]):
        q_out[t, :128] = q_low
        q_out[t, 128:144] = extra
    k_rot = rotated(kv[0], kg[...], 2)
    value = kv[1]
    k_low = k_rot.astype(BF16)
    v_low = value.astype(BF16)
    for t in range(message.shape[0]):
        message[t, :128] = k_low
        message[t, 128:256] = v_low
        message[t, 256:272] = extra
    k_cache[...] = k_rot.T.astype(BF16)
    v_cache[...] = value.T.astype(BF16)


def attend_kernel(q, keys, messages, held):
    count = keys.shape[0]
    scale = LOG2E / math.sqrt(HEAD_DIM)
    q_low = jnp.concatenate([q[d, :128] for d in range(4)], axis=1)
    seg_q = jnp.concatenate([q[d, 128:144] for d in range(4)], axis=1).astype(F32)[:1]
    top = None
    for b in range(count):
        seg_k = keys[b, 256:272].astype(F32).T[:, :1]
        scores = contract_first(keys[b, :128], q_low) * scale
        scores = jnp.where(seg_k == seg_q, scores, NEG_FILL)
        held[b] = scores
        here = jnp.max(scores, axis=0, keepdims=True)
        top = here if top is None else jnp.maximum(top, here)
    top = jnp.maximum(top, -1e20)
    total = jnp.zeros((1, 1024), F32)
    weighted = jnp.zeros((HEAD_DIM, 1024), F32)
    for b in range(count):
        weights = jnp.exp2(held[b] - top)
        total = total + jnp.sum(weights, axis=0, keepdims=True)
        weighted = weighted + jnp.dot(
            keys[b, 128:256], weights.astype(BF16), preferred_element_type=F32
        )
    some = total > 0.0
    safe = jnp.where(some, total, 1.0)
    out = weighted / safe
    lse = jnp.where(some, top + jnp.log2(safe), NEG_FILL)
    high = lse.astype(BF16)
    rest = lse - high.astype(F32)
    middle = rest.astype(BF16)
    low = (rest - middle.astype(F32)).astype(BF16)
    rows = jnp.concatenate(
        [high.astype(F32), middle.astype(F32), low.astype(F32), jnp.zeros((13, 1024), F32)], axis=0
    ).astype(BF16)
    for d in range(4):
        here = slice(256 * d, 256 * d + 256)
        messages[d, :128] = out[:, here].astype(BF16)
        messages[d, 128:144] = rows[:, here]


def merge_kernel(got, out):
    lses, parts = [], []
    for d in range(4):
        rows = got[d, 128:144].astype(F32)
        lses.append(rows[0:1] + rows[1:2] + rows[2:3])
        parts.append(got[d, :128].astype(F32))
    top = functools.reduce(jnp.maximum, lses)
    weights = [jnp.exp2(lse - top) for lse in lses]
    total = sum(weights[1:], weights[0])
    value = None
    for weight, part in zip(weights, parts, strict=True):
        term = part * (weight / total)
        value = term if value is None else value + term
    value = value.astype(BF16)
    for t in range(out.shape[0]):
        out[t] = value


def partial_kernel(heads, w, messages):
    for x in range(4):
        total = None
        for z in range(4):
            term = jnp.dot(w[2 * z + x // 2, x % 2], heads[z], preferred_element_type=F32)
            total = term if total is None else total + term
        messages[2 * x] = total[:160].astype(BF16)
        messages[2 * x + 1] = total[160:].astype(BF16)


def exchange(value, axes):
    return lax.all_to_all(value, axes, 0, 0, tiled=True)


def spread(value, axes):
    count = math.prod(SIZES[a] for a in axes)
    return exchange(jnp.broadcast_to(value, (count,) + value.shape), axes)


def body(hidden_in, seg_ids, positions, mod_table, w_qkv, q_gain, k_gain, w_out):
    tok_rows, feat_local = hidden_in.shape
    model_width = feat_local * 32
    heads_width = 4096
    at = jnp.stack([lax.axis_index("c")]).astype(jnp.int32)

    local = jnp.concatenate([jnp.transpose(w_qkv, (1, 0, 2)), w_out.T[None]], axis=0)
    pair = spread(local, ("zh",))

    x_t = hidden_in.T.astype(F32)
    sums = jnp.stack([jnp.sum(x_t, axis=0), jnp.sum(x_t * x_t, axis=0)]).reshape(4, 128)
    sums = jnp.concatenate([sums, jnp.zeros((4, 128), F32)], axis=0)
    sums = jnp.broadcast_to(sums, (32, 8, 128))
    segment_count = mod_table.shape[0]
    onehot = (seg_ids[None, :] == jnp.arange(segment_count, dtype=jnp.int32)[:, None]).astype(F32)
    modulation = lax.dot_general(
        mod_table.reshape(segment_count, 3 * feat_local),
        onehot,
        (((0,), (0,)), ((), ())),
        precision=lax.Precision.HIGHEST,
    ).reshape(3, feat_local, tok_rows)
    part_width = HEAD_DIM // 6
    widths = (HEAD_DIM - 4 * part_width, 2 * part_width, 2 * part_width)
    angles = []
    for axis_number in range(3):
        width = widths[axis_number]
        exponent = jnp.arange(0, width, 2, dtype=F32) / width
        frequency = jnp.repeat(1.0 / 10000.0**exponent, 2)
        angles.append(positions[axis_number].astype(F32)[None, :] * frequency[:, None])
    angle = jnp.concatenate(angles, axis=0)
    cosine, sine = jnp.cos(angle), jnp.sin(angle)
    marks = jnp.broadcast_to(seg_ids[None, :].astype(F32), (16, tok_rows))
    sums, pair, modulation, cosine, sine, marks = lax.optimization_barrier(
        (sums, pair, modulation, cosine, sine, marks)
    )
    sums = exchange(sums, TP)
    w_all = lax.all_gather(pair[:, :3], ("ya", "yb", "yc"), axis=0, tiled=False)
    w_all = w_all.reshape(8, 2, 3, 2, 160, 128)
    sums = jnp.sum(sums, axis=0)[:4].reshape(2, tok_rows)
    mean_value = sums[0:1] / model_width
    variance = sums[1:2] / model_width - mean_value * mean_value
    normed = (x_t - mean_value) * lax.rsqrt(variance + EPSILON)
    packet = (normed * (1.0 + modulation[1]) + modulation[0]).astype(BF16)

    held = spread(spread(packet, ("zl",)), ("xh", "xl"))
    theirs = permute(held, ("c",), lambda c: (1 - c,))

    query, key_value, stats = call(
        project_kernel,
        (shaped((128, 256), F32), shaped((2, 128, 256), F32), shaped((32, 8, 128), F32)),
        [held, theirs, w_all],
        scalars=at,
        name="project",
        cost=pl.CostEstimate(flops=2 * 256 * 5120 * 384, bytes_accessed=6 << 20, transcendentals=0),
    )
    wo_pair, stats = lax.optimization_barrier((pair[:, 3], stats))
    stats = exchange(stats, TP)
    wo_turned = permute(
        wo_pair, ("ya", "yb", "zl"), lambda ya, yb, zl: (zl >> 1, zl & 1, ya * 2 + yb)
    )
    stats, wo_turned = lax.optimization_barrier((stats, wo_turned))
    wo_all = lax.all_gather(wo_turned, ("ya", "yb", "yc"), axis=0, tiled=False)

    q_message, k_cache, v_cache, kv_message = call(
        functools.partial(rotate_kernel, heads_width),
        (
            shaped((4, 144, 256), BF16),
            shaped((256, 128), BF16),
            shaped((256, 128), BF16),
            shaped((4, 272, 256), BF16),
        ),
        [stats, query, key_value, cosine, sine, q_gain.reshape(128, 1), k_gain.reshape(128, 1), marks],
        name="rotate",
    )
    keys = exchange(kv_message, ("ya", "yb"))
    queries = exchange(q_message, ("yc", "zh"))
    o_messages = call(
        attend_kernel,
        shaped((4, 144, 256), BF16),
        [queries, keys],
        scratch=[pltpu.VMEM((4, 256, 1024), F32)],
        name="attend",
    )
    heads = call(
        merge_kernel, shaped((4, 128, 256), BF16), [exchange(o_messages, ("yc", "zh"))], name="merge"
    )
    partials = call(
        partial_kernel, shaped((8, 160, 256), BF16), [exchange(heads, ("zl",)), wo_all], name="partial"
    )
    mixed = jnp.sum(exchange(partials, ("xh", "xl", "c")).astype(F32), axis=0)
    hidden_out = (x_t + modulation[2] * mixed).T.astype(BF16)
    return (hidden_out, k_cache, v_cache)


def solution(mesh):
    split = Mesh(mesh.devices.reshape(tuple(SIZES.values())), tuple(SIZES))
    in_specs = (
        P(SEQ, TP),
        P(SEQ),
        P(None, SEQ),
        P(None, None, TP),
        P(SEQ, None, TP),
        P(TP),
        P(TP),
        P(TP, SEQ),
    )
    out_specs = (P(SEQ, TP), P(SEQ, TP), P(SEQ, TP))
    return jax.shard_map(body, mesh=split, in_specs=in_specs, out_specs=out_specs, check_vma=False)
```

time: 217 us -> 225 us (1.037)
  blocking collectives: 15.7 us -> 150 us
  starting transfers between devices: 112 us -> 22.7 us
  waiting for transfers between devices: 50.9 us -> 20.4 us
  other arithmetic: 8.65 us -> 3.54 us
    all_to_all x1 -> x8, blocking collectives: 15.7 us -> 150 us  [exchange(): return lax.all_to_all(value, axes, 0, 0, tiled=True)]
    ppermute x25 -> x2, starting transfers between devices: 90.8 us -> 4.61 us  [permute(): return lax.ppermute(value, axes, pairs)]
    ppermute x25 -> x2, waiting for transfers between devices: 29.6 us -> 1.7 us  [permute(): return lax.ppermute(value, axes, pairs)]
    all_gather x1, waiting for transfers between devices: 12.8 us -> 0.01 us  [body(): w_all = lax.all_gather(pair[:, :3], ('ya', 'yb', 'yc'), axis=0, tiled=False)]
    all_to_all x2, waiting for transfers between devices: 8.45 us -> 18.6 us  [exchange(): return lax.all_to_all(value, axes, 0, 0, tiled=True)]
    all_to_all x2, starting transfers between devices: 21.1 us -> 18.1 us  [exchange(): return lax.all_to_all(value, axes, 0, 0, tiled=True)]
    pallas_call x6 -> x5, Pallas kernels: 9.18 us -> 8.42 us  [call(): pl.pallas_call(kernel, out_shape=out_shape, in_specs=specs, out_specs=jax...]
  transfers between devices with their start and end apart: 29 -> 6, of which waited for: 15 -> 3; matrix products, arithmetic and copies ran while one was open for 3% -> 1% of each run, Pallas kernels for 1% -> 1%
where the time goes in v7:
time: 225 us; the launch traced here: 224 us
  blocking collectives  150 us (67%)
  starting transfers between devices  22.7 us (10%)
  waiting for transfers between devices  20.4 us (9%)
  between operations  14.3 us (6%)
  Pallas kernels  8.42 us (4%)
  local copies, waits for them, and re-layouts  4.94 us (2%)
  other arithmetic  3.54 us (2%)
    all_to_all x8, blocking collectives, exchange(): return lax.all_to_all(value, axes, 0, 0, tiled=True)  150 us
    all_to_all x2, waiting for transfers between devices, exchange(): return lax.all_to_all(value, axes, 0, 0, tiled=True)  18.6 us
    all_to_all x2, starting transfers between devices, exchange(): return lax.all_to_all(value, axes, 0, 0, tiled=True)  18.1 us
    pallas_call x5, Pallas kernels, call(): pl.pallas_call(kernel, out_shape=out_shape, in_specs=specs, out_specs=jax...  8.42 us
    ppermute x2, starting transfers between devices, permute(): return lax.ppermute(value, axes, pairs)  4.61 us
  transfers between devices with their start and end apart: 6, of which 3 were waited for; matrix products, arithmetic and copies ran while one was open for 1% of the time, Pallas kernels for 1%

profile of v7, /device:TPU:1, one launch (start us, length us, event | category | flops | bytes accessed | tf_op | source)
XLA Modules:
  0.0 224.3 jit_solution(5973174455192066627)
XLA Ops:
  7.2 1.0 pad_maximum_fusion
  8.3 0.9 broadcast_in_dim.38
  9.2 10.8 %all-to-all-start = ((bf16[2,4,320,128]{3,2,1,0:T(8,128)(2,1)}), bf16[2,4,320,128]{3,2,1,0:T(8,128)(2,1)S(1)}, u32[]{:S(2)}, u32[]{:S(2)}) async-start(bf16[2,4,320,128]{3,2,1,0:T(8,128)(2,1)} %broadcast_in_dim.38), calls=%async_computation | async-start | bytes 1310720 | tf_op jit(solution)/shard_map/all_to_all | solution.py:185
  21.8 10.8 %all-to-all-done = bf16[2,4,320,128]{3,2,1,0:T(8,128)(2,1)S(1)} async-done(((bf16[2,4,320,128]{3,2,1,0:T(8,128)(2,1)}), bf16[2,4,320,128]{3,2,1,0:T(8,128)(2,1)S(1)}, u32[]{:S(2)}, u32[]{:S(2)}) %all-to-all-start) | async-done | bytes 655392 | tf_op jit(solution)/shard_map/all_to_all | solution.py:185
  32.6 0.9 slice.44
  33.5 23.1 %all_to_all.50 = f32[32,8,128]{2,1,0:T(8,128)S(1)} all-to-all(f32[32,8,128]{2,1,0:T(8,128)S(1)} %broadcast_in_dim.36), channel_id=1, replica_groups=mesh['ya'=2,'yb'=2,'yc'=2,'zh'=2,'zl'=4,'xh'=2,'xl'=2,'c'=2] {'zl','xh',..., dimensions={0} | all-to-all | bytes 262144 | tf_op jit(solution)/shard_map/all_to_all | solution.py:185
  56.8 12.5 %all_to_all.51 = bf16[4,160,256]{2,1,0:T(8,128)(2,1)S(1)} all-to-all(bf16[4,160,256]{2,1,0:T(8,128)(2,1)S(1)} %broadcast_in_dim.42), channel_id=1, replica_groups=mesh['ya'=2,'yb'=2,'yc'=2,'zh'=2,'zl'=4,'xh'=2,'xl'=2,'c'=2] {'zl'}, dimensions={0} | all-to-all | bytes 655360 | tf_op jit(solution)/shard_map/all_to_all | solution.py:185
  69.4 19.3 %all_to_all.52.mine = bf16[4,4,160,256]{3,2,1,0:T(8,128)(2,1)S(1)} all-to-all(bf16[4,4,160,256]{3,2,1,0:T(8,128)(2,1)S(1)} %broadcast_in_dim.43), channel_id=1, replica_groups=mesh['ya'=2,'yb'=2,'yc'=2,'zh'=2,'zl'=4,'xh'=2,'xl'=2,'c'=2] {'xh','xl'}, dimensions={0} | all-to-all | bytes 2621440 | tf_op jit(solution)/shard_map/all_to_all | solution.py:185
  88.7 3.9 %collective-permute-start = (bf16[4,4,160,256]{3,2,1,0:T(8,128)(2,1)S(1)}, bf16[4,4,160,256]{3,2,1,0:T(8,128)(2,1)S(1)}, u32[]{:S(2)}, u32[]{:S(2)}) collective-permute-start(bf16[4,4,160,256]{3,2,1,0:T(8,128)(2,1)S(1)} %all_to_all.52.mine), channel_id=1, source_target_pairs={{0,1},{1,0},{2,3},{3,2},{4,5},{5,4},{6,7},{7,6},{8,9},{9,8},{10,11... | collective-permute-start | bytes 3932168 | tf_op jit(solution)/shard_map/ppermute | solution.py:34
  92.6 0.9 slice_bitcast_fusion
  93.6 1.7 collective-permute-done.theirs
  95.3 4.7 %project.1 = (f32[128,256]{1,0:T(8,128)S(1)}, f32[2,128,256]{2,1,0:T(8,128)S(1)}, f32[32,8,128]{2,1,0:T(8,128)}) custom-call(s32[1]{0:T(128)} %bitcast.13.at, bf16[4,4,160,256]{3,2,1,0:T(8,128)(2,1)S(1)} %all_to_all.52.mine, bf16[4,4,160,256]{3,2,1,0:T(8,128)(2,1)S(1)} %collective-permute-done.theirs, bf16[8,2,3,2,160,128]{5,4,3,2,1,0:T(8,128)(2,1)} %bitcast.65), custom_call_target="tpu_custom_call" | custom-call | flops 1006632960 | bytes 6291456 | tf_op jit(solution)/shard_map/project/pallas_call | solution.py:46
  99.9 7.3 %all-to-all-start.4 = ((f32[32,8,128]{2,1,0:T(8,128)}), f32[32,8,128]{2,1,0:T(8,128)S(1)}, u32[]{:S(2)}, u32[]{:S(2)}) async-start(f32[32,8,128]{2,1,0:T(8,128)} %get-tuple-element.24), calls=%async_computation.4 | async-start | bytes 262144 | tf_op jit(solution)/shard_map/all_to_all | solution.py:185
  108.0 7.8 %all-to-all-done.4.got = f32[32,8,128]{2,1,0:T(8,128)S(1)} async-done(((f32[32,8,128]{2,1,0:T(8,128)}), f32[32,8,128]{2,1,0:T(8,128)S(1)}, u32[]{:S(2)}, u32[]{:S(2)}) %all-to-all-start.4) | async-done | bytes 131104 | tf_op jit(solution)/shard_map/all_to_all | solution.py:185
  116.0 0.9 rotate.1
  116.9 16.4 %all_to_all.53.q = bf16[4,144,256]{2,1,0:T(8,128)(2,1)S(1)} all-to-all(bf16[4,144,256]{2,1,0:T(8,128)(2,1)S(1)} %get-tuple-element.32), channel_id=1, replica_groups=mesh['ya'=2,'yb'=2,'yc'=2,'zh'=2,'zl'=4,'xh'=2,'xl'=2,'c'=2] {'yc','zh'}, dimensions={0} | all-to-all | bytes 589824 | tf_op jit(solution)/shard_map/all_to_all | solution.py:185
  133.3 34.8 %all_to_all.54.keys = bf16[4,272,256]{2,1,0:T(8,128)(2,1)S(1)} all-to-all(bf16[4,272,256]{2,1,0:T(8,128)(2,1)S(1)} %get-tuple-element.33), channel_id=1, replica_groups=mesh['ya'=2,'yb'=2,'yc'=2,'zh'=2,'zl'=4,'xh'=2,'xl'=2,'c'=2] {'ya','yb'}, dimensions={0} | all-to-all | bytes 1114112 | tf_op jit(solution)/shard_map/all_to_all | solution.py:185
  168.2 2.0 attend.1
  170.1 12.4 %all_to_all.55.got = bf16[4,144,256]{2,1,0:T(8,128)(2,1)S(1)} all-to-all(bf16[4,144,256]{2,1,0:T(8,128)(2,1)S(1)} %attend.1), channel_id=1, replica_groups=mesh['ya'=2,'yb'=2,'yc'=2,'zh'=2,'zl'=4,'xh'=2,'xl'=2,'c'=2] {'yc','zh'}, dimensions={0} | all-to-all | bytes 589824 | tf_op jit(solution)/shard_map/all_to_all | solution.py:185
  182.7 12.6 %all_to_all.56.heads = bf16[4,128,256]{2,1,0:T(8,128)(2,1)S(1)} all-to-all(bf16[4,128,256]{2,1,0:T(8,128)(2,1)S(1)} %merge.1), channel_id=1, replica_groups=mesh['ya'=2,'yb'=2,'yc'=2,'zh'=2,'zl'=4,'xh'=2,'xl'=2,'c'=2] {'zl'}, dimensions={0} | all-to-all | bytes 524288 | tf_op jit(solution)/shard_map/all_to_all | solution.py:185
  195.3 1.3 copy-done
  196.6 0.8 partial.1
  197.4 18.4 %all_to_all.57 = bf16[8,160,256]{2,1,0:T(8,128)(2,1)S(1)} all-to-all(bf16[8,160,256]{2,1,0:T(8,128)(2,1)S(1)} %partial.1), channel_id=1, replica_groups=mesh['ya'=2,'yb'=2,'yc'=2,'zh'=2,'zl'=4,'xh'=2,'xl'=2,'c'=2] {'xh','xl',..., dimensions={0} | all-to-all | bytes 1310720 | tf_op jit(solution)/shard_map/all_to_all | solution.py:185
  215.9 1.6 fusion.11
  (58 shorter events, 3.1 us)
Async XLA Ops:
  7.2 12.9 %copy-start.3 = (bf16[256,160]{0,1:T(8,128)(2,1)S(1)}, bf16[256,160]{0,1:T(8,128)(2,1)}, u32[]{:S(2)}) copy-start(bf16[256,160]{0,1:T(8,128)(2,1)} %param.8) | copy-start | bytes 245764
  8.2 11.9 %copy-start.5 = (f32[4,3,160]{2,0,1:T(4,128)S(1)}, f32[4,3,160]{2,0,1:T(4,128)}, u32[]{:S(2)}) copy-start(f32[4,3,160]{2,0,1:T(4,128)} %param.11) | copy-start | bytes 23044
  8.2 12.0 %copy-start.7 = (s32[3,256]{1,0:T(4,128)S(1)}, s32[3,256]{1,0:T(4,128)}, u32[]{:S(2)}) copy-start(s32[3,256]{1,0:T(4,128)} %param.10) | copy-start | bytes 9220
  8.2 12.5 %copy-start.6 = (s32[256]{0:T(256)S(1)}, s32[256]{0:T(256)}, u32[]{:S(2)}) copy-start(s32[256]{0:T(256)} %param.9) | copy-start | bytes 3076
  9.2 23.4 %all-to-all-start = ((bf16[2,4,320,128]{3,2,1,0:T(8,128)(2,1)}), bf16[2,4,320,128]{3,2,1,0:T(8,128)(2,1)S(1)}, u32[]{:S(2)}, u32[]{:S(2)}) async-start(bf16[2,4,320,128]{3,2,1,0:T(8,128)(2,1)} %broadcast_in_dim.38), calls=%async_computation | async-start | bytes 1310720 | tf_op jit(solution)/shard_map/all_to_all | solution.py:185
  20.0 75.3 %all-gather.5.cloned.1.call-start = ((), (), s32[]{:S(2)}) async-start(), calls=%async_computation.10 | async-start | bytes 4423680 | tf_op jit(solution)/shard_map/all_gather | solution.py:229
  21.7 35.1 %copy-start.2 = (f32[256,480]{0,1:T(8,128)}, f32[256,480]{0,1:T(8,128)S(1)}, u32[]{:S(2)}) copy-start(f32[256,480]{0,1:T(8,128)S(1)} %fusion.12) | copy-start | bytes 1474564
  32.6 24.2 %copy-start.1 = (bf16[2,4,320,128]{3,2,1,0:T(8,128)(2,1)}, bf16[2,4,320,128]{3,2,1,0:T(8,128)(2,1)S(1)}, u32[]{:S(2)}) copy-start(bf16[2,4,320,128]{3,2,1,0:T(8,128)(2,1)S(1)} %all-to-all-done) | copy-start | bytes 1966084
  88.7 6.6 %collective-permute-start = (bf16[4,4,160,256]{3,2,1,0:T(8,128)(2,1)S(1)}, bf16[4,4,160,256]{3,2,1,0:T(8,128)(2,1)S(1)}, u32[]{:S(2)}, u32[]{:S(2)}) collective-permute-start(bf16[4,4,160,256]{3,2,1,0:T(8,128)(2,1)S(1)} %all_to_all.52.mine), channel_id=1, source_target_pairs={{0,1},{1,0},{2,3},{3,2},{4,5},{5,4},{6,7},{7,6},{8,9},{9,8},{10,11... | collective-permute-start | bytes 3932168 | tf_op jit(solution)/shard_map/ppermute | solution.py:34
  95.3 20.5 %copy-start.8 = (f32[128]{0:T(128)S(1)}, f32[128]{0:T(128)}, u32[]{:S(2)}) copy-start(f32[128]{0:T(128)} %param.13) | copy-start | bytes 1540
  95.3 20.6 %copy-start.9 = (f32[128]{0:T(128)S(1)}, f32[128]{0:T(128)}, u32[]{:S(2)}) copy-start(f32[128]{0:T(128)} %param.14) | copy-start | bytes 1540
  99.9 15.8 %all-to-all-start.4 = ((f32[32,8,128]{2,1,0:T(8,128)}), f32[32,8,128]{2,1,0:T(8,128)S(1)}, u32[]{:S(2)}, u32[]{:S(2)}) async-start(f32[32,8,128]{2,1,0:T(8,128)} %get-tuple-element.24), calls=%async_computation.4 | async-start | bytes 262144 | tf_op jit(solution)/shard_map/all_to_all | solution.py:185
  107.2 88.0 %all-gather.7.cloned.1.call-start = ((), (), s32[]{:S(2)}) async-start(), calls=%async_computation.11 | async-start | bytes 1474560 | tf_op jit(solution)/shard_map/all_gather | solution.py:254
  107.3 0.7 collective-permute-start.1
  107.9 7.8 %copy-start.4 = (bf16[2,320,128]{2,1,0:T(8,128)(2,1)}, bf16[2,320,128]{2,1,0:T(8,128)(2,1)S(1)}, u32[]{:S(2)}) copy-start(bf16[2,320,128]{2,1,0:T(8,128)(2,1)S(1)} %collective-permute-done.1) | copy-start | bytes 491524
  195.3 1.3 copy-start
Sparse Core Ops, SparseCore 0:
  33.7 60.5 all-gather.4
  115.9 53.1 all-gather.6

commit v8 on v7

--- a/solution.py
+++ b/solution.py
@@ -99,9 +99,8 @@
 
     extra = marks[...].astype(BF16)
     q_low = rotated(q[...], qg[...], 0).astype(BF16)
-    for t in range(q_out.shape[0]):
-        q_out[t, :128] = q_low
-        q_out[t, 128:144] = extra
+    q_out[:128] = q_low
+    q_out[128:144] = extra
     k_rot = rotated(kv[0], kg[...], 2)
     value = kv[1]
     k_low = k_rot.astype(BF16)
@@ -114,11 +113,12 @@
     v_cache[...] = value.T.astype(BF16)
 
 
-def attend_kernel(q, keys, messages, held):
+def attend_kernel(order, at, q0, q1, q2, q3, keys, messages, held):
     count = keys.shape[0]
     scale = LOG2E / math.sqrt(HEAD_DIM)
-    q_low = jnp.concatenate([q[d, :128] for d in range(4)], axis=1)
-    seg_q = jnp.concatenate([q[d, 128:144] for d in range(4)], axis=1).astype(F32)[:1]
+    parts = (q0, q1, q2, q3)
+    q_low = jnp.concatenate([q[:128] for q in parts], axis=1)
+    seg_q = jnp.concatenate([q[128:144] for q in parts], axis=1).astype(F32)[:1]
     top = None
     for b in range(count):
         seg_k = keys[b, 256:272].astype(F32).T[:, :1]
@@ -147,38 +147,46 @@
     rows = jnp.concatenate(
         [high.astype(F32), middle.astype(F32), low.astype(F32), jnp.zeros((13, 1024), F32)], axis=0
     ).astype(BF16)
-    for d in range(4):
-        here = slice(256 * d, 256 * d + 256)
-        messages[d, :128] = out[:, here].astype(BF16)
-        messages[d, 128:144] = rows[:, here]
+    for place, d in enumerate(order):
+        here = slice(256 * place, 256 * place + 256)
+        target = jnp.bitwise_xor(at[1], d)
+        for core in range(2):
+            messages[2 * target + core, :128] = out[:, here].astype(BF16)
+            messages[2 * target + core, 128:144] = rows[:, here]
 
 
 def merge_kernel(got, out):
-    lses, parts = [], []
-    for d in range(4):
-        rows = got[d, 128:144].astype(F32)
-        lses.append(rows[0:1] + rows[1:2] + rows[2:3])
-        parts.append(got[d, :128].astype(F32))
-    top = functools.reduce(jnp.maximum, lses)
-    weights = [jnp.exp2(lse - top) for lse in lses]
-    total = sum(weights[1:], weights[0])
-    value = None
-    for weight, part in zip(weights, parts, strict=True):
-        term = part * (weight / total)
-        value = term if value is None else value + term
-    value = value.astype(BF16)
-    for t in range(out.shape[0]):
-        out[t] = value
+    for head in range(2):
+        lses, parts = [], []
+        for d in range(4):
+            rows = got[2 * d + head, 128:144].astype(F32)
+            lses.append(rows[0:1] + rows[1:2] + rows[2:3])
+            parts.append(got[2 * d + head, :128].astype(F32))
+        top = functools.reduce(jnp.maximum, lses)
+        weights = [jnp.exp2(lse - top) for lse in lses]
+        total = sum(weights[1:], weights[0])
+        value = None
+        for weight, part in zip(weights, parts, strict=True):
+            term = part * (weight / total)
+            value = term if value is None else value + term
+        out[128 * head : 128 * head + 128] = value.astype(BF16)
 
 
 def partial_kernel(heads, w, messages):
+    both = heads[...]
     for x in range(4):
-        total = None
         for z in range(4):
-            term = jnp.dot(w[2 * z + x // 2, x % 2], heads[z], preferred_element_type=F32)
-            total = term if total is None else total + term
-        messages[2 * x] = total[:160].astype(BF16)
-        messages[2 * x + 1] = total[160:].astype(BF16)
+            block, low = 2 * z + x // 2, x % 2
+            weights = jnp.concatenate([w[block, 0, low], w[block, 1, low]], axis=1)
+            messages[x, z] = jnp.dot(weights, both, preferred_element_type=F32).astype(BF16)
+
+
+def along_x_kernel(got, out):
+    for z in range(4):
+        total = got[0, z].astype(F32)
+        for x in range(1, 4):
+            total = total + got[x, z].astype(F32)
+        out[z] = total.astype(BF16)
 
 
 def exchange(value, axes):
@@ -194,7 +202,9 @@
     tok_rows, feat_local = hidden_in.shape
     model_width = feat_local * 32
     heads_width = 4096
-    at = jnp.stack([lax.axis_index("c")]).astype(jnp.int32)
+    at = jnp.stack(
+        [lax.axis_index("c"), lax.axis_index("yc") * 2 + lax.axis_index("zh")]
+    ).astype(jnp.int32)
 
     local = jnp.concatenate([jnp.transpose(w_qkv, (1, 0, 2)), w_out.T[None]], axis=0)
     pair = spread(local, ("zh",))
@@ -228,6 +238,8 @@
     sums = exchange(sums, TP)
     w_all = lax.all_gather(pair[:, :3], ("ya", "yb", "yc"), axis=0, tiled=False)
     w_all = w_all.reshape(8, 2, 3, 2, 160, 128)
+    wo_pair = jnp.swapaxes(pair[:, 3].reshape(2, 2, 160, 128), 0, 1)
+    wo_all = lax.all_gather(exchange(wo_pair, ("c",)), ("ya", "yb", "yc"), axis=0, tiled=False)
     sums = jnp.sum(sums, axis=0)[:4].reshape(2, tok_rows)
     mean_value = sums[0:1] / model_width
     variance = sums[1:2] / model_width - mean_value * mean_value
@@ -245,18 +257,11 @@
         name="project",
         cost=pl.CostEstimate(flops=2 * 256 * 5120 * 384, bytes_accessed=6 << 20, transcendentals=0),
     )
-    wo_pair, stats = lax.optimization_barrier((pair[:, 3], stats))
     stats = exchange(stats, TP)
-    wo_turned = permute(
-        wo_pair, ("ya", "yb", "zl"), lambda ya, yb, zl: (zl >> 1, zl & 1, ya * 2 + yb)
-    )
-    stats, wo_turned = lax.optimization_barrier((stats, wo_turned))
-    wo_all = lax.all_gather(wo_turned, ("ya", "yb", "yc"), axis=0, tiled=False)
-
     q_message, k_cache, v_cache, kv_message = call(
         functools.partial(rotate_kernel, heads_width),
         (
-            shaped((4, 144, 256), BF16),
+            shaped((144, 256), BF16),
             shaped((256, 128), BF16),
             shaped((256, 128), BF16),
             shaped((4, 272, 256), BF16),
@@ -265,21 +270,30 @@
         name="rotate",
     )
     keys = exchange(kv_message, ("ya", "yb"))
-    queries = exchange(q_message, ("yc", "zh"))
+    order = (0, 1, 3, 2)
+    queries = [q_message] + [
+        permute(q_message, ("yc", "zh"), lambda yc, zh, d=d: (yc ^ (d >> 1), zh ^ (d & 1)))
+        for d in order[1:]
+    ]
     o_messages = call(
-        attend_kernel,
-        shaped((4, 144, 256), BF16),
-        [queries, keys],
+        functools.partial(attend_kernel, order),
+        shaped((8, 144, 256), BF16),
+        queries + [keys],
+        scalars=at,
         scratch=[pltpu.VMEM((4, 256, 1024), F32)],
         name="attend",
     )
     heads = call(
-        merge_kernel, shaped((4, 128, 256), BF16), [exchange(o_messages, ("yc", "zh"))], name="merge"
-    )
+        merge_kernel, shaped((256, 256), BF16), [exchange(o_messages, ("yc", "zh", "c"))], name="merge"
+    )
+    partials = call(partial_kernel, shaped((4, 4, 160, 256), BF16), [heads, wo_all], name="partial")
     partials = call(
-        partial_kernel, shaped((8, 160, 256), BF16), [exchange(heads, ("zl",)), wo_all], name="partial"
-    )
-    mixed = jnp.sum(exchange(partials, ("xh", "xl", "c")).astype(F32), axis=0)
+        along_x_kernel,
+        shaped((4, 160, 256), BF16),
+        [exchange(partials, ("xh", "xl"))],
+        name="along_x",
+    )
+    mixed = jnp.sum(exchange(partials, ("zl",)).astype(F32), axis=0)
     hidden_out = (x_t + modulation[2] * mixed).T.astype(BF16)
     return (hidden_out, k_cache, v_cache)
 

time: 225 us -> 216 us (0.960)
  blocking collectives: 150 us -> 114 us
  starting transfers between devices: 22.7 us -> 38.2 us
  waiting for transfers between devices: 20.4 us -> 30.1 us
    all_to_all x8 -> x7, blocking collectives: 150 us -> 114 us  [exchange(): return lax.all_to_all(value, axes, 0, 0, tiled=True)]
    ppermute x2 -> x4, starting transfers between devices: 4.61 us -> 16.2 us  [permute(): return lax.ppermute(value, axes, pairs)]
    ppermute x2 -> x4, waiting for transfers between devices: 1.7 us -> 10.9 us  [permute(): return lax.ppermute(value, axes, pairs)]
    all_to_all x2 -> x3, starting transfers between devices: 18.1 us -> 21.9 us  [exchange(): return lax.all_to_all(value, axes, 0, 0, tiled=True)]
    pallas_call x5 -> x6, Pallas kernels: 8.42 us -> 9.05 us  [call(): pl.pallas_call(kernel, out_shape=out_shape, in_specs=specs, out_specs=jax...]
    all_to_all x2 -> x3, waiting for transfers between devices: 18.6 us -> 19.1 us  [exchange(): return lax.all_to_all(value, axes, 0, 0, tiled=True)]
  transfers between devices with their start and end apart: 6 -> 9, of which waited for: 3 -> 3; matrix products, arithmetic and copies ran while one was open for 1% -> 1% of each run, Pallas kernels for 1% -> 4%
where the time goes in v8:
time: 216 us; the launch traced here: 213 us
  blocking collectives  114 us (53%)
  starting transfers between devices  38.2 us (18%)
  waiting for transfers between devices  30.1 us (14%)
  between operations  14.4 us (7%)
  Pallas kernels  9.05 us (4%)
  local copies, waits for them, and re-layouts  4 us (2%)
  other arithmetic  3.54 us (2%)
    all_to_all x7, blocking collectives, exchange(): return lax.all_to_all(value, axes, 0, 0, tiled=True)  114 us
    all_to_all x3, starting transfers between devices, exchange(): return lax.all_to_all(value, axes, 0, 0, tiled=True)  21.9 us
    all_to_all x3, waiting for transfers between devices, exchange(): return lax.all_to_all(value, axes, 0, 0, tiled=True)  19.1 us
    ppermute x4, starting transfers between devices, permute(): return lax.ppermute(value, axes, pairs)  16.2 us
    ppermute x4, waiting for transfers between devices, permute(): return lax.ppermute(value, axes, pairs)  10.9 us
    pallas_call x6, Pallas kernels, call(): pl.pallas_call(kernel, out_shape=out_shape, in_specs=specs, out_specs=jax...  9.05 us
  transfers between devices with their start and end apart: 9, of which 3 were waited for; matrix products, arithmetic and copies ran while one was open for 1% of the time, Pallas kernels for 4%

profile of v8, /device:TPU:1, one launch (start us, length us, event | category | flops | bytes accessed | tf_op | source)
XLA Modules:
  0.0 213.3 jit_solution(18320978519673835525)
XLA Ops:
  7.2 1.0 pad_maximum_fusion
  8.2 0.9 broadcast_in_dim.38
  9.2 10.8 %all-to-all-start = ((bf16[2,4,320,128]{3,2,1,0:T(8,128)(2,1)}), bf16[2,4,320,128]{3,2,1,0:T(8,128)(2,1)S(1)}, u32[]{:S(2)}, u32[]{:S(2)}) async-start(bf16[2,4,320,128]{3,2,1,0:T(8,128)(2,1)} %broadcast_in_dim.38), calls=%async_computation | async-start | bytes 1310720 | tf_op jit(solution)/shard_map/all_to_all | solution.py:193
  21.7 10.8 %all-to-all-done = bf16[2,4,320,128]{3,2,1,0:T(8,128)(2,1)S(1)} async-done(((bf16[2,4,320,128]{3,2,1,0:T(8,128)(2,1)}), bf16[2,4,320,128]{3,2,1,0:T(8,128)(2,1)S(1)}, u32[]{:S(2)}, u32[]{:S(2)}) %all-to-all-start) | async-done | bytes 655392 | tf_op jit(solution)/shard_map/all_to_all | solution.py:193
  33.5 23.1 %all_to_all.50 = f32[32,8,128]{2,1,0:T(8,128)S(1)} all-to-all(f32[32,8,128]{2,1,0:T(8,128)S(1)} %broadcast_in_dim.36), channel_id=1, replica_groups=mesh['ya'=2,'yb'=2,'yc'=2,'zh'=2,'zl'=4,'xh'=2,'xl'=2,'c'=2] {'zl','xh',..., dimensions={0} | all-to-all | bytes 262144 | tf_op jit(solution)/shard_map/all_to_all | solution.py:193
  56.8 12.5 %all_to_all.51 = bf16[4,160,256]{2,1,0:T(8,128)(2,1)S(1)} all-to-all(bf16[4,160,256]{2,1,0:T(8,128)(2,1)S(1)} %broadcast_in_dim.42), channel_id=1, replica_groups=mesh['ya'=2,'yb'=2,'yc'=2,'zh'=2,'zl'=4,'xh'=2,'xl'=2,'c'=2] {'zl'}, dimensions={0} | all-to-all | bytes 655360 | tf_op jit(solution)/shard_map/all_to_all | solution.py:193
  69.4 19.3 %all_to_all.52.mine = bf16[4,4,160,256]{3,2,1,0:T(8,128)(2,1)S(1)} all-to-all(bf16[4,4,160,256]{3,2,1,0:T(8,128)(2,1)S(1)} %broadcast_in_dim.43), channel_id=1, replica_groups=mesh['ya'=2,'yb'=2,'yc'=2,'zh'=2,'zl'=4,'xh'=2,'xl'=2,'c'=2] {'xh','xl'}, dimensions={0} | all-to-all | bytes 2621440 | tf_op jit(solution)/shard_map/all_to_all | solution.py:193
  88.6 3.9 %collective-permute-start = (bf16[4,4,160,256]{3,2,1,0:T(8,128)(2,1)S(1)}, bf16[4,4,160,256]{3,2,1,0:T(8,128)(2,1)S(1)}, u32[]{:S(2)}, u32[]{:S(2)}) collective-permute-start(bf16[4,4,160,256]{3,2,1,0:T(8,128)(2,1)S(1)} %all_to_all.52.mine), channel_id=1, source_target_pairs={{0,1},{1,0},{2,3},{3,2},{4,5},{5,4},{6,7},{7,6},{8,9},{9,8},{10,11... | collective-permute-start | bytes 3932168 | tf_op jit(solution)/shard_map/ppermute | solution.py:34
  92.7 4.2 %all_to_all.53 = bf16[2,2,160,128]{3,2,1,0:T(8,128)(2,1)} all-to-all(bf16[2,2,160,128]{3,2,1,0:T(8,128)(2,1)S(1)} %copy.32), channel_id=1, replica_groups=mesh['ya'=2,'yb'=2,'yc'=2,'zh'=2,'zl'=4,'xh'=2,'xl'=2,'c'=2] {'c'}, dimensions={0} | all-to-all | bytes 327680 | tf_op jit(solution)/shard_map/all_to_all | solution.py:193
  97.0 4.7 %project.1 = (f32[128,256]{1,0:T(8,128)S(1)}, f32[2,128,256]{2,1,0:T(8,128)S(1)}, f32[32,8,128]{2,1,0:T(8,128)}) custom-call(s32[2]{0:T(128)S(1)} %pad_add_fusion.at, bf16[4,4,160,256]{3,2,1,0:T(8,128)(2,1)S(1)} %all_to_all.52.mine, bf16[4,4,160,256]{3,2,1,0:T(8,128)(2,1)S(1)} %collective-permute-done.theirs, bf16[8,2,3,2,160,128]{5,4,3,2,1,0:T(8,128)(2,1)} %bitcast.67), custom_call_target="tpu_custom_call" | custom-call | flops 1006632960 | bytes 6291456 | tf_op jit(solution)/shard_map/project/pallas_call | solution.py:46
  101.7 5.4 %all-to-all-start.4 = ((f32[32,8,128]{2,1,0:T(8,128)}), f32[32,8,128]{2,1,0:T(8,128)S(1)}, u32[]{:S(2)}, u32[]{:S(2)}) async-start(f32[32,8,128]{2,1,0:T(8,128)} %get-tuple-element.19), calls=%async_computation.4 | async-start | bytes 262144 | tf_op jit(solution)/shard_map/all_to_all | solution.py:193
  107.4 8.3 %all-to-all-done.4.got = f32[32,8,128]{2,1,0:T(8,128)S(1)} async-done(((f32[32,8,128]{2,1,0:T(8,128)}), f32[32,8,128]{2,1,0:T(8,128)S(1)}, u32[]{:S(2)}, u32[]{:S(2)}) %all-to-all-start.4) | async-done | bytes 131104 | tf_op jit(solution)/shard_map/all_to_all | solution.py:193
  115.7 1.1 rotate.1
  116.8 5.7 %all-to-all-start.5 = ((bf16[4,272,256]{2,1,0:T(8,128)(2,1)}), bf16[4,272,256]{2,1,0:T(8,128)(2,1)S(1)}, u32[]{:S(2)}, u32[]{:S(2)}) async-start(bf16[4,272,256]{2,1,0:T(8,128)(2,1)} %get-tuple-element.26), calls=%async_computation.5 | async-start | bytes 1114112 | tf_op jit(solution)/shard_map/all_to_all | solution.py:193
  122.5 3.5 %collective-permute-start.1 = (bf16[144,256]{1,0:T(8,128)(2,1)S(1)}, bf16[144,256]{1,0:T(8,128)(2,1)S(1)}, u32[]{:S(2)}, u32[]{:S(2)}) collective-permute-start(bf16[144,256]{1,0:T(8,128)(2,1)S(1)} %get-tuple-element.25.q0), channel_id=1, source_target_pairs={{0,32},{32,0},{64,96},{96,64},{1,33},{33,1},{65,97},{97,65},{2,34}... | collective-permute-start | bytes 221192 | tf_op jit(solution)/shard_map/ppermute | solution.py:34
  126.0 5.7 %collective-permute-start.2 = (bf16[144,256]{1,0:T(8,128)(2,1)S(1)}, bf16[144,256]{1,0:T(8,128)(2,1)S(1)}, u32[]{:S(2)}, u32[]{:S(2)}) collective-permute-start(bf16[144,256]{1,0:T(8,128)(2,1)S(1)} %get-tuple-element.25.q0), channel_id=1, source_target_pairs={{0,96},{32,64},{64,32},{96,0},{1,97},{33,65},{65,33},{97,1},{2,98}... | collective-permute-start | bytes 221192 | tf_op jit(solution)/shard_map/ppermute | solution.py:34
  131.7 3.1 %collective-permute-start.3 = (bf16[144,256]{1,0:T(8,128)(2,1)S(1)}, bf16[144,256]{1,0:T(8,128)(2,1)S(1)}, u32[]{:S(2)}, u32[]{:S(2)}) collective-permute-start(bf16[144,256]{1,0:T(8,128)(2,1)S(1)} %get-tuple-element.25.q0), channel_id=1, source_target_pairs={{0,64},{32,96},{64,0},{96,32},{1,65},{33,97},{65,1},{97,33},{2,66}... | collective-permute-start | bytes 221192 | tf_op jit(solution)/shard_map/ppermute | solution.py:34
  134.8 10.9 %collective-permute-done.2.q2 = bf16[144,256]{1,0:T(8,128)(2,1)S(1)} collective-permute-done((bf16[144,256]{1,0:T(8,128)(2,1)S(1)}, bf16[144,256]{1,0:T(8,128)(2,1)S(1)}, u32[]{:S(2)}, u32[]{:S(2)}) %collective-permute-start.2) | collective-permute-done | bytes 73760 | tf_op jit(solution)/shard_map/ppermute | solution.py:34
  145.7 2.5 %attend.1 = bf16[8,144,256]{2,1,0:T(8,128)(2,1)S(1)} custom-call(s32[2]{0:T(128)S(1)} %pad_add_fusion.at, bf16[144,256]{1,0:T(8,128)(2,1)S(1)} %get-tuple-element.25.q0, bf16[144,256]{1,0:T(8,128)(2,1)S(1)} %collective-permute-done.1.q1, bf16[144,256]{1,0:T(8,128)(2,1)S(1)} %collective-permute-done.2.q2, bf16[144,256]{1,0:T(8,128)(2,1)S(1)} %collective-permute-done.3.q3, ...), custom_call_target="tpu_custom_call" | custom-call | tf_op jit(solution)/shard_map/attend/pallas_call | solution.py:46
  148.1 23.6 %all_to_all.54.got = bf16[8,144,256]{2,1,0:T(8,128)(2,1)S(1)} all-to-all(bf16[8,144,256]{2,1,0:T(8,128)(2,1)S(1)} %attend.1), channel_id=1, replica_groups=mesh['ya'=2,'yb'=2,'yc'=2,'zh'=2,'zl'=4,'xh'=2,'xl'=2,'c'=2] {'yc','zh',..., dimensions={0} | all-to-all | bytes 1179648 | tf_op jit(solution)/shard_map/all_to_all | solution.py:193
  172.0 1.3 copy-done
  173.8 19.3 %all_to_all.55.got = bf16[4,4,160,256]{3,2,1,0:T(8,128)(2,1)S(1)} all-to-all(bf16[4,4,160,256]{3,2,1,0:T(8,128)(2,1)S(1)} %partial.1), channel_id=1, replica_groups=mesh['ya'=2,'yb'=2,'yc'=2,'zh'=2,'zl'=4,'xh'=2,'xl'=2,'c'=2] {'xh','xl'}, dimensions={0} | all-to-all | bytes 2621440 | tf_op jit(solution)/shard_map/all_to_all | solution.py:193
  193.3 11.6 %all_to_all.56 = bf16[4,160,256]{2,1,0:T(8,128)(2,1)S(1)} all-to-all(bf16[4,160,256]{2,1,0:T(8,128)(2,1)S(1)} %along_x.1), channel_id=1, replica_groups=mesh['ya'=2,'yb'=2,'yc'=2,'zh'=2,'zl'=4,'xh'=2,'xl'=2,'c'=2] {'zl'}, dimensions={0} | all-to-all | bytes 655360 | tf_op jit(solution)/shard_map/all_to_all | solution.py:193
  204.9 1.6 fusion.11
  (65 shorter events, 4.1 us)
Async XLA Ops:
  8.2 11.8 %copy-start.2 = (bf16[256,160]{0,1:T(8,128)(2,1)S(1)}, bf16[256,160]{0,1:T(8,128)(2,1)}, u32[]{:S(2)}) copy-start(bf16[256,160]{0,1:T(8,128)(2,1)} %param.8) | copy-start | bytes 245764
  8.2 11.9 %copy-start.6 = (s32[3,256]{1,0:T(4,128)S(1)}, s32[3,256]{1,0:T(4,128)}, u32[]{:S(2)}) copy-start(s32[3,256]{1,0:T(4,128)} %param.10) | copy-start | bytes 9220
  8.2 12.3 %copy-start.4 = (f32[4,3,160]{2,0,1:T(4,128)S(1)}, f32[4,3,160]{2,0,1:T(4,128)}, u32[]{:S(2)}) copy-start(f32[4,3,160]{2,0,1:T(4,128)} %param.11) | copy-start | bytes 23044
  8.2 12.5 %copy-start.5 = (s32[256]{0:T(256)S(1)}, s32[256]{0:T(256)}, u32[]{:S(2)}) copy-start(s32[256]{0:T(256)} %param.9) | copy-start | bytes 3076
  9.2 23.4 %all-to-all-start = ((bf16[2,4,320,128]{3,2,1,0:T(8,128)(2,1)}), bf16[2,4,320,128]{3,2,1,0:T(8,128)(2,1)S(1)}, u32[]{:S(2)}, u32[]{:S(2)}) async-start(bf16[2,4,320,128]{3,2,1,0:T(8,128)(2,1)} %broadcast_in_dim.38), calls=%async_computation | async-start | bytes 1310720 | tf_op jit(solution)/shard_map/all_to_all | solution.py:193
  20.0 77.0 %all-gather.5.cloned.1.call-start = ((), (), s32[]{:S(2)}) async-start(), calls=%async_computation.10 | async-start | bytes 4423680 | tf_op jit(solution)/shard_map/all_gather | solution.py:239
  21.7 35.1 %copy-start.1 = (f32[256,480]{0,1:T(8,128)}, f32[256,480]{0,1:T(8,128)S(1)}, u32[]{:S(2)}) copy-start(f32[256,480]{0,1:T(8,128)S(1)} %fusion.12) | copy-start | bytes 1474564
  33.4 138.5 %all-gather.7.cloned.1.call-start = ((), (), s32[]{:S(2)}) async-start(), calls=%async_computation.11 | async-start | bytes 1474560 | tf_op jit(solution)/shard_map/all_gather | solution.py:242
  88.6 8.4 %collective-permute-start = (bf16[4,4,160,256]{3,2,1,0:T(8,128)(2,1)S(1)}, bf16[4,4,160,256]{3,2,1,0:T(8,128)(2,1)S(1)}, u32[]{:S(2)}, u32[]{:S(2)}) collective-permute-start(bf16[4,4,160,256]{3,2,1,0:T(8,128)(2,1)S(1)} %all_to_all.52.mine), channel_id=1, source_target_pairs={{0,1},{1,0},{2,3},{3,2},{4,5},{5,4},{6,7},{7,6},{8,9},{9,8},{10,11... | collective-permute-start | bytes 3932168 | tf_op jit(solution)/shard_map/ppermute | solution.py:34
  97.0 10.1 %copy-start.7 = (f32[128]{0:T(128)S(1)}, f32[128]{0:T(128)}, u32[]{:S(2)}) copy-start(f32[128]{0:T(128)} %param.13) | copy-start | bytes 1540
  97.0 10.2 %copy-start.8 = (f32[128]{0:T(128)S(1)}, f32[128]{0:T(128)}, u32[]{:S(2)}) copy-start(f32[128]{0:T(128)} %param.14) | copy-start | bytes 1540
  101.7 14.0 %all-to-all-start.4 = ((f32[32,8,128]{2,1,0:T(8,128)}), f32[32,8,128]{2,1,0:T(8,128)S(1)}, u32[]{:S(2)}, u32[]{:S(2)}) async-start(f32[32,8,128]{2,1,0:T(8,128)} %get-tuple-element.19), calls=%async_computation.4 | async-start | bytes 262144 | tf_op jit(solution)/shard_map/all_to_all | solution.py:193
  116.8 28.9 %all-to-all-start.5 = ((bf16[4,272,256]{2,1,0:T(8,128)(2,1)}), bf16[4,272,256]{2,1,0:T(8,128)(2,1)S(1)}, u32[]{:S(2)}, u32[]{:S(2)}) async-start(bf16[4,272,256]{2,1,0:T(8,128)(2,1)} %get-tuple-element.26), calls=%async_computation.5 | async-start | bytes 1114112 | tf_op jit(solution)/shard_map/all_to_all | solution.py:193
  122.5 12.3 %collective-permute-start.1 = (bf16[144,256]{1,0:T(8,128)(2,1)S(1)}, bf16[144,256]{1,0:T(8,128)(2,1)S(1)}, u32[]{:S(2)}, u32[]{:S(2)}) collective-permute-start(bf16[144,256]{1,0:T(8,128)(2,1)S(1)} %get-tuple-element.25.q0), channel_id=1, source_target_pairs={{0,32},{32,0},{64,96},{96,64},{1,33},{33,1},{65,97},{97,65},{2,34}... | collective-permute-start | bytes 221192 | tf_op jit(solution)/shard_map/ppermute | solution.py:34
  126.0 19.7 %collective-permute-start.2 = (bf16[144,256]{1,0:T(8,128)(2,1)S(1)}, bf16[144,256]{1,0:T(8,128)(2,1)S(1)}, u32[]{:S(2)}, u32[]{:S(2)}) collective-permute-start(bf16[144,256]{1,0:T(8,128)(2,1)S(1)} %get-tuple-element.25.q0), channel_id=1, source_target_pairs={{0,96},{32,64},{64,32},{96,0},{1,97},{33,65},{65,33},{97,1},{2,98}... | collective-permute-start | bytes 221192 | tf_op jit(solution)/shard_map/ppermute | solution.py:34
  131.7 14.0 %collective-permute-start.3 = (bf16[144,256]{1,0:T(8,128)(2,1)S(1)}, bf16[144,256]{1,0:T(8,128)(2,1)S(1)}, u32[]{:S(2)}, u32[]{:S(2)}) collective-permute-start(bf16[144,256]{1,0:T(8,128)(2,1)S(1)} %get-tuple-element.25.q0), channel_id=1, source_target_pairs={{0,64},{32,96},{64,0},{96,32},{1,65},{33,97},{65,1},{97,33},{2,66}... | collective-permute-start | bytes 221192 | tf_op jit(solution)/shard_map/ppermute | solution.py:34
  172.0 1.3 copy-start
  193.1 11.8 %copy-start.3 = (bf16[256,160]{0,1:T(8,128)(2,1)S(1)}, bf16[256,160]{0,1:T(8,128)(2,1)}, u32[]{:S(2)}) copy-start(bf16[256,160]{0,1:T(8,128)(2,1)} %param.8) | copy-start | bytes 245764
Sparse Core Ops, SparseCore 0:
  33.6 60.5 all-gather.4
  97.1 42.3 all-gather.6

commit v9 on v8

--- a/solution.py
+++ b/solution.py
@@ -150,34 +150,32 @@
     for place, d in enumerate(order):
         here = slice(256 * place, 256 * place + 256)
         target = jnp.bitwise_xor(at[1], d)
-        for core in range(2):
-            messages[2 * target + core, :128] = out[:, here].astype(BF16)
-            messages[2 * target + core, 128:144] = rows[:, here]
+        messages[target, :128] = out[:, here].astype(BF16)
+        messages[target, 128:144] = rows[:, here]
 
 
 def merge_kernel(got, out):
-    for head in range(2):
-        lses, parts = [], []
-        for d in range(4):
-            rows = got[2 * d + head, 128:144].astype(F32)
-            lses.append(rows[0:1] + rows[1:2] + rows[2:3])
-            parts.append(got[2 * d + head, :128].astype(F32))
-        top = functools.reduce(jnp.maximum, lses)
-        weights = [jnp.exp2(lse - top) for lse in lses]
-        total = sum(weights[1:], weights[0])
-        value = None
-        for weight, part in zip(weights, parts, strict=True):
-            term = part * (weight / total)
-            value = term if value is None else value + term
-        out[128 * head : 128 * head + 128] = value.astype(BF16)
-
-
-def partial_kernel(heads, w, messages):
-    both = heads[...]
+    lses, parts = [], []
+    for d in range(4):
+        rows = got[d, 128:144].astype(F32)
+        lses.append(rows[0:1] + rows[1:2] + rows[2:3])
+        parts.append(got[d, :128].astype(F32))
+    top = functools.reduce(jnp.maximum, lses)
+    weights = [jnp.exp2(lse - top) for lse in lses]
+    total = sum(weights[1:], weights[0])
+    value = None
+    for weight, part in zip(weights, parts, strict=True):
+        term = part * (weight / total)
+        value = term if value is None else value + term
+    out[...] = value.astype(BF16)
+
+
+def partial_kernel(own, other, w_own, w_other, messages):
+    both = jnp.concatenate([own[...], other[...]], axis=0)
     for x in range(4):
         for z in range(4):
             block, low = 2 * z + x // 2, x % 2
-            weights = jnp.concatenate([w[block, 0, low], w[block, 1, low]], axis=1)
+            weights = jnp.concatenate([w_own[block, low], w_other[block, low]], axis=1)
             messages[x, z] = jnp.dot(weights, both, preferred_element_type=F32).astype(BF16)
 
 
@@ -203,11 +201,14 @@
     model_width = feat_local * 32
     heads_width = 4096
     at = jnp.stack(
-        [lax.axis_index("c"), lax.axis_index("yc") * 2 + lax.axis_index("zh")]
+        [lax.axis_index("c"), lax.axis_index("yb") * 2 + lax.axis_index("yc")]
     ).astype(jnp.int32)
 
     local = jnp.concatenate([jnp.transpose(w_qkv, (1, 0, 2)), w_out.T[None]], axis=0)
-    pair = spread(local, ("zh",))
+    pair = lax.all_gather(local, "zh", axis=0, tiled=False)
+
+    w_all = lax.all_gather(pair, ("ya", "yb", "yc"), axis=0, tiled=False)
+    w_all = w_all.reshape(8, 2, 4, 2, 160, 128)
 
     x_t = hidden_in.T.astype(F32)
     sums = jnp.stack([jnp.sum(x_t, axis=0), jnp.sum(x_t * x_t, axis=0)]).reshape(4, 128)
@@ -232,14 +233,7 @@
     angle = jnp.concatenate(angles, axis=0)
     cosine, sine = jnp.cos(angle), jnp.sin(angle)
     marks = jnp.broadcast_to(seg_ids[None, :].astype(F32), (16, tok_rows))
-    sums, pair, modulation, cosine, sine, marks = lax.optimization_barrier(
-        (sums, pair, modulation, cosine, sine, marks)
-    )
     sums = exchange(sums, TP)
-    w_all = lax.all_gather(pair[:, :3], ("ya", "yb", "yc"), axis=0, tiled=False)
-    w_all = w_all.reshape(8, 2, 3, 2, 160, 128)
-    wo_pair = jnp.swapaxes(pair[:, 3].reshape(2, 2, 160, 128), 0, 1)
-    wo_all = lax.all_gather(exchange(wo_pair, ("c",)), ("ya", "yb", "yc"), axis=0, tiled=False)
     sums = jnp.sum(sums, axis=0)[:4].reshape(2, tok_rows)
     mean_value = sums[0:1] / model_width
     variance = sums[1:2] / model_width - mean_value * mean_value
@@ -258,6 +252,11 @@
         cost=pl.CostEstimate(flops=2 * 256 * 5120 * 384, bytes_accessed=6 << 20, transcendentals=0),
     )
     stats = exchange(stats, TP)
+    core = lax.axis_index("c")
+    wo_own = lax.dynamic_index_in_dim(w_all[:, :, 3], core, axis=2, keepdims=False)
+    wo_other = lax.dynamic_index_in_dim(w_all[:, :, 3], 1 - core, axis=2, keepdims=False)
+    stats, wo_own, wo_other = lax.optimization_barrier((stats, wo_own, wo_other))
+    wo_other = permute(wo_other, ("c",), lambda c: (1 - c,))
     q_message, k_cache, v_cache, kv_message = call(
         functools.partial(rotate_kernel, heads_width),
         (
@@ -269,24 +268,28 @@
         [stats, query, key_value, cosine, sine, q_gain.reshape(128, 1), k_gain.reshape(128, 1), marks],
         name="rotate",
     )
-    keys = exchange(kv_message, ("ya", "yb"))
+    keys = exchange(kv_message, ("ya", "zh"))
+    keys, wo_own, wo_other = lax.optimization_barrier((keys, wo_own, wo_other))
     order = (0, 1, 3, 2)
     queries = [q_message] + [
-        permute(q_message, ("yc", "zh"), lambda yc, zh, d=d: (yc ^ (d >> 1), zh ^ (d & 1)))
+        permute(q_message, ("yb", "yc"), lambda yb, yc, d=d: (yb ^ (d >> 1), yc ^ (d & 1)))
         for d in order[1:]
     ]
     o_messages = call(
         functools.partial(attend_kernel, order),
-        shaped((8, 144, 256), BF16),
+        shaped((4, 144, 256), BF16),
         queries + [keys],
         scalars=at,
         scratch=[pltpu.VMEM((4, 256, 1024), F32)],
         name="attend",
     )
-    heads = call(
-        merge_kernel, shaped((256, 256), BF16), [exchange(o_messages, ("yc", "zh", "c"))], name="merge"
-    )
-    partials = call(partial_kernel, shaped((4, 4, 160, 256), BF16), [heads, wo_all], name="partial")
+    own = call(
+        merge_kernel, shaped((128, 256), BF16), [exchange(o_messages, ("yb", "yc"))], name="merge"
+    )
+    other = permute(own, ("c",), lambda c: (1 - c,))
+    partials = call(
+        partial_kernel, shaped((4, 4, 160, 256), BF16), [own, other, wo_own, wo_other], name="partial"
+    )
     partials = call(
         along_x_kernel,
         shaped((4, 160, 256), BF16),

time: 216 us -> 214 us (level)
  blocking collectives: 114 us -> 90.8 us
  starting transfers between devices: 38.2 us -> 49.7 us
  waiting for transfers between devices: 30.1 us -> 41.2 us
    all_to_all x7 -> x5, blocking collectives: 114 us -> 74.2 us  [exchange(): return lax.all_to_all(value, axes, 0, 0, tiled=True)]
    all_gather x0 -> x1, blocking collectives: none -> 16.6 us  [body(): pair = lax.all_gather(local, 'zh', axis=0, tiled=False)]
    all_gather x2 -> x1, waiting for transfers between devices: 0.02 us -> 13.3 us  [body(): w_all = lax.all_gather(pair, ('ya', 'yb', 'yc'), axis=0, tiled=False)]
    all_to_all x3, starting transfers between devices: 21.9 us -> 31.1 us  [exchange(): return lax.all_to_all(value, axes, 0, 0, tiled=True)]
    ppermute x4 -> x6, starting transfers between devices: 16.2 us -> 18.7 us  [permute(): return lax.ppermute(value, axes, pairs)]
    ppermute x4 -> x6, waiting for transfers between devices: 10.9 us -> 10.4 us  [permute(): return lax.ppermute(value, axes, pairs)]
  transfers between devices with their start and end apart: 9 -> 10, of which waited for: 3 -> 8; matrix products, arithmetic and copies ran while one was open for 1% -> 2% of each run, Pallas kernels for 4% -> 0%
where the time goes in v9:
time: 214 us; the launch traced here: 213 us
  blocking collectives  90.8 us (42%)
  starting transfers between devices  49.7 us (23%)
  waiting for transfers between devices  41.2 us (19%)
  between operations  14.3 us (7%)
  Pallas kernels  9.34 us (4%)
  local copies, waits for them, and re-layouts  3.89 us (2%)
  other arithmetic  3.55 us (2%)
    all_to_all x5, blocking collectives, exchange(): return lax.all_to_all(value, axes, 0, 0, tiled=True)  74.2 us
    all_to_all x3, starting transfers between devices, exchange(): return lax.all_to_all(value, axes, 0, 0, tiled=True)  31.1 us
    ppermute x6, starting transfers between devices, permute(): return lax.ppermute(value, axes, pairs)  18.7 us
    all_to_all x3, waiting for transfers between devices, exchange(): return lax.all_to_all(value, axes, 0, 0, tiled=True)  17.5 us
    all_gather x1, blocking collectives, body(): pair = lax.all_gather(local, 'zh', axis=0, tiled=False)  16.6 us
    all_gather x1, waiting for transfers between devices, body(): w_all = lax.all_gather(pair, ('ya', 'yb', 'yc'), axis=0, tiled=False)  13.3 us
    ppermute x6, waiting for transfers between devices, permute(): return lax.ppermute(value, axes, pairs)  10.4 us
    pallas_call x6, Pallas kernels, call(): pl.pallas_call(kernel, out_shape=out_shape, in_specs=specs, out_specs=jax...  9.34 us
  transfers between devices with their start and end apart: 10, of which 8 were waited for; matrix products, arithmetic and copies ran while one was open for 2% of the time, Pallas kernels for 0%

profile of v9, /device:TPU:1, one launch (start us, length us, event | category | flops | bytes accessed | tf_op | source)
XLA Modules:
  0.0 213.3 jit_solution(17193748476244437538)
XLA Ops:
  8.3 16.6 %all-gather = bf16[8,320,128]{2,1,0:T(8,128)(2,1)} all-gather(bf16[4,320,128]{2,1,0:T(8,128)(2,1)S(1)} %pad_maximum_fusion), channel_id=2, replica_groups=mesh['ya'=2,'yb'=2,'yc'=2,'zh'=2,'zl'=4,'xh'=2,'xl'=2,'c'=2] {'zh'}, dimensions={0}, use_global_device_ids=true | all-gather | bytes 983040 | tf_op jit(solution)/shard_map/all_gather | solution.py:208
  25.7 15.7 %all-to-all-start = ((f32[32,8,128]{2,1,0:T(8,128)}), f32[32,8,128]{2,1,0:T(8,128)S(1)}, u32[]{:S(2)}, u32[]{:S(2)}) async-start(f32[32,8,128]{2,1,0:T(8,128)} %broadcast_in_dim.16), calls=%async_computation | async-start | bytes 262144 | tf_op jit(solution)/shard_map/all_to_all | solution.py:191
  42.0 8.0 %all-to-all-done = f32[32,8,128]{2,1,0:T(8,128)S(1)} async-done(((f32[32,8,128]{2,1,0:T(8,128)}), f32[32,8,128]{2,1,0:T(8,128)S(1)}, u32[]{:S(2)}, u32[]{:S(2)}) %all-to-all-start) | async-done | bytes 131104 | tf_op jit(solution)/shard_map/all_to_all | solution.py:191
  50.1 12.5 %all_to_all.40 = bf16[4,160,256]{2,1,0:T(8,128)(2,1)S(1)} all-to-all(bf16[4,160,256]{2,1,0:T(8,128)(2,1)S(1)} %broadcast_in_dim.34), channel_id=1, replica_groups=mesh['ya'=2,'yb'=2,'yc'=2,'zh'=2,'zl'=4,'xh'=2,'xl'=2,'c'=2] {'zl'}, dimensions={0} | all-to-all | bytes 655360 | tf_op jit(solution)/shard_map/all_to_all | solution.py:191
  62.8 19.4 %all_to_all.41.mine = bf16[4,4,160,256]{3,2,1,0:T(8,128)(2,1)S(1)} all-to-all(bf16[4,4,160,256]{3,2,1,0:T(8,128)(2,1)S(1)} %broadcast_in_dim.35), channel_id=1, replica_groups=mesh['ya'=2,'yb'=2,'yc'=2,'zh'=2,'zl'=4,'xh'=2,'xl'=2,'c'=2] {'xh','xl'}, dimensions={0} | all-to-all | bytes 2621440 | tf_op jit(solution)/shard_map/all_to_all | solution.py:191
  82.2 3.9 %collective-permute-start = (bf16[4,4,160,256]{3,2,1,0:T(8,128)(2,1)S(1)}, bf16[4,4,160,256]{3,2,1,0:T(8,128)(2,1)S(1)}, u32[]{:S(2)}, u32[]{:S(2)}) collective-permute-start(bf16[4,4,160,256]{3,2,1,0:T(8,128)(2,1)S(1)} %all_to_all.41.mine), channel_id=1, source_target_pairs={{0,1},{1,0},{2,3},{3,2},{4,5},{5,4},{6,7},{7,6},{8,9},{9,8},{10,11... | collective-permute-start | bytes 3932168 | tf_op jit(solution)/shard_map/ppermute | solution.py:34
  87.0 1.8 collective-permute-done.theirs
  88.8 13.3 %all-gather.4.cloned.1.call-done = bf16[16,4,320,128]{3,2,1,0:T(8,128)(2,1)} async-done(((bf16[2,4,320,128]{3,2,1,0:T(8,128)(2,1)}), bf16[16,4,320,128]{3,2,1,0:T(8,128)(2,1)}) %all-gather.4.cloned.1.call-update) | async-done | bytes 5242896 | tf_op jit(solution)/shard_map/all_gather | solution.py:210
  102.0 5.1 %project.1 = (f32[128,256]{1,0:T(8,128)S(1)}, f32[2,128,256]{2,1,0:T(8,128)S(1)}, f32[32,8,128]{2,1,0:T(8,128)}) custom-call(s32[2]{0:T(128)S(1)} %pad_add_fusion.at, bf16[4,4,160,256]{3,2,1,0:T(8,128)(2,1)S(1)} %all_to_all.41.mine, bf16[4,4,160,256]{3,2,1,0:T(8,128)(2,1)S(1)} %collective-permute-done.theirs, bf16[8,2,4,2,160,128]{5,4,3,2,1,0:T(8,128)(2,1)} %bitcast.56), custom_call_target="tpu_custom_call" | custom-call | flops 1006632960 | bytes 6291456 | tf_op jit(solution)/shard_map/project/pallas_call | solution.py:46
  107.1 8.3 %all-to-all-start.3 = ((f32[32,8,128]{2,1,0:T(8,128)}), f32[32,8,128]{2,1,0:T(8,128)S(1)}, u32[]{:S(2)}, u32[]{:S(2)}) async-start(f32[32,8,128]{2,1,0:T(8,128)} %get-tuple-element.16), calls=%async_computation.3 | async-start | bytes 262144 | tf_op jit(solution)/shard_map/all_to_all | solution.py:191
  118.3 5.7 %all-to-all-done.3.got = f32[32,8,128]{2,1,0:T(8,128)S(1)} async-done(((f32[32,8,128]{2,1,0:T(8,128)}), f32[32,8,128]{2,1,0:T(8,128)S(1)}, u32[]{:S(2)}, u32[]{:S(2)}) %all-to-all-start.3) | async-done | bytes 131104 | tf_op jit(solution)/shard_map/all_to_all | solution.py:191
  125.1 7.0 %all-to-all-start.4 = ((bf16[4,272,256]{2,1,0:T(8,128)(2,1)}), bf16[4,272,256]{2,1,0:T(8,128)(2,1)S(1)}, u32[]{:S(2)}, u32[]{:S(2)}) async-start(bf16[4,272,256]{2,1,0:T(8,128)(2,1)} %get-tuple-element.21), calls=%async_computation.4 | async-start | bytes 1114112 | tf_op jit(solution)/shard_map/all_to_all | solution.py:191
  132.1 2.6 %collective-permute-start.4 = (bf16[8,2,160,128]{3,2,1,0:T(8,128)(2,1)}, bf16[8,2,160,128]{3,2,1,0:T(8,128)(2,1)S(1)}, u32[]{:S(2)}, u32[]{:S(2)}) collective-permute-start(bf16[8,2,160,128]{3,2,1,0:T(8,128)(2,1)} %get-tuple-element.23), channel_id=1, source_target_pairs={{0,1},{1,0},{2,3},{3,2},{4,5},{5,4},{6,7},{7,6},{8,9},{9,8},{10,11... | collective-permute-start | bytes 1966088 | tf_op jit(solution)/shard_map/ppermute | solution.py:34
  134.7 3.1 %collective-permute-start.1 = (bf16[144,256]{1,0:T(8,128)(2,1)S(1)}, bf16[144,256]{1,0:T(8,128)(2,1)S(1)}, u32[]{:S(2)}, u32[]{:S(2)}) collective-permute-start(bf16[144,256]{1,0:T(8,128)(2,1)S(1)} %get-tuple-element.20.q0), channel_id=1, source_target_pairs={{0,64},{64,0},{128,192},{192,128},{1,65},{65,1},{129,193},{193,129... | collective-permute-start | bytes 221192 | tf_op jit(solution)/shard_map/ppermute | solution.py:34
  137.8 3.1 %collective-permute-start.2 = (bf16[144,256]{1,0:T(8,128)(2,1)S(1)}, bf16[144,256]{1,0:T(8,128)(2,1)S(1)}, u32[]{:S(2)}, u32[]{:S(2)}) collective-permute-start(bf16[144,256]{1,0:T(8,128)(2,1)S(1)} %get-tuple-element.20.q0), channel_id=1, source_target_pairs={{0,192},{64,128},{128,64},{192,0},{1,193},{65,129},{129,65},{193,1... | collective-permute-start | bytes 221192 | tf_op jit(solution)/shard_map/ppermute | solution.py:34
  140.9 2.2 %collective-permute-start.3 = (bf16[144,256]{1,0:T(8,128)(2,1)S(1)}, bf16[144,256]{1,0:T(8,128)(2,1)S(1)}, u32[]{:S(2)}, u32[]{:S(2)}) collective-permute-start(bf16[144,256]{1,0:T(8,128)(2,1)S(1)} %get-tuple-element.20.q0), channel_id=1, source_target_pairs={{0,128},{64,192},{128,0},{192,64},{1,129},{65,193},{129,1},{193,65... | collective-permute-start | bytes 221192 | tf_op jit(solution)/shard_map/ppermute | solution.py:34
  143.1 3.8 %all-to-all-done.4.keys = bf16[4,272,256]{2,1,0:T(8,128)(2,1)S(1)} async-done(((bf16[4,272,256]{2,1,0:T(8,128)(2,1)}), bf16[4,272,256]{2,1,0:T(8,128)(2,1)S(1)}, u32[]{:S(2)}, u32[]{:S(2)}) %all-to-all-start.4) | async-done | bytes 557088 | tf_op jit(solution)/shard_map/all_to_all | solution.py:191
  146.9 2.9 %collective-permute-done.1.q1 = bf16[144,256]{1,0:T(8,128)(2,1)S(1)} collective-permute-done((bf16[144,256]{1,0:T(8,128)(2,1)S(1)}, bf16[144,256]{1,0:T(8,128)(2,1)S(1)}, u32[]{:S(2)}, u32[]{:S(2)}) %collective-permute-start.1) | collective-permute-done | bytes 73760 | tf_op jit(solution)/shard_map/ppermute | solution.py:34
  149.8 4.9 %collective-permute-done.3.q3 = bf16[144,256]{1,0:T(8,128)(2,1)S(1)} collective-permute-done((bf16[144,256]{1,0:T(8,128)(2,1)S(1)}, bf16[144,256]{1,0:T(8,128)(2,1)S(1)}, u32[]{:S(2)}, u32[]{:S(2)}) %collective-permute-start.3) | collective-permute-done | bytes 73760 | tf_op jit(solution)/shard_map/ppermute | solution.py:34
  154.6 2.4 %attend.1 = bf16[4,144,256]{2,1,0:T(8,128)(2,1)S(1)} custom-call(s32[2]{0:T(128)S(1)} %pad_add_fusion.at, bf16[144,256]{1,0:T(8,128)(2,1)S(1)} %get-tuple-element.20.q0, bf16[144,256]{1,0:T(8,128)(2,1)S(1)} %collective-permute-done.1.q1, bf16[144,256]{1,0:T(8,128)(2,1)S(1)} %collective-permute-done.2.q2, bf16[144,256]{1,0:T(8,128)(2,1)S(1)} %collective-permute-done.3.q3, ...), custom_call_target="tpu_custom_call" | custom-call | tf_op jit(solution)/shard_map/attend/pallas_call | solution.py:46
  157.1 11.0 %all_to_all.42.got = bf16[4,144,256]{2,1,0:T(8,128)(2,1)S(1)} all-to-all(bf16[4,144,256]{2,1,0:T(8,128)(2,1)S(1)} %attend.1), channel_id=1, replica_groups=mesh['ya'=2,'yb'=2,'yc'=2,'zh'=2,'zl'=4,'xh'=2,'xl'=2,'c'=2] {'yb','yc'}, dimensions={0} | all-to-all | bytes 589824 | tf_op jit(solution)/shard_map/all_to_all | solution.py:191
  168.2 3.8 %collective-permute-start.5 = (bf16[128,256]{1,0:T(8,128)(2,1)S(1)}, bf16[128,256]{1,0:T(8,128)(2,1)S(1)}, u32[]{:S(2)}, u32[]{:S(2)}) collective-permute-start(bf16[128,256]{1,0:T(8,128)(2,1)S(1)} %merge.1.own), channel_id=1, source_target_pairs={{0,1},{1,0},{2,3},{3,2},{4,5},{5,4},{6,7},{7,6},{8,9},{9,8},{10,11... | collective-permute-start | bytes 196616 | tf_op jit(solution)/shard_map/ppermute | solution.py:34
  173.4 20.1 %all_to_all.43.got = bf16[4,4,160,256]{3,2,1,0:T(8,128)(2,1)S(1)} all-to-all(bf16[4,4,160,256]{3,2,1,0:T(8,128)(2,1)S(1)} %partial.1), channel_id=1, replica_groups=mesh['ya'=2,'yb'=2,'yc'=2,'zh'=2,'zl'=4,'xh'=2,'xl'=2,'c'=2] {'xh','xl'}, dimensions={0} | all-to-all | bytes 2621440 | tf_op jit(solution)/shard_map/all_to_all | solution.py:191
  193.6 11.2 %all_to_all.44 = bf16[4,160,256]{2,1,0:T(8,128)(2,1)S(1)} all-to-all(bf16[4,160,256]{2,1,0:T(8,128)(2,1)S(1)} %along_x.1), channel_id=1, replica_groups=mesh['ya'=2,'yb'=2,'yc'=2,'zh'=2,'zl'=4,'xh'=2,'xl'=2,'c'=2] {'zl'}, dimensions={0} | all-to-all | bytes 655360 | tf_op jit(solution)/shard_map/all_to_all | solution.py:191
  (58 shorter events, 10.7 us)
Async XLA Ops:
  7.2 17.8 %copy-start.1 = (bf16[256,160]{0,1:T(8,128)(2,1)S(1)}, bf16[256,160]{0,1:T(8,128)(2,1)}, u32[]{:S(2)}) copy-start(bf16[256,160]{0,1:T(8,128)(2,1)} %param.8) | copy-start | bytes 245764
  7.2 94.9 %all-gather.4.cloned.1.call-start = ((), (), s32[]{:S(2)}) async-start(), calls=%async_computation.8 | async-start | bytes 5898240 | tf_op jit(solution)/shard_map/all_gather | solution.py:210
  7.2 34.2 %copy-start.2 = (f32[4,3,160]{2,0,1:T(4,128)S(1)}, f32[4,3,160]{2,0,1:T(4,128)}, u32[]{:S(2)}) copy-start(f32[4,3,160]{2,0,1:T(4,128)} %param.11) | copy-start | bytes 23044
  7.2 34.3 %copy-start.3 = (s32[256]{0:T(256)S(1)}, s32[256]{0:T(256)}, u32[]{:S(2)}) copy-start(s32[256]{0:T(256)} %param.9) | copy-start | bytes 3076
  25.7 24.3 %all-to-all-start = ((f32[32,8,128]{2,1,0:T(8,128)}), f32[32,8,128]{2,1,0:T(8,128)S(1)}, u32[]{:S(2)}, u32[]{:S(2)}) async-start(f32[32,8,128]{2,1,0:T(8,128)} %broadcast_in_dim.16), calls=%async_computation | async-start | bytes 262144 | tf_op jit(solution)/shard_map/all_to_all | solution.py:191
  42.0 20.6 %copy-start = (f32[480,256]{1,0:T(8,128)}, f32[480,256]{1,0:T(8,128)S(1)}, u32[]{:S(2)}) copy-start(f32[480,256]{1,0:T(8,128)S(1)} %convolution_bitcast_fusion) | copy-start | bytes 1474564
  62.8 23.8 %copy-start.5 = (f32[128]{0:T(128)S(1)}, f32[128]{0:T(128)}, u32[]{:S(2)}) copy-start(f32[128]{0:T(128)} %param.13) | copy-start | bytes 1540
  62.8 23.9 %copy-start.6 = (f32[128]{0:T(128)S(1)}, f32[128]{0:T(128)}, u32[]{:S(2)}) copy-start(f32[128]{0:T(128)} %param.14) | copy-start | bytes 1540
  62.8 24.1 %copy-start.4 = (s32[3,256]{1,0:T(4,128)S(1)}, s32[3,256]{1,0:T(4,128)}, u32[]{:S(2)}) copy-start(s32[3,256]{1,0:T(4,128)} %param.10) | copy-start | bytes 9220
  82.2 6.6 %collective-permute-start = (bf16[4,4,160,256]{3,2,1,0:T(8,128)(2,1)S(1)}, bf16[4,4,160,256]{3,2,1,0:T(8,128)(2,1)S(1)}, u32[]{:S(2)}, u32[]{:S(2)}) collective-permute-start(bf16[4,4,160,256]{3,2,1,0:T(8,128)(2,1)S(1)} %all_to_all.41.mine), channel_id=1, source_target_pairs={{0,1},{1,0},{2,3},{3,2},{4,5},{5,4},{6,7},{7,6},{8,9},{9,8},{10,11... | collective-permute-start | bytes 3932168 | tf_op jit(solution)/shard_map/ppermute | solution.py:34
  107.1 16.9 %all-to-all-start.3 = ((f32[32,8,128]{2,1,0:T(8,128)}), f32[32,8,128]{2,1,0:T(8,128)S(1)}, u32[]{:S(2)}, u32[]{:S(2)}) async-start(f32[32,8,128]{2,1,0:T(8,128)} %get-tuple-element.16), calls=%async_computation.3 | async-start | bytes 262144 | tf_op jit(solution)/shard_map/all_to_all | solution.py:191
  125.1 21.8 %all-to-all-start.4 = ((bf16[4,272,256]{2,1,0:T(8,128)(2,1)}), bf16[4,272,256]{2,1,0:T(8,128)(2,1)S(1)}, u32[]{:S(2)}, u32[]{:S(2)}) async-start(bf16[4,272,256]{2,1,0:T(8,128)(2,1)} %get-tuple-element.21), calls=%async_computation.4 | async-start | bytes 1114112 | tf_op jit(solution)/shard_map/all_to_all | solution.py:191
  132.1 11.0 %collective-permute-start.4 = (bf16[8,2,160,128]{3,2,1,0:T(8,128)(2,1)}, bf16[8,2,160,128]{3,2,1,0:T(8,128)(2,1)S(1)}, u32[]{:S(2)}, u32[]{:S(2)}) collective-permute-start(bf16[8,2,160,128]{3,2,1,0:T(8,128)(2,1)} %get-tuple-element.23), channel_id=1, source_target_pairs={{0,1},{1,0},{2,3},{3,2},{4,5},{5,4},{6,7},{7,6},{8,9},{9,8},{10,11... | collective-permute-start | bytes 1966088 | tf_op jit(solution)/shard_map/ppermute | solution.py:34
  134.7 15.1 %collective-permute-start.1 = (bf16[144,256]{1,0:T(8,128)(2,1)S(1)}, bf16[144,256]{1,0:T(8,128)(2,1)S(1)}, u32[]{:S(2)}, u32[]{:S(2)}) collective-permute-start(bf16[144,256]{1,0:T(8,128)(2,1)S(1)} %get-tuple-element.20.q0), channel_id=1, source_target_pairs={{0,64},{64,0},{128,192},{192,128},{1,65},{65,1},{129,193},{193,129... | collective-permute-start | bytes 221192 | tf_op jit(solution)/shard_map/ppermute | solution.py:34
  137.8 12.0 %collective-permute-start.2 = (bf16[144,256]{1,0:T(8,128)(2,1)S(1)}, bf16[144,256]{1,0:T(8,128)(2,1)S(1)}, u32[]{:S(2)}, u32[]{:S(2)}) collective-permute-start(bf16[144,256]{1,0:T(8,128)(2,1)S(1)} %get-tuple-element.20.q0), channel_id=1, source_target_pairs={{0,192},{64,128},{128,64},{192,0},{1,193},{65,129},{129,65},{193,1... | collective-permute-start | bytes 221192 | tf_op jit(solution)/shard_map/ppermute | solution.py:34
  140.9 13.7 %collective-permute-start.3 = (bf16[144,256]{1,0:T(8,128)(2,1)S(1)}, bf16[144,256]{1,0:T(8,128)(2,1)S(1)}, u32[]{:S(2)}, u32[]{:S(2)}) collective-permute-start(bf16[144,256]{1,0:T(8,128)(2,1)S(1)} %get-tuple-element.20.q0), channel_id=1, source_target_pairs={{0,128},{64,192},{128,0},{192,64},{1,129},{65,193},{129,1},{193,65... | collective-permute-start | bytes 221192 | tf_op jit(solution)/shard_map/ppermute | solution.py:34
  168.2 4.7 %collective-permute-start.5 = (bf16[128,256]{1,0:T(8,128)(2,1)S(1)}, bf16[128,256]{1,0:T(8,128)(2,1)S(1)}, u32[]{:S(2)}, u32[]{:S(2)}) collective-permute-start(bf16[128,256]{1,0:T(8,128)(2,1)S(1)} %merge.1.own), channel_id=1, source_target_pairs={{0,1},{1,0},{2,3},{3,2},{4,5},{5,4},{6,7},{7,6},{8,9},{9,8},{10,11... | collective-permute-start | bytes 196616 | tf_op jit(solution)/shard_map/ppermute | solution.py:34
Sparse Core Ops, SparseCore 0:
  25.1 76.9 all-gather.3

commit v10 on v9

--- a/solution.py
+++ b/solution.py
@@ -170,12 +170,12 @@
     out[...] = value.astype(BF16)
 
 
-def partial_kernel(own, other, w_own, w_other, messages):
+def partial_kernel(own, other, w, messages):
     both = jnp.concatenate([own[...], other[...]], axis=0)
     for x in range(4):
         for z in range(4):
             block, low = 2 * z + x // 2, x % 2
-            weights = jnp.concatenate([w_own[block, low], w_other[block, low]], axis=1)
+            weights = jnp.concatenate([w[block, 0, low], w[block, 1, low]], axis=1)
             messages[x, z] = jnp.dot(weights, both, preferred_element_type=F32).astype(BF16)
 
 
@@ -207,8 +207,8 @@
     local = jnp.concatenate([jnp.transpose(w_qkv, (1, 0, 2)), w_out.T[None]], axis=0)
     pair = lax.all_gather(local, "zh", axis=0, tiled=False)
 
-    w_all = lax.all_gather(pair, ("ya", "yb", "yc"), axis=0, tiled=False)
-    w_all = w_all.reshape(8, 2, 4, 2, 160, 128)
+    w_all = lax.all_gather(pair[:, :3], ("ya", "yb", "yc"), axis=0, tiled=False)
+    w_all = w_all.reshape(8, 2, 3, 2, 160, 128)
 
     x_t = hidden_in.T.astype(F32)
     sums = jnp.stack([jnp.sum(x_t, axis=0), jnp.sum(x_t * x_t, axis=0)]).reshape(4, 128)
@@ -240,6 +240,14 @@
     normed = (x_t - mean_value) * lax.rsqrt(variance + EPSILON)
     packet = (normed * (1.0 + modulation[1]) + modulation[0]).astype(BF16)
 
+    core = lax.axis_index("c")
+    wo_pair = pair[:, 3].reshape(2, 2, 160, 128)
+    wo_own = lax.dynamic_index_in_dim(wo_pair, core, axis=1, keepdims=False)
+    wo_give = lax.dynamic_index_in_dim(wo_pair, 1 - core, axis=1, keepdims=False)
+    packet, wo_own, wo_give = lax.optimization_barrier((packet, wo_own, wo_give))
+    wo_other = permute(wo_give, ("c",), lambda c: (1 - c,))
+    wo_all = lax.all_gather(jnp.stack([wo_own, wo_other]), ("ya", "yb", "yc"), axis=0, tiled=False)
+
     held = spread(spread(packet, ("zl",)), ("xh", "xl"))
     theirs = permute(held, ("c",), lambda c: (1 - c,))
 
@@ -252,11 +260,6 @@
         cost=pl.CostEstimate(flops=2 * 256 * 5120 * 384, bytes_accessed=6 << 20, transcendentals=0),
     )
     stats = exchange(stats, TP)
-    core = lax.axis_index("c")
-    wo_own = lax.dynamic_index_in_dim(w_all[:, :, 3], core, axis=2, keepdims=False)
-    wo_other = lax.dynamic_index_in_dim(w_all[:, :, 3], 1 - core, axis=2, keepdims=False)
-    stats, wo_own, wo_other = lax.optimization_barrier((stats, wo_own, wo_other))
-    wo_other = permute(wo_other, ("c",), lambda c: (1 - c,))
     q_message, k_cache, v_cache, kv_message = call(
         functools.partial(rotate_kernel, heads_width),
         (
@@ -269,7 +272,6 @@
         name="rotate",
     )
     keys = exchange(kv_message, ("ya", "zh"))
-    keys, wo_own, wo_other = lax.optimization_barrier((keys, wo_own, wo_other))
     order = (0, 1, 3, 2)
     queries = [q_message] + [
         permute(q_message, ("yb", "yc"), lambda yb, yc, d=d: (yb ^ (d >> 1), yc ^ (d & 1)))
@@ -288,7 +290,7 @@
     )
     other = permute(own, ("c",), lambda c: (1 - c,))
     partials = call(
-        partial_kernel, shaped((4, 4, 160, 256), BF16), [own, other, wo_own, wo_other], name="partial"
+        partial_kernel, shaped((4, 4, 160, 256), BF16), [own, other, wo_all], name="partial"
     )
     partials = call(
         along_x_kernel,

time: 214 us -> 208 us (0.972)
  waiting for transfers between devices: 41.2 us -> 34.1 us
    all_gather x1 -> x2, waiting for transfers between devices: 13.3 us -> 0.04 us  [the longest x1 0.02 us: body(): lax.all_gather(jnp.stack([wo_own, wo_other]), ('ya', 'yb', 'yc'), axis=0,...]
    ppermute x6, waiting for transfers between devices: 10.4 us -> 18.1 us  [permute(): return lax.ppermute(value, axes, pairs)]
  transfers between devices with their start and end apart: 10 -> 11, of which waited for: 8 -> 7; matrix products, arithmetic and copies ran while one was open for 2% -> 2% of each run, Pallas kernels for 0% -> 4%
where the time goes in v10:
time: 208 us; the launch traced here: 207 us
  blocking collectives  91.7 us (44%)
  starting transfers between devices  49.5 us (24%)
  waiting for transfers between devices  34.1 us (16%)
  between operations  14.3 us (7%)
  Pallas kernels  8.94 us (4%)
  other arithmetic  4.23 us (2%)
  local copies, waits for them, and re-layouts  3.7 us (2%)
    all_to_all x5, blocking collectives, exchange(): return lax.all_to_all(value, axes, 0, 0, tiled=True)  74.9 us
    all_to_all x3, starting transfers between devices, exchange(): return lax.all_to_all(value, axes, 0, 0, tiled=True)  31.4 us
    ppermute x6, waiting for transfers between devices, permute(): return lax.ppermute(value, axes, pairs)  18.1 us
    ppermute x6, starting transfers between devices, permute(): return lax.ppermute(value, axes, pairs)  18.1 us
    all_gather x1, blocking collectives, body(): pair = lax.all_gather(local, 'zh', axis=0, tiled=False)  16.8 us
    all_to_all x3, waiting for transfers between devices, exchange(): return lax.all_to_all(value, axes, 0, 0, tiled=True)  15.9 us
    pallas_call x6, Pallas kernels, call(): pl.pallas_call(kernel, out_shape=out_shape, in_specs=specs, out_specs=jax...  8.94 us
  transfers between devices with their start and end apart: 11, of which 7 were waited for; matrix products, arithmetic and copies ran while one was open for 2% of the time, Pallas kernels for 4%

profile of v10, /device:TPU:1, one launch (start us, length us, event | category | flops | bytes accessed | tf_op | source)
XLA Modules:
  0.0 206.9 jit_solution(3421282563209008939)
XLA Ops:
  8.2 16.8 %all-gather = bf16[8,320,128]{2,1,0:T(8,128)(2,1)S(1)} all-gather(bf16[4,320,128]{2,1,0:T(8,128)(2,1)S(1)} %pad_maximum_fusion), channel_id=2, replica_groups=mesh['ya'=2,'yb'=2,'yc'=2,'zh'=2,'zl'=4,'xh'=2,'xl'=2,'c'=2] {'zh'}, dimensions={0}, use_global_device_ids=true | all-gather | bytes 983040 | tf_op jit(solution)/shard_map/all_gather | solution.py:208
  26.7 15.6 %all-to-all-start = ((f32[32,8,128]{2,1,0:T(8,128)}), f32[32,8,128]{2,1,0:T(8,128)S(1)}, u32[]{:S(2)}, u32[]{:S(2)}) async-start(f32[32,8,128]{2,1,0:T(8,128)} %broadcast_in_dim.16), calls=%async_computation | async-start | bytes 262144 | tf_op jit(solution)/shard_map/all_to_all | solution.py:191
  43.0 7.9 %all-to-all-done = f32[32,8,128]{2,1,0:T(8,128)S(1)} async-done(((f32[32,8,128]{2,1,0:T(8,128)}), f32[32,8,128]{2,1,0:T(8,128)S(1)}, u32[]{:S(2)}, u32[]{:S(2)}) %all-to-all-start) | async-done | bytes 131104 | tf_op jit(solution)/shard_map/all_to_all | solution.py:191
  51.0 12.5 %all_to_all.40 = bf16[4,160,256]{2,1,0:T(8,128)(2,1)S(1)} all-to-all(bf16[4,160,256]{2,1,0:T(8,128)(2,1)S(1)} %broadcast_in_dim.35), channel_id=1, replica_groups=mesh['ya'=2,'yb'=2,'yc'=2,'zh'=2,'zl'=4,'xh'=2,'xl'=2,'c'=2] {'zl'}, dimensions={0} | all-to-all | bytes 655360 | tf_op jit(solution)/shard_map/all_to_all | solution.py:191
  63.6 19.4 %all_to_all.41.mine = bf16[4,4,160,256]{3,2,1,0:T(8,128)(2,1)S(1)} all-to-all(bf16[4,4,160,256]{3,2,1,0:T(8,128)(2,1)S(1)} %broadcast_in_dim.36), channel_id=1, replica_groups=mesh['ya'=2,'yb'=2,'yc'=2,'zh'=2,'zl'=4,'xh'=2,'xl'=2,'c'=2] {'xh','xl'}, dimensions={0} | all-to-all | bytes 2621440 | tf_op jit(solution)/shard_map/all_to_all | solution.py:191
  83.0 3.9 %collective-permute-start = (bf16[4,4,160,256]{3,2,1,0:T(8,128)(2,1)S(1)}, bf16[4,4,160,256]{3,2,1,0:T(8,128)(2,1)S(1)}, u32[]{:S(2)}, u32[]{:S(2)}) collective-permute-start(bf16[4,4,160,256]{3,2,1,0:T(8,128)(2,1)S(1)} %all_to_all.41.mine), channel_id=1, source_target_pairs={{0,1},{1,0},{2,3},{3,2},{4,5},{5,4},{6,7},{7,6},{8,9},{9,8},{10,11... | collective-permute-start | bytes 3932168 | tf_op jit(solution)/shard_map/ppermute | solution.py:34
  87.2 1.9 collective-permute-start.5
  91.2 4.7 %project.1 = (f32[128,256]{1,0:T(8,128)S(1)}, f32[2,128,256]{2,1,0:T(8,128)S(1)}, f32[32,8,128]{2,1,0:T(8,128)}) custom-call(s32[2]{0:T(128)S(1)} %pad_add_fusion.at, bf16[4,4,160,256]{3,2,1,0:T(8,128)(2,1)S(1)} %all_to_all.41.mine, bf16[4,4,160,256]{3,2,1,0:T(8,128)(2,1)S(1)} %collective-permute-done.theirs, bf16[8,2,3,2,160,128]{5,4,3,2,1,0:T(8,128)(2,1)} %bitcast.61), custom_call_target="tpu_custom_call" | custom-call | flops 1006632960 | bytes 6291456 | tf_op jit(solution)/shard_map/project/pallas_call | solution.py:46
  95.9 7.7 %all-to-all-start.3 = ((f32[32,8,128]{2,1,0:T(8,128)}), f32[32,8,128]{2,1,0:T(8,128)S(1)}, u32[]{:S(2)}, u32[]{:S(2)}) async-start(f32[32,8,128]{2,1,0:T(8,128)} %get-tuple-element.14), calls=%async_computation.3 | async-start | bytes 262144 | tf_op jit(solution)/shard_map/all_to_all | solution.py:191
  104.2 8.0 %all-to-all-done.3.got = f32[32,8,128]{2,1,0:T(8,128)S(1)} async-done(((f32[32,8,128]{2,1,0:T(8,128)}), f32[32,8,128]{2,1,0:T(8,128)S(1)}, u32[]{:S(2)}, u32[]{:S(2)}) %all-to-all-start.3) | async-done | bytes 131104 | tf_op jit(solution)/shard_map/all_to_all | solution.py:191
  112.2 1.1 rotate.1
  113.3 8.1 %all-to-all-start.4 = ((bf16[4,272,256]{2,1,0:T(8,128)(2,1)}), bf16[4,272,256]{2,1,0:T(8,128)(2,1)S(1)}, u32[]{:S(2)}, u32[]{:S(2)}) async-start(bf16[4,272,256]{2,1,0:T(8,128)(2,1)} %get-tuple-element.18), calls=%async_computation.4 | async-start | bytes 1114112 | tf_op jit(solution)/shard_map/all_to_all | solution.py:191
  121.3 2.2 %collective-permute-start.1 = (bf16[144,256]{1,0:T(8,128)(2,1)S(1)}, bf16[144,256]{1,0:T(8,128)(2,1)S(1)}, u32[]{:S(2)}, u32[]{:S(2)}) collective-permute-start(bf16[144,256]{1,0:T(8,128)(2,1)S(1)} %get-tuple-element.17.q0), channel_id=1, source_target_pairs={{0,64},{64,0},{128,192},{192,128},{1,65},{65,1},{129,193},{193,129... | collective-permute-start | bytes 221192 | tf_op jit(solution)/shard_map/ppermute | solution.py:34
  123.5 3.2 %collective-permute-start.2 = (bf16[144,256]{1,0:T(8,128)(2,1)S(1)}, bf16[144,256]{1,0:T(8,128)(2,1)S(1)}, u32[]{:S(2)}, u32[]{:S(2)}) collective-permute-start(bf16[144,256]{1,0:T(8,128)(2,1)S(1)} %get-tuple-element.17.q0), channel_id=1, source_target_pairs={{0,192},{64,128},{128,64},{192,0},{1,193},{65,129},{129,65},{193,1... | collective-permute-start | bytes 221192 | tf_op jit(solution)/shard_map/ppermute | solution.py:34
  126.8 3.0 %collective-permute-start.3 = (bf16[144,256]{1,0:T(8,128)(2,1)S(1)}, bf16[144,256]{1,0:T(8,128)(2,1)S(1)}, u32[]{:S(2)}, u32[]{:S(2)}) collective-permute-start(bf16[144,256]{1,0:T(8,128)(2,1)S(1)} %get-tuple-element.17.q0), channel_id=1, source_target_pairs={{0,128},{64,192},{128,0},{192,64},{1,129},{65,193},{129,1},{193,65... | collective-permute-start | bytes 221192 | tf_op jit(solution)/shard_map/ppermute | solution.py:34
  129.7 12.4 %collective-permute-done.1.q1 = bf16[144,256]{1,0:T(8,128)(2,1)S(1)} collective-permute-done((bf16[144,256]{1,0:T(8,128)(2,1)S(1)}, bf16[144,256]{1,0:T(8,128)(2,1)S(1)}, u32[]{:S(2)}, u32[]{:S(2)}) %collective-permute-start.1) | collective-permute-done | bytes 73760 | tf_op jit(solution)/shard_map/ppermute | solution.py:34
  143.2 3.0 %collective-permute-done.3.q3 = bf16[144,256]{1,0:T(8,128)(2,1)S(1)} collective-permute-done((bf16[144,256]{1,0:T(8,128)(2,1)S(1)}, bf16[144,256]{1,0:T(8,128)(2,1)S(1)}, u32[]{:S(2)}, u32[]{:S(2)}) %collective-permute-start.3) | collective-permute-done | bytes 73760 | tf_op jit(solution)/shard_map/ppermute | solution.py:34
  146.2 2.4 %attend.1 = bf16[4,144,256]{2,1,0:T(8,128)(2,1)S(1)} custom-call(s32[2]{0:T(128)S(1)} %pad_add_fusion.at, bf16[144,256]{1,0:T(8,128)(2,1)S(1)} %get-tuple-element.17.q0, bf16[144,256]{1,0:T(8,128)(2,1)S(1)} %collective-permute-done.1.q1, bf16[144,256]{1,0:T(8,128)(2,1)S(1)} %collective-permute-done.2.q2, bf16[144,256]{1,0:T(8,128)(2,1)S(1)} %collective-permute-done.3.q3, ...), custom_call_target="tpu_custom_call" | custom-call | tf_op jit(solution)/shard_map/attend/pallas_call | solution.py:46
  148.6 11.4 %all_to_all.42.got = bf16[4,144,256]{2,1,0:T(8,128)(2,1)S(1)} all-to-all(bf16[4,144,256]{2,1,0:T(8,128)(2,1)S(1)} %attend.1), channel_id=1, replica_groups=mesh['ya'=2,'yb'=2,'yc'=2,'zh'=2,'zl'=4,'xh'=2,'xl'=2,'c'=2] {'yb','yc'}, dimensions={0} | all-to-all | bytes 589824 | tf_op jit(solution)/shard_map/all_to_all | solution.py:191
  160.1 3.8 %collective-permute-start.4 = (bf16[128,256]{1,0:T(8,128)(2,1)S(1)}, bf16[128,256]{1,0:T(8,128)(2,1)S(1)}, u32[]{:S(2)}, u32[]{:S(2)}) collective-permute-start(bf16[128,256]{1,0:T(8,128)(2,1)S(1)} %merge.1.own), channel_id=1, source_target_pairs={{0,1},{1,0},{2,3},{3,2},{4,5},{5,4},{6,7},{7,6},{8,9},{9,8},{10,11... | collective-permute-start | bytes 196616 | tf_op jit(solution)/shard_map/ppermute | solution.py:34
  164.9 1.3 copy-done
  166.7 19.5 %all_to_all.43.got = bf16[4,4,160,256]{3,2,1,0:T(8,128)(2,1)S(1)} all-to-all(bf16[4,4,160,256]{3,2,1,0:T(8,128)(2,1)S(1)} %partial.1), channel_id=1, replica_groups=mesh['ya'=2,'yb'=2,'yc'=2,'zh'=2,'zl'=4,'xh'=2,'xl'=2,'c'=2] {'xh','xl'}, dimensions={0} | all-to-all | bytes 2621440 | tf_op jit(solution)/shard_map/all_to_all | solution.py:191
  186.4 12.1 %all_to_all.44 = bf16[4,160,256]{2,1,0:T(8,128)(2,1)S(1)} all-to-all(bf16[4,160,256]{2,1,0:T(8,128)(2,1)S(1)} %along_x.1), channel_id=1, replica_groups=mesh['ya'=2,'yb'=2,'yc'=2,'zh'=2,'zl'=4,'xh'=2,'xl'=2,'c'=2] {'zl'}, dimensions={0} | all-to-all | bytes 655360 | tf_op jit(solution)/shard_map/all_to_all | solution.py:191
  198.5 1.6 fusion.11
  (65 shorter events, 9.1 us)
Async XLA Ops:
  7.2 84.1 %all-gather.6.cloned.1.call-start = ((), (), s32[]{:S(2)}) async-start(), calls=%async_computation.8 | async-start | bytes 4423680 | tf_op jit(solution)/shard_map/all_gather | solution.py:210
  8.2 17.7 %copy-start.2 = (bf16[256,160]{0,1:T(8,128)(2,1)S(1)}, bf16[256,160]{0,1:T(8,128)(2,1)}, u32[]{:S(2)}) copy-start(bf16[256,160]{0,1:T(8,128)(2,1)} %param.8) | copy-start | bytes 245764
  25.0 17.4 %copy-start.3 = (f32[4,3,160]{2,0,1:T(4,128)S(1)}, f32[4,3,160]{2,0,1:T(4,128)}, u32[]{:S(2)}) copy-start(f32[4,3,160]{2,0,1:T(4,128)} %param.11) | copy-start | bytes 23044
  25.0 17.5 %copy-start.4 = (s32[256]{0:T(256)S(1)}, s32[256]{0:T(256)}, u32[]{:S(2)}) copy-start(s32[256]{0:T(256)} %param.9) | copy-start | bytes 3076
  26.7 24.2 %all-to-all-start = ((f32[32,8,128]{2,1,0:T(8,128)}), f32[32,8,128]{2,1,0:T(8,128)S(1)}, u32[]{:S(2)}, u32[]{:S(2)}) async-start(f32[32,8,128]{2,1,0:T(8,128)} %broadcast_in_dim.16), calls=%async_computation | async-start | bytes 262144 | tf_op jit(solution)/shard_map/all_to_all | solution.py:191
  42.3 121.7 %all-gather.8.cloned.1.call-start = ((), (), s32[]{:S(2)}) async-start(), calls=%async_computation.9 | async-start | bytes 1474560 | tf_op jit(solution)/shard_map/all_gather | solution.py:249
  43.0 20.5 %copy-start.1 = (f32[480,256]{1,0:T(8,128)}, f32[480,256]{1,0:T(8,128)S(1)}, u32[]{:S(2)}) copy-start(f32[480,256]{1,0:T(8,128)S(1)} %convolution_bitcast_fusion) | copy-start | bytes 1474564
  63.6 25.7 %copy-start.6 = (f32[128]{0:T(128)S(1)}, f32[128]{0:T(128)}, u32[]{:S(2)}) copy-start(f32[128]{0:T(128)} %param.13) | copy-start | bytes 1540
  63.6 25.8 %copy-start.7 = (f32[128]{0:T(128)S(1)}, f32[128]{0:T(128)}, u32[]{:S(2)}) copy-start(f32[128]{0:T(128)} %param.14) | copy-start | bytes 1540
  63.6 27.5 %copy-start.5 = (s32[3,256]{1,0:T(4,128)S(1)}, s32[3,256]{1,0:T(4,128)}, u32[]{:S(2)}) copy-start(s32[3,256]{1,0:T(4,128)} %param.10) | copy-start | bytes 9220
  83.0 8.2 %collective-permute-start = (bf16[4,4,160,256]{3,2,1,0:T(8,128)(2,1)S(1)}, bf16[4,4,160,256]{3,2,1,0:T(8,128)(2,1)S(1)}, u32[]{:S(2)}, u32[]{:S(2)}) collective-permute-start(bf16[4,4,160,256]{3,2,1,0:T(8,128)(2,1)S(1)} %all_to_all.41.mine), channel_id=1, source_target_pairs={{0,1},{1,0},{2,3},{3,2},{4,5},{5,4},{6,7},{7,6},{8,9},{9,8},{10,11... | collective-permute-start | bytes 3932168 | tf_op jit(solution)/shard_map/ppermute | solution.py:34
  87.2 3.2 %collective-permute-start.5 = (bf16[2,160,128]{2,1,0:T(8,128)(2,1)S(1)}, bf16[2,160,128]{2,1,0:T(8,128)(2,1)S(1)}, u32[]{:S(2)}, u32[]{:S(2)}) collective-permute-start(bf16[2,160,128]{2,1,0:T(8,128)(2,1)S(1)} %get-tuple-element.20), channel_id=1, source_target_pairs={{0,1},{1,0},{2,3},{3,2},{4,5},{5,4},{6,7},{7,6},{8,9},{9,8},{10,11... | collective-permute-start | bytes 245768 | tf_op jit(solution)/shard_map/ppermute | solution.py:34
  95.9 16.2 %all-to-all-start.3 = ((f32[32,8,128]{2,1,0:T(8,128)}), f32[32,8,128]{2,1,0:T(8,128)S(1)}, u32[]{:S(2)}, u32[]{:S(2)}) async-start(f32[32,8,128]{2,1,0:T(8,128)} %get-tuple-element.14), calls=%async_computation.3 | async-start | bytes 262144 | tf_op jit(solution)/shard_map/all_to_all | solution.py:191
  113.3 32.9 %all-to-all-start.4 = ((bf16[4,272,256]{2,1,0:T(8,128)(2,1)}), bf16[4,272,256]{2,1,0:T(8,128)(2,1)S(1)}, u32[]{:S(2)}, u32[]{:S(2)}) async-start(bf16[4,272,256]{2,1,0:T(8,128)(2,1)} %get-tuple-element.18), calls=%async_computation.4 | async-start | bytes 1114112 | tf_op jit(solution)/shard_map/all_to_all | solution.py:191
  121.3 20.8 %collective-permute-start.1 = (bf16[144,256]{1,0:T(8,128)(2,1)S(1)}, bf16[144,256]{1,0:T(8,128)(2,1)S(1)}, u32[]{:S(2)}, u32[]{:S(2)}) collective-permute-start(bf16[144,256]{1,0:T(8,128)(2,1)S(1)} %get-tuple-element.17.q0), channel_id=1, source_target_pairs={{0,64},{64,0},{128,192},{192,128},{1,65},{65,1},{129,193},{193,129... | collective-permute-start | bytes 221192 | tf_op jit(solution)/shard_map/ppermute | solution.py:34
  123.5 19.6 %collective-permute-start.2 = (bf16[144,256]{1,0:T(8,128)(2,1)S(1)}, bf16[144,256]{1,0:T(8,128)(2,1)S(1)}, u32[]{:S(2)}, u32[]{:S(2)}) collective-permute-start(bf16[144,256]{1,0:T(8,128)(2,1)S(1)} %get-tuple-element.17.q0), channel_id=1, source_target_pairs={{0,192},{64,128},{128,64},{192,0},{1,193},{65,129},{129,65},{193,1... | collective-permute-start | bytes 221192 | tf_op jit(solution)/shard_map/ppermute | solution.py:34
  126.8 19.4 %collective-permute-start.3 = (bf16[144,256]{1,0:T(8,128)(2,1)S(1)}, bf16[144,256]{1,0:T(8,128)(2,1)S(1)}, u32[]{:S(2)}, u32[]{:S(2)}) collective-permute-start(bf16[144,256]{1,0:T(8,128)(2,1)S(1)} %get-tuple-element.17.q0), channel_id=1, source_target_pairs={{0,128},{64,192},{128,0},{192,64},{1,129},{65,193},{129,1},{193,65... | collective-permute-start | bytes 221192 | tf_op jit(solution)/shard_map/ppermute | solution.py:34
  160.1 4.7 %collective-permute-start.4 = (bf16[128,256]{1,0:T(8,128)(2,1)S(1)}, bf16[128,256]{1,0:T(8,128)(2,1)S(1)}, u32[]{:S(2)}, u32[]{:S(2)}) collective-permute-start(bf16[128,256]{1,0:T(8,128)(2,1)S(1)} %merge.1.own), channel_id=1, source_target_pairs={{0,1},{1,0},{2,3},{3,2},{4,5},{5,4},{6,7},{7,6},{8,9},{9,8},{10,11... | collective-permute-start | bytes 196616 | tf_op jit(solution)/shard_map/ppermute | solution.py:34
  164.9 1.3 copy-start
Sparse Core Ops, SparseCore 0:
  26.0 64.5 all-gather.5
  92.7 43.5 all-gather.7

commit v11 on v10

--- a/solution.py
+++ b/solution.py
@@ -149,7 +149,7 @@
     ).astype(BF16)
     for place, d in enumerate(order):
         here = slice(256 * place, 256 * place + 256)
-        target = jnp.bitwise_xor(at[1], d)
+        target = lax.rem(at[1] + 4 - d, 4)
         messages[target, :128] = out[:, here].astype(BF16)
         messages[target, 128:144] = rows[:, here]
 
@@ -201,12 +201,11 @@
     model_width = feat_local * 32
     heads_width = 4096
     at = jnp.stack(
-        [lax.axis_index("c"), lax.axis_index("yb") * 2 + lax.axis_index("yc")]
+        [lax.axis_index("c"), lax.axis_index("ya") * 2 + lax.axis_index("yb")]
     ).astype(jnp.int32)
 
     local = jnp.concatenate([jnp.transpose(w_qkv, (1, 0, 2)), w_out.T[None]], axis=0)
     pair = lax.all_gather(local, "zh", axis=0, tiled=False)
-
     w_all = lax.all_gather(pair[:, :3], ("ya", "yb", "yc"), axis=0, tiled=False)
     w_all = w_all.reshape(8, 2, 3, 2, 160, 128)
 
@@ -271,10 +270,10 @@
         [stats, query, key_value, cosine, sine, q_gain.reshape(128, 1), k_gain.reshape(128, 1), marks],
         name="rotate",
     )
-    keys = exchange(kv_message, ("ya", "zh"))
+    keys = exchange(kv_message, ("yc", "zh"))
     order = (0, 1, 3, 2)
     queries = [q_message] + [
-        permute(q_message, ("yb", "yc"), lambda yb, yc, d=d: (yb ^ (d >> 1), yc ^ (d & 1)))
+        permute(q_message, ("ya", "yb"), lambda ya, yb, d=d: divmod((ya * 2 + yb + d) % 4, 2))
         for d in order[1:]
     ]
     o_messages = call(
@@ -286,7 +285,7 @@
         name="attend",
     )
     own = call(
-        merge_kernel, shaped((128, 256), BF16), [exchange(o_messages, ("yb", "yc"))], name="merge"
+        merge_kernel, shaped((128, 256), BF16), [exchange(o_messages, ("ya", "yb"))], name="merge"
     )
     other = permute(own, ("c",), lambda c: (1 - c,))
     partials = call(

time: 208 us -> 205 us (0.986)
  waiting for transfers between devices: 34.1 us -> 26 us
  starting transfers between devices: 49.5 us -> 53 us
    ppermute x6, waiting for transfers between devices: 18.1 us -> 10 us  [permute(): return lax.ppermute(value, axes, pairs)]
    ppermute x6, starting transfers between devices: 18.1 us -> 25.2 us  [permute(): return lax.ppermute(value, axes, pairs)]
    all_to_all x3, starting transfers between devices: 31.4 us -> 27.7 us  [exchange(): return lax.all_to_all(value, axes, 0, 0, tiled=True)]
  transfers between devices with their start and end apart: 11 -> 11, of which waited for: 7 -> 6; matrix products, arithmetic and copies ran while one was open for 2% -> 2% of each run, Pallas kernels for 4% -> 4%
where the time goes in v11:
time: 205 us; the launch traced here: 203 us
  blocking collectives  92.8 us (45%)
  starting transfers between devices  53 us (26%)
  waiting for transfers between devices  26 us (13%)
  between operations  14.3 us (7%)
  Pallas kernels  9.04 us (4%)
  other arithmetic  4.23 us (2%)
  local copies, waits for them, and re-layouts  3.7 us (2%)
    all_to_all x5, blocking collectives, exchange(): return lax.all_to_all(value, axes, 0, 0, tiled=True)  76 us
    all_to_all x3, starting transfers between devices, exchange(): return lax.all_to_all(value, axes, 0, 0, tiled=True)  27.7 us
    ppermute x6, starting transfers between devices, permute(): return lax.ppermute(value, axes, pairs)  25.2 us
    all_gather x1, blocking collectives, body(): pair = lax.all_gather(local, 'zh', axis=0, tiled=False)  16.8 us
    all_to_all x3, waiting for transfers between devices, exchange(): return lax.all_to_all(value, axes, 0, 0, tiled=True)  15.9 us
    ppermute x6, waiting for transfers between devices, permute(): return lax.ppermute(value, axes, pairs)  10 us
    pallas_call x6, Pallas kernels, call(): pl.pallas_call(kernel, out_shape=out_shape, in_specs=specs, out_specs=jax...  9.04 us
  transfers between devices with their start and end apart: 11, of which 6 were waited for; matrix products, arithmetic and copies ran while one was open for 2% of the time, Pallas kernels for 4%

profile of v11, /device:TPU:1, one launch (start us, length us, event | category | flops | bytes accessed | tf_op | source)
XLA Modules:
  0.0 203.5 jit_solution(15694991710994378448)
XLA Ops:
  8.2 16.8 %all-gather = bf16[8,320,128]{2,1,0:T(8,128)(2,1)S(1)} all-gather(bf16[4,320,128]{2,1,0:T(8,128)(2,1)S(1)} %pad_maximum_fusion), channel_id=2, replica_groups=mesh['ya'=2,'yb'=2,'yc'=2,'zh'=2,'zl'=4,'xh'=2,'xl'=2,'c'=2] {'zh'}, dimensions={0}, use_global_device_ids=true | all-gather | bytes 983040 | tf_op jit(solution)/shard_map/all_gather | solution.py:208
  26.7 15.6 %all-to-all-start = ((f32[32,8,128]{2,1,0:T(8,128)}), f32[32,8,128]{2,1,0:T(8,128)S(1)}, u32[]{:S(2)}, u32[]{:S(2)}) async-start(f32[32,8,128]{2,1,0:T(8,128)} %broadcast_in_dim.16), calls=%async_computation | async-start | bytes 262144 | tf_op jit(solution)/shard_map/all_to_all | solution.py:191
  43.0 7.9 %all-to-all-done = f32[32,8,128]{2,1,0:T(8,128)S(1)} async-done(((f32[32,8,128]{2,1,0:T(8,128)}), f32[32,8,128]{2,1,0:T(8,128)S(1)}, u32[]{:S(2)}, u32[]{:S(2)}) %all-to-all-start) | async-done | bytes 131104 | tf_op jit(solution)/shard_map/all_to_all | solution.py:191
  51.0 12.5 %all_to_all.40 = bf16[4,160,256]{2,1,0:T(8,128)(2,1)S(1)} all-to-all(bf16[4,160,256]{2,1,0:T(8,128)(2,1)S(1)} %broadcast_in_dim.35), channel_id=1, replica_groups=mesh['ya'=2,'yb'=2,'yc'=2,'zh'=2,'zl'=4,'xh'=2,'xl'=2,'c'=2] {'zl'}, dimensions={0} | all-to-all | bytes 655360 | tf_op jit(solution)/shard_map/all_to_all | solution.py:191
  63.6 19.4 %all_to_all.41.mine = bf16[4,4,160,256]{3,2,1,0:T(8,128)(2,1)S(1)} all-to-all(bf16[4,4,160,256]{3,2,1,0:T(8,128)(2,1)S(1)} %broadcast_in_dim.36), channel_id=1, replica_groups=mesh['ya'=2,'yb'=2,'yc'=2,'zh'=2,'zl'=4,'xh'=2,'xl'=2,'c'=2] {'xh','xl'}, dimensions={0} | all-to-all | bytes 2621440 | tf_op jit(solution)/shard_map/all_to_all | solution.py:191
  83.0 3.9 %collective-permute-start = (bf16[4,4,160,256]{3,2,1,0:T(8,128)(2,1)S(1)}, bf16[4,4,160,256]{3,2,1,0:T(8,128)(2,1)S(1)}, u32[]{:S(2)}, u32[]{:S(2)}) collective-permute-start(bf16[4,4,160,256]{3,2,1,0:T(8,128)(2,1)S(1)} %all_to_all.41.mine), channel_id=1, source_target_pairs={{0,1},{1,0},{2,3},{3,2},{4,5},{5,4},{6,7},{7,6},{8,9},{9,8},{10,11... | collective-permute-start | bytes 3932168 | tf_op jit(solution)/shard_map/ppermute | solution.py:34
  87.2 1.9 collective-permute-start.5
  91.2 4.7 %project.1 = (f32[128,256]{1,0:T(8,128)S(1)}, f32[2,128,256]{2,1,0:T(8,128)S(1)}, f32[32,8,128]{2,1,0:T(8,128)}) custom-call(s32[2]{0:T(128)S(1)} %pad_add_fusion.at, bf16[4,4,160,256]{3,2,1,0:T(8,128)(2,1)S(1)} %all_to_all.41.mine, bf16[4,4,160,256]{3,2,1,0:T(8,128)(2,1)S(1)} %collective-permute-done.theirs, bf16[8,2,3,2,160,128]{5,4,3,2,1,0:T(8,128)(2,1)} %bitcast.61), custom_call_target="tpu_custom_call" | custom-call | flops 1006632960 | bytes 6291456 | tf_op jit(solution)/shard_map/project/pallas_call | solution.py:46
  95.9 7.7 %all-to-all-start.3 = ((f32[32,8,128]{2,1,0:T(8,128)}), f32[32,8,128]{2,1,0:T(8,128)S(1)}, u32[]{:S(2)}, u32[]{:S(2)}) async-start(f32[32,8,128]{2,1,0:T(8,128)} %get-tuple-element.14), calls=%async_computation.3 | async-start | bytes 262144 | tf_op jit(solution)/shard_map/all_to_all | solution.py:191
  104.2 8.0 %all-to-all-done.3.got = f32[32,8,128]{2,1,0:T(8,128)S(1)} async-done(((f32[32,8,128]{2,1,0:T(8,128)}), f32[32,8,128]{2,1,0:T(8,128)S(1)}, u32[]{:S(2)}, u32[]{:S(2)}) %all-to-all-start.3) | async-done | bytes 131104 | tf_op jit(solution)/shard_map/all_to_all | solution.py:191
  112.2 1.1 rotate.1
  113.3 4.4 %all-to-all-start.4 = ((bf16[4,272,256]{2,1,0:T(8,128)(2,1)}), bf16[4,272,256]{2,1,0:T(8,128)(2,1)S(1)}, u32[]{:S(2)}, u32[]{:S(2)}) async-start(bf16[4,272,256]{2,1,0:T(8,128)(2,1)} %get-tuple-element.18), calls=%async_computation.4 | async-start | bytes 1114112 | tf_op jit(solution)/shard_map/all_to_all | solution.py:191
  117.6 4.8 %collective-permute-start.1 = (bf16[144,256]{1,0:T(8,128)(2,1)S(1)}, bf16[144,256]{1,0:T(8,128)(2,1)S(1)}, u32[]{:S(2)}, u32[]{:S(2)}) collective-permute-start(bf16[144,256]{1,0:T(8,128)(2,1)S(1)} %get-tuple-element.17.q0), channel_id=1, source_target_pairs={{0,128},{128,256},{256,384},{384,0},{1,129},{129,257},{257,385},{3... | collective-permute-start | bytes 221192 | tf_op jit(solution)/shard_map/ppermute | solution.py:34
  122.4 2.6 %collective-permute-start.2 = (bf16[144,256]{1,0:T(8,128)(2,1)S(1)}, bf16[144,256]{1,0:T(8,128)(2,1)S(1)}, u32[]{:S(2)}, u32[]{:S(2)}) collective-permute-start(bf16[144,256]{1,0:T(8,128)(2,1)S(1)} %get-tuple-element.17.q0), channel_id=1, source_target_pairs={{0,384},{128,0},{256,128},{384,256},{1,385},{129,1},{257,129},{385... | collective-permute-start | bytes 221192 | tf_op jit(solution)/shard_map/ppermute | solution.py:34
  125.0 5.9 %collective-permute-start.3 = (bf16[144,256]{1,0:T(8,128)(2,1)S(1)}, bf16[144,256]{1,0:T(8,128)(2,1)S(1)}, u32[]{:S(2)}, u32[]{:S(2)}) collective-permute-start(bf16[144,256]{1,0:T(8,128)(2,1)S(1)} %get-tuple-element.17.q0), channel_id=1, source_target_pairs={{0,256},{128,384},{256,0},{384,128},{1,257},{129,385},{257,1},{385... | collective-permute-start | bytes 221192 | tf_op jit(solution)/shard_map/ppermute | solution.py:34
  130.9 4.3 %collective-permute-done.1.q1 = bf16[144,256]{1,0:T(8,128)(2,1)S(1)} collective-permute-done((bf16[144,256]{1,0:T(8,128)(2,1)S(1)}, bf16[144,256]{1,0:T(8,128)(2,1)S(1)}, u32[]{:S(2)}, u32[]{:S(2)}) %collective-permute-start.1) | collective-permute-done | bytes 73760 | tf_op jit(solution)/shard_map/ppermute | solution.py:34
  135.2 4.1 %collective-permute-done.3.q3 = bf16[144,256]{1,0:T(8,128)(2,1)S(1)} collective-permute-done((bf16[144,256]{1,0:T(8,128)(2,1)S(1)}, bf16[144,256]{1,0:T(8,128)(2,1)S(1)}, u32[]{:S(2)}, u32[]{:S(2)}) %collective-permute-start.3) | collective-permute-done | bytes 73760 | tf_op jit(solution)/shard_map/ppermute | solution.py:34
  139.3 2.5 %attend.1 = bf16[4,144,256]{2,1,0:T(8,128)(2,1)S(1)} custom-call(s32[2]{0:T(128)S(1)} %pad_add_fusion.at, bf16[144,256]{1,0:T(8,128)(2,1)S(1)} %get-tuple-element.17.q0, bf16[144,256]{1,0:T(8,128)(2,1)S(1)} %collective-permute-done.1.q1, bf16[144,256]{1,0:T(8,128)(2,1)S(1)} %collective-permute-done.2.q2, bf16[144,256]{1,0:T(8,128)(2,1)S(1)} %collective-permute-done.3.q3, ...), custom_call_target="tpu_custom_call" | custom-call | tf_op jit(solution)/shard_map/attend/pallas_call | solution.py:46
  141.9 12.5 %all_to_all.42.got = bf16[4,144,256]{2,1,0:T(8,128)(2,1)S(1)} all-to-all(bf16[4,144,256]{2,1,0:T(8,128)(2,1)S(1)} %attend.1), channel_id=1, replica_groups=mesh['ya'=2,'yb'=2,'yc'=2,'zh'=2,'zl'=4,'xh'=2,'xl'=2,'c'=2] {'ya','yb'}, dimensions={0} | all-to-all | bytes 589824 | tf_op jit(solution)/shard_map/all_to_all | solution.py:191
  154.4 6.1 %collective-permute-start.4 = (bf16[128,256]{1,0:T(8,128)(2,1)S(1)}, bf16[128,256]{1,0:T(8,128)(2,1)S(1)}, u32[]{:S(2)}, u32[]{:S(2)}) collective-permute-start(bf16[128,256]{1,0:T(8,128)(2,1)S(1)} %merge.1.own), channel_id=1, source_target_pairs={{0,1},{1,0},{2,3},{3,2},{4,5},{5,4},{6,7},{7,6},{8,9},{9,8},{10,11... | collective-permute-start | bytes 196616 | tf_op jit(solution)/shard_map/ppermute | solution.py:34
  161.3 1.3 copy-done
  163.2 20.3 %all_to_all.43.got = bf16[4,4,160,256]{3,2,1,0:T(8,128)(2,1)S(1)} all-to-all(bf16[4,4,160,256]{3,2,1,0:T(8,128)(2,1)S(1)} %partial.1), channel_id=1, replica_groups=mesh['ya'=2,'yb'=2,'yc'=2,'zh'=2,'zl'=4,'xh'=2,'xl'=2,'c'=2] {'xh','xl'}, dimensions={0} | all-to-all | bytes 2621440 | tf_op jit(solution)/shard_map/all_to_all | solution.py:191
  183.7 11.4 %all_to_all.44 = bf16[4,160,256]{2,1,0:T(8,128)(2,1)S(1)} all-to-all(bf16[4,160,256]{2,1,0:T(8,128)(2,1)S(1)} %along_x.1), channel_id=1, replica_groups=mesh['ya'=2,'yb'=2,'yc'=2,'zh'=2,'zl'=4,'xh'=2,'xl'=2,'c'=2] {'zl'}, dimensions={0} | all-to-all | bytes 655360 | tf_op jit(solution)/shard_map/all_to_all | solution.py:191
  195.1 1.6 fusion.11
  (65 shorter events, 8.1 us)
Async XLA Ops:
  7.2 84.1 %all-gather.6.cloned.1.call-start = ((), (), s32[]{:S(2)}) async-start(), calls=%async_computation.8 | async-start | bytes 4423680 | tf_op jit(solution)/shard_map/all_gather | solution.py:209
  8.2 17.7 %copy-start.2 = (bf16[256,160]{0,1:T(8,128)(2,1)S(1)}, bf16[256,160]{0,1:T(8,128)(2,1)}, u32[]{:S(2)}) copy-start(bf16[256,160]{0,1:T(8,128)(2,1)} %param.8) | copy-start | bytes 245764
  25.0 17.4 %copy-start.3 = (f32[4,3,160]{2,0,1:T(4,128)S(1)}, f32[4,3,160]{2,0,1:T(4,128)}, u32[]{:S(2)}) copy-start(f32[4,3,160]{2,0,1:T(4,128)} %param.11) | copy-start | bytes 23044
  25.0 17.5 %copy-start.4 = (s32[256]{0:T(256)S(1)}, s32[256]{0:T(256)}, u32[]{:S(2)}) copy-start(s32[256]{0:T(256)} %param.9) | copy-start | bytes 3076
  26.7 24.2 %all-to-all-start = ((f32[32,8,128]{2,1,0:T(8,128)}), f32[32,8,128]{2,1,0:T(8,128)S(1)}, u32[]{:S(2)}, u32[]{:S(2)}) async-start(f32[32,8,128]{2,1,0:T(8,128)} %broadcast_in_dim.16), calls=%async_computation | async-start | bytes 262144 | tf_op jit(solution)/shard_map/all_to_all | solution.py:191
  42.3 118.2 %all-gather.8.cloned.1.call-start = ((), (), s32[]{:S(2)}) async-start(), calls=%async_computation.9 | async-start | bytes 1474560 | tf_op jit(solution)/shard_map/all_gather | solution.py:248
  43.0 20.5 %copy-start.1 = (f32[480,256]{1,0:T(8,128)}, f32[480,256]{1,0:T(8,128)S(1)}, u32[]{:S(2)}) copy-start(f32[480,256]{1,0:T(8,128)S(1)} %convolution_bitcast_fusion) | copy-start | bytes 1474564
  63.6 25.7 %copy-start.6 = (f32[128]{0:T(128)S(1)}, f32[128]{0:T(128)}, u32[]{:S(2)}) copy-start(f32[128]{0:T(128)} %param.13) | copy-start | bytes 1540
  63.6 25.8 %copy-start.7 = (f32[128]{0:T(128)S(1)}, f32[128]{0:T(128)}, u32[]{:S(2)}) copy-start(f32[128]{0:T(128)} %param.14) | copy-start | bytes 1540
  63.6 27.5 %copy-start.5 = (s32[3,256]{1,0:T(4,128)S(1)}, s32[3,256]{1,0:T(4,128)}, u32[]{:S(2)}) copy-start(s32[3,256]{1,0:T(4,128)} %param.10) | copy-start | bytes 9220
  83.0 8.2 %collective-permute-start = (bf16[4,4,160,256]{3,2,1,0:T(8,128)(2,1)S(1)}, bf16[4,4,160,256]{3,2,1,0:T(8,128)(2,1)S(1)}, u32[]{:S(2)}, u32[]{:S(2)}) collective-permute-start(bf16[4,4,160,256]{3,2,1,0:T(8,128)(2,1)S(1)} %all_to_all.41.mine), channel_id=1, source_target_pairs={{0,1},{1,0},{2,3},{3,2},{4,5},{5,4},{6,7},{7,6},{8,9},{9,8},{10,11... | collective-permute-start | bytes 3932168 | tf_op jit(solution)/shard_map/ppermute | solution.py:34
  87.2 3.2 %collective-permute-start.5 = (bf16[2,160,128]{2,1,0:T(8,128)(2,1)S(1)}, bf16[2,160,128]{2,1,0:T(8,128)(2,1)S(1)}, u32[]{:S(2)}, u32[]{:S(2)}) collective-permute-start(bf16[2,160,128]{2,1,0:T(8,128)(2,1)S(1)} %get-tuple-element.20), channel_id=1, source_target_pairs={{0,1},{1,0},{2,3},{3,2},{4,5},{5,4},{6,7},{7,6},{8,9},{9,8},{10,11... | collective-permute-start | bytes 245768 | tf_op jit(solution)/shard_map/ppermute | solution.py:34
  95.9 16.2 %all-to-all-start.3 = ((f32[32,8,128]{2,1,0:T(8,128)}), f32[32,8,128]{2,1,0:T(8,128)S(1)}, u32[]{:S(2)}, u32[]{:S(2)}) async-start(f32[32,8,128]{2,1,0:T(8,128)} %get-tuple-element.14), calls=%async_computation.3 | async-start | bytes 262144 | tf_op jit(solution)/shard_map/all_to_all | solution.py:191
  113.3 26.1 %all-to-all-start.4 = ((bf16[4,272,256]{2,1,0:T(8,128)(2,1)}), bf16[4,272,256]{2,1,0:T(8,128)(2,1)S(1)}, u32[]{:S(2)}, u32[]{:S(2)}) async-start(bf16[4,272,256]{2,1,0:T(8,128)(2,1)} %get-tuple-element.18), calls=%async_computation.4 | async-start | bytes 1114112 | tf_op jit(solution)/shard_map/all_to_all | solution.py:191
  117.6 17.6 %collective-permute-start.1 = (bf16[144,256]{1,0:T(8,128)(2,1)S(1)}, bf16[144,256]{1,0:T(8,128)(2,1)S(1)}, u32[]{:S(2)}, u32[]{:S(2)}) collective-permute-start(bf16[144,256]{1,0:T(8,128)(2,1)S(1)} %get-tuple-element.17.q0), channel_id=1, source_target_pairs={{0,128},{128,256},{256,384},{384,0},{1,129},{129,257},{257,385},{3... | collective-permute-start | bytes 221192 | tf_op jit(solution)/shard_map/ppermute | solution.py:34
  122.4 12.8 %collective-permute-start.2 = (bf16[144,256]{1,0:T(8,128)(2,1)S(1)}, bf16[144,256]{1,0:T(8,128)(2,1)S(1)}, u32[]{:S(2)}, u32[]{:S(2)}) collective-permute-start(bf16[144,256]{1,0:T(8,128)(2,1)S(1)} %get-tuple-element.17.q0), channel_id=1, source_target_pairs={{0,384},{128,0},{256,128},{384,256},{1,385},{129,1},{257,129},{385... | collective-permute-start | bytes 221192 | tf_op jit(solution)/shard_map/ppermute | solution.py:34
  125.0 14.3 %collective-permute-start.3 = (bf16[144,256]{1,0:T(8,128)(2,1)S(1)}, bf16[144,256]{1,0:T(8,128)(2,1)S(1)}, u32[]{:S(2)}, u32[]{:S(2)}) collective-permute-start(bf16[144,256]{1,0:T(8,128)(2,1)S(1)} %get-tuple-element.17.q0), channel_id=1, source_target_pairs={{0,256},{128,384},{256,0},{384,128},{1,257},{129,385},{257,1},{385... | collective-permute-start | bytes 221192 | tf_op jit(solution)/shard_map/ppermute | solution.py:34
  154.4 7.0 %collective-permute-start.4 = (bf16[128,256]{1,0:T(8,128)(2,1)S(1)}, bf16[128,256]{1,0:T(8,128)(2,1)S(1)}, u32[]{:S(2)}, u32[]{:S(2)}) collective-permute-start(bf16[128,256]{1,0:T(8,128)(2,1)S(1)} %merge.1.own), channel_id=1, source_target_pairs={{0,1},{1,0},{2,3},{3,2},{4,5},{5,4},{6,7},{7,6},{8,9},{9,8},{10,11... | collective-permute-start | bytes 196616 | tf_op jit(solution)/shard_map/ppermute | solution.py:34
  161.3 1.3 copy-start
Sparse Core Ops, SparseCore 0:
  26.0 64.5 all-gather.5
  92.7 40.4 all-gather.7

commit v12 on v11

--- a/solution.py
+++ b/solution.py
@@ -65,11 +65,13 @@
     for i, held in enumerate((mine, theirs)):
         core = lax.rem(c + i, 2)
         for x in range(4):
-            for z in range(4):
-                block, low = 2 * z + x // 2, x % 2
-                weights = jnp.concatenate([w[block, low, p, core] for p in range(3)], axis=1)
-                term = contract_first(weights, held[x, z])
-                total = term if total is None else total + term
+            rows = [w.at[2 * z + x // 2, x % 2] for z in range(4)]
+            weights = jnp.concatenate(
+                [jnp.concatenate([part[p, core] for part in rows], axis=0) for p in range(3)], axis=1
+            )
+            features = jnp.concatenate([held[x, z] for z in range(4)], axis=0)
+            term = contract_first(weights, features)
+            total = term if total is None else total + term
     query, key, value = total[:128], total[128:256], total[256:]
     out_q[...] = query
     out_kv[0] = key
@@ -83,34 +85,38 @@
         stats[t] = packed
 
 
-def rotate_kernel(width, got, q, kv, cosine, sine, qg, kg, marks, q_out, k_cache, v_cache, message):
-    totals = jnp.sum(got[...], axis=0)
+def rotated(value, gain, totals, cos, sin, width):
     even = lax.rem(lax.broadcasted_iota(jnp.int32, (HEAD_DIM, 256), 0), 2) == 0
-    cos, sin = cosine[...], sine[...]
-
-    def rotated(value, gain, row):
-        factor = jnp.concatenate([totals[row : row + 1], totals[row + 1 : row + 2]], axis=1)
-        factor = lax.rsqrt(factor / width + EPSILON)
-        normed = value * factor * gain
-        after = pltpu.roll(normed, HEAD_DIM - 1, 0)
-        before = pltpu.roll(normed, 1, 0)
-        partner = jnp.where(even, -after, before)
-        return normed * cos + partner * sin
-
-    extra = marks[...].astype(BF16)
-    q_low = rotated(q[...], qg[...], 0).astype(BF16)
-    q_out[:128] = q_low
-    q_out[128:144] = extra
-    k_rot = rotated(kv[0], kg[...], 2)
+    factor = jnp.concatenate([totals[0:1], totals[1:2]], axis=1)
+    factor = lax.rsqrt(factor / width + EPSILON)
+    normed = value * factor * gain
+    after = pltpu.roll(normed, HEAD_DIM - 1, 0)
+    before = pltpu.roll(normed, 1, 0)
+    partner = jnp.where(even, -after, before)
+    return normed * cos + partner * sin
+
+
+def keys_kernel(width, got, kv, cosine, sine, kg, marks, k_cache, v_cache, message):
+    totals = jnp.sum(got[...], axis=0)[2:4]
+    k_rot = rotated(kv[0], kg[...], totals, cosine[...], sine[...], width)
     value = kv[1]
     k_low = k_rot.astype(BF16)
     v_low = value.astype(BF16)
+    extra = marks[...].astype(BF16)
     for t in range(message.shape[0]):
         message[t, :128] = k_low
         message[t, 128:256] = v_low
         message[t, 256:272] = extra
     k_cache[...] = k_rot.T.astype(BF16)
     v_cache[...] = value.T.astype(BF16)
+
+
+def queries_kernel(width, got, q, cosine, sine, qg, marks, message):
+    totals = jnp.sum(got[...], axis=0)[:2]
+    q_low = rotated(q[...], qg[...], totals, cosine[...], sine[...], width).astype(BF16)
+    extra = marks[...].astype(BF16)
+    message[:128] = q_low
+    message[128:144] = extra
 
 
 def attend_kernel(order, at, q0, q1, q2, q3, keys, messages, held):
@@ -259,16 +265,18 @@
         cost=pl.CostEstimate(flops=2 * 256 * 5120 * 384, bytes_accessed=6 << 20, transcendentals=0),
     )
     stats = exchange(stats, TP)
-    q_message, k_cache, v_cache, kv_message = call(
-        functools.partial(rotate_kernel, heads_width),
-        (
-            shaped((144, 256), BF16),
-            shaped((256, 128), BF16),
-            shaped((256, 128), BF16),
-            shaped((4, 272, 256), BF16),
-        ),
-        [stats, query, key_value, cosine, sine, q_gain.reshape(128, 1), k_gain.reshape(128, 1), marks],
-        name="rotate",
+    k_cache, v_cache, kv_message = call(
+        functools.partial(keys_kernel, heads_width),
+        (shaped((256, 128), BF16), shaped((256, 128), BF16), shaped((4, 272, 256), BF16)),
+        [stats, key_value, cosine, sine, k_gain.reshape(128, 1), marks],
+        name="keys",
+    )
+    kv_message, stats = lax.optimization_barrier((kv_message, stats))
+    q_message = call(
+        functools.partial(queries_kernel, heads_width),
+        shaped((144, 256), BF16),
+        [stats, query, cosine, sine, q_gain.reshape(128, 1), marks],
+        name="queries",
     )
     keys = exchange(kv_message, ("yc", "zh"))
     order = (0, 1, 3, 2)
@@ -284,6 +292,7 @@
         scratch=[pltpu.VMEM((4, 256, 1024), F32)],
         name="attend",
     )
+    o_messages, wo_all = lax.optimization_barrier((o_messages, wo_all))
     own = call(
         merge_kernel, shaped((128, 256), BF16), [exchange(o_messages, ("ya", "yb"))], name="merge"
     )

time: 205 us -> 206 us (level)
    pallas_call x6 -> x7, Pallas kernels: 9.04 us -> 8.61 us  [call(): pl.pallas_call(kernel, out_shape=out_shape, in_specs=specs, out_specs=jax...]
where the time goes in v12:
time: 206 us; the launch traced here: 203 us
  blocking collectives  91.7 us (45%)
  starting transfers between devices  53.8 us (26%)
  waiting for transfers between devices  26.4 us (13%)
  between operations  14.3 us (7%)
  Pallas kernels  8.61 us (4%)
  other arithmetic  4.23 us (2%)
  local copies, waits for them, and re-layouts  3.7 us (2%)
    all_to_all x5, blocking collectives, exchange(): return lax.all_to_all(value, axes, 0, 0, tiled=True)  74.9 us
    all_to_all x3, starting transfers between devices, exchange(): return lax.all_to_all(value, axes, 0, 0, tiled=True)  27.6 us
    ppermute x6, starting transfers between devices, permute(): return lax.ppermute(value, axes, pairs)  26 us
    all_gather x1, blocking collectives, body(): pair = lax.all_gather(local, 'zh', axis=0, tiled=False)  16.8 us
    all_to_all x3, waiting for transfers between devices, exchange(): return lax.all_to_all(value, axes, 0, 0, tiled=True)  15.9 us
    ppermute x6, waiting for transfers between devices, permute(): return lax.ppermute(value, axes, pairs)  10.5 us
    pallas_call x7, Pallas kernels, call(): pl.pallas_call(kernel, out_shape=out_shape, in_specs=specs, out_specs=jax...  8.61 us
  transfers between devices with their start and end apart: 11, of which 6 were waited for; matrix products, arithmetic and copies ran while one was open for 2% of the time, Pallas kernels for 4%

profile of v12, /device:TPU:1, one launch (start us, length us, event | category | flops | bytes accessed | tf_op | source)
XLA Modules:
  0.0 203.3 jit_solution(2322534647460746071)
XLA Ops:
  8.2 16.8 %all-gather = bf16[8,320,128]{2,1,0:T(8,128)(2,1)S(1)} all-gather(bf16[4,320,128]{2,1,0:T(8,128)(2,1)S(1)} %pad_maximum_fusion), channel_id=2, replica_groups=mesh['ya'=2,'yb'=2,'yc'=2,'zh'=2,'zl'=4,'xh'=2,'xl'=2,'c'=2] {'zh'}, dimensions={0}, use_global_device_ids=true | all-gather | bytes 983040 | tf_op jit(solution)/shard_map/all_gather | solution.py:214
  26.7 15.6 %all-to-all-start = ((f32[32,8,128]{2,1,0:T(8,128)}), f32[32,8,128]{2,1,0:T(8,128)S(1)}, u32[]{:S(2)}, u32[]{:S(2)}) async-start(f32[32,8,128]{2,1,0:T(8,128)} %broadcast_in_dim.16), calls=%async_computation | async-start | bytes 262144 | tf_op jit(solution)/shard_map/all_to_all | solution.py:197
  43.0 7.9 %all-to-all-done = f32[32,8,128]{2,1,0:T(8,128)S(1)} async-done(((f32[32,8,128]{2,1,0:T(8,128)}), f32[32,8,128]{2,1,0:T(8,128)S(1)}, u32[]{:S(2)}, u32[]{:S(2)}) %all-to-all-start) | async-done | bytes 131104 | tf_op jit(solution)/shard_map/all_to_all | solution.py:197
  51.0 12.5 %all_to_all.40 = bf16[4,160,256]{2,1,0:T(8,128)(2,1)S(1)} all-to-all(bf16[4,160,256]{2,1,0:T(8,128)(2,1)S(1)} %broadcast_in_dim.35), channel_id=1, replica_groups=mesh['ya'=2,'yb'=2,'yc'=2,'zh'=2,'zl'=4,'xh'=2,'xl'=2,'c'=2] {'zl'}, dimensions={0} | all-to-all | bytes 655360 | tf_op jit(solution)/shard_map/all_to_all | solution.py:197
  63.6 19.3 %all_to_all.41.mine = bf16[4,4,160,256]{3,2,1,0:T(8,128)(2,1)S(1)} all-to-all(bf16[4,4,160,256]{3,2,1,0:T(8,128)(2,1)S(1)} %broadcast_in_dim.36), channel_id=1, replica_groups=mesh['ya'=2,'yb'=2,'yc'=2,'zh'=2,'zl'=4,'xh'=2,'xl'=2,'c'=2] {'xh','xl'}, dimensions={0} | all-to-all | bytes 2621440 | tf_op jit(solution)/shard_map/all_to_all | solution.py:197
  82.9 3.9 %collective-permute-start = (bf16[4,4,160,256]{3,2,1,0:T(8,128)(2,1)S(1)}, bf16[4,4,160,256]{3,2,1,0:T(8,128)(2,1)S(1)}, u32[]{:S(2)}, u32[]{:S(2)}) collective-permute-start(bf16[4,4,160,256]{3,2,1,0:T(8,128)(2,1)S(1)} %all_to_all.41.mine), channel_id=1, source_target_pairs={{0,1},{1,0},{2,3},{3,2},{4,5},{5,4},{6,7},{7,6},{8,9},{9,8},{10,11... | collective-permute-start | bytes 3932168 | tf_op jit(solution)/shard_map/ppermute | solution.py:34
  86.8 1.9 collective-permute-start.4
  88.8 1.2 collective-permute-done.4
  91.4 4.3 %project.1 = (f32[128,256]{1,0:T(8,128)S(1)}, f32[2,128,256]{2,1,0:T(8,128)S(1)}, f32[32,8,128]{2,1,0:T(8,128)}) custom-call(s32[2]{0:T(128)S(1)} %pad_add_fusion.at, bf16[4,4,160,256]{3,2,1,0:T(8,128)(2,1)S(1)} %all_to_all.41.mine, bf16[4,4,160,256]{3,2,1,0:T(8,128)(2,1)S(1)} %collective-permute-done.theirs, bf16[8,2,3,2,160,128]{5,4,3,2,1,0:T(8,128)(2,1)} %bitcast.61), custom_call_target="tpu_custom_call" | custom-call | flops 1006632960 | bytes 6291456 | tf_op jit(solution)/shard_map/project/pallas_call | solution.py:46
  95.7 7.6 %all-to-all-start.3 = ((f32[32,8,128]{2,1,0:T(8,128)}), f32[32,8,128]{2,1,0:T(8,128)S(1)}, u32[]{:S(2)}, u32[]{:S(2)}) async-start(f32[32,8,128]{2,1,0:T(8,128)} %get-tuple-element.17), calls=%async_computation.3 | async-start | bytes 262144 | tf_op jit(solution)/shard_map/all_to_all | solution.py:197
  103.9 8.0 %all-to-all-done.3.got = f32[32,8,128]{2,1,0:T(8,128)S(1)} async-done(((f32[32,8,128]{2,1,0:T(8,128)}), f32[32,8,128]{2,1,0:T(8,128)S(1)}, u32[]{:S(2)}, u32[]{:S(2)}) %all-to-all-start.3) | async-done | bytes 131104 | tf_op jit(solution)/shard_map/all_to_all | solution.py:197
  112.8 4.4 %all-to-all-start.4 = ((bf16[4,272,256]{2,1,0:T(8,128)(2,1)}), bf16[4,272,256]{2,1,0:T(8,128)(2,1)S(1)}, u32[]{:S(2)}, u32[]{:S(2)}) async-start(bf16[4,272,256]{2,1,0:T(8,128)(2,1)} %get-tuple-element.22), calls=%async_computation.4 | async-start | bytes 1114112 | tf_op jit(solution)/shard_map/all_to_all | solution.py:197
  117.5 4.8 %collective-permute-start.1 = (bf16[144,256]{1,0:T(8,128)(2,1)S(1)}, bf16[144,256]{1,0:T(8,128)(2,1)S(1)}, u32[]{:S(2)}, u32[]{:S(2)}) collective-permute-start(bf16[144,256]{1,0:T(8,128)(2,1)S(1)} %queries.1.q0), channel_id=1, source_target_pairs={{0,128},{128,256},{256,384},{384,0},{1,129},{129,257},{257,385},{3... | collective-permute-start | bytes 221192 | tf_op jit(solution)/shard_map/ppermute | solution.py:34
  122.3 2.6 %collective-permute-start.2 = (bf16[144,256]{1,0:T(8,128)(2,1)S(1)}, bf16[144,256]{1,0:T(8,128)(2,1)S(1)}, u32[]{:S(2)}, u32[]{:S(2)}) collective-permute-start(bf16[144,256]{1,0:T(8,128)(2,1)S(1)} %queries.1.q0), channel_id=1, source_target_pairs={{0,384},{128,0},{256,128},{384,256},{1,385},{129,1},{257,129},{385... | collective-permute-start | bytes 221192 | tf_op jit(solution)/shard_map/ppermute | solution.py:34
  124.9 6.1 %collective-permute-start.3 = (bf16[144,256]{1,0:T(8,128)(2,1)S(1)}, bf16[144,256]{1,0:T(8,128)(2,1)S(1)}, u32[]{:S(2)}, u32[]{:S(2)}) collective-permute-start(bf16[144,256]{1,0:T(8,128)(2,1)S(1)} %queries.1.q0), channel_id=1, source_target_pairs={{0,256},{128,384},{256,0},{384,128},{1,257},{129,385},{257,1},{385... | collective-permute-start | bytes 221192 | tf_op jit(solution)/shard_map/ppermute | solution.py:34
  131.0 4.3 %collective-permute-done.1.q1 = bf16[144,256]{1,0:T(8,128)(2,1)S(1)} collective-permute-done((bf16[144,256]{1,0:T(8,128)(2,1)S(1)}, bf16[144,256]{1,0:T(8,128)(2,1)S(1)}, u32[]{:S(2)}, u32[]{:S(2)}) %collective-permute-start.1) | collective-permute-done | bytes 73760 | tf_op jit(solution)/shard_map/ppermute | solution.py:34
  135.3 4.0 %collective-permute-done.3.q3 = bf16[144,256]{1,0:T(8,128)(2,1)S(1)} collective-permute-done((bf16[144,256]{1,0:T(8,128)(2,1)S(1)}, bf16[144,256]{1,0:T(8,128)(2,1)S(1)}, u32[]{:S(2)}, u32[]{:S(2)}) %collective-permute-start.3) | collective-permute-done | bytes 73760 | tf_op jit(solution)/shard_map/ppermute | solution.py:34
  139.4 2.5 %attend.1 = bf16[4,144,256]{2,1,0:T(8,128)(2,1)S(1)} custom-call(s32[2]{0:T(128)S(1)} %pad_add_fusion.at, bf16[144,256]{1,0:T(8,128)(2,1)S(1)} %queries.1.q0, bf16[144,256]{1,0:T(8,128)(2,1)S(1)} %collective-permute-done.1.q1, bf16[144,256]{1,0:T(8,128)(2,1)S(1)} %collective-permute-done.2.q2, bf16[144,256]{1,0:T(8,128)(2,1)S(1)} %collective-permute-done.3.q3, ...), custom_call_target="tpu_custom_call" | custom-call | tf_op jit(solution)/shard_map/attend/pallas_call | solution.py:46
  141.9 11.8 %all_to_all.42.got = bf16[4,144,256]{2,1,0:T(8,128)(2,1)S(1)} all-to-all(bf16[4,144,256]{2,1,0:T(8,128)(2,1)S(1)} %attend.1), channel_id=1, replica_groups=mesh['ya'=2,'yb'=2,'yc'=2,'zh'=2,'zl'=4,'xh'=2,'xl'=2,'c'=2] {'ya','yb'}, dimensions={0} | all-to-all | bytes 589824 | tf_op jit(solution)/shard_map/all_to_all | solution.py:197
  153.8 6.7 %collective-permute-start.5 = (bf16[128,256]{1,0:T(8,128)(2,1)S(1)}, bf16[128,256]{1,0:T(8,128)(2,1)S(1)}, u32[]{:S(2)}, u32[]{:S(2)}) collective-permute-start(bf16[128,256]{1,0:T(8,128)(2,1)S(1)} %merge.1.own), channel_id=1, source_target_pairs={{0,1},{1,0},{2,3},{3,2},{4,5},{5,4},{6,7},{7,6},{8,9},{9,8},{10,11... | collective-permute-start | bytes 196616 | tf_op jit(solution)/shard_map/ppermute | solution.py:34
  161.4 1.3 copy-done
  163.2 19.9 %all_to_all.43.got = bf16[4,4,160,256]{3,2,1,0:T(8,128)(2,1)S(1)} all-to-all(bf16[4,4,160,256]{3,2,1,0:T(8,128)(2,1)S(1)} %partial.1), channel_id=1, replica_groups=mesh['ya'=2,'yb'=2,'yc'=2,'zh'=2,'zl'=4,'xh'=2,'xl'=2,'c'=2] {'xh','xl'}, dimensions={0} | all-to-all | bytes 2621440 | tf_op jit(solution)/shard_map/all_to_all | solution.py:197
  183.3 11.5 %all_to_all.44 = bf16[4,160,256]{2,1,0:T(8,128)(2,1)S(1)} all-to-all(bf16[4,160,256]{2,1,0:T(8,128)(2,1)S(1)} %along_x.1), channel_id=1, replica_groups=mesh['ya'=2,'yb'=2,'yc'=2,'zh'=2,'zl'=4,'xh'=2,'xl'=2,'c'=2] {'zl'}, dimensions={0} | all-to-all | bytes 655360 | tf_op jit(solution)/shard_map/all_to_all | solution.py:197
  194.8 1.6 fusion.11
  (66 shorter events, 8.4 us)
Async XLA Ops:
  7.2 84.2 %all-gather.6.cloned.1.call-start = ((), (), s32[]{:S(2)}) async-start(), calls=%async_computation.8 | async-start | bytes 4423680 | tf_op jit(solution)/shard_map/all_gather | solution.py:215
  8.2 17.7 %copy-start.2 = (bf16[256,160]{0,1:T(8,128)(2,1)S(1)}, bf16[256,160]{0,1:T(8,128)(2,1)}, u32[]{:S(2)}) copy-start(bf16[256,160]{0,1:T(8,128)(2,1)} %param.8) | copy-start | bytes 245764
  25.0 17.4 %copy-start.3 = (f32[4,3,160]{2,0,1:T(4,128)S(1)}, f32[4,3,160]{2,0,1:T(4,128)}, u32[]{:S(2)}) copy-start(f32[4,3,160]{2,0,1:T(4,128)} %param.11) | copy-start | bytes 23044
  25.0 17.5 %copy-start.4 = (s32[256]{0:T(256)S(1)}, s32[256]{0:T(256)}, u32[]{:S(2)}) copy-start(s32[256]{0:T(256)} %param.9) | copy-start | bytes 3076
  26.7 24.2 %all-to-all-start = ((f32[32,8,128]{2,1,0:T(8,128)}), f32[32,8,128]{2,1,0:T(8,128)S(1)}, u32[]{:S(2)}, u32[]{:S(2)}) async-start(f32[32,8,128]{2,1,0:T(8,128)} %broadcast_in_dim.16), calls=%async_computation | async-start | bytes 262144 | tf_op jit(solution)/shard_map/all_to_all | solution.py:197
  42.3 99.6 %all-gather.8.cloned.1.call-start = ((), (), s32[]{:S(2)}) async-start(), calls=%async_computation.9 | async-start | bytes 1474560 | tf_op jit(solution)/shard_map/all_gather | solution.py:254
  43.0 20.5 %copy-start.1 = (f32[480,256]{1,0:T(8,128)}, f32[480,256]{1,0:T(8,128)S(1)}, u32[]{:S(2)}) copy-start(f32[480,256]{1,0:T(8,128)S(1)} %convolution_bitcast_fusion) | copy-start | bytes 1474564
  63.6 27.5 %copy-start.6 = (f32[128]{0:T(128)S(1)}, f32[128]{0:T(128)}, u32[]{:S(2)}) copy-start(f32[128]{0:T(128)} %param.14) | copy-start | bytes 1540
  63.6 27.7 %copy-start.5 = (s32[3,256]{1,0:T(4,128)S(1)}, s32[3,256]{1,0:T(4,128)}, u32[]{:S(2)}) copy-start(s32[3,256]{1,0:T(4,128)} %param.10) | copy-start | bytes 9220
  82.9 8.5 %collective-permute-start = (bf16[4,4,160,256]{3,2,1,0:T(8,128)(2,1)S(1)}, bf16[4,4,160,256]{3,2,1,0:T(8,128)(2,1)S(1)}, u32[]{:S(2)}, u32[]{:S(2)}) collective-permute-start(bf16[4,4,160,256]{3,2,1,0:T(8,128)(2,1)S(1)} %all_to_all.41.mine), channel_id=1, source_target_pairs={{0,1},{1,0},{2,3},{3,2},{4,5},{5,4},{6,7},{7,6},{8,9},{9,8},{10,11... | collective-permute-start | bytes 3932168 | tf_op jit(solution)/shard_map/ppermute | solution.py:34
  86.8 3.2 %collective-permute-start.4 = (bf16[2,160,128]{2,1,0:T(8,128)(2,1)S(1)}, bf16[2,160,128]{2,1,0:T(8,128)(2,1)S(1)}, u32[]{:S(2)}, u32[]{:S(2)}) collective-permute-start(bf16[2,160,128]{2,1,0:T(8,128)(2,1)S(1)} %get-tuple-element.24), channel_id=1, source_target_pairs={{0,1},{1,0},{2,3},{3,2},{4,5},{5,4},{6,7},{7,6},{8,9},{9,8},{10,11... | collective-permute-start | bytes 245768 | tf_op jit(solution)/shard_map/ppermute | solution.py:34
  95.7 21.6 %copy-start.7 = (f32[128]{0:T(128)S(1)}, f32[128]{0:T(128)}, u32[]{:S(2)}) copy-start(f32[128]{0:T(128)} %param.13) | copy-start | bytes 1540
  95.7 16.2 %all-to-all-start.3 = ((f32[32,8,128]{2,1,0:T(8,128)}), f32[32,8,128]{2,1,0:T(8,128)S(1)}, u32[]{:S(2)}, u32[]{:S(2)}) async-start(f32[32,8,128]{2,1,0:T(8,128)} %get-tuple-element.17), calls=%async_computation.3 | async-start | bytes 262144 | tf_op jit(solution)/shard_map/all_to_all | solution.py:197
  112.8 26.5 %all-to-all-start.4 = ((bf16[4,272,256]{2,1,0:T(8,128)(2,1)}), bf16[4,272,256]{2,1,0:T(8,128)(2,1)S(1)}, u32[]{:S(2)}, u32[]{:S(2)}) async-start(bf16[4,272,256]{2,1,0:T(8,128)(2,1)} %get-tuple-element.22), calls=%async_computation.4 | async-start | bytes 1114112 | tf_op jit(solution)/shard_map/all_to_all | solution.py:197
  117.5 17.8 %collective-permute-start.1 = (bf16[144,256]{1,0:T(8,128)(2,1)S(1)}, bf16[144,256]{1,0:T(8,128)(2,1)S(1)}, u32[]{:S(2)}, u32[]{:S(2)}) collective-permute-start(bf16[144,256]{1,0:T(8,128)(2,1)S(1)} %queries.1.q0), channel_id=1, source_target_pairs={{0,128},{128,256},{256,384},{384,0},{1,129},{129,257},{257,385},{3... | collective-permute-start | bytes 221192 | tf_op jit(solution)/shard_map/ppermute | solution.py:34
  122.3 13.0 %collective-permute-start.2 = (bf16[144,256]{1,0:T(8,128)(2,1)S(1)}, bf16[144,256]{1,0:T(8,128)(2,1)S(1)}, u32[]{:S(2)}, u32[]{:S(2)}) collective-permute-start(bf16[144,256]{1,0:T(8,128)(2,1)S(1)} %queries.1.q0), channel_id=1, source_target_pairs={{0,384},{128,0},{256,128},{384,256},{1,385},{129,1},{257,129},{385... | collective-permute-start | bytes 221192 | tf_op jit(solution)/shard_map/ppermute | solution.py:34
  124.9 14.5 %collective-permute-start.3 = (bf16[144,256]{1,0:T(8,128)(2,1)S(1)}, bf16[144,256]{1,0:T(8,128)(2,1)S(1)}, u32[]{:S(2)}, u32[]{:S(2)}) collective-permute-start(bf16[144,256]{1,0:T(8,128)(2,1)S(1)} %queries.1.q0), channel_id=1, source_target_pairs={{0,256},{128,384},{256,0},{384,128},{1,257},{129,385},{257,1},{385... | collective-permute-start | bytes 221192 | tf_op jit(solution)/shard_map/ppermute | solution.py:34
  153.8 7.6 %collective-permute-start.5 = (bf16[128,256]{1,0:T(8,128)(2,1)S(1)}, bf16[128,256]{1,0:T(8,128)(2,1)S(1)}, u32[]{:S(2)}, u32[]{:S(2)}) collective-permute-start(bf16[128,256]{1,0:T(8,128)(2,1)S(1)} %merge.1.own), channel_id=1, source_target_pairs={{0,1},{1,0},{2,3},{3,2},{4,5},{5,4},{6,7},{7,6},{8,9},{9,8},{10,11... | collective-permute-start | bytes 196616 | tf_op jit(solution)/shard_map/ppermute | solution.py:34
  161.4 1.3 copy-start
Sparse Core Ops, SparseCore 0:
  26.0 64.5 all-gather.5
  92.7 40.4 all-gather.7

commit v13 on v12

--- a/solution.py
+++ b/solution.py
@@ -210,9 +210,9 @@
         [lax.axis_index("c"), lax.axis_index("ya") * 2 + lax.axis_index("yb")]
     ).astype(jnp.int32)
 
-    local = jnp.concatenate([jnp.transpose(w_qkv, (1, 0, 2)), w_out.T[None]], axis=0)
-    pair = lax.all_gather(local, "zh", axis=0, tiled=False)
-    w_all = lax.all_gather(pair[:, :3], ("ya", "yb", "yc"), axis=0, tiled=False)
+    w_pair = lax.all_gather(jnp.transpose(w_qkv, (1, 0, 2)), "zh", axis=0, tiled=False)
+    wo_pair = lax.all_gather(w_out.T, "zh", axis=0, tiled=False)
+    w_all = lax.all_gather(w_pair, ("ya", "yb", "yc"), axis=0, tiled=False)
     w_all = w_all.reshape(8, 2, 3, 2, 160, 128)
 
     x_t = hidden_in.T.astype(F32)
@@ -244,17 +244,11 @@
     variance = sums[1:2] / model_width - mean_value * mean_value
     normed = (x_t - mean_value) * lax.rsqrt(variance + EPSILON)
     packet = (normed * (1.0 + modulation[1]) + modulation[0]).astype(BF16)
-
-    core = lax.axis_index("c")
-    wo_pair = pair[:, 3].reshape(2, 2, 160, 128)
-    wo_own = lax.dynamic_index_in_dim(wo_pair, core, axis=1, keepdims=False)
-    wo_give = lax.dynamic_index_in_dim(wo_pair, 1 - core, axis=1, keepdims=False)
-    packet, wo_own, wo_give = lax.optimization_barrier((packet, wo_own, wo_give))
-    wo_other = permute(wo_give, ("c",), lambda c: (1 - c,))
-    wo_all = lax.all_gather(jnp.stack([wo_own, wo_other]), ("ya", "yb", "yc"), axis=0, tiled=False)
+    packet, wo_pair = lax.optimization_barrier((packet, wo_pair))
 
     held = spread(spread(packet, ("zl",)), ("xh", "xl"))
     theirs = permute(held, ("c",), lambda c: (1 - c,))
+    theirs, cosine, sine, marks = lax.optimization_barrier((theirs, cosine, sine, marks))
 
     query, key_value, stats = call(
         project_kernel,
@@ -264,7 +258,14 @@
         name="project",
         cost=pl.CostEstimate(flops=2 * 256 * 5120 * 384, bytes_accessed=6 << 20, transcendentals=0),
     )
-    stats = exchange(stats, TP)
+    core = lax.axis_index("c")
+    wo_pair = wo_pair.reshape(2, 2, 160, 128)
+    wo_own = lax.dynamic_index_in_dim(wo_pair, core, axis=1, keepdims=False)
+    wo_give = lax.dynamic_index_in_dim(wo_pair, 1 - core, axis=1, keepdims=False)
+    wo_own, wo_give, stats = lax.optimization_barrier((wo_own, wo_give, stats))
+    wo_other = permute(wo_give, ("c",), lambda c: (1 - c,))
+    stats, wo_other = lax.optimization_barrier((exchange(stats, TP), wo_other))
+    wo_all = lax.all_gather(jnp.stack([wo_own, wo_other]), ("ya", "yb", "yc"), axis=0, tiled=False)
     k_cache, v_cache, kv_message = call(
         functools.partial(keys_kernel, heads_width),
         (shaped((256, 128), BF16), shaped((256, 128), BF16), shaped((4, 272, 256), BF16)),

time: 206 us -> 217 us (1.053)
  blocking collectives: 91.7 us -> 108 us
  starting transfers between devices: 53.8 us -> 51.4 us
    all_gather x1 -> x2, blocking collectives: 16.8 us -> 27.7 us  [the longest x1 19.3 us: body(): lax.all_gather(jnp.transpose(w_qkv, (1, 0, 2)), 'zh', axis=0, tiled=False)]
    all_gather x1, waiting for transfers between devices: 0.02 us -> 10.9 us  [body(): lax.all_gather(jnp.stack([wo_own, wo_other]), ('ya', 'yb', 'yc'), axis=0,...]
    all_to_all x3, waiting for transfers between devices: 15.9 us -> 5.33 us  [exchange(): return lax.all_to_all(value, axes, 0, 0, tiled=True)]
    all_to_all x5, blocking collectives: 74.9 us -> 80.4 us  [exchange(): return lax.all_to_all(value, axes, 0, 0, tiled=True)]
    all_to_all x3, starting transfers between devices: 27.6 us -> 23.2 us  [exchange(): return lax.all_to_all(value, axes, 0, 0, tiled=True)]
  transfers between devices with their start and end apart: 11 -> 11, of which waited for: 6 -> 7; matrix products, arithmetic and copies ran while one was open for 2% -> 2% of each run, Pallas kernels for 4% -> 2%
where the time goes in v13:
time: 217 us; the launch traced here: 215 us
  blocking collectives  108 us (50%)
  starting transfers between devices  51.4 us (24%)
  waiting for transfers between devices  25.4 us (12%)
  between operations  14.3 us (7%)
  Pallas kernels  8.58 us (4%)
  other arithmetic  4.1 us (2%)
  local copies, waits for them, and re-layouts  2.85 us (1%)
    all_to_all x5, blocking collectives, exchange(): return lax.all_to_all(value, axes, 0, 0, tiled=True)  80.4 us
    ppermute x6, starting transfers between devices, permute(): return lax.ppermute(value, axes, pairs)  28.2 us
    all_to_all x3, starting transfers between devices, exchange(): return lax.all_to_all(value, axes, 0, 0, tiled=True)  23.2 us
    all_gather x1, blocking collectives, body(): lax.all_gather(jnp.transpose(w_qkv, (1, 0, 2)), 'zh', axis=0, tiled=False)  19.3 us
    all_gather x1, waiting for transfers between devices, body(): lax.all_gather(jnp.stack([wo_own, wo_other]), ('ya', 'yb', 'yc'), axis=0,...  10.9 us
    ppermute x6, waiting for transfers between devices, permute(): return lax.ppermute(value, axes, pairs)  9.13 us
    pallas_call x7, Pallas kernels, call(): pl.pallas_call(kernel, out_shape=out_shape, in_specs=specs, out_specs=jax...  8.58 us
    all_gather x1, blocking collectives, body(): wo_pair = lax.all_gather(w_out.T, 'zh', axis=0, tiled=False)  8.4 us
  transfers between devices with their start and end apart: 11, of which 7 were waited for; matrix products, arithmetic and copies ran while one was open for 2% of the time, Pallas kernels for 2%

profile of v13, /device:TPU:1, one launch (start us, length us, event | category | flops | bytes accessed | tf_op | source)
XLA Modules:
  0.0 215.2 jit_solution(6982750717300941283)
XLA Ops:
  7.3 19.3 %all-gather.1 = bf16[6,320,128]{2,1,0:T(8,128)(2,1)} all-gather(bf16[3,320,128]{2,1,0:T(8,128)(2,1)} %bitcast.64), channel_id=3, replica_groups=mesh['ya'=2,'yb'=2,'yc'=2,'zh'=2,'zl'=4,'xh'=2,'xl'=2,'c'=2] {'zh'}, dimensions={0}, use_global_device_ids=true | all-gather | bytes 737280 | tf_op jit(solution)/shard_map/all_gather | solution.py:213
  28.3 13.6 %all-to-all-start = ((f32[32,8,128]{2,1,0:T(8,128)}), f32[32,8,128]{2,1,0:T(8,128)S(1)}, u32[]{:S(2)}, u32[]{:S(2)}) async-start(f32[32,8,128]{2,1,0:T(8,128)} %broadcast_in_dim.14), calls=%async_computation | async-start | bytes 262144 | tf_op jit(solution)/shard_map/all_to_all | solution.py:197
  41.9 8.4 %all-gather = bf16[640,128]{1,0:T(8,128)(2,1)S(1)} all-gather(bf16[320,128]{1,0:T(8,128)(2,1)S(1)} %bitcast.66), channel_id=2, replica_groups=mesh['ya'=2,'yb'=2,'yc'=2,'zh'=2,'zl'=4,'xh'=2,'xl'=2,'c'=2] {'zh'}, dimensions={0}, use_global_device_ids=true | all-gather | bytes 245760 | tf_op jit(solution)/shard_map/all_gather | solution.py:214
  51.0 15.0 %all_to_all.40 = bf16[4,160,256]{2,1,0:T(8,128)(2,1)S(1)} all-to-all(bf16[4,160,256]{2,1,0:T(8,128)(2,1)S(1)} %broadcast_in_dim.15), channel_id=1, replica_groups=mesh['ya'=2,'yb'=2,'yc'=2,'zh'=2,'zl'=4,'xh'=2,'xl'=2,'c'=2] {'zl'}, dimensions={0} | all-to-all | bytes 655360 | tf_op jit(solution)/shard_map/all_to_all | solution.py:197
  66.1 19.1 %all_to_all.41.mine = bf16[4,4,160,256]{3,2,1,0:T(8,128)(2,1)S(1)} all-to-all(bf16[4,4,160,256]{3,2,1,0:T(8,128)(2,1)S(1)} %broadcast_in_dim.32), channel_id=1, replica_groups=mesh['ya'=2,'yb'=2,'yc'=2,'zh'=2,'zl'=4,'xh'=2,'xl'=2,'c'=2] {'xh','xl'}, dimensions={0} | all-to-all | bytes 2621440 | tf_op jit(solution)/shard_map/all_to_all | solution.py:197
  85.2 5.4 %collective-permute-start = (bf16[4,4,160,256]{3,2,1,0:T(8,128)(2,1)S(1)}, bf16[4,4,160,256]{3,2,1,0:T(8,128)(2,1)S(1)}, u32[]{:S(2)}, u32[]{:S(2)}) collective-permute-start(bf16[4,4,160,256]{3,2,1,0:T(8,128)(2,1)S(1)} %all_to_all.41.mine), channel_id=1, source_target_pairs={{0,1},{1,0},{2,3},{3,2},{4,5},{5,4},{6,7},{7,6},{8,9},{9,8},{10,11... | collective-permute-start | bytes 3932168 | tf_op jit(solution)/shard_map/ppermute | solution.py:34
  91.8 1.5 collective-permute-done.theirs
  93.3 4.2 %project.1 = (f32[128,256]{1,0:T(8,128)S(1)}, f32[2,128,256]{2,1,0:T(8,128)S(1)}, f32[32,8,128]{2,1,0:T(8,128)}) custom-call(s32[2]{0:T(128)S(1)} %pad_add_fusion.at, bf16[4,4,160,256]{3,2,1,0:T(8,128)(2,1)S(1)} %all_to_all.41.mine, bf16[4,4,160,256]{3,2,1,0:T(8,128)(2,1)S(1)} %collective-permute-done.theirs, bf16[8,2,3,2,160,128]{5,4,3,2,1,0:T(8,128)(2,1)} %bitcast.60), custom_call_target="tpu_custom_call" | custom-call | flops 1006632960 | bytes 6291456 | tf_op jit(solution)/shard_map/project/pallas_call | solution.py:46
  97.5 5.3 %all-to-all-start.3 = ((f32[32,8,128]{2,1,0:T(8,128)}), f32[32,8,128]{2,1,0:T(8,128)S(1)}, u32[]{:S(2)}, u32[]{:S(2)}) async-start(f32[32,8,128]{2,1,0:T(8,128)} %get-tuple-element.28), calls=%async_computation.3 | async-start | bytes 262144 | tf_op jit(solution)/shard_map/all_to_all | solution.py:197
  102.9 2.1 collective-permute-start.1
  106.0 5.3 %all-to-all-done.3.got = f32[32,8,128]{2,1,0:T(8,128)S(1)} async-done(((f32[32,8,128]{2,1,0:T(8,128)}), f32[32,8,128]{2,1,0:T(8,128)S(1)}, u32[]{:S(2)}, u32[]{:S(2)}) %all-to-all-start.3) | async-done | bytes 131104 | tf_op jit(solution)/shard_map/all_to_all | solution.py:197
  113.2 4.3 %all-to-all-start.4 = ((bf16[4,272,256]{2,1,0:T(8,128)(2,1)}), bf16[4,272,256]{2,1,0:T(8,128)(2,1)S(1)}, u32[]{:S(2)}, u32[]{:S(2)}) async-start(bf16[4,272,256]{2,1,0:T(8,128)(2,1)} %get-tuple-element.38), calls=%async_computation.4 | async-start | bytes 1114112 | tf_op jit(solution)/shard_map/all_to_all | solution.py:197
  117.7 4.6 %collective-permute-start.2 = (bf16[144,256]{1,0:T(8,128)(2,1)S(1)}, bf16[144,256]{1,0:T(8,128)(2,1)S(1)}, u32[]{:S(2)}, u32[]{:S(2)}) collective-permute-start(bf16[144,256]{1,0:T(8,128)(2,1)S(1)} %queries.1.q0), channel_id=1, source_target_pairs={{0,128},{128,256},{256,384},{384,0},{1,129},{129,257},{257,385},{3... | collective-permute-start | bytes 221192 | tf_op jit(solution)/shard_map/ppermute | solution.py:34
  122.3 2.8 %collective-permute-start.3 = (bf16[144,256]{1,0:T(8,128)(2,1)S(1)}, bf16[144,256]{1,0:T(8,128)(2,1)S(1)}, u32[]{:S(2)}, u32[]{:S(2)}) collective-permute-start(bf16[144,256]{1,0:T(8,128)(2,1)S(1)} %queries.1.q0), channel_id=1, source_target_pairs={{0,384},{128,0},{256,128},{384,256},{1,385},{129,1},{257,129},{385... | collective-permute-start | bytes 221192 | tf_op jit(solution)/shard_map/ppermute | solution.py:34
  125.1 6.8 %collective-permute-start.4 = (bf16[144,256]{1,0:T(8,128)(2,1)S(1)}, bf16[144,256]{1,0:T(8,128)(2,1)S(1)}, u32[]{:S(2)}, u32[]{:S(2)}) collective-permute-start(bf16[144,256]{1,0:T(8,128)(2,1)S(1)} %queries.1.q0), channel_id=1, source_target_pairs={{0,256},{128,384},{256,0},{384,128},{1,257},{129,385},{257,1},{385... | collective-permute-start | bytes 221192 | tf_op jit(solution)/shard_map/ppermute | solution.py:34
  133.1 4.5 %collective-permute-done.4.q3 = bf16[144,256]{1,0:T(8,128)(2,1)S(1)} collective-permute-done((bf16[144,256]{1,0:T(8,128)(2,1)S(1)}, bf16[144,256]{1,0:T(8,128)(2,1)S(1)}, u32[]{:S(2)}, u32[]{:S(2)}) %collective-permute-start.4) | collective-permute-done | bytes 73760 | tf_op jit(solution)/shard_map/ppermute | solution.py:34
  137.7 2.5 %attend.1 = bf16[4,144,256]{2,1,0:T(8,128)(2,1)S(1)} custom-call(s32[2]{0:T(128)S(1)} %pad_add_fusion.at, bf16[144,256]{1,0:T(8,128)(2,1)S(1)} %queries.1.q0, bf16[144,256]{1,0:T(8,128)(2,1)S(1)} %collective-permute-done.2.q1, bf16[144,256]{1,0:T(8,128)(2,1)S(1)} %collective-permute-done.3.q2, bf16[144,256]{1,0:T(8,128)(2,1)S(1)} %collective-permute-done.4.q3, ...), custom_call_target="tpu_custom_call" | custom-call | tf_op jit(solution)/shard_map/attend/pallas_call | solution.py:46
  140.2 10.9 %all-gather.9.cloned.1.call-done = bf16[16,2,160,128]{3,2,1,0:T(8,128)(2,1)} async-done(((bf16[2,2,160,128]{3,2,1,0:T(8,128)(2,1)}), bf16[16,2,160,128]{3,2,1,0:T(8,128)(2,1)}) %all-gather.9.cloned.1.call-update) | async-done | bytes 1310736 | tf_op jit(solution)/shard_map/all_gather | solution.py:268
  151.1 13.0 %all_to_all.42.got = bf16[4,144,256]{2,1,0:T(8,128)(2,1)S(1)} all-to-all(bf16[4,144,256]{2,1,0:T(8,128)(2,1)S(1)} %attend.1), channel_id=1, replica_groups=mesh['ya'=2,'yb'=2,'yc'=2,'zh'=2,'zl'=4,'xh'=2,'xl'=2,'c'=2] {'ya','yb'}, dimensions={0} | all-to-all | bytes 589824 | tf_op jit(solution)/shard_map/all_to_all | solution.py:197
  164.1 6.5 %collective-permute-start.5 = (bf16[128,256]{1,0:T(8,128)(2,1)S(1)}, bf16[128,256]{1,0:T(8,128)(2,1)S(1)}, u32[]{:S(2)}, u32[]{:S(2)}) collective-permute-start(bf16[128,256]{1,0:T(8,128)(2,1)S(1)} %merge.1.own), channel_id=1, source_target_pairs={{0,1},{1,0},{2,3},{3,2},{4,5},{5,4},{6,7},{7,6},{8,9},{9,8},{10,11... | collective-permute-start | bytes 196616 | tf_op jit(solution)/shard_map/ppermute | solution.py:34
  171.5 1.3 copy-done
  173.3 20.2 %all_to_all.43.got = bf16[4,4,160,256]{3,2,1,0:T(8,128)(2,1)S(1)} all-to-all(bf16[4,4,160,256]{3,2,1,0:T(8,128)(2,1)S(1)} %partial.1), channel_id=1, replica_groups=mesh['ya'=2,'yb'=2,'yc'=2,'zh'=2,'zl'=4,'xh'=2,'xl'=2,'c'=2] {'xh','xl'}, dimensions={0} | all-to-all | bytes 2621440 | tf_op jit(solution)/shard_map/all_to_all | solution.py:197
  193.7 13.1 %all_to_all.44 = bf16[4,160,256]{2,1,0:T(8,128)(2,1)S(1)} all-to-all(bf16[4,160,256]{2,1,0:T(8,128)(2,1)S(1)} %along_x.1), channel_id=1, replica_groups=mesh['ya'=2,'yb'=2,'yc'=2,'zh'=2,'zl'=4,'xh'=2,'xl'=2,'c'=2] {'zl'}, dimensions={0} | all-to-all | bytes 655360 | tf_op jit(solution)/shard_map/all_to_all | solution.py:197
  206.8 1.6 fusion.11
  (66 shorter events, 9.6 us)
Async XLA Ops:
  7.2 20.4 %copy-start.2 = (bf16[256,160]{0,1:T(8,128)(2,1)S(1)}, bf16[256,160]{0,1:T(8,128)(2,1)}, u32[]{:S(2)}) copy-start(bf16[256,160]{0,1:T(8,128)(2,1)} %param.8) | copy-start | bytes 245764
  7.2 34.7 %copy-start.3 = (bf16[128,320]{0,1:T(8,128)(2,1)S(1)}, bf16[128,320]{0,1:T(8,128)(2,1)}, u32[]{:S(2)}) copy-start(bf16[128,320]{0,1:T(8,128)(2,1)} %param.15) | copy-start | bytes 245764
  7.2 43.1 %copy-start.4 = (f32[4,3,160]{2,0,1:T(4,128)S(1)}, f32[4,3,160]{2,0,1:T(4,128)}, u32[]{:S(2)}) copy-start(f32[4,3,160]{2,0,1:T(4,128)} %param.11) | copy-start | bytes 23044
  7.2 43.2 %copy-start.5 = (s32[256]{0:T(256)S(1)}, s32[256]{0:T(256)}, u32[]{:S(2)}) copy-start(s32[256]{0:T(256)} %param.9) | copy-start | bytes 3076
  7.2 86.1 %all-gather.7.cloned.1.call-start = ((), (), s32[]{:S(2)}) async-start(), calls=%async_computation.8 | async-start | bytes 4423680 | tf_op jit(solution)/shard_map/all_gather | solution.py:215
  28.3 22.6 %all-to-all-start = ((f32[32,8,128]{2,1,0:T(8,128)}), f32[32,8,128]{2,1,0:T(8,128)S(1)}, u32[]{:S(2)}, u32[]{:S(2)}) async-start(f32[32,8,128]{2,1,0:T(8,128)} %broadcast_in_dim.14), calls=%async_computation | async-start | bytes 262144 | tf_op jit(solution)/shard_map/all_to_all | solution.py:197
  50.8 15.1 %copy-start.1 = (f32[480,256]{1,0:T(8,128)}, f32[480,256]{1,0:T(8,128)S(1)}, u32[]{:S(2)}) copy-start(f32[480,256]{1,0:T(8,128)S(1)} %convolution_bitcast_fusion) | copy-start | bytes 1474564
  66.1 25.0 %copy-start.6 = (s32[3,256]{1,0:T(4,128)S(1)}, s32[3,256]{1,0:T(4,128)}, u32[]{:S(2)}) copy-start(s32[3,256]{1,0:T(4,128)} %param.10) | copy-start | bytes 9220
  85.2 8.1 %collective-permute-start = (bf16[4,4,160,256]{3,2,1,0:T(8,128)(2,1)S(1)}, bf16[4,4,160,256]{3,2,1,0:T(8,128)(2,1)S(1)}, u32[]{:S(2)}, u32[]{:S(2)}) collective-permute-start(bf16[4,4,160,256]{3,2,1,0:T(8,128)(2,1)S(1)} %all_to_all.41.mine), channel_id=1, source_target_pairs={{0,1},{1,0},{2,3},{3,2},{4,5},{5,4},{6,7},{7,6},{8,9},{9,8},{10,11... | collective-permute-start | bytes 3932168 | tf_op jit(solution)/shard_map/ppermute | solution.py:34
  93.3 18.8 %copy-start.7 = (f32[128]{0:T(128)S(1)}, f32[128]{0:T(128)}, u32[]{:S(2)}) copy-start(f32[128]{0:T(128)} %param.14) | copy-start | bytes 1540
  97.5 20.0 %copy-start.8 = (f32[128]{0:T(128)S(1)}, f32[128]{0:T(128)}, u32[]{:S(2)}) copy-start(f32[128]{0:T(128)} %param.13) | copy-start | bytes 1540
  97.5 13.8 %all-to-all-start.3 = ((f32[32,8,128]{2,1,0:T(8,128)}), f32[32,8,128]{2,1,0:T(8,128)S(1)}, u32[]{:S(2)}, u32[]{:S(2)}) async-start(f32[32,8,128]{2,1,0:T(8,128)} %get-tuple-element.28), calls=%async_computation.3 | async-start | bytes 262144 | tf_op jit(solution)/shard_map/all_to_all | solution.py:197
  102.8 48.2 %all-gather.9.cloned.1.call-start = ((), (), s32[]{:S(2)}) async-start(), calls=%async_computation.9 | async-start | bytes 1474560 | tf_op jit(solution)/shard_map/all_gather | solution.py:268
  102.9 3.2 %collective-permute-start.1 = (bf16[2,160,128]{2,1,0:T(8,128)(2,1)S(1)}, bf16[2,160,128]{2,1,0:T(8,128)(2,1)S(1)}, u32[]{:S(2)}, u32[]{:S(2)}) collective-permute-start(bf16[2,160,128]{2,1,0:T(8,128)(2,1)S(1)} %get-tuple-element.29), channel_id=1, source_target_pairs={{0,1},{1,0},{2,3},{3,2},{4,5},{5,4},{6,7},{7,6},{8,9},{9,8},{10,11... | collective-permute-start | bytes 245768 | tf_op jit(solution)/shard_map/ppermute | solution.py:34
  113.2 24.5 %all-to-all-start.4 = ((bf16[4,272,256]{2,1,0:T(8,128)(2,1)}), bf16[4,272,256]{2,1,0:T(8,128)(2,1)S(1)}, u32[]{:S(2)}, u32[]{:S(2)}) async-start(bf16[4,272,256]{2,1,0:T(8,128)(2,1)} %get-tuple-element.38), calls=%async_computation.4 | async-start | bytes 1114112 | tf_op jit(solution)/shard_map/all_to_all | solution.py:197
  117.7 15.4 %collective-permute-start.2 = (bf16[144,256]{1,0:T(8,128)(2,1)S(1)}, bf16[144,256]{1,0:T(8,128)(2,1)S(1)}, u32[]{:S(2)}, u32[]{:S(2)}) collective-permute-start(bf16[144,256]{1,0:T(8,128)(2,1)S(1)} %queries.1.q0), channel_id=1, source_target_pairs={{0,128},{128,256},{256,384},{384,0},{1,129},{129,257},{257,385},{3... | collective-permute-start | bytes 221192 | tf_op jit(solution)/shard_map/ppermute | solution.py:34
  122.3 10.8 %collective-permute-start.3 = (bf16[144,256]{1,0:T(8,128)(2,1)S(1)}, bf16[144,256]{1,0:T(8,128)(2,1)S(1)}, u32[]{:S(2)}, u32[]{:S(2)}) collective-permute-start(bf16[144,256]{1,0:T(8,128)(2,1)S(1)} %queries.1.q0), channel_id=1, source_target_pairs={{0,384},{128,0},{256,128},{384,256},{1,385},{129,1},{257,129},{385... | collective-permute-start | bytes 221192 | tf_op jit(solution)/shard_map/ppermute | solution.py:34
  125.1 12.5 %collective-permute-start.4 = (bf16[144,256]{1,0:T(8,128)(2,1)S(1)}, bf16[144,256]{1,0:T(8,128)(2,1)S(1)}, u32[]{:S(2)}, u32[]{:S(2)}) collective-permute-start(bf16[144,256]{1,0:T(8,128)(2,1)S(1)} %queries.1.q0), channel_id=1, source_target_pairs={{0,256},{128,384},{256,0},{384,128},{1,257},{129,385},{257,1},{385... | collective-permute-start | bytes 221192 | tf_op jit(solution)/shard_map/ppermute | solution.py:34
  164.1 7.4 %collective-permute-start.5 = (bf16[128,256]{1,0:T(8,128)(2,1)S(1)}, bf16[128,256]{1,0:T(8,128)(2,1)S(1)}, u32[]{:S(2)}, u32[]{:S(2)}) collective-permute-start(bf16[128,256]{1,0:T(8,128)(2,1)S(1)} %merge.1.own), channel_id=1, source_target_pairs={{0,1},{1,0},{2,3},{3,2},{4,5},{5,4},{6,7},{7,6},{8,9},{9,8},{10,11... | collective-permute-start | bytes 196616 | tf_op jit(solution)/shard_map/ppermute | solution.py:34
  171.5 1.3 copy-start
Sparse Core Ops, SparseCore 0:
  26.7 59.2 all-gather.6
  112.2 38.8 all-gather.8

commit v14 on v13

--- a/solution.py
+++ b/solution.py
@@ -293,7 +293,6 @@
         scratch=[pltpu.VMEM((4, 256, 1024), F32)],
         name="attend",
     )
-    o_messages, wo_all = lax.optimization_barrier((o_messages, wo_all))
     own = call(
         merge_kernel, shaped((128, 256), BF16), [exchange(o_messages, ("ya", "yb"))], name="merge"
     )

time: 217 us -> 206 us (0.949)
  waiting for transfers between devices: 25.4 us -> 14.5 us
    all_gather x1, waiting for transfers between devices: 10.9 us -> 0.01 us  [body(): lax.all_gather(jnp.stack([wo_own, wo_other]), ('ya', 'yb', 'yc'), axis=0,...]
  transfers between devices with their start and end apart: 11 -> 11, of which waited for: 7 -> 6; matrix products, arithmetic and copies ran while one was open for 2% -> 2% of each run, Pallas kernels for 2% -> 2%
where the time goes in v14:
time: 206 us; the launch traced here: 203 us
  blocking collectives  107 us (52%)
  starting transfers between devices  51.5 us (25%)
  waiting for transfers between devices  14.5 us (7%)
  between operations  14.3 us (7%)
  Pallas kernels  8.58 us (4%)
  other arithmetic  4.1 us (2%)
  local copies, waits for them, and re-layouts  2.85 us (1%)
    all_to_all x5, blocking collectives, exchange(): return lax.all_to_all(value, axes, 0, 0, tiled=True)  79.2 us
    ppermute x6, starting transfers between devices, permute(): return lax.ppermute(value, axes, pairs)  28.3 us
    all_to_all x3, starting transfers between devices, exchange(): return lax.all_to_all(value, axes, 0, 0, tiled=True)  23.2 us
    all_gather x1, blocking collectives, body(): lax.all_gather(jnp.transpose(w_qkv, (1, 0, 2)), 'zh', axis=0, tiled=False)  19.3 us
    ppermute x6, waiting for transfers between devices, permute(): return lax.ppermute(value, axes, pairs)  9.13 us
    pallas_call x7, Pallas kernels, call(): pl.pallas_call(kernel, out_shape=out_shape, in_specs=specs, out_specs=jax...  8.58 us
    all_gather x1, blocking collectives, body(): wo_pair = lax.all_gather(w_out.T, 'zh', axis=0, tiled=False)  8.4 us
    all_to_all x3, waiting for transfers between devices, exchange(): return lax.all_to_all(value, axes, 0, 0, tiled=True)  5.33 us
  transfers between devices with their start and end apart: 11, of which 6 were waited for; matrix products, arithmetic and copies ran while one was open for 2% of the time, Pallas kernels for 2%

profile of v14, /device:TPU:1, one launch (start us, length us, event | category | flops | bytes accessed | tf_op | source)
XLA Modules:
  0.0 203.2 jit_solution(17029677532752207083)
XLA Ops:
  7.3 19.3 %all-gather.1 = bf16[6,320,128]{2,1,0:T(8,128)(2,1)} all-gather(bf16[3,320,128]{2,1,0:T(8,128)(2,1)} %bitcast.64), channel_id=3, replica_groups=mesh['ya'=2,'yb'=2,'yc'=2,'zh'=2,'zl'=4,'xh'=2,'xl'=2,'c'=2] {'zh'}, dimensions={0}, use_global_device_ids=true | all-gather | bytes 737280 | tf_op jit(solution)/shard_map/all_gather | solution.py:213
  28.3 13.6 %all-to-all-start = ((f32[32,8,128]{2,1,0:T(8,128)}), f32[32,8,128]{2,1,0:T(8,128)S(1)}, u32[]{:S(2)}, u32[]{:S(2)}) async-start(f32[32,8,128]{2,1,0:T(8,128)} %broadcast_in_dim.14), calls=%async_computation | async-start | bytes 262144 | tf_op jit(solution)/shard_map/all_to_all | solution.py:197
  41.9 8.4 %all-gather = bf16[640,128]{1,0:T(8,128)(2,1)S(1)} all-gather(bf16[320,128]{1,0:T(8,128)(2,1)S(1)} %bitcast.66), channel_id=2, replica_groups=mesh['ya'=2,'yb'=2,'yc'=2,'zh'=2,'zl'=4,'xh'=2,'xl'=2,'c'=2] {'zh'}, dimensions={0}, use_global_device_ids=true | all-gather | bytes 245760 | tf_op jit(solution)/shard_map/all_gather | solution.py:214
  51.0 15.0 %all_to_all.40 = bf16[4,160,256]{2,1,0:T(8,128)(2,1)S(1)} all-to-all(bf16[4,160,256]{2,1,0:T(8,128)(2,1)S(1)} %broadcast_in_dim.15), channel_id=1, replica_groups=mesh['ya'=2,'yb'=2,'yc'=2,'zh'=2,'zl'=4,'xh'=2,'xl'=2,'c'=2] {'zl'}, dimensions={0} | all-to-all | bytes 655360 | tf_op jit(solution)/shard_map/all_to_all | solution.py:197
  66.1 19.1 %all_to_all.41.mine = bf16[4,4,160,256]{3,2,1,0:T(8,128)(2,1)S(1)} all-to-all(bf16[4,4,160,256]{3,2,1,0:T(8,128)(2,1)S(1)} %broadcast_in_dim.32), channel_id=1, replica_groups=mesh['ya'=2,'yb'=2,'yc'=2,'zh'=2,'zl'=4,'xh'=2,'xl'=2,'c'=2] {'xh','xl'}, dimensions={0} | all-to-all | bytes 2621440 | tf_op jit(solution)/shard_map/all_to_all | solution.py:197
  85.2 5.4 %collective-permute-start = (bf16[4,4,160,256]{3,2,1,0:T(8,128)(2,1)S(1)}, bf16[4,4,160,256]{3,2,1,0:T(8,128)(2,1)S(1)}, u32[]{:S(2)}, u32[]{:S(2)}) collective-permute-start(bf16[4,4,160,256]{3,2,1,0:T(8,128)(2,1)S(1)} %all_to_all.41.mine), channel_id=1, source_target_pairs={{0,1},{1,0},{2,3},{3,2},{4,5},{5,4},{6,7},{7,6},{8,9},{9,8},{10,11... | collective-permute-start | bytes 3932168 | tf_op jit(solution)/shard_map/ppermute | solution.py:34
  91.8 1.5 collective-permute-done.theirs
  93.3 4.2 %project.1 = (f32[128,256]{1,0:T(8,128)S(1)}, f32[2,128,256]{2,1,0:T(8,128)S(1)}, f32[32,8,128]{2,1,0:T(8,128)}) custom-call(s32[2]{0:T(128)S(1)} %pad_add_fusion.at, bf16[4,4,160,256]{3,2,1,0:T(8,128)(2,1)S(1)} %all_to_all.41.mine, bf16[4,4,160,256]{3,2,1,0:T(8,128)(2,1)S(1)} %collective-permute-done.theirs, bf16[8,2,3,2,160,128]{5,4,3,2,1,0:T(8,128)(2,1)} %bitcast.60), custom_call_target="tpu_custom_call" | custom-call | flops 1006632960 | bytes 6291456 | tf_op jit(solution)/shard_map/project/pallas_call | solution.py:46
  97.5 5.3 %all-to-all-start.3 = ((f32[32,8,128]{2,1,0:T(8,128)}), f32[32,8,128]{2,1,0:T(8,128)S(1)}, u32[]{:S(2)}, u32[]{:S(2)}) async-start(f32[32,8,128]{2,1,0:T(8,128)} %get-tuple-element.26), calls=%async_computation.3 | async-start | bytes 262144 | tf_op jit(solution)/shard_map/all_to_all | solution.py:197
  102.9 2.1 %collective-permute-start.1 = (bf16[2,160,128]{2,1,0:T(8,128)(2,1)S(1)}, bf16[2,160,128]{2,1,0:T(8,128)(2,1)S(1)}, u32[]{:S(2)}, u32[]{:S(2)}) collective-permute-start(bf16[2,160,128]{2,1,0:T(8,128)(2,1)S(1)} %get-tuple-element.27), channel_id=1, source_target_pairs={{0,1},{1,0},{2,3},{3,2},{4,5},{5,4},{6,7},{7,6},{8,9},{9,8},{10,11... | collective-permute-start | bytes 245768 | tf_op jit(solution)/shard_map/ppermute | solution.py:34
  106.0 5.3 %all-to-all-done.3.got = f32[32,8,128]{2,1,0:T(8,128)S(1)} async-done(((f32[32,8,128]{2,1,0:T(8,128)}), f32[32,8,128]{2,1,0:T(8,128)S(1)}, u32[]{:S(2)}, u32[]{:S(2)}) %all-to-all-start.3) | async-done | bytes 131104 | tf_op jit(solution)/shard_map/all_to_all | solution.py:197
  113.2 4.3 %all-to-all-start.4 = ((bf16[4,272,256]{2,1,0:T(8,128)(2,1)}), bf16[4,272,256]{2,1,0:T(8,128)(2,1)S(1)}, u32[]{:S(2)}, u32[]{:S(2)}) async-start(bf16[4,272,256]{2,1,0:T(8,128)(2,1)} %get-tuple-element.36), calls=%async_computation.4 | async-start | bytes 1114112 | tf_op jit(solution)/shard_map/all_to_all | solution.py:197
  117.7 4.6 %collective-permute-start.2 = (bf16[144,256]{1,0:T(8,128)(2,1)S(1)}, bf16[144,256]{1,0:T(8,128)(2,1)S(1)}, u32[]{:S(2)}, u32[]{:S(2)}) collective-permute-start(bf16[144,256]{1,0:T(8,128)(2,1)S(1)} %queries.1.q0), channel_id=1, source_target_pairs={{0,128},{128,256},{256,384},{384,0},{1,129},{129,257},{257,385},{3... | collective-permute-start | bytes 221192 | tf_op jit(solution)/shard_map/ppermute | solution.py:34
  122.3 2.8 %collective-permute-start.3 = (bf16[144,256]{1,0:T(8,128)(2,1)S(1)}, bf16[144,256]{1,0:T(8,128)(2,1)S(1)}, u32[]{:S(2)}, u32[]{:S(2)}) collective-permute-start(bf16[144,256]{1,0:T(8,128)(2,1)S(1)} %queries.1.q0), channel_id=1, source_target_pairs={{0,384},{128,0},{256,128},{384,256},{1,385},{129,1},{257,129},{385... | collective-permute-start | bytes 221192 | tf_op jit(solution)/shard_map/ppermute | solution.py:34
  125.1 6.8 %collective-permute-start.4 = (bf16[144,256]{1,0:T(8,128)(2,1)S(1)}, bf16[144,256]{1,0:T(8,128)(2,1)S(1)}, u32[]{:S(2)}, u32[]{:S(2)}) collective-permute-start(bf16[144,256]{1,0:T(8,128)(2,1)S(1)} %queries.1.q0), channel_id=1, source_target_pairs={{0,256},{128,384},{256,0},{384,128},{1,257},{129,385},{257,1},{385... | collective-permute-start | bytes 221192 | tf_op jit(solution)/shard_map/ppermute | solution.py:34
  131.9 1.2 collective-permute-done.2.q1
  133.1 4.5 %collective-permute-done.4.q3 = bf16[144,256]{1,0:T(8,128)(2,1)S(1)} collective-permute-done((bf16[144,256]{1,0:T(8,128)(2,1)S(1)}, bf16[144,256]{1,0:T(8,128)(2,1)S(1)}, u32[]{:S(2)}, u32[]{:S(2)}) %collective-permute-start.4) | collective-permute-done | bytes 73760 | tf_op jit(solution)/shard_map/ppermute | solution.py:34
  137.7 2.5 %attend.1 = bf16[4,144,256]{2,1,0:T(8,128)(2,1)S(1)} custom-call(s32[2]{0:T(128)S(1)} %pad_add_fusion.at, bf16[144,256]{1,0:T(8,128)(2,1)S(1)} %queries.1.q0, bf16[144,256]{1,0:T(8,128)(2,1)S(1)} %collective-permute-done.2.q1, bf16[144,256]{1,0:T(8,128)(2,1)S(1)} %collective-permute-done.3.q2, bf16[144,256]{1,0:T(8,128)(2,1)S(1)} %collective-permute-done.4.q3, ...), custom_call_target="tpu_custom_call" | custom-call | tf_op jit(solution)/shard_map/attend/pallas_call | solution.py:46
  140.2 14.0 %all_to_all.42.got = bf16[4,144,256]{2,1,0:T(8,128)(2,1)S(1)} all-to-all(bf16[4,144,256]{2,1,0:T(8,128)(2,1)S(1)} %attend.1), channel_id=1, replica_groups=mesh['ya'=2,'yb'=2,'yc'=2,'zh'=2,'zl'=4,'xh'=2,'xl'=2,'c'=2] {'ya','yb'}, dimensions={0} | all-to-all | bytes 589824 | tf_op jit(solution)/shard_map/all_to_all | solution.py:197
  154.2 6.5 %collective-permute-start.5 = (bf16[128,256]{1,0:T(8,128)(2,1)S(1)}, bf16[128,256]{1,0:T(8,128)(2,1)S(1)}, u32[]{:S(2)}, u32[]{:S(2)}) collective-permute-start(bf16[128,256]{1,0:T(8,128)(2,1)S(1)} %merge.1.own), channel_id=1, source_target_pairs={{0,1},{1,0},{2,3},{3,2},{4,5},{5,4},{6,7},{7,6},{8,9},{9,8},{10,11... | collective-permute-start | bytes 196616 | tf_op jit(solution)/shard_map/ppermute | solution.py:34
  161.7 1.3 copy-done
  163.5 19.9 %all_to_all.43.got = bf16[4,4,160,256]{3,2,1,0:T(8,128)(2,1)S(1)} all-to-all(bf16[4,4,160,256]{3,2,1,0:T(8,128)(2,1)S(1)} %partial.1), channel_id=1, replica_groups=mesh['ya'=2,'yb'=2,'yc'=2,'zh'=2,'zl'=4,'xh'=2,'xl'=2,'c'=2] {'xh','xl'}, dimensions={0} | all-to-all | bytes 2621440 | tf_op jit(solution)/shard_map/all_to_all | solution.py:197
  183.6 11.2 %all_to_all.44 = bf16[4,160,256]{2,1,0:T(8,128)(2,1)S(1)} all-to-all(bf16[4,160,256]{2,1,0:T(8,128)(2,1)S(1)} %along_x.1), channel_id=1, replica_groups=mesh['ya'=2,'yb'=2,'yc'=2,'zh'=2,'zl'=4,'xh'=2,'xl'=2,'c'=2] {'zl'}, dimensions={0} | all-to-all | bytes 655360 | tf_op jit(solution)/shard_map/all_to_all | solution.py:197
  194.8 1.6 fusion.11
  (66 shorter events, 8.4 us)
Async XLA Ops:
  7.2 20.4 %copy-start.2 = (bf16[256,160]{0,1:T(8,128)(2,1)S(1)}, bf16[256,160]{0,1:T(8,128)(2,1)}, u32[]{:S(2)}) copy-start(bf16[256,160]{0,1:T(8,128)(2,1)} %param.8) | copy-start | bytes 245764
  7.2 34.7 %copy-start.3 = (bf16[128,320]{0,1:T(8,128)(2,1)S(1)}, bf16[128,320]{0,1:T(8,128)(2,1)}, u32[]{:S(2)}) copy-start(bf16[128,320]{0,1:T(8,128)(2,1)} %param.15) | copy-start | bytes 245764
  7.2 43.1 %copy-start.4 = (f32[4,3,160]{2,0,1:T(4,128)S(1)}, f32[4,3,160]{2,0,1:T(4,128)}, u32[]{:S(2)}) copy-start(f32[4,3,160]{2,0,1:T(4,128)} %param.11) | copy-start | bytes 23044
  7.2 43.2 %copy-start.5 = (s32[256]{0:T(256)S(1)}, s32[256]{0:T(256)}, u32[]{:S(2)}) copy-start(s32[256]{0:T(256)} %param.9) | copy-start | bytes 3076
  7.2 86.1 %all-gather.7.cloned.1.call-start = ((), (), s32[]{:S(2)}) async-start(), calls=%async_computation.8 | async-start | bytes 4423680 | tf_op jit(solution)/shard_map/all_gather | solution.py:215
  28.3 22.6 %all-to-all-start = ((f32[32,8,128]{2,1,0:T(8,128)}), f32[32,8,128]{2,1,0:T(8,128)S(1)}, u32[]{:S(2)}, u32[]{:S(2)}) async-start(f32[32,8,128]{2,1,0:T(8,128)} %broadcast_in_dim.14), calls=%async_computation | async-start | bytes 262144 | tf_op jit(solution)/shard_map/all_to_all | solution.py:197
  50.8 15.1 %copy-start.1 = (f32[480,256]{1,0:T(8,128)}, f32[480,256]{1,0:T(8,128)S(1)}, u32[]{:S(2)}) copy-start(f32[480,256]{1,0:T(8,128)S(1)} %convolution_bitcast_fusion) | copy-start | bytes 1474564
  66.1 25.0 %copy-start.6 = (s32[3,256]{1,0:T(4,128)S(1)}, s32[3,256]{1,0:T(4,128)}, u32[]{:S(2)}) copy-start(s32[3,256]{1,0:T(4,128)} %param.10) | copy-start | bytes 9220
  85.2 8.1 %collective-permute-start = (bf16[4,4,160,256]{3,2,1,0:T(8,128)(2,1)S(1)}, bf16[4,4,160,256]{3,2,1,0:T(8,128)(2,1)S(1)}, u32[]{:S(2)}, u32[]{:S(2)}) collective-permute-start(bf16[4,4,160,256]{3,2,1,0:T(8,128)(2,1)S(1)} %all_to_all.41.mine), channel_id=1, source_target_pairs={{0,1},{1,0},{2,3},{3,2},{4,5},{5,4},{6,7},{7,6},{8,9},{9,8},{10,11... | collective-permute-start | bytes 3932168 | tf_op jit(solution)/shard_map/ppermute | solution.py:34
  93.3 18.8 %copy-start.7 = (f32[128]{0:T(128)S(1)}, f32[128]{0:T(128)}, u32[]{:S(2)}) copy-start(f32[128]{0:T(128)} %param.14) | copy-start | bytes 1540
  97.5 20.0 %copy-start.8 = (f32[128]{0:T(128)S(1)}, f32[128]{0:T(128)}, u32[]{:S(2)}) copy-start(f32[128]{0:T(128)} %param.13) | copy-start | bytes 1540
  97.5 13.8 %all-to-all-start.3 = ((f32[32,8,128]{2,1,0:T(8,128)}), f32[32,8,128]{2,1,0:T(8,128)S(1)}, u32[]{:S(2)}, u32[]{:S(2)}) async-start(f32[32,8,128]{2,1,0:T(8,128)} %get-tuple-element.26), calls=%async_computation.3 | async-start | bytes 262144 | tf_op jit(solution)/shard_map/all_to_all | solution.py:197
  102.8 58.9 %all-gather.9.cloned.1.call-start = ((), (), s32[]{:S(2)}) async-start(), calls=%async_computation.9 | async-start | bytes 1474560 | tf_op jit(solution)/shard_map/all_gather | solution.py:268
  102.9 3.2 %collective-permute-start.1 = (bf16[2,160,128]{2,1,0:T(8,128)(2,1)S(1)}, bf16[2,160,128]{2,1,0:T(8,128)(2,1)S(1)}, u32[]{:S(2)}, u32[]{:S(2)}) collective-permute-start(bf16[2,160,128]{2,1,0:T(8,128)(2,1)S(1)} %get-tuple-element.27), channel_id=1, source_target_pairs={{0,1},{1,0},{2,3},{3,2},{4,5},{5,4},{6,7},{7,6},{8,9},{9,8},{10,11... | collective-permute-start | bytes 245768 | tf_op jit(solution)/shard_map/ppermute | solution.py:34
  113.2 24.5 %all-to-all-start.4 = ((bf16[4,272,256]{2,1,0:T(8,128)(2,1)}), bf16[4,272,256]{2,1,0:T(8,128)(2,1)S(1)}, u32[]{:S(2)}, u32[]{:S(2)}) async-start(bf16[4,272,256]{2,1,0:T(8,128)(2,1)} %get-tuple-element.36), calls=%async_computation.4 | async-start | bytes 1114112 | tf_op jit(solution)/shard_map/all_to_all | solution.py:197
  117.7 15.4 %collective-permute-start.2 = (bf16[144,256]{1,0:T(8,128)(2,1)S(1)}, bf16[144,256]{1,0:T(8,128)(2,1)S(1)}, u32[]{:S(2)}, u32[]{:S(2)}) collective-permute-start(bf16[144,256]{1,0:T(8,128)(2,1)S(1)} %queries.1.q0), channel_id=1, source_target_pairs={{0,128},{128,256},{256,384},{384,0},{1,129},{129,257},{257,385},{3... | collective-permute-start | bytes 221192 | tf_op jit(solution)/shard_map/ppermute | solution.py:34
  122.3 10.8 %collective-permute-start.3 = (bf16[144,256]{1,0:T(8,128)(2,1)S(1)}, bf16[144,256]{1,0:T(8,128)(2,1)S(1)}, u32[]{:S(2)}, u32[]{:S(2)}) collective-permute-start(bf16[144,256]{1,0:T(8,128)(2,1)S(1)} %queries.1.q0), channel_id=1, source_target_pairs={{0,384},{128,0},{256,128},{384,256},{1,385},{129,1},{257,129},{385... | collective-permute-start | bytes 221192 | tf_op jit(solution)/shard_map/ppermute | solution.py:34
  125.1 12.5 %collective-permute-start.4 = (bf16[144,256]{1,0:T(8,128)(2,1)S(1)}, bf16[144,256]{1,0:T(8,128)(2,1)S(1)}, u32[]{:S(2)}, u32[]{:S(2)}) collective-permute-start(bf16[144,256]{1,0:T(8,128)(2,1)S(1)} %queries.1.q0), channel_id=1, source_target_pairs={{0,256},{128,384},{256,0},{384,128},{1,257},{129,385},{257,1},{385... | collective-permute-start | bytes 221192 | tf_op jit(solution)/shard_map/ppermute | solution.py:34
  154.2 7.4 %collective-permute-start.5 = (bf16[128,256]{1,0:T(8,128)(2,1)S(1)}, bf16[128,256]{1,0:T(8,128)(2,1)S(1)}, u32[]{:S(2)}, u32[]{:S(2)}) collective-permute-start(bf16[128,256]{1,0:T(8,128)(2,1)S(1)} %merge.1.own), channel_id=1, source_target_pairs={{0,1},{1,0},{2,3},{3,2},{4,5},{5,4},{6,7},{7,6},{8,9},{9,8},{10,11... | collective-permute-start | bytes 196616 | tf_op jit(solution)/shard_map/ppermute | solution.py:34
  161.7 1.3 copy-start
Sparse Core Ops, SparseCore 0:
  26.7 59.2 all-gather.6
  112.2 40.6 all-gather.8
